TPU v7x, 128 devices: a whole 4x4x4 slice. The times are simulated.
128 devices in a mesh: gz: 32 (over z_lo, y, x), ch: 4 (over z_hi, core).
Axes of the slice: x: 4, y: 4, z: 4 (z_hi: 2, z_lo: 2; z = z_hi * 2 + z_lo), core: 2. Of those that a mesh axis runs over, the one named last changes fastest.
Arguments:
- volume: bfloat16 [128, 64, 16, 128], P('ch', 'gz'), may hold values from -6 to 6
- weight: bfloat16 [27, 128, 128], replicated, may hold values from -0.109375 to 0.109375
- cotangent: bfloat16 [128, 64, 16, 128], P('ch', 'gz'), may hold values from -6 to 6
Outputs:
- output: bfloat16 [128, 64, 16, 128], P('ch', 'gz')
- input_grad: bfloat16 [128, 64, 16, 128], P('ch', 'gz')
- weight_grad: float32 [27, 128, 128], P(None, 'gz', 'ch')
All inputs are finite; a program needn't handle non-finite values.
Results may differ from a plain program's by a relative error of at most 0.023.
Values may be sent and summed in bfloat16 or wider, within the bound.
A program may use at most 128 MiB of HBM per device.

v0:
```python
import math

import jax
import jax.numpy as jnp
from jax import lax
from jax.sharding import PartitionSpec as P


def with_halo(shard, axis, dim):
    devices, length = lax.axis_size(axis), shard.shape[dim]
    up = [(i, i + 1) for i in range(devices - 1)]
    down = [(j, i) for i, j in up]
    last = lax.slice_in_dim(shard, length - 1, length, axis=dim)
    first = lax.slice_in_dim(shard, 0, 1, axis=dim)
    before = lax.ppermute(last, axis, up)
    after = lax.ppermute(first, axis, down)
    return jnp.concatenate([before, shard, after], axis=dim)


SAME_YX = ((0, 0), (1, 1), (1, 1))


def body(volume, weight, cotangent):
    in_local, planes_local, grid_rows, grid_cols = volume.shape
    out_local = cotangent.shape[0]
    groups = lax.axis_size("ch")
    my_group = lax.axis_index("ch")
    voxels = planes_local * lax.axis_size("gz") * grid_rows * grid_cols

    both = jnp.concatenate([volume, cotangent], axis=0)
    padded = with_halo(both, "gz", 1)
    gathered = lax.all_gather(padded, "ch", axis=0)
    planes = padded.shape[1]
    vol_full = gathered[:, :in_local].reshape(groups * in_local, planes, grid_rows, grid_cols)
    cot_full = gathered[:, in_local:].reshape(groups * out_local, planes, grid_rows, grid_cols)
    cin = vol_full.shape[0]
    cout = cot_full.shape[0]

    weight_cols = lax.dynamic_slice_in_dim(weight, my_group * out_local, out_local, 2)
    out = lax.conv_general_dilated(
        vol_full[None],
        weight_cols.reshape(3, 3, 3, cin, out_local),
        (1, 1, 1),
        SAME_YX,
        dimension_numbers=("NCDHW", "DHWIO", "NCDHW"),
        preferred_element_type=jnp.float32,
    )[0]

    weight_rows = lax.dynamic_slice_in_dim(weight, my_group * in_local, in_local, 1)
    flipped = jnp.swapaxes(weight_rows[::-1], 1, 2).reshape(3, 3, 3, cout, in_local)
    cot_padded = cot_full[None]
    in_grad = lax.conv_general_dilated(
        cot_padded,
        flipped,
        (1, 1, 1),
        SAME_YX,
        dimension_numbers=("NCDHW", "DHWIO", "NCDHW"),
        preferred_element_type=jnp.float32,
    )[0]

    wpart = lax.conv_general_dilated(
        vol_full[None],
        cotangent[None],
        (1, 1, 1),
        SAME_YX,
        dimension_numbers=("CNDHW", "IODHW", "NCDHW"),
        preferred_element_type=jnp.float32,
    )
    wpart = jnp.transpose(wpart, (2, 3, 4, 0, 1)).reshape(27, cin, out_local)
    wgrad = lax.psum_scatter(wpart, "gz", scatter_dimension=1, tiled=True)
    wgrad = wgrad * jnp.float32(1.0 / math.sqrt(voxels))
    return out.astype(jnp.bfloat16), in_grad.astype(jnp.bfloat16), wgrad


def solution(mesh):
    placed = P("ch", "gz", None, None)
    return jax.shard_map(
        body,
        mesh=mesh,
        in_specs=(placed, P(), placed),
        out_specs=(placed, placed, P(None, "gz", "ch")),
        check_vma=False,
    )
```

profile of v0, /device:TPU:0, one launch (start us, length us, event | category | flops | bytes accessed | tf_op | source)
XLA Modules:
  0.0 461.0 jit_solution(17572783929538806791)
XLA Ops:
  7.2 0.0 copy-start
  7.2 0.0 all-gather.3.cloned.1.call-start
  7.2 1.0 constant_dynamic-update-slice_fusion.1
  8.3 1.0 constant_dynamic-update-slice_fusion
  9.3 0.0 copy-start.5
  9.3 3.7 collective-permute-start
  13.0 1.3 collective-permute-start.1
  14.3 4.2 collective-permute-done
  18.5 4.1 collective-permute-done.1
  22.6 1.1 pad_maximum_fusion
  23.7 0.0 all-gather.3.cloned.1.call-update
  23.8 0.0 all-reduce.3.cloned.1.call-start
  23.8 0.0 copy-done
  23.9 0.7 rev.3
  24.6 0.0 copy-done.5
  24.6 2.6 copy.34
  27.1 0.0 copy-done.8
  27.1 0.6 dynamic-slice
  28.4 1.3 constant_dynamic-slice_fusion.1
  29.7 38.6 %all-gather.3.cloned.1.call-done = bf16[256,4,16,128]{3,2,1,0:T(8,128)(2,1)} async-done(((bf16[64,4,16,128]{3,2,1,0:T(8,128)(2,1)}), bf16[256,4,16,128]{3,2,1,0:T(8,128)(2,1)}) %all-gather.3.cloned.1.call-update) | async-done | bytes 4194320 | tf_op jit(solution)/shard_map/all_gather | solution.py:32
  68.2 5.0 %fusion.28 = (bf16[4,32,4,16,128]{4,3,2,1,0:T(8,128)(2,1)}, bf16[4,32,4,16,128]{4,3,2,1,0:T(8,128)(2,1)S(1)}) fusion(bf16[4,64,4,16,128]{4,3,2,1,0:T(8,128)(2,1)} %bitcast.48), kind=kLoop, calls=%fused_computation.33 | loop fusion | bytes 8388608 | tf_op jit(solution)/shard_map/slice | solution.py:35
  73.2 3.8 copy.40
  77.1 2.0 pad.clone
  79.1 0.0 copy-start.6
  79.1 0.0 copy-start.9
  79.1 0.6 copy.26
  79.7 0.1 slice.23
  79.7 0.5 copy-done.6
  80.2 0.0 copy-done.9
  80.2 8.0 %select_convert_fusion.1 = bf16[2,16,8,17,32]{4,2,3,1,0:T(8,128)(2,1)S(1)} fusion(bf16[3,3,3,128,32]{4,3,2,1,0:T(8,128)(2,1)S(1)} %bitcast.51, bf16[128,4,16,1,7,2]{0,4,5,2,1,3:T(8,128)(2,1)S(1)} %slice.23, bf16[128,4,16,1,8,17]{0,4,5,2,1,3:T(8,128)(2,1)S(1)} %copy.26, pred[8,17]{0,1:T(8,128)(4,1)S(1)} %copy-done.9), kind=kOutput, calls=%fused_computation.16 | convolution fusion | flops 930234368 | bytes 2957448 | tf_op jit(solution)/shard_map/conv_general_dilated | solution.py:40
  88.2 1.2 copy.28
  89.4 5.2 %copy.29 = bf16[128,4,16,1,128]{0,2,4,1,3:T(8,128)(2,1)} copy(bf16[128,4,16,1,128]{4,2,1,0,3:T(8,128)(2,1)} %bitcast.45) | data formatting | bytes 4194304 | tf_op jit(solution)/shard_map/broadcast_in_dim;reshape | solution.py:51
  94.5 2.0 pad.2
  96.5 0.6 copy.31
  97.1 1.4 copy-done.2
  98.5 0.8 slice.26
  99.2 5.0 %copy.33 = bf16[1,128,4,16,128]{1,0,4,3,2:T(2,128)(2,1)} copy(bf16[1,128,4,16,128]{4,3,2,1,0:T(8,128)(2,1)S(1)} %bitcast.42) | data formatting | bytes 4194304 | tf_op jit(solution)/shard_map/broadcast_in_dim;reshape | solution.py:41
  104.2 36.0 %fusion.30 = f32[3,3,3,128,32]{4,3,2,1,0:T(8,128)} fusion(bf16[1,128,4,16,128]{1,0,4,3,2:T(2,128)(2,1)} %copy.33, bf16[1,32,2,16,128]{1,0,4,3,2:T(2,128)(2,1)} %copy.34), kind=kOutput, calls=%fused_computation.35 | convolution fusion | flops 863698944 | bytes 2801664 | tf_op jit(solution)/shard_map/transpose | solution.py:69
  140.2 0.0 all-reduce.3.cloned.1.call-update
  140.3 10.0 %select_convert_fusion = bf16[2,16,8,17,32]{4,2,3,1,0:T(8,128)(2,1)} fusion(bf16[3,3,3,128,32]{3,4,2,1,0:T(8,128)(2,1)} %bitcast.52, bf16[128,4,16,1,7,2]{0,4,5,2,1,3:T(8,128)(2,1)S(1)} %copy-done.7, bf16[128,4,16,1,8,17]{0,4,5,2,1,3:T(8,128)(2,1)S(1)} %copy-done.3, pred[8,17]{0,1:T(8,128)(4,1)S(1)} %copy-done.10), kind=kOutput, calls=%fused_computation.15 | convolution fusion | flops 930234368 | bytes 2957448 | tf_op jit(solution)/shard_map/conv_general_dilated | solution.py:52
  150.2 0.0 copy-done.1
  150.2 0.2 slice_bitcast_fusion.1
  150.4 1.7 copy.36
  152.2 0.1 copy.32
  152.3 0.2 slice_bitcast_fusion
  152.5 1.7 copy.37
  154.2 298.4 %all-reduce.3.cloned.1.call-done = f32[27,128,32]{2,1,0:T(8,128)} async-done(((f32[27,128,32]{2,1,0:T(8,128)}), f32[27,128,32]{2,1,0:T(8,128)}) %all-reduce.3.cloned.1.call-update) | async-done | bytes 442384
  452.7 1.5 dynamic-slice_multiply_fusion
  (13 shorter events, 0.1 us)
Async XLA Ops:
  7.2 16.6 %copy-start = (bf16[27,128,128]{2,1,0:T(8,128)(2,1)S(1)}, bf16[27,128,128]{2,1,0:T(8,128)(2,1)}, u32[]{:S(2)}) copy-start(bf16[27,128,128]{2,1,0:T(8,128)(2,1)} %param.4) | copy-start | bytes 2654212
  7.2 61.1 %all-gather.3.cloned.1.call-start = ((), (), s32[]{:S(2)}) async-start(), calls=%async_computation | async-start | bytes 5242880 | tf_op jit(solution)/shard_map/all_gather | solution.py:32
  9.3 15.3 %copy-start.5 = (bf16[32,2,16,128]{3,2,1,0:T(8,128)(2,1)S(1)}, bf16[32,2,16,128]{3,2,1,0:T(8,128)(2,1)}, u32[]{:S(2)}) copy-start(bf16[32,2,16,128]{3,2,1,0:T(8,128)(2,1)} %param.5) | copy-start | bytes 786436
  9.3 9.2 %collective-permute-start = (bf16[64,1,16,128]{3,2,1,0:T(8,128)(2,1)S(1)}, bf16[64,1,16,128]{3,2,1,0:T(8,128)(2,1)S(1)}, u32[]{:S(2)}, u32[]{:S(2)}) collective-permute-start(bf16[64,1,16,128]{3,2,1,0:T(8,128)(2,1)S(1)} %get-tuple-element.11), channel_id=1, source_target_pairs={{0,4},{4,8},{8,12},{12,16},{16,20},{20,24},{24,28},{28,32},{32,36}... | collective-permute-start | bytes 786440 | tf_op jit(solution)/shard_map/ppermute | solution.py:15
  13.0 9.7 %collective-permute-start.1 = (bf16[64,1,16,128]{3,2,1,0:T(8,128)(2,1)S(1)}, bf16[64,1,16,128]{3,2,1,0:T(8,128)(2,1)S(1)}, u32[]{:S(2)}, u32[]{:S(2)}) collective-permute-start(bf16[64,1,16,128]{3,2,1,0:T(8,128)(2,1)S(1)} %get-tuple-element.12), channel_id=1, source_target_pairs={{4,0},{8,4},{12,8},{16,12},{20,16},{24,20},{28,24},{32,28},{36,32}... | collective-permute-start | bytes 786440 | tf_op jit(solution)/shard_map/ppermute | solution.py:16
  23.7 3.4 copy-start.8
  23.8 428.9 %all-reduce.3.cloned.1.call-start = ((), (), s32[]{:S(2)}) async-start(), calls=%async_computation.1 | async-start | bytes 3538944
  79.1 1.2 copy-start.6
  79.1 1.2 copy-start.9
  97.1 1.4 copy-start.2
  104.2 36.0 %copy-start.3 = (bf16[128,4,16,1,8,17]{0,4,5,2,1,3:T(8,128)(2,1)S(1)}, bf16[128,4,16,1,8,17]{0,4,5,2,1,3:T(8,128)(2,1)}, u32[]{:S(2)}) copy-start(bf16[128,4,16,1,8,17]{0,4,5,2,1,3:T(8,128)(2,1)} %copy-done.2) | copy-start | bytes 6684676
  104.2 36.0 %copy-start.7 = (bf16[128,4,16,1,7,2]{0,4,5,2,1,3:T(8,128)(2,1)S(1)}, bf16[128,4,16,1,7,2]{0,4,5,2,1,3:T(8,128)(2,1)}, u32[]{:S(2)}) copy-start(bf16[128,4,16,1,7,2]{0,4,5,2,1,3:T(8,128)(2,1)} %slice.26) | copy-start | bytes 688132
  104.2 36.0 %copy-start.10 = (pred[8,17]{0,1:T(8,128)(4,1)S(1)}, pred[8,17]{0,1:T(8,128)(4,1)}, u32[]{:S(2)}) copy-start(pred[8,17]{0,1:T(8,128)(4,1)} %constant.22) | copy-start | bytes 412
  140.3 10.0 %copy-start.1 = (bf16[2,16,8,17,32]{4,1,3,2,0:T(8,128)(2,1)S(1)}, bf16[2,16,8,17,32]{4,1,3,2,0:T(8,128)(2,1)}, u32[]{:S(2)}) copy-start(bf16[2,16,8,17,32]{4,1,3,2,0:T(8,128)(2,1)} %copy.28) | copy-start | bytes 835588
  150.2 1.9 copy-start.4
Sparse Core Ops, SparseCore 0:
  23.9 44.3 all-gather.2
  140.3 312.2 all-reduce.2
where the time goes:
time: 461 us
  waiting for transfers between devices  345 us (75%)
  matrix products  53.9 us (12%)
  local copies, waits for them, and re-layouts  39.2 us (9%)
  between operations  14.9 us (3%)
  starting transfers between devices  5.03 us (1%)
    unnamed x3, waiting for transfers between devices  298 us
    all_gather x1, waiting for transfers between devices, body(): gathered = lax.all_gather(padded, 'ch', axis=0)  38.6 us
    transpose x1, matrix products, body(): wpart = jnp.transpose(wpart, (2, 3, 4, 0, 1)).reshape(27, cin, out_local)  36 us
    unnamed x27, local copies, waits for them, and re-layouts  10.9 us
    conv_general_dilated x1, matrix products, body(): lax.conv_general_dilated(cot_padded, flipped, (1, 1, 1), SAME_YX, dimensi...  9.97 us
  transfers between devices with their start and end apart: 4, of which 4 were waited for; matrix products, arithmetic and copies ran while one was open for 4% of the time, Pallas kernels for 0%

commit v1 on v0

v1 whole, which is shorter than its diff:
```python
import math

import jax
import jax.numpy as jnp
from jax import lax
from jax.sharding import PartitionSpec as P


def with_halo(shard, axis, dim):
    devices, length = lax.axis_size(axis), shard.shape[dim]
    up = [(i, i + 1) for i in range(devices - 1)]
    down = [(j, i) for i, j in up]
    last = lax.slice_in_dim(shard, length - 1, length, axis=dim)
    first = lax.slice_in_dim(shard, 0, 1, axis=dim)
    before = lax.ppermute(last, axis, up)
    after = lax.ppermute(first, axis, down)
    return jnp.concatenate([before, shard, after], axis=dim)


def shift_x(field, step):
    pads = [(0, 0, 0)] * (field.ndim - 1) + [(-step, step, 0)]
    return lax.pad(field, jnp.zeros((), field.dtype), pads)


def from_everyone(shard, axis):
    copies = jnp.broadcast_to(shard, (lax.axis_size(axis), *shard.shape))
    return lax.all_to_all(copies, axis, split_axis=0, concat_axis=0, tiled=True)


def conv_taps(padded, matrices, planes_local, grid_rows, flipped):
    summed = None
    for tap_z in range(3):
        for tap_y in range(3):
            for tap_x in range(3):
                low_z = 2 - tap_z if flipped else tap_z
                low_y = 2 - tap_y if flipped else tap_y
                step = 1 - tap_x if flipped else tap_x - 1
                segment = shift_x(
                    padded[:, low_z : low_z + planes_local, low_y : low_y + grid_rows, :], step
                )
                contrib = jnp.einsum(
                    "czyx,cd->dzyx",
                    segment,
                    matrices[9 * tap_z + 3 * tap_y + tap_x],
                    preferred_element_type=jnp.float32,
                )
                summed = contrib if summed is None else summed + contrib
    return summed


def weight_taps(vol_full, cotangent, planes_local):
    shifted = []
    for tap_y in range(3):
        for tap_x in range(3):
            rows = jnp.pad(cotangent, ((0, 0), (0, 0), (tap_y, 2 - tap_y), (0, 0)))
            shifted.append(shift_x(rows, 1 - tap_x))
    stack = jnp.stack(shifted, axis=0)
    parts = []
    for tap_z in range(3):
        slab = vol_full[:, tap_z : tap_z + planes_local]
        parts.append(
            jnp.einsum("izyx,tozyx->ito", slab, stack, preferred_element_type=jnp.float32)
        )
    return jnp.concatenate(parts, axis=1)


def body(volume, weight, cotangent):
    in_local, planes_local, grid_rows, grid_cols = volume.shape
    out_local = cotangent.shape[0]
    groups = lax.axis_size("ch")
    slabs = lax.axis_size("gz")
    my_group = lax.axis_index("ch")
    voxels = planes_local * slabs * grid_rows * grid_cols

    both = jnp.concatenate([volume, cotangent], axis=0)
    padded = with_halo(both, "gz", 1)
    padded = jnp.pad(padded, ((0, 0), (0, 0), (1, 1), (0, 0)))
    gathered = from_everyone(padded, "ch")
    vol_full = gathered[:, :in_local].reshape(groups * in_local, *padded.shape[1:])
    cot_full = gathered[:, in_local:].reshape(groups * out_local, *padded.shape[1:])
    cin = vol_full.shape[0]

    wpart = weight_taps(vol_full, cotangent, planes_local).astype(jnp.bfloat16)
    blocks = wpart.reshape(slabs, cin // slabs, *wpart.shape[1:])
    arrived = lax.all_to_all(blocks, "gz", split_axis=0, concat_axis=0, tiled=True)
    wgrad = arrived.astype(jnp.float32).sum(axis=0)
    wgrad = jnp.transpose(wgrad, (1, 0, 2)) * jnp.float32(1.0 / math.sqrt(voxels))

    weight_cols = lax.dynamic_slice_in_dim(weight, my_group * out_local, out_local, 2)
    out = conv_taps(vol_full, weight_cols, planes_local, grid_rows, False)
    weight_rows = lax.dynamic_slice_in_dim(weight, my_group * in_local, in_local, 1)
    in_grad = conv_taps(
        cot_full, jnp.swapaxes(weight_rows, 1, 2), planes_local, grid_rows, True
    )
    return out.astype(jnp.bfloat16), in_grad.astype(jnp.bfloat16), wgrad


def solution(mesh):
    placed = P("ch", "gz", None, None)
    return jax.shard_map(
        body,
        mesh=mesh,
        in_specs=(placed, P(), placed),
        out_specs=(placed, placed, P(None, "gz", "ch")),
        check_vma=False,
    )
```

time: 461 us -> 181 us (0.39)
  waiting for transfers between devices: 345 us -> 55.9 us
  starting transfers between devices: 5.03 us -> 21.2 us
  between operations: 14.9 us -> 0.95 us
  matrix products: 53.9 us -> 59.2 us
    unnamed x3 -> x0, waiting for transfers between devices: 298 us -> none
    dot_general x0 -> x57, matrix products: none -> 59.2 us  [the longest x54 49.1 us: conv_taps(): jnp.einsum('czyx,cd->dzyx', segment, matrices[9 * tap_z + 3 * tap_y + tap...]
    all_to_all x0 -> x2, waiting for transfers between devices: none -> 47.5 us  [the longest x1 47.5 us: from_everyone(): return lax.all_to_all(copies, axis, split_axis=0, concat_axis=0, tiled=True)]
    all_gather x1 -> x0, waiting for transfers between devices: 38.6 us -> none  [body(): gathered = lax.all_gather(padded, 'ch', axis=0)]
    transpose x1 -> x0, matrix products: 36 us -> none  [body(): wpart = jnp.transpose(wpart, (2, 3, 4, 0, 1)).reshape(27, cin, out_local)]
    conv_general_dilated x2 -> x0, matrix products: 17.9 us -> none  [the longest x1 9.97 us: body(): lax.conv_general_dilated(cot_padded, flipped, (1, 1, 1), SAME_YX, dimensi...]
    all_to_all x0 -> x2, starting transfers between devices: none -> 16.3 us  [the longest x1 11.1 us: body(): lax.all_to_all(blocks, 'gz', split_axis=0, concat_axis=0, tiled=True)]
    another operation x4, local copies, waits for them, and re-layouts: 14.1 us -> 5.56 us  [the longest x2 7.11 us: body(): cot_padded = cot_full[None]]
  transfers between devices with their start and end apart: 4 -> 4, of which waited for: 4 -> 3; matrix products, arithmetic and copies ran while one was open for 4% -> 12% of each run, Pallas kernels for 0% -> 0%
where the time goes in v1:
time: 181 us; the launch traced here: 179 us
  matrix products  59.2 us (33%)
  waiting for transfers between devices  55.9 us (31%)
  local copies, waits for them, and re-layouts  38.2 us (21%)
  starting transfers between devices  21.2 us (12%)
  other arithmetic  3.73 us (2%)
    dot_general x54, matrix products, conv_taps(): jnp.einsum('czyx,cd->dzyx', segment, matrices[9 * tap_z + 3 * tap_y + tap...  49.1 us
    all_to_all x1, waiting for transfers between devices, from_everyone(): return lax.all_to_all(copies, axis, split_axis=0, concat_axis=0, tiled=True)  47.5 us
    unnamed x43, local copies, waits for them, and re-layouts  15.9 us
    all_to_all x1, starting transfers between devices, body(): lax.all_to_all(blocks, 'gz', split_axis=0, concat_axis=0, tiled=True)  11.1 us
    dot_general x3, matrix products, weight_taps(): jnp.einsum('izyx,tozyx->ito', slab, stack, preferred_element_type=jnp.flo...  10.1 us
    slice x2, local copies, waits for them, and re-layouts, conv_taps(): padded[:, low_z:low_z + planes_local, low_y:low_y + grid_rows, :]  7.4 us
    all_to_all x1, starting transfers between devices, from_everyone(): return lax.all_to_all(copies, axis, split_axis=0, concat_axis=0, tiled=True)  5.28 us
    another operation x3, local copies, waits for them, and re-layouts  4.68 us
  transfers between devices with their start and end apart: 4, of which 3 were waited for; matrix products, arithmetic and copies ran while one was open for 12% of the time, Pallas kernels for 0%

profile of v1, /device:TPU:0, one launch (start us, length us, event | category | flops | bytes accessed | tf_op | source)
XLA Modules:
  0.0 179.1 jit_solution(7670291532983723073)
XLA Ops:
  0.6 1.0 constant_dynamic-update-slice_fusion.1
  2.7 3.5 %collective-permute-start = (bf16[64,1,16,128]{3,2,1,0:T(8,128)(2,1)S(1)}, bf16[64,1,16,128]{3,2,1,0:T(8,128)(2,1)S(1)}, u32[]{:S(2)}, u32[]{:S(2)}) collective-permute-start(bf16[64,1,16,128]{3,2,1,0:T(8,128)(2,1)S(1)} %get-tuple-element.32), channel_id=1, source_target_pairs={{0,4},{4,8},{8,12},{12,16},{16,20},{20,24},{24,28},{28,32},{32,36}... | collective-permute-start | bytes 786440 | tf_op jit(solution)/shard_map/ppermute | solution.py:15
  6.3 1.3 collective-permute-start.1
  7.6 4.2 %collective-permute-done = bf16[64,1,16,128]{3,2,1,0:T(8,128)(2,1)S(1)} collective-permute-done((bf16[64,1,16,128]{3,2,1,0:T(8,128)(2,1)S(1)}, bf16[64,1,16,128]{3,2,1,0:T(8,128)(2,1)S(1)}, u32[]{:S(2)}, u32[]{:S(2)}) %collective-permute-start) | collective-permute-done | bytes 262176 | tf_op jit(solution)/shard_map/ppermute | solution.py:15
  11.8 4.1 %collective-permute-done.1 = bf16[64,1,16,128]{3,2,1,0:T(8,128)(2,1)S(1)} collective-permute-done((bf16[64,1,16,128]{3,2,1,0:T(8,128)(2,1)S(1)}, bf16[64,1,16,128]{3,2,1,0:T(8,128)(2,1)S(1)}, u32[]{:S(2)}, u32[]{:S(2)}) %collective-permute-start.1) | collective-permute-done | bytes 262176 | tf_op jit(solution)/shard_map/ppermute | solution.py:16
  16.9 3.4 %broadcast_in_dim.3 = bf16[4,64,4,18,128]{4,1,3,2,0:T(8,128)(2,1)} broadcast(bf16[64,4,18,128]{3,0,2,1:T(8,128)(2,1)S(1)} %pad.166.clone), dimensions={1,2,3,4} | broadcast | bytes 5898240 | tf_op jit(solution)/shard_map/broadcast_in_dim | solution.py:26
  20.3 5.3 %all-to-all-start = ((bf16[4,64,4,18,128]{4,1,3,2,0:T(8,128)(2,1)}), bf16[4,64,4,18,128]{4,1,3,2,0:T(8,128)(2,1)}, u32[]{:S(2)}, u32[]{:S(2)}) async-start(bf16[4,64,4,18,128]{4,1,3,2,0:T(8,128)(2,1)} %broadcast_in_dim.3), calls=%async_computation | async-start | bytes 9437184 | tf_op jit(solution)/shard_map/all_to_all | solution.py:27
  33.4 47.5 %all-to-all-done = bf16[4,64,4,18,128]{4,1,3,2,0:T(8,128)(2,1)} async-done(((bf16[4,64,4,18,128]{4,1,3,2,0:T(8,128)(2,1)}), bf16[4,64,4,18,128]{4,1,3,2,0:T(8,128)(2,1)}, u32[]{:S(2)}, u32[]{:S(2)}) %all-to-all-start) | async-done | bytes 4718624 | tf_op jit(solution)/shard_map/all_to_all | solution.py:27
  80.9 3.3 %fusion.106 = (bf16[4,32,4,18,128]{4,1,3,2,0:T(8,128)(2,1)S(1)}, bf16[4,32,4,18,128]{4,1,3,2,0:T(8,128)(2,1)S(1)}) fusion(bf16[4,64,4,18,128]{4,1,3,2,0:T(8,128)(2,1)} %all-to-all-done), kind=kLoop, calls=%fused_computation.267 | loop fusion | bytes 9437184 | tf_op jit(solution)/shard_map/slice | solution.py:80
  85.0 3.5 %fusion.108 = (bf16[128,2,16,128]{3,0,2,1:T(8,128)(2,1)}, bf16[128,2,16,128]{3,0,2,1:T(8,128)(2,1)}, bf16[128,2,16,128]{3,0,2,1:T(8,128)(2,1)}, bf16[128,2,16,12...) fusion(bf16[128,4,18,128]{3,0,2,1:T(8,128)(2,1)S(1)} %bitcast.518), kind=kLoop, calls=%fused_computation.269 | loop fusion | bytes 18874368 | tf_op jit(solution)/shard_map/slice | solution.py:39
  88.5 3.6 %fusion.10 = bf16[128,9,32]{0,2,1:T(8,128)(2,1)} fusion(bf16[9,32,2,18,128]{4,1,3,0,2:T(8,128)(2,1)} %fusion.24, bf16[128,4,18,128]{3,0,2,1:T(8,128)(2,1)S(1)} %bitcast.519), kind=kOutput, calls=%fused_computation.102 | convolution fusion | flops 339775488 | bytes 3907584 | tf_op jit(solution)/shard_map/izyx,tozyx->ito/dot_general | solution.py:62
  92.1 3.2 %fusion.9 = bf16[128,9,32]{0,2,1:T(8,128)(2,1)} fusion(bf16[9,32,2,18,128]{4,1,3,0,2:T(8,128)(2,1)} %fusion.24, bf16[128,4,18,128]{3,0,2,1:T(8,128)(2,1)S(1)} %bitcast.520), kind=kOutput, calls=%fused_computation.101 | convolution fusion | flops 339775488 | bytes 3907584 | tf_op jit(solution)/shard_map/izyx,tozyx->ito/dot_general | solution.py:62
  95.3 3.2 %fusion.8 = bf16[128,9,32]{0,2,1:T(8,128)(2,1)} fusion(bf16[9,32,2,18,128]{4,1,3,0,2:T(8,128)(2,1)} %fusion.24, bf16[128,4,18,128]{3,0,2,1:T(8,128)(2,1)S(1)} %bitcast.521), kind=kOutput, calls=%fused_computation.100 | convolution fusion | flops 339775488 | bytes 3907584 | tf_op jit(solution)/shard_map/izyx,tozyx->ito/dot_general | solution.py:62
  99.2 3.9 %fusion.107 = (bf16[128,2,16,128]{3,0,2,1:T(8,128)(2,1)S(1)}, bf16[128,2,16,128]{3,0,2,1:T(8,128)(2,1)S(1)}, bf16[128,2,16,128]{3,0,2,1:T(8,128)(2,1)S(1)}, bf16...) fusion(bf16[128,4,18,128]{3,0,2,1:T(8,128)(2,1)S(1)} %bitcast.508), kind=kLoop, calls=%fused_computation.268 | loop fusion | bytes 18874368 | tf_op jit(solution)/shard_map/slice | solution.py:39
  103.6 1.5 convolution_add_fusion.25
  105.1 1.2 convolution_add_fusion.24
  106.3 1.2 convolution_add_fusion.23
  107.5 1.5 convolution_add_fusion.22
  109.0 1.2 convolution_add_fusion.21
  110.2 1.2 convolution_add_fusion.20
  111.3 1.5 convolution_add_fusion.19
  112.9 1.2 convolution_add_fusion.18
  114.0 1.2 convolution_add_fusion.17
  115.2 1.5 convolution_add_fusion.16
  116.8 1.2 convolution_add_fusion.15
  117.9 1.2 convolution_add_fusion.14
  119.1 1.5 convolution_add_fusion.13
  120.6 1.2 convolution_add_fusion.12
  121.8 1.2 convolution_add_fusion.11
  123.0 1.5 convolution_add_fusion.10
  124.5 1.2 convolution_add_fusion.9
  125.7 1.2 convolution_add_fusion.8
  126.9 1.5 convolution_add_fusion.7
  128.4 1.2 convolution_add_fusion.6
  129.6 1.2 convolution_add_fusion.5
  130.8 1.5 convolution_add_fusion.4
  132.3 1.2 convolution_add_fusion.3
  133.4 1.2 convolution_add_fusion.2
  134.6 1.5 convolution_add_fusion.1
  136.2 1.2 fusion.1
  138.2 1.3 fusion.11
  139.5 1.1 copy.42
  140.6 1.8 %copy.43 = bf16[128,9,32]{2,0,1:T(8,128)(2,1)} copy(bf16[128,9,32]{0,2,1:T(8,128)(2,1)} %fusion.9) | data formatting | bytes 147456 | tf_op jit(solution)/shard_map/convert.4
  142.4 1.8 copy.44
  144.2 2.5 %copy_bitcast_fusion = bf16[32,27,4,32]{3,2,1,0:T(4,128)(2,1)} fusion(bf16[32,4,9,32]{3,1,0,2:T(4,128)(2,1)} %bitcast.533, bf16[32,4,9,32]{3,1,0,2:T(4,128)(2,1)} %bitcast.532, bf16[32,4,9,32]{3,1,0,2:T(4,128)(2,1)S(1)} %bitcast.531), kind=kLoop, calls=%fused_computation.272 | loop fusion | flops 221184 | bytes 442368
  146.7 2.9 %reshape.81 = bf16[32,2,1728]{2,1,0:T(2,128)(2,1)} reshape(bf16[32,27,4,32]{3,2,1,0:T(4,128)(2,1)} %copy_bitcast_fusion) | data formatting | bytes 442368
  149.5 11.1 %all-to-all-start.1 = ((bf16[32,2,1728]{2,1,0:T(2,128)(2,1)}), bf16[32,2,1728]{2,1,0:T(2,128)(2,1)S(1)}, u32[]{:S(2)}, u32[]{:S(2)}) async-start(bf16[32,2,1728]{2,1,0:T(2,128)(2,1)} %reshape.81), calls=%async_computation.1 | async-start | bytes 458752 | tf_op jit(solution)/shard_map/all_to_all | solution.py:85
  160.6 1.6 convolution_add_fusion.51
  (79 shorter events, 29.2 us)
Async XLA Ops:
  0.6 25.0 %copy-start = (bf16[27,128,128]{2,1,0:T(8,128)(2,1)S(1)}, bf16[27,128,128]{2,1,0:T(8,128)(2,1)}, u32[]{:S(2)}) copy-start(bf16[27,128,128]{2,1,0:T(8,128)(2,1)} %param.4) | copy-start | bytes 2654212
  2.7 9.1 %collective-permute-start = (bf16[64,1,16,128]{3,2,1,0:T(8,128)(2,1)S(1)}, bf16[64,1,16,128]{3,2,1,0:T(8,128)(2,1)S(1)}, u32[]{:S(2)}, u32[]{:S(2)}) collective-permute-start(bf16[64,1,16,128]{3,2,1,0:T(8,128)(2,1)S(1)} %get-tuple-element.32), channel_id=1, source_target_pairs={{0,4},{4,8},{8,12},{12,16},{16,20},{20,24},{24,28},{28,32},{32,36}... | collective-permute-start | bytes 786440 | tf_op jit(solution)/shard_map/ppermute | solution.py:15
  6.3 9.7 %collective-permute-start.1 = (bf16[64,1,16,128]{3,2,1,0:T(8,128)(2,1)S(1)}, bf16[64,1,16,128]{3,2,1,0:T(8,128)(2,1)S(1)}, u32[]{:S(2)}, u32[]{:S(2)}) collective-permute-start(bf16[64,1,16,128]{3,2,1,0:T(8,128)(2,1)S(1)} %get-tuple-element.33), channel_id=1, source_target_pairs={{4,0},{8,4},{12,8},{16,12},{20,16},{24,20},{28,24},{32,28},{36,32}... | collective-permute-start | bytes 786440 | tf_op jit(solution)/shard_map/ppermute | solution.py:16
  20.3 5.3 %copy-start.12 = (bf16[32,2,16,128]{3,2,1,0:T(8,128)(2,1)S(1)}, bf16[32,2,16,128]{3,2,1,0:T(8,128)(2,1)}, u32[]{:S(2)}) copy-start(bf16[32,2,16,128]{3,2,1,0:T(8,128)(2,1)} %param.5) | copy-start | bytes 786436
  20.3 60.6 %all-to-all-start = ((bf16[4,64,4,18,128]{4,1,3,2,0:T(8,128)(2,1)}), bf16[4,64,4,18,128]{4,1,3,2,0:T(8,128)(2,1)}, u32[]{:S(2)}, u32[]{:S(2)}) async-start(bf16[4,64,4,18,128]{4,1,3,2,0:T(8,128)(2,1)} %broadcast_in_dim.3), calls=%async_computation | async-start | bytes 9437184 | tf_op jit(solution)/shard_map/all_to_all | solution.py:27
  25.7 77.4 %copy-start.13 = (bf16[27,128,32]{1,2,0:T(8,128)(2,1)}, bf16[27,128,32]{1,2,0:T(8,128)(2,1)S(1)}, u32[]{:S(2)}) copy-start(bf16[27,128,32]{1,2,0:T(8,128)(2,1)S(1)} %dynamic-slice_bitcast_fusion) | copy-start | bytes 663556
  88.5 49.7 %copy-start.3 = (bf16[128,2,16,128]{3,0,2,1:T(8,128)(2,1)}, bf16[128,2,16,128]{3,0,2,1:T(8,128)(2,1)S(1)}, u32[]{:S(2)}) copy-start(bf16[128,2,16,128]{3,0,2,1:T(8,128)(2,1)S(1)} %get-tuple-element.31) | copy-start | bytes 3145732
  99.2 3.9 %copy-start.1 = (bf16[4,32,4,18,128]{4,1,0,3,2:T(8,128)(2,1)}, bf16[4,32,4,18,128]{4,1,0,3,2:T(8,128)(2,1)S(1)}, u32[]{:S(2)}) copy-start(bf16[4,32,4,18,128]{4,1,0,3,2:T(8,128)(2,1)S(1)} %copy.32) | copy-start | bytes 7077892
  149.5 27.7 %all-to-all-start.1 = ((bf16[32,2,1728]{2,1,0:T(2,128)(2,1)}), bf16[32,2,1728]{2,1,0:T(2,128)(2,1)S(1)}, u32[]{:S(2)}, u32[]{:S(2)}) async-start(bf16[32,2,1728]{2,1,0:T(2,128)(2,1)} %reshape.81), calls=%async_computation.1 | async-start | bytes 458752 | tf_op jit(solution)/shard_map/all_to_all | solution.py:85
  160.6 1.6 copy-start.4
  160.6 2.1 %copy-start.11 = (bf16[128,2,16,128]{3,0,2,1:T(8,128)(2,1)S(1)}, bf16[128,2,16,128]{3,0,2,1:T(8,128)(2,1)}, u32[]{:S(2)}) copy-start(bf16[128,2,16,128]{3,0,2,1:T(8,128)(2,1)} %get-tuple-element.30) | copy-start | bytes 3145732
  163.3 1.2 copy-start.10
  165.0 1.2 copy-start.9
  166.8 1.2 copy-start.8
  168.5 1.2 copy-start.7
  170.3 1.2 copy-start.6
  172.0 1.2 copy-start.5
  173.8 1.2 copy-start.2

commit v2 on v0

v2 whole, which is shorter than its diff:
```python
import math

import jax
import jax.numpy as jnp
from jax import lax
from jax.experimental import pallas as pl
from jax.experimental.pallas import tpu as pltpu
from jax.sharding import Mesh
from jax.sharding import PartitionSpec as P

CH = ("ch_0", "ch_1")
ROW = 128


def padded_2(shard, axis, dim):
    devices, length = (lax.axis_size(axis), shard.shape[dim])
    up = [(i, (i + 1) % devices) for i in range(devices - 1)]
    down = [(j, i) for i, j in up]
    last = lax.slice_in_dim(shard, length - 1, length, axis=dim)
    first = lax.slice_in_dim(shard, 0, 1, axis=dim)
    before = lax.ppermute(last, axis, up)
    after = lax.ppermute(first, axis, down)
    return jnp.concatenate([before, shard, after], axis=dim)


def from_everyone(shard, axis):
    copies = jnp.broadcast_to(shard, (lax.axis_size(axis), *shard.shape))
    return lax.all_to_all(copies, axis, split_axis=0, concat_axis=0, tiled=True)


def summed_on_arrival(shard, axis, dim):
    before, after = (shard.shape[:dim], shard.shape[dim + 1 :])
    devices = lax.axis_size(axis)
    blocks = jnp.moveaxis(shard.reshape(*before, devices, -1, *after), dim, 0)
    arrived = lax.all_to_all(blocks, axis, split_axis=0, concat_axis=0, tiled=True)
    return arrived.astype(jnp.float32).sum(axis=0)

def fused_kernel(g_ref, c_ref, wf_ref, wb_ref, out_ref, ing_ref, wg_ref, vs_ref, cs_ref):
    groups, _, flat = g_ref.shape
    loc = c_ref.shape[0] // 2
    planes = out_ref.shape[0]
    plane = flat // (planes + 2)
    span = (planes - 1) * plane + out_ref.shape[2]
    for k in range(groups):
        vs_ref[k * loc : (k + 1) * loc, :] = g_ref[k, 0:loc, :]
        cs_ref[k * loc : (k + 1) * loc, :] = g_ref[k, loc : 2 * loc, :]
    lane = lax.broadcasted_iota(jnp.int32, (loc, span), 1) % ROW
    first = lane == 0
    last = lane == ROW - 1
    zero = jnp.zeros((loc, span), jnp.float32)
    start = plane + ROW
    cm = c_ref[loc : 2 * loc, start : start + span].astype(jnp.float32)
    c_prev = jnp.where(last, zero, pltpu.roll(cm, span - 1, 1))
    c_next = jnp.where(first, zero, pltpu.roll(cm, 1, 1))
    cstack = jnp.concatenate([c_prev, cm, c_next], axis=0).astype(jnp.bfloat16)

    def shifted_sum(r):
        left = jnp.where(first, zero, pltpu.roll(r[0:loc], 1, 1))
        right = jnp.where(last, zero, pltpu.roll(r[2 * loc : 3 * loc], span - 1, 1))
        return left + r[loc : 2 * loc] + right

    acc_o = zero
    acc_i = zero
    for tap_z in range(3):
        for tap_y in range(3):
            base = tap_z * plane + tap_y * ROW
            pair = 3 * tap_z + tap_y
            sv = vs_ref[:, base : base + span]
            sc = cs_ref[:, base : base + span]
            acc_o = acc_o + shifted_sum(
                jnp.dot(wf_ref[pair], sv, preferred_element_type=jnp.float32)
            )
            acc_i = acc_i + shifted_sum(
                jnp.dot(wb_ref[pair], sc, preferred_element_type=jnp.float32)
            )
            w = lax.dot_general(
                sv, cstack, (((1,), (1,)), ((), ())), preferred_element_type=jnp.float32
            )
            for tap_x in range(3):
                wg_ref[3 * pair + tap_x] = w[:, tap_x * loc : (tap_x + 1) * loc]
    width = out_ref.shape[2]
    for z in range(planes):
        out_ref[z] = acc_o[:, z * plane : z * plane + width].astype(out_ref.dtype)
        ing_ref[z] = acc_i[:, z * plane : z * plane + width].astype(ing_ref.dtype)


def fused(gathered, local, wf, wb, planes, width):
    groups, both, flat = gathered.shape
    loc = both // 2
    cin = groups * loc
    return pl.pallas_call(
        fused_kernel,
        out_shape=(
            jax.ShapeDtypeStruct((planes, loc, width), jnp.bfloat16),
            jax.ShapeDtypeStruct((planes, loc, width), jnp.bfloat16),
            jax.ShapeDtypeStruct((27, cin, loc), jnp.float32),
        ),
        scratch_shapes=[
            pltpu.VMEM((cin, flat), jnp.bfloat16),
            pltpu.VMEM((cin, flat), jnp.bfloat16),
        ],
    )(gathered, local, wf, wb)


def body(volume, weight, cotangent):
    in_local, planes_local, grid_rows, grid_cols = volume.shape
    out_local = cotangent.shape[0]
    my_group = lax.axis_index(CH)
    voxels = planes_local * lax.axis_size("gz") * grid_rows * grid_cols
    both = padded_2(jnp.concatenate([volume, cotangent], axis=0), "gz", 1)
    both = jnp.pad(both, ((0, 0), (0, 0), (1, 1), (0, 0))).reshape(both.shape[0], -1)
    far, near = CH
    blocks = from_everyone(from_everyone(both, far), near)
    gathered = blocks.swapaxes(0, 1).reshape(-1, *both.shape)
    cin = gathered.shape[0] * in_local
    cout = gathered.shape[0] * out_local
    weight_cols = lax.dynamic_slice_in_dim(weight, my_group * out_local, out_local, 2)
    wf = jnp.transpose(weight_cols.reshape(3, 3, 3, cin, out_local), (0, 1, 2, 4, 3))
    wf = wf.reshape(9, 3 * out_local, cin)
    weight_rows = lax.dynamic_slice_in_dim(weight, my_group * in_local, in_local, 1)
    wb = weight_rows[::-1].reshape(9, 3 * in_local, cout)
    out, ing, wg = fused(gathered, both, wf, wb, planes_local, grid_rows * grid_cols)
    shape = (out_local, planes_local, grid_rows, grid_cols)
    out = jnp.transpose(out, (1, 0, 2)).reshape(shape)
    ing = jnp.transpose(ing, (1, 0, 2)).reshape(shape)
    weight_grad = summed_on_arrival(wg.astype(jnp.bfloat16), "gz", 1) * jnp.float32(
        1.0 / math.sqrt(voxels)
    )
    return out, ing, weight_grad


def solution(mesh):
    split = Mesh(mesh.devices.reshape(mesh.shape["gz"], 2, 2), ("gz", "ch_0", "ch_1"))
    placed = (P(CH, "gz", None, None), P(), P(CH, "gz", None, None))
    return jax.shard_map(
        body,
        mesh=split,
        in_specs=placed,
        out_specs=(P(CH, "gz", None, None), P(CH, "gz", None, None), P(None, "gz", CH)),
        check_vma=False,
    )
```

time: 461 us -> 106 us (0.23)
  waiting for transfers between devices: 345 us -> 39.3 us
  matrix products: 53.9 us -> 0 us
  local copies, waits for them, and re-layouts: 39.2 us -> 16.3 us
  starting transfers between devices: 5.03 us -> 23.6 us
  between operations: 14.9 us -> 0.77 us
  Pallas kernels: 0 us -> 12.9 us
  blocking collectives: 0 us -> 7.53 us
    unnamed x3 -> x0, waiting for transfers between devices: 298 us -> none
    all_gather x1 -> x0, waiting for transfers between devices: 38.6 us -> none  [body(): gathered = lax.all_gather(padded, 'ch', axis=0)]
    transpose x1 -> x0, matrix products: 36 us -> none  [body(): wpart = jnp.transpose(wpart, (2, 3, 4, 0, 1)).reshape(27, cin, out_local)]
    all_to_all x0 -> x2, waiting for transfers between devices: none -> 34.2 us  [the longest x1 26.8 us: from_everyone(): return lax.all_to_all(copies, axis, split_axis=0, concat_axis=0, tiled=True)]
    conv_general_dilated x2 -> x0, matrix products: 17.9 us -> none  [the longest x1 9.97 us: body(): lax.conv_general_dilated(cot_padded, flipped, (1, 1, 1), SAME_YX, dimensi...]
    all_to_all x0 -> x2, starting transfers between devices: none -> 17.8 us  [the longest x1 12.4 us: summed_on_arrival(): lax.all_to_all(blocks, axis, split_axis=0, concat_axis=0, tiled=True)]
    another operation x4 -> x0, local copies, waits for them, and re-layouts: 14.1 us -> none  [the longest x2 7.11 us: body(): cot_padded = cot_full[None]]
    pallas_call x0 -> x1, Pallas kernels: none -> 12.9 us  [fused(): pl.pallas_call(fused_kernel, out_shape=(jax.ShapeDtypeStruct((planes, loc...]
  transfers between devices with their start and end apart: 4 -> 4, of which waited for: 4 -> 4; matrix products, arithmetic and copies ran while one was open for 4% -> 3% of each run, Pallas kernels for 0% -> 0%
where the time goes in v2:
time: 106 us; the launch traced here: 105 us
  waiting for transfers between devices  39.3 us (37%)
  starting transfers between devices  23.6 us (22%)
  local copies, waits for them, and re-layouts  16.3 us (15%)
  Pallas kernels  12.9 us (12%)
  blocking collectives  7.53 us (7%)
  other arithmetic  4.74 us (4%)
    all_to_all x1, waiting for transfers between devices, from_everyone(): return lax.all_to_all(copies, axis, split_axis=0, concat_axis=0, tiled=True)  26.8 us
    pallas_call x1, Pallas kernels, fused(): pl.pallas_call(fused_kernel, out_shape=(jax.ShapeDtypeStruct((planes, loc...  12.9 us
    all_to_all x1, starting transfers between devices, summed_on_arrival(): lax.all_to_all(blocks, axis, split_axis=0, concat_axis=0, tiled=True)  12.4 us
    all_to_all x1, blocking collectives, from_everyone(): return lax.all_to_all(copies, axis, split_axis=0, concat_axis=0, tiled=True)  7.53 us
    all_to_all x1, waiting for transfers between devices, summed_on_arrival(): lax.all_to_all(blocks, axis, split_axis=0, concat_axis=0, tiled=True)  7.45 us
    unnamed x16, local copies, waits for them, and re-layouts  5.74 us
    all_to_all x1, starting transfers between devices, from_everyone(): return lax.all_to_all(copies, axis, split_axis=0, concat_axis=0, tiled=True)  5.39 us
    ppermute x1, starting transfers between devices, padded_2(): before = lax.ppermute(last, axis, up)  4.56 us
  transfers between devices with their start and end apart: 4, of which 4 were waited for; matrix products, arithmetic and copies ran while one was open for 3% of the time, Pallas kernels for 0%

profile of v2, /device:TPU:0, one launch (start us, length us, event | category | flops | bytes accessed | tf_op | source)
XLA Modules:
  0.0 105.2 jit_solution(5313863723849271989)
XLA Ops:
  0.6 0.0 copy-start
  0.6 1.0 constant_dynamic-update-slice_fusion.1
  1.7 1.0 constant_dynamic-update-slice_fusion
  2.7 1.3 %collective-permute-start.1 = (bf16[64,1,16,128]{3,2,1,0:T(8,128)(2,1)S(1)}, bf16[64,1,16,128]{3,2,1,0:T(8,128)(2,1)S(1)}, u32[]{:S(2)}, u32[]{:S(2)}) collective-permute-start(bf16[64,1,16,128]{3,2,1,0:T(8,128)(2,1)S(1)} %get-tuple-element.19), channel_id=1, source_target_pairs={{4,0},{8,4},{12,8},{16,12},{20,16},{24,20},{28,24},{32,28},{36,32}... | collective-permute-start | bytes 786440 | tf_op jit(solution)/shard_map/ppermute | solution.py:22
  4.0 4.6 %collective-permute-start = (bf16[64,1,16,128]{3,2,1,0:T(8,128)(2,1)S(1)}, bf16[64,1,16,128]{3,2,1,0:T(8,128)(2,1)S(1)}, u32[]{:S(2)}, u32[]{:S(2)}) collective-permute-start(bf16[64,1,16,128]{3,2,1,0:T(8,128)(2,1)S(1)} %get-tuple-element.18), channel_id=1, source_target_pairs={{0,4},{4,8},{8,12},{12,16},{16,20},{20,24},{24,28},{28,32},{32,36}... | collective-permute-start | bytes 786440 | tf_op jit(solution)/shard_map/ppermute | solution.py:21
  8.6 3.9 %collective-permute-done.1 = bf16[64,1,16,128]{3,2,1,0:T(8,128)(2,1)S(1)} collective-permute-done((bf16[64,1,16,128]{3,2,1,0:T(8,128)(2,1)S(1)}, bf16[64,1,16,128]{3,2,1,0:T(8,128)(2,1)S(1)}, u32[]{:S(2)}, u32[]{:S(2)}) %collective-permute-start.1) | collective-permute-done | bytes 262176 | tf_op jit(solution)/shard_map/ppermute | solution.py:22
  12.5 1.2 %collective-permute-done = bf16[64,1,16,128]{3,2,1,0:T(8,128)(2,1)S(1)} collective-permute-done((bf16[64,1,16,128]{3,2,1,0:T(8,128)(2,1)S(1)}, bf16[64,1,16,128]{3,2,1,0:T(8,128)(2,1)S(1)}, u32[]{:S(2)}, u32[]{:S(2)}) %collective-permute-start) | collective-permute-done | bytes 262176 | tf_op jit(solution)/shard_map/ppermute | solution.py:21
  13.7 2.0 %fusion.5 = bf16[64,4,18,128]{3,2,1,0:T(8,128)(2,1)} fusion(bf16[64,1,16,128]{3,2,1,0:T(8,128)(2,1)S(1)} %collective-permute-done.1, bf16[64,2,16,128]{3,2,1,0:T(8,128)(2,1)S(1)} %constant_dynamic-update-slice_fusion, bf16[64,1,16,128]{3,2,1,0:T(8,128)(2,1)S(1)} %collective-permute-done), kind=kLoop, calls=%fused_computation.8 | loop fusion | flops 7077888 | bytes 2228224 | tf_op jit(solution)/shard_map/concatenate | solution.py:23
  15.7 1.8 %reshape.30.c_ref = bf16[64,9216]{1,0:T(8,128)(2,1)S(1)} reshape(bf16[64,4,18,128]{3,2,1,0:T(8,128)(2,1)} %fusion.5) | data formatting | bytes 2359296 | tf_op jit(solution)/shard_map/reshape | solution.py:111
  17.5 0.0 copy-start.1
  17.5 1.8 %broadcast_in_dim.6 = bf16[2,64,9216]{2,1,0:T(8,128)(2,1)} broadcast(bf16[64,9216]{1,0:T(8,128)(2,1)S(1)} %reshape.30.c_ref), dimensions={1,2} | broadcast | bytes 3538944 | tf_op jit(solution)/shard_map/broadcast_in_dim | solution.py:27
  19.2 0.0 copy-done.1
  19.2 5.4 %all-to-all-start = ((bf16[2,64,9216]{2,1,0:T(8,128)(2,1)}), bf16[2,64,9216]{2,1,0:T(8,128)(2,1)}, u32[]{:S(2)}, u32[]{:S(2)}) async-start(bf16[2,64,9216]{2,1,0:T(8,128)(2,1)} %broadcast_in_dim.6), calls=%async_computation | async-start | bytes 4718592 | tf_op jit(solution)/shard_map/all_to_all | solution.py:28
  24.6 0.0 copy-done
  24.6 0.3 constant_dynamic-slice_fusion.1
  24.9 1.0 copy.16
  25.9 0.7 rev.3
  26.6 26.8 %all-to-all-done = bf16[2,64,9216]{2,1,0:T(8,128)(2,1)} async-done(((bf16[2,64,9216]{2,1,0:T(8,128)(2,1)}), bf16[2,64,9216]{2,1,0:T(8,128)(2,1)}, u32[]{:S(2)}, u32[]{:S(2)}) %all-to-all-start) | async-done | bytes 2359328 | tf_op jit(solution)/shard_map/all_to_all | solution.py:28
  53.4 2.2 %broadcast_in_dim.7 = bf16[2,2,64,9216]{3,2,1,0:T(8,128)(2,1)S(1)} broadcast(bf16[2,64,9216]{2,1,0:T(8,128)(2,1)} %all-to-all-done), dimensions={1,2,3} | broadcast | bytes 7077888 | tf_op jit(solution)/shard_map/broadcast_in_dim | solution.py:27
  55.6 7.5 %all_to_all.15 = bf16[2,2,64,9216]{3,2,1,0:T(8,128)(2,1)S(1)} all-to-all(bf16[2,2,64,9216]{3,2,1,0:T(8,128)(2,1)S(1)} %broadcast_in_dim.7), channel_id=1, replica_groups=mesh['gz'=32,'ch_0'=2,'ch_1'=2] {'ch_1'}, dimensions={0} | all-to-all | bytes 9437184 | tf_op jit(solution)/shard_map/all_to_all | solution.py:28
  63.1 2.4 %copy.11 = bf16[2,2,64,9216]{3,2,1,0:T(8,128)(2,1)} copy(bf16[2,2,64,9216]{3,2,0,1:T(8,128)(2,1)S(1)} %bitcast.27) | data formatting | bytes 9437184 | tf_op jit(solution)/shard_map/transpose | solution.py:114
  65.6 12.9 %shard_map.58 = (bf16[2,32,2048]{2,1,0:T(8,128)(2,1)}, bf16[2,32,2048]{2,1,0:T(8,128)(2,1)}, f32[27,128,32]{2,1,0:T(8,128)}) custom-call(bf16[4,64,9216]{2,1,0:T(8,128)(2,1)} %bitcast.26, bf16[64,9216]{1,0:T(8,128)(2,1)} %copy-done.1, bf16[9,96,128]{2,1,0:T(8,128)(2,1)} %bitcast.33, bf16[9,96,128]{2,1,0:T(8,128)(2,1)} %bitcast.32), custom_call_target="tpu_custom_call" | custom-call | tf_op jit(solution)/shard_map/pallas_call | solution.py:91
  78.5 0.0 copy-start.3
  78.5 1.7 %convert_element_type.8 = bf16[27,128,32]{2,1,0:T(8,128)(2,1)S(1)} convert(f32[27,128,32]{2,1,0:T(8,128)} %get-tuple-element.8) | non-fusion elementwise | flops 110592 | bytes 663552 | tf_op jit(solution)/shard_map/convert_element_type | solution.py:126
  80.1 0.0 copy-start.2
  80.2 0.3 copy.20
  80.5 1.4 %reshape.38 = bf16[32,2,1728]{2,1,0:T(2,128)(2,1)} reshape(bf16[32,27,4,32]{3,2,1,0:T(4,128)(2,1)S(1)} %bitcast.28) | data formatting | bytes 442368
  81.9 12.4 %all-to-all-start.2 = ((bf16[32,2,1728]{2,1,0:T(2,128)(2,1)}), bf16[32,2,1728]{2,1,0:T(2,128)(2,1)S(1)}, u32[]{:S(2)}, u32[]{:S(2)}) async-start(bf16[32,2,1728]{2,1,0:T(2,128)(2,1)} %reshape.38), calls=%async_computation.2 | async-start | bytes 458752 | tf_op jit(solution)/shard_map/all_to_all | solution.py:35
  94.3 0.0 copy-done.3
  94.4 0.7 copy.14
  95.1 0.0 copy-done.2
  95.1 0.7 copy.15
  95.9 7.5 %all-to-all-done.2 = bf16[32,2,1728]{2,1,0:T(2,128)(2,1)S(1)} async-done(((bf16[32,2,1728]{2,1,0:T(2,128)(2,1)}), bf16[32,2,1728]{2,1,0:T(2,128)(2,1)S(1)}, u32[]{:S(2)}, u32[]{:S(2)}) %all-to-all-start.2) | async-done | bytes 221216 | tf_op jit(solution)/shard_map/all_to_all | solution.py:35
  103.3 0.8 reshape.39
  104.1 0.5 convert_reduce_fusion
  104.5 0.6 broadcast_multiply_fusion
  (4 shorter events, 0.1 us)
Async XLA Ops:
  0.6 24.0 %copy-start = (bf16[27,128,128]{2,1,0:T(8,128)(2,1)S(1)}, bf16[27,128,128]{2,1,0:T(8,128)(2,1)}, u32[]{:S(2)}) copy-start(bf16[27,128,128]{2,1,0:T(8,128)(2,1)} %param.4) | copy-start | bytes 2654212
  2.7 9.8 %collective-permute-start.1 = (bf16[64,1,16,128]{3,2,1,0:T(8,128)(2,1)S(1)}, bf16[64,1,16,128]{3,2,1,0:T(8,128)(2,1)S(1)}, u32[]{:S(2)}, u32[]{:S(2)}) collective-permute-start(bf16[64,1,16,128]{3,2,1,0:T(8,128)(2,1)S(1)} %get-tuple-element.19), channel_id=1, source_target_pairs={{4,0},{8,4},{12,8},{16,12},{20,16},{24,20},{28,24},{32,28},{36,32}... | collective-permute-start | bytes 786440 | tf_op jit(solution)/shard_map/ppermute | solution.py:22
  4.0 9.7 %collective-permute-start = (bf16[64,1,16,128]{3,2,1,0:T(8,128)(2,1)S(1)}, bf16[64,1,16,128]{3,2,1,0:T(8,128)(2,1)S(1)}, u32[]{:S(2)}, u32[]{:S(2)}) collective-permute-start(bf16[64,1,16,128]{3,2,1,0:T(8,128)(2,1)S(1)} %get-tuple-element.18), channel_id=1, source_target_pairs={{0,4},{4,8},{8,12},{12,16},{16,20},{20,24},{24,28},{28,32},{32,36}... | collective-permute-start | bytes 786440 | tf_op jit(solution)/shard_map/ppermute | solution.py:21
  17.5 1.8 %copy-start.1 = (bf16[64,9216]{1,0:T(8,128)(2,1)}, bf16[64,9216]{1,0:T(8,128)(2,1)S(1)}, u32[]{:S(2)}) copy-start(bf16[64,9216]{1,0:T(8,128)(2,1)S(1)} %reshape.30.c_ref) | copy-start | bytes 3538948
  19.2 34.2 %all-to-all-start = ((bf16[2,64,9216]{2,1,0:T(8,128)(2,1)}), bf16[2,64,9216]{2,1,0:T(8,128)(2,1)}, u32[]{:S(2)}, u32[]{:S(2)}) async-start(bf16[2,64,9216]{2,1,0:T(8,128)(2,1)} %broadcast_in_dim.6), calls=%async_computation | async-start | bytes 4718592 | tf_op jit(solution)/shard_map/all_to_all | solution.py:28
  78.5 15.8 %copy-start.3 = (bf16[2,32,2048]{2,1,0:T(8,128)(2,1)S(1)}, bf16[2,32,2048]{2,1,0:T(8,128)(2,1)}, u32[]{:S(2)}) copy-start(bf16[2,32,2048]{2,1,0:T(8,128)(2,1)} %get-tuple-element.6) | copy-start | bytes 786436
  80.1 14.9 %copy-start.2 = (bf16[2,32,2048]{2,1,0:T(8,128)(2,1)S(1)}, bf16[2,32,2048]{2,1,0:T(8,128)(2,1)}, u32[]{:S(2)}) copy-start(bf16[2,32,2048]{2,1,0:T(8,128)(2,1)} %get-tuple-element.7) | copy-start | bytes 786436
  81.9 21.4 %all-to-all-start.2 = ((bf16[32,2,1728]{2,1,0:T(2,128)(2,1)}), bf16[32,2,1728]{2,1,0:T(2,128)(2,1)S(1)}, u32[]{:S(2)}, u32[]{:S(2)}) async-start(bf16[32,2,1728]{2,1,0:T(2,128)(2,1)} %reshape.38), calls=%async_computation.2 | async-start | bytes 458752 | tf_op jit(solution)/shard_map/all_to_all | solution.py:35

commit v3 on v2

--- a/solution.py
+++ b/solution.py
@@ -12,22 +12,6 @@
 ROW = 128
 
 
-def padded_2(shard, axis, dim):
-    devices, length = (lax.axis_size(axis), shard.shape[dim])
-    up = [(i, (i + 1) % devices) for i in range(devices - 1)]
-    down = [(j, i) for i, j in up]
-    last = lax.slice_in_dim(shard, length - 1, length, axis=dim)
-    first = lax.slice_in_dim(shard, 0, 1, axis=dim)
-    before = lax.ppermute(last, axis, up)
-    after = lax.ppermute(first, axis, down)
-    return jnp.concatenate([before, shard, after], axis=dim)
-
-
-def from_everyone(shard, axis):
-    copies = jnp.broadcast_to(shard, (lax.axis_size(axis), *shard.shape))
-    return lax.all_to_all(copies, axis, split_axis=0, concat_axis=0, tiled=True)
-
-
 def summed_on_arrival(shard, axis, dim):
     before, after = (shard.shape[:dim], shard.shape[dim + 1 :])
     devices = lax.axis_size(axis)
@@ -35,21 +19,32 @@
     arrived = lax.all_to_all(blocks, axis, split_axis=0, concat_axis=0, tiled=True)
     return arrived.astype(jnp.float32).sum(axis=0)
 
-def fused_kernel(g_ref, c_ref, wf_ref, wb_ref, out_ref, ing_ref, wg_ref, vs_ref, cs_ref):
-    groups, _, flat = g_ref.shape
-    loc = c_ref.shape[0] // 2
-    planes = out_ref.shape[0]
-    plane = flat // (planes + 2)
-    span = (planes - 1) * plane + out_ref.shape[2]
+def fused_kernel(b_ref, lo_ref, hi_ref, wf_ref, wb_ref, out_ref, ing_ref, wg_ref, vs_ref, cs_ref):
+    groups, both, _ = b_ref.shape
+    loc = both // 2
+    planes, _, width = out_ref.shape
+    plane = width + 2 * ROW
+    span = (planes - 1) * plane + width
+    blank = jnp.zeros((loc, ROW), jnp.bfloat16)
     for k in range(groups):
-        vs_ref[k * loc : (k + 1) * loc, :] = g_ref[k, 0:loc, :]
-        cs_ref[k * loc : (k + 1) * loc, :] = g_ref[k, loc : 2 * loc, :]
+        rows = slice(k * loc, (k + 1) * loc)
+        for ref, low in ((vs_ref, 0), (cs_ref, loc)):
+            chans = slice(low, low + loc)
+            for zp in range(planes + 2):
+                ref[rows, zp * plane : zp * plane + ROW] = blank
+                ref[rows, zp * plane + ROW + width : (zp + 1) * plane] = blank
+            ref[rows, ROW : ROW + width] = lo_ref[k, chans, :]
+            for z in range(planes):
+                at = (z + 1) * plane + ROW
+                ref[rows, at : at + width] = b_ref[k, chans, z * width : (z + 1) * width]
+            at = (planes + 1) * plane + ROW
+            ref[rows, at : at + width] = hi_ref[k, chans, :]
     lane = lax.broadcasted_iota(jnp.int32, (loc, span), 1) % ROW
     first = lane == 0
     last = lane == ROW - 1
     zero = jnp.zeros((loc, span), jnp.float32)
     start = plane + ROW
-    cm = c_ref[loc : 2 * loc, start : start + span].astype(jnp.float32)
+    cm = cs_ref[0:loc, start : start + span].astype(jnp.float32)
     c_prev = jnp.where(last, zero, pltpu.roll(cm, span - 1, 1))
     c_next = jnp.where(first, zero, pltpu.roll(cm, 1, 1))
     cstack = jnp.concatenate([c_prev, cm, c_next], axis=0).astype(jnp.bfloat16)
@@ -84,10 +79,11 @@
         ing_ref[z] = acc_i[:, z * plane : z * plane + width].astype(ing_ref.dtype)
 
 
-def fused(gathered, local, wf, wb, planes, width):
-    groups, both, flat = gathered.shape
+def fused(body, low, high, wf, wb, planes, width):
+    groups, both, _ = body.shape
     loc = both // 2
     cin = groups * loc
+    flat = (planes + 2) * (width + 2 * ROW)
     return pl.pallas_call(
         fused_kernel,
         out_shape=(
@@ -99,27 +95,46 @@
             pltpu.VMEM((cin, flat), jnp.bfloat16),
             pltpu.VMEM((cin, flat), jnp.bfloat16),
         ],
-    )(gathered, local, wf, wb)
+    )(body, low, high, wf, wb)
+
+
+def by_group(array, order, size, dim):
+    return jnp.concatenate(
+        [lax.dynamic_slice_in_dim(array, group * size, size, dim) for group in order], axis=dim
+    )
 
 
 def body(volume, weight, cotangent):
     in_local, planes_local, grid_rows, grid_cols = volume.shape
     out_local = cotangent.shape[0]
     my_group = lax.axis_index(CH)
-    voxels = planes_local * lax.axis_size("gz") * grid_rows * grid_cols
-    both = padded_2(jnp.concatenate([volume, cotangent], axis=0), "gz", 1)
-    both = jnp.pad(both, ((0, 0), (0, 0), (1, 1), (0, 0))).reshape(both.shape[0], -1)
+    slabs = lax.axis_size("gz")
+    voxels = planes_local * slabs * grid_rows * grid_cols
+    width = grid_rows * grid_cols
+    both = jnp.concatenate([volume, cotangent], axis=0).reshape(in_local + out_local, -1)
     far, near = CH
-    blocks = from_everyone(from_everyone(both, far), near)
-    gathered = blocks.swapaxes(0, 1).reshape(-1, *both.shape)
-    cin = gathered.shape[0] * in_local
-    cout = gathered.shape[0] * out_local
+    swap = [(0, 1), (1, 0)]
+    got_far = lax.ppermute(both, far, swap)
+    got_near = lax.ppermute(both, near, swap)
+    got_diag = lax.ppermute(got_far, near, swap)
+    blocks = jnp.stack([both, got_near, got_far, got_diag])
+    groups = blocks.shape[0]
+    order = [jnp.bitwise_xor(my_group, j) for j in range(groups)]
+    up = [(i, i + 1) for i in range(slabs - 1)]
+    down = [(j, i) for i, j in up]
+    low = lax.ppermute(blocks[:, :, -width:], "gz", up)
+    high = lax.ppermute(blocks[:, :, :width], "gz", down)
+    cin = groups * in_local
+    cout = groups * out_local
     weight_cols = lax.dynamic_slice_in_dim(weight, my_group * out_local, out_local, 2)
+    weight_cols = by_group(weight_cols, order, in_local, 1)
     wf = jnp.transpose(weight_cols.reshape(3, 3, 3, cin, out_local), (0, 1, 2, 4, 3))
     wf = wf.reshape(9, 3 * out_local, cin)
     weight_rows = lax.dynamic_slice_in_dim(weight, my_group * in_local, in_local, 1)
+    weight_rows = by_group(weight_rows, order, out_local, 2)
     wb = weight_rows[::-1].reshape(9, 3 * in_local, cout)
-    out, ing, wg = fused(gathered, both, wf, wb, planes_local, grid_rows * grid_cols)
+    out, ing, wg = fused(blocks, low, high, wf, wb, planes_local, width)
+    wg = by_group(wg, order, in_local, 1)
     shape = (out_local, planes_local, grid_rows, grid_cols)
     out = jnp.transpose(out, (1, 0, 2)).reshape(shape)
     ing = jnp.transpose(ing, (1, 0, 2)).reshape(shape)

time: 106 us -> 91.8 us (0.87)
  blocking collectives: 7.53 us -> 0 us
  local copies, waits for them, and re-layouts: 16.3 us -> 12.7 us
  other arithmetic: 4.74 us -> 2.9 us
    all_to_all x1 -> x0, waiting for transfers between devices: 26.8 us -> none  [from_everyone(): return lax.all_to_all(copies, axis, split_axis=0, concat_axis=0, tiled=True)]
    ppermute x2 -> x5, waiting for transfers between devices: 5.12 us -> 31.6 us  [the longest x1 16.7 us: body(): high = lax.ppermute(blocks[:, :, :width], 'gz', down)]
    all_to_all x1 -> x0, blocking collectives: 7.53 us -> none  [from_everyone(): return lax.all_to_all(copies, axis, split_axis=0, concat_axis=0, tiled=True)]
    all_to_all x1 -> x0, starting transfers between devices: 5.39 us -> none  [from_everyone(): return lax.all_to_all(copies, axis, split_axis=0, concat_axis=0, tiled=True)]
    ppermute x2 -> x5, starting transfers between devices: 5.85 us -> 10.9 us  [the longest x1 5.52 us: body(): low = lax.ppermute(blocks[:, :, -width:], 'gz', up)]
    broadcast_in_dim x2 -> x0, local copies, waits for them, and re-layouts: 3.96 us -> none  [from_everyone(): copies = jnp.broadcast_to(shard, (lax.axis_size(axis), *shard.shape))]
    transpose x1, local copies, waits for them, and re-layouts: 2.43 us -> 0.31 us  [summed_on_arrival(): blocks = jnp.moveaxis(shard.reshape(*before, devices, -1, *after), dim, 0)]
    reshape x2 -> x0, local copies, waits for them, and re-layouts: 2.08 us -> none  [the longest x1 1.78 us: body(): jnp.pad(both, ((0, 0), (0, 0), (1, 1), (0, 0))).reshape(both.shape[0], -1)]
  transfers between devices with their start and end apart: 4 -> 6, of which waited for: 4 -> 5; matrix products, arithmetic and copies ran while one was open for 3% -> 6% of each run, Pallas kernels for 0% -> 0%
where the time goes in v3:
time: 91.8 us; the launch traced here: 91.5 us
  waiting for transfers between devices  38.9 us (42%)
  starting transfers between devices  23.9 us (26%)
  local copies, waits for them, and re-layouts  12.7 us (14%)
  Pallas kernels  12.4 us (14%)
  other arithmetic  2.9 us (3%)
    ppermute x1, waiting for transfers between devices, body(): high = lax.ppermute(blocks[:, :, :width], 'gz', down)  16.7 us
    all_to_all x1, starting transfers between devices, summed_on_arrival(): lax.all_to_all(blocks, axis, split_axis=0, concat_axis=0, tiled=True)  13 us
    pallas_call x1, Pallas kernels, fused(): pl.pallas_call(fused_kernel, out_shape=(jax.ShapeDtypeStruct((planes, loc...  12.4 us
    ppermute x1, waiting for transfers between devices, body(): got_far = lax.ppermute(both, far, swap)  11.9 us
    all_to_all x1, waiting for transfers between devices, summed_on_arrival(): lax.all_to_all(blocks, axis, split_axis=0, concat_axis=0, tiled=True)  7.3 us
    unnamed x22, local copies, waits for them, and re-layouts  6.26 us
    ppermute x1, starting transfers between devices, body(): low = lax.ppermute(blocks[:, :, -width:], 'gz', up)  5.52 us
    ppermute x1, starting transfers between devices, body(): got_far = lax.ppermute(both, far, swap)  4.07 us
  transfers between devices with their start and end apart: 6, of which 5 were waited for; matrix products, arithmetic and copies ran while one was open for 6% of the time, Pallas kernels for 0%

profile of v3, /device:TPU:0, one launch (start us, length us, event | category | flops | bytes accessed | tf_op | source)
XLA Modules:
  0.0 91.5 jit_solution(11924563277553333217)
XLA Ops:
  0.6 1.0 %constant_dynamic-update-slice_fusion.1 = bf16[64,2,16,128]{3,2,1,0:T(8,128)(2,1)S(1)} fusion(bf16[32,2,16,128]{3,2,1,0:T(8,128)(2,1)} %param.3), kind=kLoop, calls=%fused_computation.12 | loop fusion | bytes 524288
  1.6 1.0 %constant_dynamic-update-slice_fusion = bf16[64,2,16,128]{3,2,1,0:T(8,128)(2,1)S(1)} fusion(bf16[64,2,16,128]{3,2,1,0:T(8,128)(2,1)S(1)} %constant_dynamic-update-slice_fusion.1, bf16[32,2,16,128]{3,2,1,0:T(8,128)(2,1)} %param.5), kind=kLoop, calls=%fused_computation.11 | loop fusion | bytes 524288 | tf_op jit(solution)/shard_map/concatenate | solution.py:114
  2.6 0.2 copy.68
  2.8 4.1 %collective-permute-start.1 = (bf16[64,4096]{1,0:T(8,128)(2,1)S(1)}, bf16[64,4096]{1,0:T(8,128)(2,1)S(1)}, u32[]{:S(2)}, u32[]{:S(2)}) collective-permute-start(bf16[64,4096]{1,0:T(8,128)(2,1)S(1)} %bitcast.39), channel_id=1, source_target_pairs={{0,2},{2,0},{1,3},{3,1},{4,6},{6,4},{5,7},{7,5},{8,10},{10,8},{9,1... | collective-permute-start | bytes 1572872 | tf_op jit(solution)/shard_map/ppermute | solution.py:117
  6.9 0.0 collective-permute-start
  6.9 11.9 %collective-permute-done.1 = bf16[64,4096]{1,0:T(8,128)(2,1)S(1)} collective-permute-done((bf16[64,4096]{1,0:T(8,128)(2,1)S(1)}, bf16[64,4096]{1,0:T(8,128)(2,1)S(1)}, u32[]{:S(2)}, u32[]{:S(2)}) %collective-permute-start.1) | collective-permute-done | bytes 524320 | tf_op jit(solution)/shard_map/ppermute | solution.py:117
  18.8 0.0 collective-permute-start.2
  18.8 0.2 stack_reshape.3
  19.0 0.0 collective-permute-done
  19.0 1.7 %collective-permute-done.2 = bf16[64,4096]{1,0:T(8,128)(2,1)S(1)} collective-permute-done((bf16[64,4096]{1,0:T(8,128)(2,1)S(1)}, bf16[64,4096]{1,0:T(8,128)(2,1)S(1)}, u32[]{:S(2)}, u32[]{:S(2)}) %collective-permute-start.2) | collective-permute-done | bytes 524320 | tf_op jit(solution)/shard_map/ppermute | solution.py:119
  20.7 0.3 pad_maximum_fusion.b_ref
  21.0 0.0 copy-start
  21.0 0.0 copy-start.1
  21.0 1.5 %fusion = (bf16[4,64,2048]{2,1,0:T(8,128)(2,1)}, bf16[4,64,2048]{2,1,0:T(8,128)(2,1)}) fusion(bf16[4,64,4096]{2,1,0:T(8,128)(2,1)S(1)} %pad_maximum_fusion.b_ref), kind=kLoop, calls=%fused_computation.20 | loop fusion | bytes 4194304 | tf_op jit(solution)/shard_map/slice | solution.py:126
  22.4 0.5 copy-done
  23.0 1.3 %collective-permute-start.4 = (bf16[4,64,2048]{2,1,0:T(8,128)(2,1)}, bf16[4,64,2048]{2,1,0:T(8,128)(2,1)S(1)}, u32[]{:S(2)}, u32[]{:S(2)}) collective-permute-start(bf16[4,64,2048]{2,1,0:T(8,128)(2,1)} %get-tuple-element.24), channel_id=1, source_target_pairs={{4,0},{8,4},{12,8},{16,12},{20,16},{24,20},{28,24},{32,28},{36,32}... | collective-permute-start | bytes 3145736 | tf_op jit(solution)/shard_map/ppermute | solution.py:126
  24.3 5.5 %collective-permute-start.3 = (bf16[4,64,2048]{2,1,0:T(8,128)(2,1)}, bf16[4,64,2048]{2,1,0:T(8,128)(2,1)}, u32[]{:S(2)}, u32[]{:S(2)}) collective-permute-start(bf16[4,64,2048]{2,1,0:T(8,128)(2,1)} %get-tuple-element.25), channel_id=1, source_target_pairs={{0,4},{4,8},{8,12},{12,16},{16,20},{20,24},{24,28},{28,32},{32,36}... | collective-permute-start | bytes 3145736 | tf_op jit(solution)/shard_map/ppermute | solution.py:125
  29.8 0.0 copy-done.1
  29.8 1.1 %constant_dynamic-slice_fusion.2 = (bf16[27,32,32]{2,1,0:T(8,128)(2,1)S(1)}, bf16[27,32,32]{2,1,0:T(8,128)(2,1)S(1)}, bf16[27,32,32]{2,1,0:T(8,128)(2,1)S(1)}, b...) fusion(bf16[27,128,128]{2,1,0:T(8,128)(2,1)S(1)} %copy-done.1, ...), kind=kLoop, calls=%fused_computation.15 | loop fusion | bytes 774160 | tf_op jit(solution)/shard_map/dynamic_slice | solution.py:103
  31.0 0.2 copy.60
  31.1 0.3 pad_maximum_fusion.3
  31.4 0.7 rev.3
  32.1 0.2 copy.62
  32.3 0.2 copy.61
  32.4 0.2 copy.63
  32.6 1.0 %pad_maximum_fusion.2 = bf16[27,128,32]{1,2,0:T(8,128)(2,1)} fusion(bf16[27,32,32]{1,2,0:T(8,128)(2,1)S(1)} %copy.63, bf16[27,32,32]{1,2,0:T(8,128)(2,1)S(1)} %copy.62, bf16[27,32,32]{1,2,0:T(8,128)(2,1)S(1)} %copy.61, bf16[27,32,32]{1,2,0:T(8,128)(2,1)S(1)} %copy.60), kind=kLoop, calls=%fused_computation.8 | loop fusion | flops 884736 | bytes 442368 | tf_op jit(solution)/shard_map/concatenate | solution.py:102
  33.6 16.7 %collective-permute-done.4.hi_ref = bf16[4,64,2048]{2,1,0:T(8,128)(2,1)S(1)} collective-permute-done((bf16[4,64,2048]{2,1,0:T(8,128)(2,1)}, bf16[4,64,2048]{2,1,0:T(8,128)(2,1)S(1)}, u32[]{:S(2)}, u32[]{:S(2)}) %collective-permute-start.4) | collective-permute-done | bytes 1048608 | tf_op jit(solution)/shard_map/ppermute | solution.py:126
  50.3 0.0 copy-start.2
  50.3 1.3 %collective-permute-done.3.lo_ref = bf16[4,64,2048]{2,1,0:T(8,128)(2,1)} collective-permute-done((bf16[4,64,2048]{2,1,0:T(8,128)(2,1)}, bf16[4,64,2048]{2,1,0:T(8,128)(2,1)}, u32[]{:S(2)}, u32[]{:S(2)}) %collective-permute-start.3) | collective-permute-done | bytes 1048608 | tf_op jit(solution)/shard_map/ppermute | solution.py:125
  51.6 0.0 copy-done.2
  51.6 12.4 %shard_map.58 = (bf16[2,32,2048]{2,1,0:T(8,128)(2,1)}, bf16[2,32,2048]{2,1,0:T(8,128)(2,1)}, f32[27,128,32]{2,1,0:T(8,128)}) custom-call(bf16[4,64,4096]{2,1,0:T(8,128)(2,1)} %copy-done, bf16[4,64,2048]{2,1,0:T(8,128)(2,1)} %collective-permute-done.3.lo_ref, bf16[4,64,2048]{2,1,0:T(8,128)(2,1)} %copy-done.2, bf16[9,96,128]{2,1,0:T(8,128)(2,1)} %bitcast.38, ...), custom_call_target="tpu_custom_call" | custom-call | tf_op jit(solution)/shard_map/pallas_call | solution.py:87
  64.0 1.6 %dynamic-slice_convert_fusion.3 = (bf16[27,32,32]{2,1,0:T(8,128)(2,1)S(1)}, bf16[27,32,32]{2,1,0:T(8,128)(2,1)S(1)}, bf16[27,32,32]{2,1,0:T(8,128)(2,1)S(1)}, bf16[27,32,32]{2,1,0:T(8,128)(2,1)S(1)}) fusion(f32[27,128,32]{2,1,0:T(8,128)} %get-tuple-element.8, s32[]{:T(128)S(6)} %select_n.30, s32[]{:T(128)S(6)} %select_n.36, s32[]{:T(128)S(6)} %select_n.34, ...), kind=kLoop, calls=%fused_computation.7 | loop fusion | bytes 442384 | tf_op jit(solution)/shard_map/convert
  65.6 0.2 pad_maximum_fusion.1
  65.8 0.0 copy-start.4
  65.9 0.0 copy-start.3
  65.9 0.3 copy.57
  66.2 1.6 %reshape.33 = bf16[32,2,1728]{2,1,0:T(2,128)(2,1)} reshape(bf16[32,27,4,32]{3,2,1,0:T(4,128)(2,1)S(1)} %copy.57) | data formatting | bytes 442368
  67.8 13.0 %all-to-all-start = ((bf16[32,2,1728]{2,1,0:T(2,128)(2,1)}), bf16[32,2,1728]{2,1,0:T(2,128)(2,1)S(1)}, u32[]{:S(2)}, u32[]{:S(2)}) async-start(bf16[32,2,1728]{2,1,0:T(2,128)(2,1)} %reshape.33), calls=%async_computation | async-start | bytes 458752 | tf_op jit(solution)/shard_map/all_to_all | solution.py:19
  80.8 0.0 copy-done.4
  80.9 0.7 copy.58
  81.6 0.0 copy-done.3
  81.6 0.7 copy.59
  82.4 7.3 %all-to-all-done = bf16[32,2,1728]{2,1,0:T(2,128)(2,1)S(1)} async-done(((bf16[32,2,1728]{2,1,0:T(2,128)(2,1)}), bf16[32,2,1728]{2,1,0:T(2,128)(2,1)S(1)}, u32[]{:S(2)}, u32[]{:S(2)}) %all-to-all-start) | async-done | bytes 221216 | tf_op jit(solution)/shard_map/all_to_all | solution.py:19
  89.7 0.8 reshape.34
  90.4 0.5 convert_reduce_fusion
  90.9 0.6 broadcast_multiply_fusion
  (2 shorter events, 0.1 us)
Async XLA Ops:
  2.8 16.0 %collective-permute-start.1 = (bf16[64,4096]{1,0:T(8,128)(2,1)S(1)}, bf16[64,4096]{1,0:T(8,128)(2,1)S(1)}, u32[]{:S(2)}, u32[]{:S(2)}) collective-permute-start(bf16[64,4096]{1,0:T(8,128)(2,1)S(1)} %bitcast.39), channel_id=1, source_target_pairs={{0,2},{2,0},{1,3},{3,1},{4,6},{6,4},{5,7},{7,5},{8,10},{10,8},{9,1... | collective-permute-start | bytes 1572872 | tf_op jit(solution)/shard_map/ppermute | solution.py:117
  6.9 12.2 %collective-permute-start = (bf16[64,4096]{1,0:T(8,128)(2,1)S(1)}, bf16[64,4096]{1,0:T(8,128)(2,1)S(1)}, u32[]{:S(2)}, u32[]{:S(2)}) collective-permute-start(bf16[64,4096]{1,0:T(8,128)(2,1)S(1)} %bitcast.40), channel_id=1, source_target_pairs={{0,1},{1,0},{2,3},{3,2},{4,5},{5,4},{6,7},{7,6},{8,9},{9,8},{10,11... | collective-permute-start | bytes 1572872 | tf_op jit(solution)/shard_map/ppermute | solution.py:118
  18.8 1.9 %collective-permute-start.2 = (bf16[64,4096]{1,0:T(8,128)(2,1)S(1)}, bf16[64,4096]{1,0:T(8,128)(2,1)S(1)}, u32[]{:S(2)}, u32[]{:S(2)}) collective-permute-start(bf16[64,4096]{1,0:T(8,128)(2,1)S(1)} %collective-permute-done.1), channel_id=1, source_target_pairs={{0,1},{1,0},{2,3},{3,2},{4,5},{5,4},{6,7},{7,6},{8,9},{9,8},{10,11... | collective-permute-start | bytes 1572872 | tf_op jit(solution)/shard_map/ppermute | solution.py:119
  21.0 2.0 %copy-start = (bf16[4,64,4096]{2,1,0:T(8,128)(2,1)}, bf16[4,64,4096]{2,1,0:T(8,128)(2,1)S(1)}, u32[]{:S(2)}) copy-start(bf16[4,64,4096]{2,1,0:T(8,128)(2,1)S(1)} %pad_maximum_fusion.b_ref) | copy-start | bytes 6291460
  21.0 8.8 %copy-start.1 = (bf16[27,128,128]{2,1,0:T(8,128)(2,1)S(1)}, bf16[27,128,128]{2,1,0:T(8,128)(2,1)}, u32[]{:S(2)}) copy-start(bf16[27,128,128]{2,1,0:T(8,128)(2,1)} %param.4) | copy-start | bytes 2654212
  23.0 27.3 %collective-permute-start.4 = (bf16[4,64,2048]{2,1,0:T(8,128)(2,1)}, bf16[4,64,2048]{2,1,0:T(8,128)(2,1)S(1)}, u32[]{:S(2)}, u32[]{:S(2)}) collective-permute-start(bf16[4,64,2048]{2,1,0:T(8,128)(2,1)} %get-tuple-element.24), channel_id=1, source_target_pairs={{4,0},{8,4},{12,8},{16,12},{20,16},{24,20},{28,24},{32,28},{36,32}... | collective-permute-start | bytes 3145736 | tf_op jit(solution)/shard_map/ppermute | solution.py:126
  24.3 27.3 %collective-permute-start.3 = (bf16[4,64,2048]{2,1,0:T(8,128)(2,1)}, bf16[4,64,2048]{2,1,0:T(8,128)(2,1)}, u32[]{:S(2)}, u32[]{:S(2)}) collective-permute-start(bf16[4,64,2048]{2,1,0:T(8,128)(2,1)} %get-tuple-element.25), channel_id=1, source_target_pairs={{0,4},{4,8},{8,12},{12,16},{16,20},{20,24},{24,28},{28,32},{32,36}... | collective-permute-start | bytes 3145736 | tf_op jit(solution)/shard_map/ppermute | solution.py:125
  50.3 1.3 %copy-start.2 = (bf16[4,64,2048]{2,1,0:T(8,128)(2,1)}, bf16[4,64,2048]{2,1,0:T(8,128)(2,1)S(1)}, u32[]{:S(2)}) copy-start(bf16[4,64,2048]{2,1,0:T(8,128)(2,1)S(1)} %collective-permute-done.4.hi_ref) | copy-start | bytes 3145732
  65.8 15.0 %copy-start.4 = (bf16[2,32,2048]{2,1,0:T(8,128)(2,1)S(1)}, bf16[2,32,2048]{2,1,0:T(8,128)(2,1)}, u32[]{:S(2)}) copy-start(bf16[2,32,2048]{2,1,0:T(8,128)(2,1)} %get-tuple-element.6) | copy-start | bytes 786436
  65.9 15.7 %copy-start.3 = (bf16[2,32,2048]{2,1,0:T(8,128)(2,1)S(1)}, bf16[2,32,2048]{2,1,0:T(8,128)(2,1)}, u32[]{:S(2)}) copy-start(bf16[2,32,2048]{2,1,0:T(8,128)(2,1)} %get-tuple-element.7) | copy-start | bytes 786436
  67.8 21.9 %all-to-all-start = ((bf16[32,2,1728]{2,1,0:T(2,128)(2,1)}), bf16[32,2,1728]{2,1,0:T(2,128)(2,1)S(1)}, u32[]{:S(2)}, u32[]{:S(2)}) async-start(bf16[32,2,1728]{2,1,0:T(2,128)(2,1)} %reshape.33), calls=%async_computation | async-start | bytes 458752 | tf_op jit(solution)/shard_map/all_to_all | solution.py:19

commit v4 on v3

--- a/solution.py
+++ b/solution.py
@@ -19,26 +19,35 @@
     arrived = lax.all_to_all(blocks, axis, split_axis=0, concat_axis=0, tiled=True)
     return arrived.astype(jnp.float32).sum(axis=0)
 
-def fused_kernel(b_ref, lo_ref, hi_ref, wf_ref, wb_ref, out_ref, ing_ref, wg_ref, vs_ref, cs_ref):
-    groups, both, _ = b_ref.shape
+def fused_kernel(
+    own_ref, far_ref, near_ref, lo_ref, hi_ref, flo_ref, fhi_ref, hal_ref, wf_ref, wb_ref,
+    out_ref, ing_ref, wg_ref, vs_ref, cs_ref,
+):
+    both = own_ref.shape[0]
     loc = both // 2
     planes, _, width = out_ref.shape
     plane = width + 2 * ROW
     span = (planes - 1) * plane + width
     blank = jnp.zeros((loc, ROW), jnp.bfloat16)
-    for k in range(groups):
+    pieces = (
+        (lambda c: own_ref[c, :], lambda c: lo_ref[c, :], lambda c: hi_ref[c, :]),
+        (lambda c: near_ref[0, c, :], lambda c: hal_ref[0, c, :], lambda c: hal_ref[1, c, :]),
+        (lambda c: far_ref[c, :], lambda c: flo_ref[c, :], lambda c: fhi_ref[c, :]),
+        (lambda c: near_ref[1, c, :], lambda c: hal_ref[2, c, :], lambda c: hal_ref[3, c, :]),
+    )
+    for k, (body_of, low_of, high_of) in enumerate(pieces):
         rows = slice(k * loc, (k + 1) * loc)
         for ref, low in ((vs_ref, 0), (cs_ref, loc)):
             chans = slice(low, low + loc)
             for zp in range(planes + 2):
                 ref[rows, zp * plane : zp * plane + ROW] = blank
                 ref[rows, zp * plane + ROW + width : (zp + 1) * plane] = blank
-            ref[rows, ROW : ROW + width] = lo_ref[k, chans, :]
+            ref[rows, ROW : ROW + width] = low_of(chans)
             for z in range(planes):
                 at = (z + 1) * plane + ROW
-                ref[rows, at : at + width] = b_ref[k, chans, z * width : (z + 1) * width]
+                ref[rows, at : at + width] = body_of(chans)[:, z * width : (z + 1) * width]
             at = (planes + 1) * plane + ROW
-            ref[rows, at : at + width] = hi_ref[k, chans, :]
+            ref[rows, at : at + width] = high_of(chans)
     lane = lax.broadcasted_iota(jnp.int32, (loc, span), 1) % ROW
     first = lane == 0
     last = lane == ROW - 1
@@ -79,10 +88,10 @@
         ing_ref[z] = acc_i[:, z * plane : z * plane + width].astype(ing_ref.dtype)
 
 
-def fused(body, low, high, wf, wb, planes, width):
-    groups, both, _ = body.shape
+def fused(own, far, near, low, high, far_low, far_high, halos, wf, wb, planes, width):
+    both = own.shape[0]
     loc = both // 2
-    cin = groups * loc
+    cin = 4 * loc
     flat = (planes + 2) * (width + 2 * ROW)
     return pl.pallas_call(
         fused_kernel,
@@ -95,7 +104,7 @@
             pltpu.VMEM((cin, flat), jnp.bfloat16),
             pltpu.VMEM((cin, flat), jnp.bfloat16),
         ],
-    )(body, low, high, wf, wb)
+    )(own, far, near, low, high, far_low, far_high, halos, wf, wb)
 
 
 def by_group(array, order, size, dim):
@@ -114,16 +123,17 @@
     both = jnp.concatenate([volume, cotangent], axis=0).reshape(in_local + out_local, -1)
     far, near = CH
     swap = [(0, 1), (1, 0)]
-    got_far = lax.ppermute(both, far, swap)
-    got_near = lax.ppermute(both, near, swap)
-    got_diag = lax.ppermute(got_far, near, swap)
-    blocks = jnp.stack([both, got_near, got_far, got_diag])
-    groups = blocks.shape[0]
-    order = [jnp.bitwise_xor(my_group, j) for j in range(groups)]
     up = [(i, i + 1) for i in range(slabs - 1)]
     down = [(j, i) for i, j in up]
-    low = lax.ppermute(blocks[:, :, -width:], "gz", up)
-    high = lax.ppermute(blocks[:, :, :width], "gz", down)
+    got_far = lax.ppermute(both, far, swap)
+    low = lax.ppermute(both[:, -width:], "gz", up)
+    high = lax.ppermute(both[:, :width], "gz", down)
+    far_low = lax.ppermute(got_far[:, -width:], "gz", up)
+    far_high = lax.ppermute(got_far[:, :width], "gz", down)
+    got_near = lax.ppermute(jnp.stack([both, got_far]), near, swap)
+    halos = lax.ppermute(jnp.stack([low, high, far_low, far_high]), near, swap)
+    groups = 4
+    order = [jnp.bitwise_xor(my_group, j) for j in range(groups)]
     cin = groups * in_local
     cout = groups * out_local
     weight_cols = lax.dynamic_slice_in_dim(weight, my_group * out_local, out_local, 2)
@@ -133,7 +143,9 @@
     weight_rows = lax.dynamic_slice_in_dim(weight, my_group * in_local, in_local, 1)
     weight_rows = by_group(weight_rows, order, out_local, 2)
     wb = weight_rows[::-1].reshape(9, 3 * in_local, cout)
-    out, ing, wg = fused(blocks, low, high, wf, wb, planes_local, width)
+    out, ing, wg = fused(
+        both, got_far, got_near, low, high, far_low, far_high, halos, wf, wb, planes_local, width
+    )
     wg = by_group(wg, order, in_local, 1)
     shape = (out_local, planes_local, grid_rows, grid_cols)
     out = jnp.transpose(out, (1, 0, 2)).reshape(shape)

time: 91.8 us -> 76.5 us (0.83)
  waiting for transfers between devices: 38.9 us -> 16.5 us
  starting transfers between devices: 23.9 us -> 29.7 us
  other arithmetic: 2.9 us -> 4.97 us
  local copies, waits for them, and re-layouts: 12.7 us -> 11.6 us
    ppermute x4 -> x6, waiting for transfers between devices: 19.6 us -> 4.44 us  [the longest x1 3.25 us: body(): far_high = lax.ppermute(got_far[:, :width], 'gz', down)]
    ppermute x1, waiting for transfers between devices: 11.9 us -> 4.32 us  [body(): got_far = lax.ppermute(both, far, swap)]
    ppermute x4 -> x6, starting transfers between devices: 6.81 us -> 12.5 us  [the longest x1 5.27 us: body(): low = lax.ppermute(both[:, -width:], 'gz', up)]
    another operation x1 -> x2, other arithmetic: 0.26 us -> 2.33 us  [the longest x1 2.24 us: body(): halos = lax.ppermute(jnp.stack([low, high, far_low, far_high]), near, swap)]
    unnamed x22 -> x26, local copies, waits for them, and re-layouts: 6.26 us -> 5.72 us
  transfers between devices with their start and end apart: 6 -> 8, of which waited for: 5 -> 4; matrix products, arithmetic and copies ran while one was open for 6% -> 11% of each run, Pallas kernels for 0% -> 0%
where the time goes in v4:
time: 76.5 us; the launch traced here: 76.1 us
  starting transfers between devices  29.7 us (39%)
  waiting for transfers between devices  16.5 us (22%)
  Pallas kernels  12.5 us (16%)
  local copies, waits for them, and re-layouts  11.6 us (15%)
  other arithmetic  4.97 us (6%)
  between operations  0.89 us (1%)
    all_to_all x1, starting transfers between devices, summed_on_arrival(): lax.all_to_all(blocks, axis, split_axis=0, concat_axis=0, tiled=True)  13.1 us
    pallas_call x1, Pallas kernels, fused(): pl.pallas_call(fused_kernel, out_shape=(jax.ShapeDtypeStruct((planes, loc...  12.5 us
    all_to_all x1, waiting for transfers between devices, summed_on_arrival(): lax.all_to_all(blocks, axis, split_axis=0, concat_axis=0, tiled=True)  7.73 us
    unnamed x26, local copies, waits for them, and re-layouts  5.72 us
    ppermute x1, starting transfers between devices, body(): low = lax.ppermute(both[:, -width:], 'gz', up)  5.27 us
    ppermute x1, starting transfers between devices, body(): far_low = lax.ppermute(got_far[:, -width:], 'gz', up)  4.56 us
    ppermute x1, waiting for transfers between devices, body(): got_far = lax.ppermute(both, far, swap)  4.32 us
    ppermute x1, starting transfers between devices, body(): got_far = lax.ppermute(both, far, swap)  4.07 us
  transfers between devices with their start and end apart: 8, of which 4 were waited for; matrix products, arithmetic and copies ran while one was open for 11% of the time, Pallas kernels for 0%

profile of v4, /device:TPU:0, one launch (start us, length us, event | category | flops | bytes accessed | tf_op | source)
XLA Modules:
  0.0 76.1 jit_solution(4726298074680709253)
XLA Ops:
  0.6 1.0 %constant_dynamic-update-slice_fusion.1 = bf16[64,2,16,128]{3,2,1,0:T(8,128)(2,1)S(1)} fusion(bf16[32,2,16,128]{3,2,1,0:T(8,128)(2,1)} %param.3), kind=kLoop, calls=%fused_computation.13 | loop fusion | bytes 524288
  1.6 1.0 %constant_dynamic-update-slice_fusion = bf16[64,2,16,128]{3,2,1,0:T(8,128)(2,1)S(1)} fusion(bf16[64,2,16,128]{3,2,1,0:T(8,128)(2,1)S(1)} %constant_dynamic-update-slice_fusion.1, bf16[32,2,16,128]{3,2,1,0:T(8,128)(2,1)} %param.5), kind=kLoop, calls=%fused_computation.12 | loop fusion | bytes 524288 | tf_op jit(solution)/shard_map/concatenate | solution.py:123
  2.6 0.2 copy.68
  2.8 0.0 copy-start
  2.8 4.1 %collective-permute-start = (bf16[64,4096]{1,0:T(8,128)(2,1)S(1)}, bf16[64,4096]{1,0:T(8,128)(2,1)S(1)}, u32[]{:S(2)}, u32[]{:S(2)}) collective-permute-start(bf16[64,4096]{1,0:T(8,128)(2,1)S(1)} %bitcast.35), channel_id=1, source_target_pairs={{0,2},{2,0},{1,3},{3,1},{4,6},{6,4},{5,7},{7,5},{8,10},{10,8},{9,1... | collective-permute-start | bytes 1572872 | tf_op jit(solution)/shard_map/ppermute | solution.py:128
  6.9 0.8 %fusion.1 = (bf16[64,2048]{1,0:T(8,128)(2,1)}, bf16[64,2048]{1,0:T(8,128)(2,1)}) fusion(bf16[64,4096]{1,0:T(8,128)(2,1)S(1)} %bitcast.36), kind=kLoop, calls=%fused_computation.22 | loop fusion | bytes 1048576 | tf_op jit(solution)/shard_map/slice | solution.py:130
  7.7 1.3 %collective-permute-start.3 = (bf16[64,2048]{1,0:T(8,128)(2,1)}, bf16[64,2048]{1,0:T(8,128)(2,1)}, u32[]{:S(2)}, u32[]{:S(2)}) collective-permute-start(bf16[64,2048]{1,0:T(8,128)(2,1)} %get-tuple-element.37), channel_id=1, source_target_pairs={{4,0},{8,4},{12,8},{16,12},{20,16},{24,20},{28,24},{32,28},{36,32}... | collective-permute-start | bytes 786440 | tf_op jit(solution)/shard_map/ppermute | solution.py:130
  9.0 5.3 %collective-permute-start.2 = (bf16[64,2048]{1,0:T(8,128)(2,1)}, bf16[64,2048]{1,0:T(8,128)(2,1)}, u32[]{:S(2)}, u32[]{:S(2)}) collective-permute-start(bf16[64,2048]{1,0:T(8,128)(2,1)} %get-tuple-element.38), channel_id=1, source_target_pairs={{0,4},{4,8},{8,12},{12,16},{16,20},{20,24},{24,28},{28,32},{32,36}... | collective-permute-start | bytes 786440 | tf_op jit(solution)/shard_map/ppermute | solution.py:129
  14.3 0.2 stack_reshape.3
  14.5 4.3 %collective-permute-done.far_ref = bf16[64,4096]{1,0:T(8,128)(2,1)S(1)} collective-permute-done((bf16[64,4096]{1,0:T(8,128)(2,1)S(1)}, bf16[64,4096]{1,0:T(8,128)(2,1)S(1)}, u32[]{:S(2)}, u32[]{:S(2)}) %collective-permute-start) | collective-permute-done | bytes 524320 | tf_op jit(solution)/shard_map/ppermute | solution.py:128
  18.9 1.3 %collective-permute-start.5 = (bf16[64,2048]{1,0:T(8,128)(2,1)S(1)}, bf16[64,2048]{1,0:T(8,128)(2,1)S(1)}, u32[]{:S(2)}, u32[]{:S(2)}) collective-permute-start(bf16[64,2048]{1,0:T(8,128)(2,1)S(1)} %get-tuple-element.35), channel_id=1, source_target_pairs={{4,0},{8,4},{12,8},{16,12},{20,16},{24,20},{28,24},{32,28},{36,32}... | collective-permute-start | bytes 786440 | tf_op jit(solution)/shard_map/ppermute | solution.py:132
  20.2 4.6 %collective-permute-start.4 = (bf16[64,2048]{1,0:T(8,128)(2,1)S(1)}, bf16[64,2048]{1,0:T(8,128)(2,1)S(1)}, u32[]{:S(2)}, u32[]{:S(2)}) collective-permute-start(bf16[64,2048]{1,0:T(8,128)(2,1)S(1)} %get-tuple-element.36), channel_id=1, source_target_pairs={{0,4},{4,8},{8,12},{12,16},{16,20},{20,24},{24,28},{28,32},{32,36}... | collective-permute-start | bytes 786440 | tf_op jit(solution)/shard_map/ppermute | solution.py:131
  24.7 0.0 copy-start.2
  24.7 0.1 pad_maximum_fusion
  24.9 0.1 collective-permute-start.1
  25.0 0.0 collective-permute-done.3.hi_ref
  25.0 0.0 collective-permute-done.2.lo_ref
  25.0 3.2 %collective-permute-done.5.fhi_ref = bf16[64,2048]{1,0:T(8,128)(2,1)S(1)} collective-permute-done((bf16[64,2048]{1,0:T(8,128)(2,1)S(1)}, bf16[64,2048]{1,0:T(8,128)(2,1)S(1)}, u32[]{:S(2)}, u32[]{:S(2)}) %collective-permute-start.5) | collective-permute-done | bytes 262176 | tf_op jit(solution)/shard_map/ppermute | solution.py:132
  28.2 1.2 %collective-permute-done.4.flo_ref = bf16[64,2048]{1,0:T(8,128)(2,1)S(1)} collective-permute-done((bf16[64,2048]{1,0:T(8,128)(2,1)S(1)}, bf16[64,2048]{1,0:T(8,128)(2,1)S(1)}, u32[]{:S(2)}, u32[]{:S(2)}) %collective-permute-start.4) | collective-permute-done | bytes 262176 | tf_op jit(solution)/shard_map/ppermute | solution.py:131
  29.4 2.2 %pad_maximum_fusion.1 = bf16[4,64,2048]{2,1,0:T(8,128)(2,1)} fusion(bf16[1,64,2048]{2,1,0:T(8,128)(2,1)S(1)} %bitcast.43, bf16[1,64,2048]{2,1,0:T(8,128)(2,1)S(1)} %bitcast.44, bf16[1,64,2048]{2,1,0:T(8,128)(2,1)} %bitcast.2, bf16[1,64,2048]{2,1,0:T(8,128)(2,1)} %bitcast.1), kind=kLoop, calls=%fused_computation.2 | loop fusion | flops 1572864 | bytes 2097152 | tf_op jit(solution)/shard_map/stack | solution.py:134
  31.6 0.0 collective-permute-start.6
  31.7 0.0 copy-done.4
  31.7 1.2 %constant_dynamic-slice_fusion.2 = (bf16[27,32,32]{2,1,0:T(8,128)(2,1)S(1)}, bf16[27,32,32]{2,1,0:T(8,128)(2,1)S(1)}, bf16[27,32,32]{2,1,0:T(8,128)(2,1)S(1)}, b...) fusion(bf16[27,128,128]{2,1,0:T(8,128)(2,1)S(1)} %copy-done.2, ...), kind=kLoop, calls=%fused_computation.16 | loop fusion | bytes 774160 | tf_op jit(solution)/shard_map/dynamic_slice | solution.py:112
  32.9 0.2 copy.60
  33.0 0.3 pad_maximum_fusion.4
  33.3 0.7 rev.3
  34.0 0.2 copy.62
  34.2 0.2 copy.61
  34.4 0.2 copy.63
  34.5 1.0 %pad_maximum_fusion.3 = bf16[27,128,32]{1,2,0:T(8,128)(2,1)} fusion(bf16[27,32,32]{1,2,0:T(8,128)(2,1)S(1)} %copy.63, bf16[27,32,32]{1,2,0:T(8,128)(2,1)S(1)} %copy.62, bf16[27,32,32]{1,2,0:T(8,128)(2,1)S(1)} %copy.61, bf16[27,32,32]{1,2,0:T(8,128)(2,1)S(1)} %copy.60), kind=kLoop, calls=%fused_computation.9 | loop fusion | flops 884736 | bytes 442368 | tf_op jit(solution)/shard_map/concatenate | solution.py:111
  35.5 0.0 collective-permute-done.1.near_ref
  35.5 0.0 collective-permute-done.6.hal_ref
  35.5 12.5 %shard_map.58 = (bf16[2,32,2048]{2,1,0:T(8,128)(2,1)}, bf16[2,32,2048]{2,1,0:T(8,128)(2,1)}, f32[27,128,32]{2,1,0:T(8,128)}) custom-call(bf16[64,4096]{1,0:T(8,128)(2,1)} %bitcast.37, bf16[64,4096]{1,0:T(8,128)(2,1)} %copy-done.1, bf16[2,64,4096]{2,1,0:T(8,128)(2,1)} %collective-permute-done.1.near_ref, bf16[64,2048]{1,0:T(8,128)(2,1)} %collective-permute-done.2.lo_ref, ...), custom_call_target="tpu_custom_call" | custom-call | tf_op jit(solution)/shard_map/pallas_call | solution.py:96
  48.0 1.6 %dynamic-slice_convert_fusion.3 = (bf16[27,32,32]{2,1,0:T(8,128)(2,1)S(1)}, bf16[27,32,32]{2,1,0:T(8,128)(2,1)S(1)}, bf16[27,32,32]{2,1,0:T(8,128)(2,1)S(1)}, bf16[27,32,32]{2,1,0:T(8,128)(2,1)S(1)}) fusion(f32[27,128,32]{2,1,0:T(8,128)} %get-tuple-element.8, s32[]{:T(128)S(6)} %select_n.30, s32[]{:T(128)S(6)} %select_n.36, s32[]{:T(128)S(6)} %select_n.34, ...), kind=kLoop, calls=%fused_computation.8 | loop fusion | bytes 442384 | tf_op jit(solution)/shard_map/convert
  49.6 0.2 pad_maximum_fusion.2
  49.9 0.0 copy-start.6
  49.9 0.0 copy-start.5
  49.9 0.3 copy.57
  50.2 1.6 %reshape.33 = bf16[32,2,1728]{2,1,0:T(2,128)(2,1)} reshape(bf16[32,27,4,32]{3,2,1,0:T(4,128)(2,1)S(1)} %copy.57) | data formatting | bytes 442368
  51.8 13.1 %all-to-all-start = ((bf16[32,2,1728]{2,1,0:T(2,128)(2,1)}), bf16[32,2,1728]{2,1,0:T(2,128)(2,1)S(1)}, u32[]{:S(2)}, u32[]{:S(2)}) async-start(bf16[32,2,1728]{2,1,0:T(2,128)(2,1)} %reshape.33), calls=%async_computation | async-start | bytes 458752 | tf_op jit(solution)/shard_map/all_to_all | solution.py:19
  64.9 0.0 copy-done.6
  65.0 0.7 copy.58
  65.7 0.0 copy-done.5
  65.8 0.7 copy.59
  66.5 7.7 %all-to-all-done = bf16[32,2,1728]{2,1,0:T(2,128)(2,1)S(1)} async-done(((bf16[32,2,1728]{2,1,0:T(2,128)(2,1)}), bf16[32,2,1728]{2,1,0:T(2,128)(2,1)S(1)}, u32[]{:S(2)}, u32[]{:S(2)}) %all-to-all-start) | async-done | bytes 221216 | tf_op jit(solution)/shard_map/all_to_all | solution.py:19
  74.2 0.8 reshape.34
  75.0 0.5 convert_reduce_fusion
  75.4 0.6 broadcast_multiply_fusion
  (10 shorter events, 0.1 us)
Async XLA Ops:
  2.8 22.0 %copy-start = (bf16[8,8,32,128]{3,1,2,0:T(8,128)(2,1)}, bf16[8,8,32,128]{3,1,2,0:T(8,128)(2,1)S(1)}, u32[]{:S(2)}) copy-start(bf16[8,8,32,128]{3,1,2,0:T(8,128)(2,1)S(1)} %copy.68) | copy-start | bytes 1572868
  2.8 16.0 %collective-permute-start = (bf16[64,4096]{1,0:T(8,128)(2,1)S(1)}, bf16[64,4096]{1,0:T(8,128)(2,1)S(1)}, u32[]{:S(2)}, u32[]{:S(2)}) collective-permute-start(bf16[64,4096]{1,0:T(8,128)(2,1)S(1)} %bitcast.35), channel_id=1, source_target_pairs={{0,2},{2,0},{1,3},{3,1},{4,6},{6,4},{5,7},{7,5},{8,10},{10,8},{9,1... | collective-permute-start | bytes 1572872 | tf_op jit(solution)/shard_map/ppermute | solution.py:128
  7.7 17.2 %collective-permute-start.3 = (bf16[64,2048]{1,0:T(8,128)(2,1)}, bf16[64,2048]{1,0:T(8,128)(2,1)}, u32[]{:S(2)}, u32[]{:S(2)}) collective-permute-start(bf16[64,2048]{1,0:T(8,128)(2,1)} %get-tuple-element.37), channel_id=1, source_target_pairs={{4,0},{8,4},{12,8},{16,12},{20,16},{24,20},{28,24},{32,28},{36,32}... | collective-permute-start | bytes 786440 | tf_op jit(solution)/shard_map/ppermute | solution.py:130
  9.0 16.0 %collective-permute-start.2 = (bf16[64,2048]{1,0:T(8,128)(2,1)}, bf16[64,2048]{1,0:T(8,128)(2,1)}, u32[]{:S(2)}, u32[]{:S(2)}) collective-permute-start(bf16[64,2048]{1,0:T(8,128)(2,1)} %get-tuple-element.38), channel_id=1, source_target_pairs={{0,4},{4,8},{8,12},{12,16},{16,20},{20,24},{24,28},{28,32},{32,36}... | collective-permute-start | bytes 786440 | tf_op jit(solution)/shard_map/ppermute | solution.py:129
  18.8 12.8 %copy-start.1 = (bf16[64,4096]{1,0:T(8,128)(2,1)}, bf16[64,4096]{1,0:T(8,128)(2,1)S(1)}, u32[]{:S(2)}) copy-start(bf16[64,4096]{1,0:T(8,128)(2,1)S(1)} %collective-permute-done.far_ref) | copy-start | bytes 1572868
  18.9 9.4 %collective-permute-start.5 = (bf16[64,2048]{1,0:T(8,128)(2,1)S(1)}, bf16[64,2048]{1,0:T(8,128)(2,1)S(1)}, u32[]{:S(2)}, u32[]{:S(2)}) collective-permute-start(bf16[64,2048]{1,0:T(8,128)(2,1)S(1)} %get-tuple-element.35), channel_id=1, source_target_pairs={{4,0},{8,4},{12,8},{16,12},{20,16},{24,20},{28,24},{32,28},{36,32}... | collective-permute-start | bytes 786440 | tf_op jit(solution)/shard_map/ppermute | solution.py:132
  20.2 9.2 %collective-permute-start.4 = (bf16[64,2048]{1,0:T(8,128)(2,1)S(1)}, bf16[64,2048]{1,0:T(8,128)(2,1)S(1)}, u32[]{:S(2)}, u32[]{:S(2)}) collective-permute-start(bf16[64,2048]{1,0:T(8,128)(2,1)S(1)} %get-tuple-element.36), channel_id=1, source_target_pairs={{0,4},{4,8},{8,12},{12,16},{16,20},{20,24},{24,28},{28,32},{32,36}... | collective-permute-start | bytes 786440 | tf_op jit(solution)/shard_map/ppermute | solution.py:131
  24.7 7.0 %copy-start.2 = (bf16[27,128,128]{2,1,0:T(8,128)(2,1)S(1)}, bf16[27,128,128]{2,1,0:T(8,128)(2,1)}, u32[]{:S(2)}) copy-start(bf16[27,128,128]{2,1,0:T(8,128)(2,1)} %param.4) | copy-start | bytes 2654212
  24.9 10.7 %collective-permute-start.1 = (bf16[2,64,4096]{2,1,0:T(8,128)(2,1)S(1)}, bf16[2,64,4096]{2,1,0:T(8,128)(2,1)}, u32[]{:S(2)}, u32[]{:S(2)}) collective-permute-start(bf16[2,64,4096]{2,1,0:T(8,128)(2,1)S(1)} %pad_maximum_fusion), channel_id=1, source_target_pairs={{0,1},{1,0},{2,3},{3,2},{4,5},{5,4},{6,7},{7,6},{8,9},{9,8},{10,11... | collective-permute-start | bytes 3145736 | tf_op jit(solution)/shard_map/ppermute | solution.py:133
  28.2 3.4 %copy-start.3 = (bf16[64,2048]{1,0:T(8,128)(2,1)}, bf16[64,2048]{1,0:T(8,128)(2,1)S(1)}, u32[]{:S(2)}) copy-start(bf16[64,2048]{1,0:T(8,128)(2,1)S(1)} %collective-permute-done.5.fhi_ref) | copy-start | bytes 786436
  29.4 2.3 %copy-start.4 = (bf16[64,2048]{1,0:T(8,128)(2,1)}, bf16[64,2048]{1,0:T(8,128)(2,1)S(1)}, u32[]{:S(2)}) copy-start(bf16[64,2048]{1,0:T(8,128)(2,1)S(1)} %collective-permute-done.4.flo_ref) | copy-start | bytes 786436
  31.6 3.9 %collective-permute-start.6 = (bf16[4,64,2048]{2,1,0:T(8,128)(2,1)}, bf16[4,64,2048]{2,1,0:T(8,128)(2,1)}, u32[]{:S(2)}, u32[]{:S(2)}) collective-permute-start(bf16[4,64,2048]{2,1,0:T(8,128)(2,1)} %pad_maximum_fusion.1), channel_id=1, source_target_pairs={{0,1},{1,0},{2,3},{3,2},{4,5},{5,4},{6,7},{7,6},{8,9},{9,8},{10,11... | collective-permute-start | bytes 3145736 | tf_op jit(solution)/shard_map/ppermute | solution.py:134
  49.9 15.1 %copy-start.6 = (bf16[2,32,2048]{2,1,0:T(8,128)(2,1)S(1)}, bf16[2,32,2048]{2,1,0:T(8,128)(2,1)}, u32[]{:S(2)}) copy-start(bf16[2,32,2048]{2,1,0:T(8,128)(2,1)} %get-tuple-element.6) | copy-start | bytes 786436
  49.9 15.8 %copy-start.5 = (bf16[2,32,2048]{2,1,0:T(8,128)(2,1)S(1)}, bf16[2,32,2048]{2,1,0:T(8,128)(2,1)}, u32[]{:S(2)}) copy-start(bf16[2,32,2048]{2,1,0:T(8,128)(2,1)} %get-tuple-element.7) | copy-start | bytes 786436
  51.8 22.4 %all-to-all-start = ((bf16[32,2,1728]{2,1,0:T(2,128)(2,1)}), bf16[32,2,1728]{2,1,0:T(2,128)(2,1)S(1)}, u32[]{:S(2)}, u32[]{:S(2)}) async-start(bf16[32,2,1728]{2,1,0:T(2,128)(2,1)} %reshape.33), calls=%async_computation | async-start | bytes 458752 | tf_op jit(solution)/shard_map/all_to_all | solution.py:19

commit v5 on v4

--- a/solution.py
+++ b/solution.py
@@ -9,15 +9,9 @@
 from jax.sharding import PartitionSpec as P
 
 CH = ("ch_0", "ch_1")
+GZ = ("gz0", "gz1", "gz2")
 ROW = 128
 
-
-def summed_on_arrival(shard, axis, dim):
-    before, after = (shard.shape[:dim], shard.shape[dim + 1 :])
-    devices = lax.axis_size(axis)
-    blocks = jnp.moveaxis(shard.reshape(*before, devices, -1, *after), dim, 0)
-    arrived = lax.all_to_all(blocks, axis, split_axis=0, concat_axis=0, tiled=True)
-    return arrived.astype(jnp.float32).sum(axis=0)
 
 def fused_kernel(
     own_ref, far_ref, near_ref, lo_ref, hi_ref, flo_ref, fhi_ref, hal_ref, wf_ref, wb_ref,
@@ -117,7 +111,7 @@
     in_local, planes_local, grid_rows, grid_cols = volume.shape
     out_local = cotangent.shape[0]
     my_group = lax.axis_index(CH)
-    slabs = lax.axis_size("gz")
+    slabs = lax.axis_size(GZ)
     voxels = planes_local * slabs * grid_rows * grid_cols
     width = grid_rows * grid_cols
     both = jnp.concatenate([volume, cotangent], axis=0).reshape(in_local + out_local, -1)
@@ -126,10 +120,10 @@
     up = [(i, i + 1) for i in range(slabs - 1)]
     down = [(j, i) for i, j in up]
     got_far = lax.ppermute(both, far, swap)
-    low = lax.ppermute(both[:, -width:], "gz", up)
-    high = lax.ppermute(both[:, :width], "gz", down)
-    far_low = lax.ppermute(got_far[:, -width:], "gz", up)
-    far_high = lax.ppermute(got_far[:, :width], "gz", down)
+    low = lax.ppermute(both[:, -width:], GZ, up)
+    high = lax.ppermute(both[:, :width], GZ, down)
+    far_low = lax.ppermute(got_far[:, -width:], GZ, up)
+    far_high = lax.ppermute(got_far[:, :width], GZ, down)
     got_near = lax.ppermute(jnp.stack([both, got_far]), near, swap)
     halos = lax.ppermute(jnp.stack([low, high, far_low, far_high]), near, swap)
     groups = 4
@@ -150,19 +144,25 @@
     shape = (out_local, planes_local, grid_rows, grid_cols)
     out = jnp.transpose(out, (1, 0, 2)).reshape(shape)
     ing = jnp.transpose(ing, (1, 0, 2)).reshape(shape)
-    weight_grad = summed_on_arrival(wg.astype(jnp.bfloat16), "gz", 1) * jnp.float32(
-        1.0 / math.sqrt(voxels)
-    )
+    rows = [mesh_size for mesh_size in (lax.axis_size(GZ[0]), lax.axis_size(GZ[1]), lax.axis_size(GZ[2]))]
+    part = wg.astype(jnp.bfloat16).reshape(27, rows[0] * rows[1], rows[2], -1, out_local)
+    part = jnp.moveaxis(part, 2, 0)
+    part = lax.all_to_all(part, GZ[2], split_axis=0, concat_axis=0, tiled=True)
+    part = jnp.moveaxis(part.astype(jnp.float32).sum(axis=0), 1, 0)
+    part = lax.all_to_all(part, GZ[:2], split_axis=0, concat_axis=0, tiled=True)
+    weight_grad = part.sum(axis=0) * jnp.float32(1.0 / math.sqrt(voxels))
     return out, ing, weight_grad
 
 
 def solution(mesh):
-    split = Mesh(mesh.devices.reshape(mesh.shape["gz"], 2, 2), ("gz", "ch_0", "ch_1"))
-    placed = (P(CH, "gz", None, None), P(), P(CH, "gz", None, None))
+    plan = dict(mesh.shape)
+    sizes = (2, 4, plan["gz"] // 8, 2, plan["ch"] // 2)
+    split = Mesh(mesh.devices.reshape(sizes), GZ + CH)
+    placed = (P(CH, GZ, None, None), P(), P(CH, GZ, None, None))
     return jax.shard_map(
         body,
         mesh=split,
         in_specs=placed,
-        out_specs=(P(CH, "gz", None, None), P(CH, "gz", None, None), P(None, "gz", CH)),
+        out_specs=(P(CH, GZ, None, None), P(CH, GZ, None, None), P(None, GZ, CH)),
         check_vma=False,
     )

time: 76.5 us -> 86.1 us (1.13)
  starting transfers between devices: 29.7 us -> 19.3 us
  blocking collectives: 0 us -> 9.51 us
  waiting for transfers between devices: 16.5 us -> 23.9 us
  local copies, waits for them, and re-layouts: 11.6 us -> 13.5 us
  other arithmetic: 4.97 us -> 6.03 us
    all_to_all x0 -> x1, blocking collectives: none -> 9.51 us  [body(): part = lax.all_to_all(part, GZ[2], split_axis=0, concat_axis=0, tiled=True)]
    ppermute x1, waiting for transfers between devices: 4.32 us -> 11.1 us  [body(): got_far = lax.ppermute(both, far, swap)]
    all_to_all x1, starting transfers between devices: 13.1 us -> 7.16 us  [body(): part = lax.all_to_all(part, GZ[:2], split_axis=0, concat_axis=0, tiled=True)]
    ppermute x4, starting transfers between devices: 12.4 us -> 7.97 us  [the longest x1 4.09 us: body(): low = lax.ppermute(both[:, -width:], GZ, up)]
    ppermute x4, waiting for transfers between devices: 4.43 us -> 7.82 us  [the longest x1 4.13 us: body(): far_high = lax.ppermute(got_far[:, :width], GZ, down)]
    all_to_all x1, waiting for transfers between devices: 7.73 us -> 4.93 us  [body(): part = lax.all_to_all(part, GZ[:2], split_axis=0, concat_axis=0, tiled=True)]
    all_to_all x0 -> x1, other arithmetic: none -> 0.9 us  [body(): part = lax.all_to_all(part, GZ[:2], split_axis=0, concat_axis=0, tiled=True)]
    unnamed x26 -> x34, local copies, waits for them, and re-layouts: 5.72 us -> 6.12 us
where the time goes in v5:
time: 86.1 us; the launch traced here: 85.6 us
  waiting for transfers between devices  23.9 us (28%)
  starting transfers between devices  19.3 us (22%)
  local copies, waits for them, and re-layouts  13.5 us (16%)
  Pallas kernels  12.5 us (15%)
  blocking collectives  9.51 us (11%)
  other arithmetic  6.03 us (7%)
  between operations  0.92 us (1%)
    pallas_call x1, Pallas kernels, fused(): pl.pallas_call(fused_kernel, out_shape=(jax.ShapeDtypeStruct((planes, loc...  12.5 us
    ppermute x1, waiting for transfers between devices, body(): got_far = lax.ppermute(both, far, swap)  11.1 us
    all_to_all x1, blocking collectives, body(): part = lax.all_to_all(part, GZ[2], split_axis=0, concat_axis=0, tiled=True)  9.51 us
    all_to_all x1, starting transfers between devices, body(): part = lax.all_to_all(part, GZ[:2], split_axis=0, concat_axis=0, tiled=True)  7.16 us
    unnamed x34, local copies, waits for them, and re-layouts  6.12 us
    all_to_all x1, waiting for transfers between devices, body(): part = lax.all_to_all(part, GZ[:2], split_axis=0, concat_axis=0, tiled=True)  4.93 us
    ppermute x1, waiting for transfers between devices, body(): far_high = lax.ppermute(got_far[:, :width], GZ, down)  4.13 us
    ppermute x1, starting transfers between devices, body(): low = lax.ppermute(both[:, -width:], GZ, up)  4.09 us
  transfers between devices with their start and end apart: 8, of which 4 were waited for; matrix products, arithmetic and copies ran while one was open for 11% of the time, Pallas kernels for 0%

profile of v5, /device:TPU:0, one launch (start us, length us, event | category | flops | bytes accessed | tf_op | source)
XLA Modules:
  0.0 85.6 jit_solution(8186433162061731514)
XLA Ops:
  0.6 1.0 %constant_dynamic-update-slice_fusion.1 = bf16[64,2,16,128]{3,2,1,0:T(8,128)(2,1)S(1)} fusion(bf16[32,2,16,128]{3,2,1,0:T(8,128)(2,1)} %param.3), kind=kLoop, calls=%fused_computation.13 | loop fusion | bytes 524288
  1.6 1.0 %constant_dynamic-update-slice_fusion = bf16[64,2,16,128]{3,2,1,0:T(8,128)(2,1)S(1)} fusion(bf16[64,2,16,128]{3,2,1,0:T(8,128)(2,1)S(1)} %constant_dynamic-update-slice_fusion.1, bf16[32,2,16,128]{3,2,1,0:T(8,128)(2,1)} %param.5), kind=kLoop, calls=%fused_computation.12 | loop fusion | bytes 524288 | tf_op jit(solution)/shard_map/concatenate | solution.py:117
  2.6 0.2 copy.70
  2.8 4.1 %collective-permute-start = (bf16[64,4096]{1,0:T(8,128)(2,1)S(1)}, bf16[64,4096]{1,0:T(8,128)(2,1)S(1)}, u32[]{:S(2)}, u32[]{:S(2)}) collective-permute-start(bf16[64,4096]{1,0:T(8,128)(2,1)S(1)} %bitcast.36), channel_id=1, source_target_pairs={{0,2},{2,0},{1,3},{3,1},{4,6},{6,4},{5,7},{7,5},{8,10},{10,8},{9,1... | collective-permute-start | bytes 1572872 | tf_op jit(solution)/shard_map/ppermute | solution.py:122
  6.9 0.8 fusion.1
  7.7 4.1 %collective-permute-start.2 = (bf16[64,2048]{1,0:T(8,128)(2,1)}, bf16[64,2048]{1,0:T(8,128)(2,1)}, u32[]{:S(2)}, u32[]{:S(2)}) collective-permute-start(bf16[64,2048]{1,0:T(8,128)(2,1)} %get-tuple-element.38), channel_id=1, source_target_pairs={{0,4},{4,8},{8,12},{12,16},{16,20},{20,24},{24,28},{28,32},{32,36}... | collective-permute-start | bytes 786440 | tf_op jit(solution)/shard_map/ppermute | solution.py:123
  11.8 1.3 %collective-permute-start.3 = (bf16[64,2048]{1,0:T(8,128)(2,1)}, bf16[64,2048]{1,0:T(8,128)(2,1)}, u32[]{:S(2)}, u32[]{:S(2)}) collective-permute-start(bf16[64,2048]{1,0:T(8,128)(2,1)} %get-tuple-element.37), channel_id=1, source_target_pairs={{4,0},{8,4},{12,8},{16,12},{20,16},{24,20},{28,24},{32,28},{36,32}... | collective-permute-start | bytes 786440 | tf_op jit(solution)/shard_map/ppermute | solution.py:124
  13.1 0.2 stack_reshape.3
  13.3 11.1 %collective-permute-done.far_ref = bf16[64,4096]{1,0:T(8,128)(2,1)S(1)} collective-permute-done((bf16[64,4096]{1,0:T(8,128)(2,1)S(1)}, bf16[64,4096]{1,0:T(8,128)(2,1)S(1)}, u32[]{:S(2)}, u32[]{:S(2)}) %collective-permute-start) | collective-permute-done | bytes 524320 | tf_op jit(solution)/shard_map/ppermute | solution.py:122
  24.5 1.3 %collective-permute-start.4 = (bf16[64,2048]{1,0:T(8,128)(2,1)S(1)}, bf16[64,2048]{1,0:T(8,128)(2,1)S(1)}, u32[]{:S(2)}, u32[]{:S(2)}) collective-permute-start(bf16[64,2048]{1,0:T(8,128)(2,1)S(1)} %get-tuple-element.36), channel_id=1, source_target_pairs={{0,4},{4,8},{8,12},{12,16},{16,20},{20,24},{24,28},{28,32},{32,36}... | collective-permute-start | bytes 786440 | tf_op jit(solution)/shard_map/ppermute | solution.py:125
  25.8 1.3 %collective-permute-start.5 = (bf16[64,2048]{1,0:T(8,128)(2,1)S(1)}, bf16[64,2048]{1,0:T(8,128)(2,1)S(1)}, u32[]{:S(2)}, u32[]{:S(2)}) collective-permute-start(bf16[64,2048]{1,0:T(8,128)(2,1)S(1)} %get-tuple-element.35), channel_id=1, source_target_pairs={{4,0},{8,4},{12,8},{16,12},{20,16},{24,20},{28,24},{32,28},{36,32}... | collective-permute-start | bytes 786440 | tf_op jit(solution)/shard_map/ppermute | solution.py:126
  27.1 0.0 copy-start.2
  27.1 0.1 pad_maximum_fusion
  27.2 0.1 collective-permute-start.1
  27.3 0.0 collective-permute-done.2.lo_ref
  27.3 3.7 %collective-permute-done.4.flo_ref = bf16[64,2048]{1,0:T(8,128)(2,1)S(1)} collective-permute-done((bf16[64,2048]{1,0:T(8,128)(2,1)S(1)}, bf16[64,2048]{1,0:T(8,128)(2,1)S(1)}, u32[]{:S(2)}, u32[]{:S(2)}) %collective-permute-start.4) | collective-permute-done | bytes 262176 | tf_op jit(solution)/shard_map/ppermute | solution.py:125
  31.0 4.1 %collective-permute-done.5.fhi_ref = bf16[64,2048]{1,0:T(8,128)(2,1)S(1)} collective-permute-done((bf16[64,2048]{1,0:T(8,128)(2,1)S(1)}, bf16[64,2048]{1,0:T(8,128)(2,1)S(1)}, u32[]{:S(2)}, u32[]{:S(2)}) %collective-permute-start.5) | collective-permute-done | bytes 262176 | tf_op jit(solution)/shard_map/ppermute | solution.py:126
  35.2 2.2 %pad_maximum_fusion.1 = bf16[4,64,2048]{2,1,0:T(8,128)(2,1)} fusion(bf16[1,64,2048]{2,1,0:T(8,128)(2,1)S(1)} %bitcast.46, bf16[1,64,2048]{2,1,0:T(8,128)(2,1)S(1)} %bitcast.45, bf16[1,64,2048]{2,1,0:T(8,128)(2,1)} %bitcast.2, bf16[1,64,2048]{2,1,0:T(8,128)(2,1)} %bitcast.1), kind=kLoop, calls=%fused_computation.2 | loop fusion | flops 1572864 | bytes 2097152 | tf_op jit(solution)/shard_map/stack | solution.py:128
  37.5 2.0 %constant_dynamic-slice_fusion.2 = (bf16[27,32,32]{2,1,0:T(8,128)(2,1)}, bf16[27,32,32]{2,1,0:T(8,128)(2,1)S(1)}, bf16[27,32,32]{2,1,0:T(8,128)(2,1)S(1)}, bf16[...) fusion(bf16[27,128,128]{2,1,0:T(8,128)(2,1)S(1)} %copy-done.2, ...), kind=kLoop, calls=%fused_computation.16 | loop fusion | bytes 774160 | tf_op jit(solution)/shard_map/dynamic_slice | solution.py:106
  39.5 0.2 copy.62
  39.6 0.2 copy.63
  39.8 0.2 copy.64
  39.9 0.2 copy.65
  40.1 0.3 copy-done.5
  40.4 0.1 copy-done.6
  40.5 0.1 copy-done.7
  40.6 0.3 pad_maximum_fusion.4
  40.9 0.7 rev.3
  41.6 1.0 %pad_maximum_fusion.3 = bf16[27,128,32]{1,2,0:T(8,128)(2,1)} fusion(bf16[27,32,32]{1,2,0:T(8,128)(2,1)S(1)} %copy.65, bf16[27,32,32]{1,2,0:T(8,128)(2,1)S(1)} %copy.64, bf16[27,32,32]{1,2,0:T(8,128)(2,1)S(1)} %copy.63, bf16[27,32,32]{1,2,0:T(8,128)(2,1)S(1)} %copy.62), kind=kLoop, calls=%fused_computation.9 | loop fusion | flops 884736 | bytes 442368 | tf_op jit(solution)/shard_map/concatenate | solution.py:105
  42.6 12.5 %shard_map.58 = (bf16[2,32,2048]{2,1,0:T(8,128)(2,1)}, bf16[2,32,2048]{2,1,0:T(8,128)(2,1)}, f32[27,128,32]{2,1,0:T(8,128)}) custom-call(bf16[64,4096]{1,0:T(8,128)(2,1)} %bitcast.38, bf16[64,4096]{1,0:T(8,128)(2,1)} %copy-done.1, bf16[2,64,4096]{2,1,0:T(8,128)(2,1)} %collective-permute-done.1.near_ref, bf16[64,2048]{1,0:T(8,128)(2,1)} %collective-permute-done.2.lo_ref, ...), custom_call_target="tpu_custom_call" | custom-call | tf_op jit(solution)/shard_map/pallas_call | solution.py:90
  55.0 1.6 %dynamic-slice_convert_fusion.3 = (bf16[27,32,32]{2,1,0:T(8,128)(2,1)S(1)}, bf16[27,32,32]{2,1,0:T(8,128)(2,1)S(1)}, bf16[27,32,32]{2,1,0:T(8,128)(2,1)S(1)}, bf16[27,32,32]{2,1,0:T(8,128)(2,1)S(1)}) fusion(f32[27,128,32]{2,1,0:T(8,128)} %get-tuple-element.8, s32[]{:T(128)S(6)} %select_n.30, s32[]{:T(128)S(6)} %select_n.36, s32[]{:T(128)S(6)} %select_n.34, ...), kind=kLoop, calls=%fused_computation.8 | loop fusion | bytes 442384 | tf_op jit(solution)/shard_map/convert
  56.7 0.2 pad_maximum_fusion.2
  56.9 0.5 copy.58
  57.4 0.6 reshape.33
  58.0 9.5 %all_to_all.10 = bf16[4,2,13824]{2,1,0:T(2,128)(2,1)S(1)} all-to-all(bf16[4,2,13824]{2,1,0:T(2,128)(2,1)S(1)} %reshape.33), channel_id=1, replica_groups=mesh['gz0'=2,'gz1'=4,'gz2'=4,'ch_0'=2,'ch_1'=2] {'gz2'}, dimensions={0} | all-to-all | bytes 442368 | tf_op jit(solution)/shard_map/all_to_all | solution.py:150
  67.5 0.5 reshape.34
  68.0 0.5 convert_reduce_fusion
  68.5 0.1 copy.59
  68.6 0.9 %reshape.35 = f32[8,1,3456]{2,1,0:T(1,128)} reshape(f32[8,27,4,32]{3,2,1,0:T(4,128)S(1)} %copy.59) | data formatting | bytes 221184
  69.6 7.2 %all-to-all-start.1 = ((f32[8,1,3456]{2,1,0:T(1,128)}), f32[8,1,3456]{2,1,0:T(1,128)S(1)}, u32[]{:S(2)}, u32[]{:S(2)}) async-start(f32[8,1,3456]{2,1,0:T(1,128)} %reshape.35), calls=%async_computation.1 | async-start | bytes 221184 | tf_op jit(solution)/shard_map/all_to_all | solution.py:152
  76.8 0.7 copy.60
  77.5 0.7 copy.61
  78.3 4.9 %all-to-all-done.1 = f32[8,1,3456]{2,1,0:T(1,128)S(1)} async-done(((f32[8,1,3456]{2,1,0:T(1,128)}), f32[8,1,3456]{2,1,0:T(1,128)S(1)}, u32[]{:S(2)}, u32[]{:S(2)}) %all-to-all-start.1) | async-done | bytes 110624 | tf_op jit(solution)/shard_map/all_to_all | solution.py:152
  83.2 0.5 broadcast
  83.7 0.9 %reduce = f32[8,3456]{1,0:T(8,128)S(1)} reduce(f32[8,1,3456]{2,1,0:T(1,128)S(1)} %all-to-all-done.1, f32[]{:T(128)} %broadcast), dimensions={1}, to_apply=%all_to_all.7.reduce_sub_computation | reduce | bytes 221188 | tf_op jit(solution)/shard_map/all_to_all | solution.py:152
  84.6 0.2 reshape.36
  84.9 0.1 reduce_sum.19
  85.0 0.6 broadcast_multiply_fusion
  (23 shorter events, 0.2 us)
Async XLA Ops:
  2.8 24.4 %copy-start = (bf16[8,8,32,128]{3,1,2,0:T(8,128)(2,1)}, bf16[8,8,32,128]{3,1,2,0:T(8,128)(2,1)S(1)}, u32[]{:S(2)}) copy-start(bf16[8,8,32,128]{3,1,2,0:T(8,128)(2,1)S(1)} %copy.70) | copy-start | bytes 1572868
  2.8 21.6 %collective-permute-start = (bf16[64,4096]{1,0:T(8,128)(2,1)S(1)}, bf16[64,4096]{1,0:T(8,128)(2,1)S(1)}, u32[]{:S(2)}, u32[]{:S(2)}) collective-permute-start(bf16[64,4096]{1,0:T(8,128)(2,1)S(1)} %bitcast.36), channel_id=1, source_target_pairs={{0,2},{2,0},{1,3},{3,1},{4,6},{6,4},{5,7},{7,5},{8,10},{10,8},{9,1... | collective-permute-start | bytes 1572872 | tf_op jit(solution)/shard_map/ppermute | solution.py:122
  7.7 19.6 %collective-permute-start.2 = (bf16[64,2048]{1,0:T(8,128)(2,1)}, bf16[64,2048]{1,0:T(8,128)(2,1)}, u32[]{:S(2)}, u32[]{:S(2)}) collective-permute-start(bf16[64,2048]{1,0:T(8,128)(2,1)} %get-tuple-element.38), channel_id=1, source_target_pairs={{0,4},{4,8},{8,12},{12,16},{16,20},{20,24},{24,28},{28,32},{32,36}... | collective-permute-start | bytes 786440 | tf_op jit(solution)/shard_map/ppermute | solution.py:123
  11.8 15.5 %collective-permute-start.3 = (bf16[64,2048]{1,0:T(8,128)(2,1)}, bf16[64,2048]{1,0:T(8,128)(2,1)}, u32[]{:S(2)}, u32[]{:S(2)}) collective-permute-start(bf16[64,2048]{1,0:T(8,128)(2,1)} %get-tuple-element.37), channel_id=1, source_target_pairs={{4,0},{8,4},{12,8},{16,12},{20,16},{24,20},{28,24},{32,28},{36,32}... | collective-permute-start | bytes 786440 | tf_op jit(solution)/shard_map/ppermute | solution.py:124
  24.4 13.0 %copy-start.1 = (bf16[64,4096]{1,0:T(8,128)(2,1)}, bf16[64,4096]{1,0:T(8,128)(2,1)S(1)}, u32[]{:S(2)}) copy-start(bf16[64,4096]{1,0:T(8,128)(2,1)S(1)} %collective-permute-done.far_ref) | copy-start | bytes 1572868
  24.5 6.5 %collective-permute-start.4 = (bf16[64,2048]{1,0:T(8,128)(2,1)S(1)}, bf16[64,2048]{1,0:T(8,128)(2,1)S(1)}, u32[]{:S(2)}, u32[]{:S(2)}) collective-permute-start(bf16[64,2048]{1,0:T(8,128)(2,1)S(1)} %get-tuple-element.36), channel_id=1, source_target_pairs={{0,4},{4,8},{8,12},{12,16},{16,20},{20,24},{24,28},{28,32},{32,36}... | collective-permute-start | bytes 786440 | tf_op jit(solution)/shard_map/ppermute | solution.py:125
  25.8 9.4 %collective-permute-start.5 = (bf16[64,2048]{1,0:T(8,128)(2,1)S(1)}, bf16[64,2048]{1,0:T(8,128)(2,1)S(1)}, u32[]{:S(2)}, u32[]{:S(2)}) collective-permute-start(bf16[64,2048]{1,0:T(8,128)(2,1)S(1)} %get-tuple-element.35), channel_id=1, source_target_pairs={{4,0},{8,4},{12,8},{16,12},{20,16},{24,20},{28,24},{32,28},{36,32}... | collective-permute-start | bytes 786440 | tf_op jit(solution)/shard_map/ppermute | solution.py:126
  27.1 10.4 %copy-start.2 = (bf16[27,128,128]{2,1,0:T(8,128)(2,1)S(1)}, bf16[27,128,128]{2,1,0:T(8,128)(2,1)}, u32[]{:S(2)}) copy-start(bf16[27,128,128]{2,1,0:T(8,128)(2,1)} %param.4) | copy-start | bytes 2654212
  27.2 15.4 %collective-permute-start.1 = (bf16[2,64,4096]{2,1,0:T(8,128)(2,1)S(1)}, bf16[2,64,4096]{2,1,0:T(8,128)(2,1)}, u32[]{:S(2)}, u32[]{:S(2)}) collective-permute-start(bf16[2,64,4096]{2,1,0:T(8,128)(2,1)S(1)} %pad_maximum_fusion), channel_id=1, source_target_pairs={{0,1},{1,0},{2,3},{3,2},{4,5},{5,4},{6,7},{7,6},{8,9},{9,8},{10,11... | collective-permute-start | bytes 3145736 | tf_op jit(solution)/shard_map/ppermute | solution.py:127
  31.0 6.4 %copy-start.3 = (bf16[64,2048]{1,0:T(8,128)(2,1)}, bf16[64,2048]{1,0:T(8,128)(2,1)S(1)}, u32[]{:S(2)}) copy-start(bf16[64,2048]{1,0:T(8,128)(2,1)S(1)} %collective-permute-done.4.flo_ref) | copy-start | bytes 786436
  35.2 2.2 %copy-start.4 = (bf16[64,2048]{1,0:T(8,128)(2,1)}, bf16[64,2048]{1,0:T(8,128)(2,1)S(1)}, u32[]{:S(2)}) copy-start(bf16[64,2048]{1,0:T(8,128)(2,1)S(1)} %collective-permute-done.5.fhi_ref) | copy-start | bytes 786436
  37.4 5.2 %collective-permute-start.6 = (bf16[4,64,2048]{2,1,0:T(8,128)(2,1)}, bf16[4,64,2048]{2,1,0:T(8,128)(2,1)}, u32[]{:S(2)}, u32[]{:S(2)}) collective-permute-start(bf16[4,64,2048]{2,1,0:T(8,128)(2,1)} %pad_maximum_fusion.1), channel_id=1, source_target_pairs={{0,1},{1,0},{2,3},{3,2},{4,5},{5,4},{6,7},{7,6},{8,9},{9,8},{10,11... | collective-permute-start | bytes 3145736 | tf_op jit(solution)/shard_map/ppermute | solution.py:128
  39.4 0.9 %copy-start.5 = (bf16[27,32,32]{2,1,0:T(8,128)(2,1)S(1)}, bf16[27,32,32]{2,1,0:T(8,128)(2,1)}, u32[]{:S(2)}) copy-start(bf16[27,32,32]{2,1,0:T(8,128)(2,1)} %get-tuple-element.28) | copy-start | bytes 165892
  39.4 1.0 %copy-start.6 = (bf16[27,32,32]{2,1,0:T(8,128)(2,1)S(1)}, bf16[27,32,32]{2,1,0:T(8,128)(2,1)}, u32[]{:S(2)}) copy-start(bf16[27,32,32]{2,1,0:T(8,128)(2,1)} %get-tuple-element.33) | copy-start | bytes 165892
  39.4 1.1 %copy-start.7 = (bf16[27,32,32]{2,1,0:T(8,128)(2,1)S(1)}, bf16[27,32,32]{2,1,0:T(8,128)(2,1)}, u32[]{:S(2)}) copy-start(bf16[27,32,32]{2,1,0:T(8,128)(2,1)} %get-tuple-element.34) | copy-start | bytes 165892
  68.0 8.7 %copy-start.9 = (bf16[2,32,2048]{2,1,0:T(8,128)(2,1)S(1)}, bf16[2,32,2048]{2,1,0:T(8,128)(2,1)}, u32[]{:S(2)}) copy-start(bf16[2,32,2048]{2,1,0:T(8,128)(2,1)} %get-tuple-element.6) | copy-start | bytes 786436
  68.0 9.5 %copy-start.8 = (bf16[2,32,2048]{2,1,0:T(8,128)(2,1)S(1)}, bf16[2,32,2048]{2,1,0:T(8,128)(2,1)}, u32[]{:S(2)}) copy-start(bf16[2,32,2048]{2,1,0:T(8,128)(2,1)} %get-tuple-element.7) | copy-start | bytes 786436
  69.6 13.6 %all-to-all-start.1 = ((f32[8,1,3456]{2,1,0:T(1,128)}), f32[8,1,3456]{2,1,0:T(1,128)S(1)}, u32[]{:S(2)}, u32[]{:S(2)}) async-start(f32[8,1,3456]{2,1,0:T(1,128)} %reshape.35), calls=%async_computation.1 | async-start | bytes 221184 | tf_op jit(solution)/shard_map/all_to_all | solution.py:152

commit v6 on v4

--- a/solution.py
+++ b/solution.py
@@ -128,10 +128,6 @@
     got_far = lax.ppermute(both, far, swap)
     low = lax.ppermute(both[:, -width:], "gz", up)
     high = lax.ppermute(both[:, :width], "gz", down)
-    far_low = lax.ppermute(got_far[:, -width:], "gz", up)
-    far_high = lax.ppermute(got_far[:, :width], "gz", down)
-    got_near = lax.ppermute(jnp.stack([both, got_far]), near, swap)
-    halos = lax.ppermute(jnp.stack([low, high, far_low, far_high]), near, swap)
     groups = 4
     order = [jnp.bitwise_xor(my_group, j) for j in range(groups)]
     cin = groups * in_local
@@ -143,6 +139,11 @@
     weight_rows = lax.dynamic_slice_in_dim(weight, my_group * in_local, in_local, 1)
     weight_rows = by_group(weight_rows, order, out_local, 2)
     wb = weight_rows[::-1].reshape(9, 3 * in_local, cout)
+    got_far, wf, wb = lax.optimization_barrier((got_far, wf, wb))
+    far_low = lax.ppermute(got_far[:, -width:], "gz", up)
+    far_high = lax.ppermute(got_far[:, :width], "gz", down)
+    got_near = lax.ppermute(jnp.stack([both, got_far]), near, swap)
+    halos = lax.ppermute(jnp.stack([low, high, far_low, far_high]), near, swap)
     out, ing, wg = fused(
         both, got_far, got_near, low, high, far_low, far_high, halos, wf, wb, planes_local, width
     )

time: 76.5 us -> 79.1 us (1.034)
  starting transfers between devices: 29.7 us -> 33.4 us
  waiting for transfers between devices: 16.5 us -> 14.3 us
  local copies, waits for them, and re-layouts: 11.6 us -> 12.5 us
    ppermute x1, waiting for transfers between devices: 4.32 us -> 0.01 us  [body(): got_far = lax.ppermute(both, far, swap)]
    all_to_all x1, starting transfers between devices: 13.1 us -> 16.6 us  [summed_on_arrival(): lax.all_to_all(blocks, axis, split_axis=0, concat_axis=0, tiled=True)]
    ppermute x1, waiting for transfers between devices: 0.01 us -> 2.76 us  [body(): halos = lax.ppermute(jnp.stack([low, high, far_low, far_high]), near, swap)]
    concatenate x3, other arithmetic: 1.52 us -> 2.72 us  [by_group(): jnp.concatenate([lax.dynamic_slice_in_dim(array, group * size, size, dim)...]
    another operation x1, other arithmetic: 2.24 us -> 1.18 us  [body(): halos = lax.ppermute(jnp.stack([low, high, far_low, far_high]), near, swap)]
    dynamic_slice x1, local copies, waits for them, and re-layouts: 1.15 us -> 2.14 us  [by_group(): lax.dynamic_slice_in_dim(array, group * size, size, dim)]
    unnamed x26 -> x34, local copies, waits for them, and re-layouts: 5.72 us -> 5.56 us
  transfers between devices with their start and end apart: 8 -> 8, of which waited for: 4 -> 4; matrix products, arithmetic and copies ran while one was open for 11% -> 13% of each run, Pallas kernels for 0% -> 0%
where the time goes in v6:
time: 79.1 us; the launch traced here: 78.7 us
  starting transfers between devices  33.4 us (42%)
  waiting for transfers between devices  14.3 us (18%)
  local copies, waits for them, and re-layouts  12.5 us (16%)
  Pallas kernels  12.5 us (16%)
  other arithmetic  5.11 us (6%)
  between operations  0.92 us (1%)
    all_to_all x1, starting transfers between devices, summed_on_arrival(): lax.all_to_all(blocks, axis, split_axis=0, concat_axis=0, tiled=True)  16.6 us
    pallas_call x1, Pallas kernels, fused(): pl.pallas_call(fused_kernel, out_shape=(jax.ShapeDtypeStruct((planes, loc...  12.5 us
    all_to_all x1, waiting for transfers between devices, summed_on_arrival(): lax.all_to_all(blocks, axis, split_axis=0, concat_axis=0, tiled=True)  7.38 us
    unnamed x34, local copies, waits for them, and re-layouts  5.56 us
    ppermute x1, starting transfers between devices, body(): low = lax.ppermute(both[:, -width:], 'gz', up)  5.26 us
    ppermute x1, starting transfers between devices, body(): far_low = lax.ppermute(got_far[:, -width:], 'gz', up)  4.56 us
    ppermute x1, starting transfers between devices, body(): got_far = lax.ppermute(both, far, swap)  4.07 us
    ppermute x1, waiting for transfers between devices, body(): far_high = lax.ppermute(got_far[:, :width], 'gz', down)  3 us
  transfers between devices with their start and end apart: 8, of which 4 were waited for; matrix products, arithmetic and copies ran while one was open for 13% of the time, Pallas kernels for 0%

profile of v6, /device:TPU:0, one launch (start us, length us, event | category | flops | bytes accessed | tf_op | source)
XLA Modules:
  0.0 78.7 jit_solution(10817076126669682282)
XLA Ops:
  0.6 1.0 %constant_dynamic-update-slice_fusion.1 = bf16[64,2,16,128]{3,2,1,0:T(8,128)(2,1)S(1)} fusion(bf16[32,2,16,128]{3,2,1,0:T(8,128)(2,1)} %param.3), kind=kLoop, calls=%fused_computation.13 | loop fusion | bytes 524288
  1.6 0.0 copy-start.2
  1.6 1.1 %constant_dynamic-update-slice_fusion = bf16[64,2,16,128]{3,2,1,0:T(8,128)(2,1)S(1)} fusion(bf16[64,2,16,128]{3,2,1,0:T(8,128)(2,1)S(1)} %constant_dynamic-update-slice_fusion.1, bf16[32,2,16,128]{3,2,1,0:T(8,128)(2,1)} %param.5), kind=kLoop, calls=%fused_computation.12 | loop fusion | bytes 524288 | tf_op jit(solution)/shard_map/concatenate | solution.py:123
  2.7 0.2 copy.68
  2.9 0.0 copy-start
  2.9 4.1 %collective-permute-start = (bf16[64,4096]{1,0:T(8,128)(2,1)S(1)}, bf16[64,4096]{1,0:T(8,128)(2,1)S(1)}, u32[]{:S(2)}, u32[]{:S(2)}) collective-permute-start(bf16[64,4096]{1,0:T(8,128)(2,1)S(1)} %bitcast.35), channel_id=1, source_target_pairs={{0,2},{2,0},{1,3},{3,1},{4,6},{6,4},{5,7},{7,5},{8,10},{10,8},{9,1... | collective-permute-start | bytes 1572872 | tf_op jit(solution)/shard_map/ppermute | solution.py:128
  7.0 0.8 %fusion.1 = (bf16[64,2048]{1,0:T(8,128)(2,1)}, bf16[64,2048]{1,0:T(8,128)(2,1)}) fusion(bf16[64,4096]{1,0:T(8,128)(2,1)S(1)} %bitcast.36), kind=kLoop, calls=%fused_computation.22 | loop fusion | bytes 1048576 | tf_op jit(solution)/shard_map/slice | solution.py:130
  7.8 1.3 %collective-permute-start.3 = (bf16[64,2048]{1,0:T(8,128)(2,1)}, bf16[64,2048]{1,0:T(8,128)(2,1)S(1)}, u32[]{:S(2)}, u32[]{:S(2)}) collective-permute-start(bf16[64,2048]{1,0:T(8,128)(2,1)} %get-tuple-element.43), channel_id=1, source_target_pairs={{4,0},{8,4},{12,8},{16,12},{20,16},{24,20},{28,24},{32,28},{36,32}... | collective-permute-start | bytes 786440 | tf_op jit(solution)/shard_map/ppermute | solution.py:130
  9.1 5.3 %collective-permute-start.2 = (bf16[64,2048]{1,0:T(8,128)(2,1)}, bf16[64,2048]{1,0:T(8,128)(2,1)}, u32[]{:S(2)}, u32[]{:S(2)}) collective-permute-start(bf16[64,2048]{1,0:T(8,128)(2,1)} %get-tuple-element.44), channel_id=1, source_target_pairs={{0,4},{4,8},{8,12},{12,16},{16,20},{20,24},{24,28},{28,32},{32,36}... | collective-permute-start | bytes 786440 | tf_op jit(solution)/shard_map/ppermute | solution.py:129
  14.3 0.2 stack_reshape.3
  14.6 2.1 %constant_dynamic-slice_fusion.2 = (bf16[27,32,32]{2,1,0:T(8,128)(2,1)}, bf16[27,32,32]{2,1,0:T(8,128)(2,1)}, bf16[27,32,32]{2,1,0:T(8,128)(2,1)}, bf16[27,32,32...) fusion(bf16[27,128,128]{2,1,0:T(8,128)(2,1)S(1)} %copy-done.2, ...), kind=kLoop, calls=%fused_computation.16 | loop fusion | bytes 774160 | tf_op jit(solution)/shard_map/dynamic_slice | solution.py:112
  16.8 0.2 copy.60
  16.9 1.5 %pad_maximum_fusion.4 = bf16[27,32,128]{2,1,0:T(8,128)(2,1)S(1)} fusion(bf16[27,32,32]{2,1,0:T(8,128)(2,1)} %get-tuple-element.39, bf16[27,32,32]{2,1,0:T(8,128)(2,1)} %get-tuple-element.40, bf16[27,32,32]{2,1,0:T(8,128)(2,1)} %get-tuple-element.34, bf16[27,32,32]{2,1,0:T(8,128)(2,1)S(1)} %get-tuple-element.37), kind=kLoop, calls=%fused_computation.10 | loop fusion | flops 884736 | bytes 442368 | tf_op jit(solution)/shard_map/concatenate | solution.py:111
  18.4 0.7 rev.3
  19.1 0.0 copy-done.8
  19.1 0.2 copy.62
  19.3 0.2 copy.61
  19.5 0.2 copy.63
  19.6 1.0 %pad_maximum_fusion.3 = bf16[27,128,32]{1,2,0:T(8,128)(2,1)} fusion(bf16[27,32,32]{1,2,0:T(8,128)(2,1)S(1)} %copy.63, bf16[27,32,32]{1,2,0:T(8,128)(2,1)S(1)} %copy.62, bf16[27,32,32]{1,2,0:T(8,128)(2,1)S(1)} %copy.61, bf16[27,32,32]{1,2,0:T(8,128)(2,1)S(1)} %copy.60), kind=kLoop, calls=%fused_computation.9 | loop fusion | flops 884736 | bytes 442368 | tf_op jit(solution)/shard_map/concatenate | solution.py:111
  20.6 0.0 collective-permute-done.far_ref
  20.7 1.3 %collective-permute-start.5 = (bf16[64,2048]{1,0:T(8,128)(2,1)S(1)}, bf16[64,2048]{1,0:T(8,128)(2,1)S(1)}, u32[]{:S(2)}, u32[]{:S(2)}) collective-permute-start(bf16[64,2048]{1,0:T(8,128)(2,1)S(1)} %get-tuple-element.41), channel_id=1, source_target_pairs={{4,0},{8,4},{12,8},{16,12},{20,16},{24,20},{28,24},{32,28},{36,32}... | collective-permute-start | bytes 786440 | tf_op jit(solution)/shard_map/ppermute | solution.py:144
  22.0 4.6 %collective-permute-start.4 = (bf16[64,2048]{1,0:T(8,128)(2,1)S(1)}, bf16[64,2048]{1,0:T(8,128)(2,1)S(1)}, u32[]{:S(2)}, u32[]{:S(2)}) collective-permute-start(bf16[64,2048]{1,0:T(8,128)(2,1)S(1)} %get-tuple-element.42), channel_id=1, source_target_pairs={{0,4},{4,8},{8,12},{12,16},{16,20},{20,24},{24,28},{28,32},{32,36}... | collective-permute-start | bytes 786440 | tf_op jit(solution)/shard_map/ppermute | solution.py:143
  26.5 0.1 pad_maximum_fusion
  26.7 0.1 collective-permute-start.1
  26.7 0.0 collective-permute-done.3.hi_ref
  26.8 0.0 copy-start.4
  26.8 0.0 collective-permute-done.2.lo_ref
  26.8 3.0 %collective-permute-done.5.fhi_ref = bf16[64,2048]{1,0:T(8,128)(2,1)S(1)} collective-permute-done((bf16[64,2048]{1,0:T(8,128)(2,1)S(1)}, bf16[64,2048]{1,0:T(8,128)(2,1)S(1)}, u32[]{:S(2)}, u32[]{:S(2)}) %collective-permute-start.5) | collective-permute-done | bytes 262176 | tf_op jit(solution)/shard_map/ppermute | solution.py:144
  29.8 1.2 %collective-permute-done.4.flo_ref = bf16[64,2048]{1,0:T(8,128)(2,1)S(1)} collective-permute-done((bf16[64,2048]{1,0:T(8,128)(2,1)S(1)}, bf16[64,2048]{1,0:T(8,128)(2,1)S(1)}, u32[]{:S(2)}, u32[]{:S(2)}) %collective-permute-start.4) | collective-permute-done | bytes 262176 | tf_op jit(solution)/shard_map/ppermute | solution.py:143
  31.0 1.2 %pad_maximum_fusion.1 = bf16[4,64,2048]{2,1,0:T(8,128)(2,1)S(1)} fusion(bf16[1,64,2048]{2,1,0:T(8,128)(2,1)S(1)} %bitcast.44, bf16[1,64,2048]{2,1,0:T(8,128)(2,1)S(1)} %bitcast.45, bf16[1,64,2048]{2,1,0:T(8,128)(2,1)S(1)} %bitcast.43, bf16[1,64,2048]{2,1,0:T(8,128)(2,1)} %bitcast.5), kind=kLoop, calls=%fused_computation.2 | loop fusion | flops 1572864 | bytes 2097152 | tf_op jit(solution)/shard_map/stack | solution.py:146
  32.2 0.3 collective-permute-start.6
  32.4 0.0 collective-permute-done.1.near_ref
  32.4 2.8 %collective-permute-done.6.hal_ref = bf16[4,64,2048]{2,1,0:T(8,128)(2,1)} collective-permute-done((bf16[4,64,2048]{2,1,0:T(8,128)(2,1)S(1)}, bf16[4,64,2048]{2,1,0:T(8,128)(2,1)}, u32[]{:S(2)}, u32[]{:S(2)}) %collective-permute-start.6) | collective-permute-done | bytes 1048608 | tf_op jit(solution)/shard_map/ppermute | solution.py:146
  35.2 0.0 copy-done.6
  35.2 12.5 %shard_map.58 = (bf16[2,32,2048]{2,1,0:T(8,128)(2,1)}, bf16[2,32,2048]{2,1,0:T(8,128)(2,1)}, f32[27,128,32]{2,1,0:T(8,128)}) custom-call(bf16[64,4096]{1,0:T(8,128)(2,1)} %bitcast.37, bf16[64,4096]{1,0:T(8,128)(2,1)} %copy-done.1, bf16[2,64,4096]{2,1,0:T(8,128)(2,1)} %copy-done.3, bf16[64,2048]{1,0:T(8,128)(2,1)} %collective-permute-done.2.lo_ref, ...), custom_call_target="tpu_custom_call" | custom-call | tf_op jit(solution)/shard_map/pallas_call | solution.py:96
  47.7 1.6 %dynamic-slice_convert_fusion.3 = (bf16[27,32,32]{2,1,0:T(8,128)(2,1)S(1)}, bf16[27,32,32]{2,1,0:T(8,128)(2,1)S(1)}, bf16[27,32,32]{2,1,0:T(8,128)(2,1)S(1)}, bf16[27,32,32]{2,1,0:T(8,128)(2,1)S(1)}) fusion(f32[27,128,32]{2,1,0:T(8,128)} %get-tuple-element.14, s32[]{:T(128)S(6)} %select_n.30, s32[]{:T(128)S(6)} %select_n.36, s32[]{:T(128)S(6)} %select_n.34, ...), kind=kLoop, calls=%fused_computation.8 | loop fusion | bytes 442384 | tf_op jit(solution)/shard_map/convert
  49.3 0.2 pad_maximum_fusion.2
  49.6 0.3 copy.57
  49.9 1.4 %reshape.33 = bf16[32,2,1728]{2,1,0:T(2,128)(2,1)} reshape(bf16[32,27,4,32]{3,2,1,0:T(4,128)(2,1)S(1)} %copy.57) | data formatting | bytes 442368
  51.3 16.6 %all-to-all-start = ((bf16[32,2,1728]{2,1,0:T(2,128)(2,1)}), bf16[32,2,1728]{2,1,0:T(2,128)(2,1)S(1)}, u32[]{:S(2)}, u32[]{:S(2)}) async-start(bf16[32,2,1728]{2,1,0:T(2,128)(2,1)} %reshape.33), calls=%async_computation | async-start | bytes 458752 | tf_op jit(solution)/shard_map/all_to_all | solution.py:19
  67.9 0.0 copy-done.10
  67.9 0.7 copy.58
  68.6 0.0 copy-done.9
  68.7 0.7 copy.59
  69.4 7.4 %all-to-all-done = bf16[32,2,1728]{2,1,0:T(2,128)(2,1)S(1)} async-done(((bf16[32,2,1728]{2,1,0:T(2,128)(2,1)}), bf16[32,2,1728]{2,1,0:T(2,128)(2,1)S(1)}, u32[]{:S(2)}, u32[]{:S(2)}) %all-to-all-start) | async-done | bytes 221216 | tf_op jit(solution)/shard_map/all_to_all | solution.py:19
  76.8 0.8 reshape.34
  77.6 0.5 convert_reduce_fusion
  78.0 0.6 broadcast_multiply_fusion
  (18 shorter events, 0.1 us)
Async XLA Ops:
  1.6 13.0 %copy-start.2 = (bf16[27,128,128]{2,1,0:T(8,128)(2,1)S(1)}, bf16[27,128,128]{2,1,0:T(8,128)(2,1)}, u32[]{:S(2)}) copy-start(bf16[27,128,128]{2,1,0:T(8,128)(2,1)} %param.4) | copy-start | bytes 2654212
  2.9 13.9 %copy-start = (bf16[8,8,32,128]{3,1,2,0:T(8,128)(2,1)}, bf16[8,8,32,128]{3,1,2,0:T(8,128)(2,1)S(1)}, u32[]{:S(2)}) copy-start(bf16[8,8,32,128]{3,1,2,0:T(8,128)(2,1)S(1)} %copy.68) | copy-start | bytes 1572868
  2.9 17.7 %collective-permute-start = (bf16[64,4096]{1,0:T(8,128)(2,1)S(1)}, bf16[64,4096]{1,0:T(8,128)(2,1)S(1)}, u32[]{:S(2)}, u32[]{:S(2)}) collective-permute-start(bf16[64,4096]{1,0:T(8,128)(2,1)S(1)} %bitcast.35), channel_id=1, source_target_pairs={{0,2},{2,0},{1,3},{3,1},{4,6},{6,4},{5,7},{7,5},{8,10},{10,8},{9,1... | collective-permute-start | bytes 1572872 | tf_op jit(solution)/shard_map/ppermute | solution.py:128
  7.8 19.0 %collective-permute-start.3 = (bf16[64,2048]{1,0:T(8,128)(2,1)}, bf16[64,2048]{1,0:T(8,128)(2,1)S(1)}, u32[]{:S(2)}, u32[]{:S(2)}) collective-permute-start(bf16[64,2048]{1,0:T(8,128)(2,1)} %get-tuple-element.43), channel_id=1, source_target_pairs={{4,0},{8,4},{12,8},{16,12},{20,16},{24,20},{28,24},{32,28},{36,32}... | collective-permute-start | bytes 786440 | tf_op jit(solution)/shard_map/ppermute | solution.py:130
  9.1 17.7 %collective-permute-start.2 = (bf16[64,2048]{1,0:T(8,128)(2,1)}, bf16[64,2048]{1,0:T(8,128)(2,1)}, u32[]{:S(2)}, u32[]{:S(2)}) collective-permute-start(bf16[64,2048]{1,0:T(8,128)(2,1)} %get-tuple-element.44), channel_id=1, source_target_pairs={{0,4},{4,8},{8,12},{12,16},{16,20},{20,24},{24,28},{28,32},{32,36}... | collective-permute-start | bytes 786440 | tf_op jit(solution)/shard_map/ppermute | solution.py:129
  16.8 2.4 %copy-start.8 = (bf16[27,32,32]{2,1,0:T(8,128)(2,1)S(1)}, bf16[27,32,32]{2,1,0:T(8,128)(2,1)}, u32[]{:S(2)}) copy-start(bf16[27,32,32]{2,1,0:T(8,128)(2,1)} %get-tuple-element.35) | copy-start | bytes 165892
  16.8 2.5 %copy-start.7 = (bf16[27,32,32]{2,1,0:T(8,128)(2,1)S(1)}, bf16[27,32,32]{2,1,0:T(8,128)(2,1)}, u32[]{:S(2)}) copy-start(bf16[27,32,32]{2,1,0:T(8,128)(2,1)} %get-tuple-element.36) | copy-start | bytes 165892
  20.6 11.5 %copy-start.1 = (bf16[64,4096]{1,0:T(8,128)(2,1)}, bf16[64,4096]{1,0:T(8,128)(2,1)S(1)}, u32[]{:S(2)}) copy-start(bf16[64,4096]{1,0:T(8,128)(2,1)S(1)} %collective-permute-done.far_ref) | copy-start | bytes 1572868
  20.7 9.1 %collective-permute-start.5 = (bf16[64,2048]{1,0:T(8,128)(2,1)S(1)}, bf16[64,2048]{1,0:T(8,128)(2,1)S(1)}, u32[]{:S(2)}, u32[]{:S(2)}) collective-permute-start(bf16[64,2048]{1,0:T(8,128)(2,1)S(1)} %get-tuple-element.41), channel_id=1, source_target_pairs={{4,0},{8,4},{12,8},{16,12},{20,16},{24,20},{28,24},{32,28},{36,32}... | collective-permute-start | bytes 786440 | tf_op jit(solution)/shard_map/ppermute | solution.py:144
  22.0 9.0 %collective-permute-start.4 = (bf16[64,2048]{1,0:T(8,128)(2,1)S(1)}, bf16[64,2048]{1,0:T(8,128)(2,1)S(1)}, u32[]{:S(2)}, u32[]{:S(2)}) collective-permute-start(bf16[64,2048]{1,0:T(8,128)(2,1)S(1)} %get-tuple-element.42), channel_id=1, source_target_pairs={{0,4},{4,8},{8,12},{12,16},{16,20},{20,24},{24,28},{28,32},{32,36}... | collective-permute-start | bytes 786440 | tf_op jit(solution)/shard_map/ppermute | solution.py:143
  26.7 5.8 %collective-permute-start.1 = (bf16[2,64,4096]{2,1,0:T(8,128)(2,1)S(1)}, bf16[2,64,4096]{2,1,0:T(8,128)(2,1)S(1)}, u32[]{:S(2)}, u32[]{:S(2)}) collective-permute-start(bf16[2,64,4096]{2,1,0:T(8,128)(2,1)S(1)} %pad_maximum_fusion), channel_id=1, source_target_pairs={{0,1},{1,0},{2,3},{3,2},{4,5},{5,4},{6,7},{7,6},{8,9},{9,8},{10,11... | collective-permute-start | bytes 3145736 | tf_op jit(solution)/shard_map/ppermute | solution.py:145
  26.8 8.4 %copy-start.4 = (bf16[64,2048]{1,0:T(8,128)(2,1)}, bf16[64,2048]{1,0:T(8,128)(2,1)S(1)}, u32[]{:S(2)}) copy-start(bf16[64,2048]{1,0:T(8,128)(2,1)S(1)} %collective-permute-done.3.hi_ref) | copy-start | bytes 786436
  29.8 5.4 %copy-start.5 = (bf16[64,2048]{1,0:T(8,128)(2,1)}, bf16[64,2048]{1,0:T(8,128)(2,1)S(1)}, u32[]{:S(2)}) copy-start(bf16[64,2048]{1,0:T(8,128)(2,1)S(1)} %collective-permute-done.5.fhi_ref) | copy-start | bytes 786436
  31.0 4.3 %copy-start.6 = (bf16[64,2048]{1,0:T(8,128)(2,1)}, bf16[64,2048]{1,0:T(8,128)(2,1)S(1)}, u32[]{:S(2)}) copy-start(bf16[64,2048]{1,0:T(8,128)(2,1)S(1)} %collective-permute-done.4.flo_ref) | copy-start | bytes 786436
  32.2 3.1 %collective-permute-start.6 = (bf16[4,64,2048]{2,1,0:T(8,128)(2,1)S(1)}, bf16[4,64,2048]{2,1,0:T(8,128)(2,1)}, u32[]{:S(2)}, u32[]{:S(2)}) collective-permute-start(bf16[4,64,2048]{2,1,0:T(8,128)(2,1)S(1)} %pad_maximum_fusion.1), channel_id=1, source_target_pairs={{0,1},{1,0},{2,3},{3,2},{4,5},{5,4},{6,7},{7,6},{8,9},{9,8},{10,11... | collective-permute-start | bytes 3145736 | tf_op jit(solution)/shard_map/ppermute | solution.py:146
  32.4 2.8 %copy-start.3 = (bf16[2,64,4096]{2,1,0:T(8,128)(2,1)}, bf16[2,64,4096]{2,1,0:T(8,128)(2,1)S(1)}, u32[]{:S(2)}) copy-start(bf16[2,64,4096]{2,1,0:T(8,128)(2,1)S(1)} %collective-permute-done.1.near_ref) | copy-start | bytes 3145732
  49.5 18.3 %copy-start.10 = (bf16[2,32,2048]{2,1,0:T(8,128)(2,1)S(1)}, bf16[2,32,2048]{2,1,0:T(8,128)(2,1)}, u32[]{:S(2)}) copy-start(bf16[2,32,2048]{2,1,0:T(8,128)(2,1)} %get-tuple-element.12) | copy-start | bytes 786436
  49.6 19.1 %copy-start.9 = (bf16[2,32,2048]{2,1,0:T(8,128)(2,1)S(1)}, bf16[2,32,2048]{2,1,0:T(8,128)(2,1)}, u32[]{:S(2)}) copy-start(bf16[2,32,2048]{2,1,0:T(8,128)(2,1)} %get-tuple-element.13) | copy-start | bytes 786436
  51.3 25.5 %all-to-all-start = ((bf16[32,2,1728]{2,1,0:T(2,128)(2,1)}), bf16[32,2,1728]{2,1,0:T(2,128)(2,1)S(1)}, u32[]{:S(2)}, u32[]{:S(2)}) async-start(bf16[32,2,1728]{2,1,0:T(2,128)(2,1)} %reshape.33), calls=%async_computation | async-start | bytes 458752 | tf_op jit(solution)/shard_map/all_to_all | solution.py:19

commit v7 on v4

--- a/solution.py
+++ b/solution.py
@@ -21,11 +21,12 @@
 
 def fused_kernel(
     own_ref, far_ref, near_ref, lo_ref, hi_ref, flo_ref, fhi_ref, hal_ref, wf_ref, wb_ref,
-    out_ref, ing_ref, wg_ref, vs_ref, cs_ref,
+    out_ref, ing_ref, wg_ref, vs_ref, cs_ref, *, grads,
 ):
     both = own_ref.shape[0]
     loc = both // 2
-    planes, _, width = out_ref.shape
+    width = lo_ref.shape[1]
+    planes = own_ref.shape[1] // width
     plane = width + 2 * ROW
     span = (planes - 1) * plane + width
     blank = jnp.zeros((loc, ROW), jnp.bfloat16)
@@ -37,7 +38,8 @@
     )
     for k, (body_of, low_of, high_of) in enumerate(pieces):
         rows = slice(k * loc, (k + 1) * loc)
-        for ref, low in ((vs_ref, 0), (cs_ref, loc)):
+        targets = ((vs_ref, 0), (cs_ref, loc)) if (not grads or k == 0) else ((vs_ref, 0),)
+        for ref, low in targets:
             chans = slice(low, low + loc)
             for zp in range(planes + 2):
                 ref[rows, zp * plane : zp * plane + ROW] = blank
@@ -52,11 +54,12 @@
     first = lane == 0
     last = lane == ROW - 1
     zero = jnp.zeros((loc, span), jnp.float32)
-    start = plane + ROW
-    cm = cs_ref[0:loc, start : start + span].astype(jnp.float32)
-    c_prev = jnp.where(last, zero, pltpu.roll(cm, span - 1, 1))
-    c_next = jnp.where(first, zero, pltpu.roll(cm, 1, 1))
-    cstack = jnp.concatenate([c_prev, cm, c_next], axis=0).astype(jnp.bfloat16)
+    if grads:
+        start = plane + ROW
+        cm = cs_ref[0:loc, start : start + span].astype(jnp.float32)
+        c_prev = jnp.where(last, zero, pltpu.roll(cm, span - 1, 1))
+        c_next = jnp.where(first, zero, pltpu.roll(cm, 1, 1))
+        cstack = jnp.concatenate([c_prev, cm, c_next], axis=0).astype(jnp.bfloat16)
 
     def shifted_sum(r):
         left = jnp.where(first, zero, pltpu.roll(r[0:loc], 1, 1))
@@ -70,6 +73,13 @@
             base = tap_z * plane + tap_y * ROW
             pair = 3 * tap_z + tap_y
             sv = vs_ref[:, base : base + span]
+            if grads:
+                w = lax.dot_general(
+                    sv, cstack, (((1,), (1,)), ((), ())), preferred_element_type=jnp.float32
+                )
+                for tap_x in range(3):
+                    wg_ref[3 * pair + tap_x] = w[:, tap_x * loc : (tap_x + 1) * loc]
+                continue
             sc = cs_ref[:, base : base + span]
             acc_o = acc_o + shifted_sum(
                 jnp.dot(wf_ref[pair], sv, preferred_element_type=jnp.float32)
@@ -77,34 +87,45 @@
             acc_i = acc_i + shifted_sum(
                 jnp.dot(wb_ref[pair], sc, preferred_element_type=jnp.float32)
             )
-            w = lax.dot_general(
-                sv, cstack, (((1,), (1,)), ((), ())), preferred_element_type=jnp.float32
-            )
-            for tap_x in range(3):
-                wg_ref[3 * pair + tap_x] = w[:, tap_x * loc : (tap_x + 1) * loc]
+    if grads:
+        return
     width = out_ref.shape[2]
     for z in range(planes):
         out_ref[z] = acc_o[:, z * plane : z * plane + width].astype(out_ref.dtype)
         ing_ref[z] = acc_i[:, z * plane : z * plane + width].astype(ing_ref.dtype)
 
 
-def fused(own, far, near, low, high, far_low, far_high, halos, wf, wb, planes, width):
-    both = own.shape[0]
+def fused(pieces, wf, wb, planes, width, grads):
+    both = pieces[0].shape[0]
     loc = both // 2
     cin = 4 * loc
     flat = (planes + 2) * (width + 2 * ROW)
-    return pl.pallas_call(
-        fused_kernel,
-        out_shape=(
+    if grads:
+        shapes = (jax.ShapeDtypeStruct((27, cin, loc), jnp.float32),)
+    else:
+        shapes = (
             jax.ShapeDtypeStruct((planes, loc, width), jnp.bfloat16),
             jax.ShapeDtypeStruct((planes, loc, width), jnp.bfloat16),
-            jax.ShapeDtypeStruct((27, cin, loc), jnp.float32),
-        ),
+        )
+
+    def kernel(*refs):
+        ins = refs[:10]
+        outs = refs[10:-2]
+        scratch = refs[-2:]
+        if grads:
+            outs = (None, None) + tuple(outs)
+        else:
+            outs = tuple(outs) + (None,)
+        fused_kernel(*ins, *outs, *scratch, grads=grads)
+
+    return pl.pallas_call(
+        kernel,
+        out_shape=shapes,
         scratch_shapes=[
             pltpu.VMEM((cin, flat), jnp.bfloat16),
             pltpu.VMEM((cin, flat), jnp.bfloat16),
         ],
-    )(own, far, near, low, high, far_low, far_high, halos, wf, wb)
+    )(*pieces, wf, wb)
 
 
 def by_group(array, order, size, dim):
@@ -143,10 +164,10 @@
     weight_rows = lax.dynamic_slice_in_dim(weight, my_group * in_local, in_local, 1)
     weight_rows = by_group(weight_rows, order, out_local, 2)
     wb = weight_rows[::-1].reshape(9, 3 * in_local, cout)
-    out, ing, wg = fused(
-        both, got_far, got_near, low, high, far_low, far_high, halos, wf, wb, planes_local, width
-    )
+    pieces = (both, got_far, got_near, low, high, far_low, far_high, halos)
+    (wg,) = fused(pieces, wf, wb, planes_local, width, True)
     wg = by_group(wg, order, in_local, 1)
+    out, ing = fused(pieces, wf, wb, planes_local, width, False)
     shape = (out_local, planes_local, grid_rows, grid_cols)
     out = jnp.transpose(out, (1, 0, 2)).reshape(shape)
     ing = jnp.transpose(ing, (1, 0, 2)).reshape(shape)

time: 76.5 us -> 82.3 us (1.076); the launches traced: 76.1 us -> 80.6 us
  starting transfers between devices: 29.7 us -> 20.8 us
  local copies, waits for them, and re-layouts: 11.6 us -> 18.1 us
  Pallas kernels: 12.5 us -> 15.8 us
  other arithmetic: 4.97 us -> 7.04 us
  waiting for transfers between devices: 16.5 us -> 18 us
    all_to_all x1, waiting for transfers between devices: 7.73 us -> 0.01 us  [summed_on_arrival(): lax.all_to_all(blocks, axis, split_axis=0, concat_axis=0, tiled=True)]
    ppermute x1, waiting for transfers between devices: 4.32 us -> 11.1 us  [body(): got_far = lax.ppermute(both, far, swap)]
    unnamed x26, local copies, waits for them, and re-layouts: 5.72 us -> 11.3 us
    all_to_all x1, starting transfers between devices: 13.1 us -> 8.74 us  [summed_on_arrival(): lax.all_to_all(blocks, axis, split_axis=0, concat_axis=0, tiled=True)]
    pallas_call x1 -> x2, Pallas kernels: 12.5 us -> 15.8 us  [fused(): pl.pallas_call(kernel, out_shape=shapes, scratch_shapes=[pltpu.VMEM((cin,...]
    ppermute x1, starting transfers between devices: 4.56 us -> 1.31 us  [body(): far_low = lax.ppermute(got_far[:, -width:], 'gz', up)]
    ppermute x1, waiting for transfers between devices: 1.18 us -> 2.81 us  [body(): far_low = lax.ppermute(got_far[:, -width:], 'gz', up)]
    concatenate x3, other arithmetic: 1.52 us -> 2.69 us  [by_group(): jnp.concatenate([lax.dynamic_slice_in_dim(array, group * size, size, dim)...]
  transfers between devices with their start and end apart: 8 -> 8, of which waited for: 4 -> 3; matrix products, arithmetic and copies ran while one was open for 11% -> 19% of each run, Pallas kernels for 0% -> 12%
where the time goes in v7:
time: 82.3 us; the launch traced here: 80.6 us
  starting transfers between devices  20.8 us (25%)
  local copies, waits for them, and re-layouts  18.1 us (22%)
  waiting for transfers between devices  18 us (22%)
  Pallas kernels  15.8 us (19%)
  other arithmetic  7.04 us (9%)
    pallas_call x2, Pallas kernels, fused(): pl.pallas_call(kernel, out_shape=shapes, scratch_shapes=[pltpu.VMEM((cin,...  15.8 us
    unnamed x26, local copies, waits for them, and re-layouts  11.3 us
    ppermute x1, waiting for transfers between devices, body(): got_far = lax.ppermute(both, far, swap)  11.1 us
    all_to_all x1, starting transfers between devices, summed_on_arrival(): lax.all_to_all(blocks, axis, split_axis=0, concat_axis=0, tiled=True)  8.74 us
    ppermute x1, waiting for transfers between devices, body(): far_high = lax.ppermute(got_far[:, :width], 'gz', down)  4.13 us
    ppermute x1, starting transfers between devices, body(): low = lax.ppermute(both[:, -width:], 'gz', up)  4.1 us
    ppermute x1, starting transfers between devices, body(): got_far = lax.ppermute(both, far, swap)  4.07 us
    ppermute x1, waiting for transfers between devices, body(): far_low = lax.ppermute(got_far[:, -width:], 'gz', up)  2.81 us
  transfers between devices with their start and end apart: 8, of which 3 were waited for; matrix products, arithmetic and copies ran while one was open for 19% of the time, Pallas kernels for 12%

profile of v7, /device:TPU:0, one launch (start us, length us, event | category | flops | bytes accessed | tf_op | source)
XLA Modules:
  0.0 80.6 jit_solution(5199175241917337662)
XLA Ops:
  0.6 1.0 %constant_dynamic-update-slice_fusion.1 = bf16[64,2,16,128]{3,2,1,0:T(8,128)(2,1)S(1)} fusion(bf16[32,2,16,128]{3,2,1,0:T(8,128)(2,1)} %param.3), kind=kLoop, calls=%fused_computation.13 | loop fusion | bytes 524288
  1.6 1.0 %constant_dynamic-update-slice_fusion = bf16[64,2,16,128]{3,2,1,0:T(8,128)(2,1)S(1)} fusion(bf16[64,2,16,128]{3,2,1,0:T(8,128)(2,1)S(1)} %constant_dynamic-update-slice_fusion.1, bf16[32,2,16,128]{3,2,1,0:T(8,128)(2,1)} %param.5), kind=kLoop, calls=%fused_computation.12 | loop fusion | bytes 524288 | tf_op jit(solution)/shard_map/concatenate | solution.py:144
  2.6 0.2 copy.68
  2.8 4.1 %collective-permute-start = (bf16[64,4096]{1,0:T(8,128)(2,1)S(1)}, bf16[64,4096]{1,0:T(8,128)(2,1)S(1)}, u32[]{:S(2)}, u32[]{:S(2)}) collective-permute-start(bf16[64,4096]{1,0:T(8,128)(2,1)S(1)} %bitcast.35), channel_id=1, source_target_pairs={{0,2},{2,0},{1,3},{3,1},{4,6},{6,4},{5,7},{7,5},{8,10},{10,8},{9,1... | collective-permute-start | bytes 1572872 | tf_op jit(solution)/shard_map/ppermute | solution.py:149
  6.9 0.8 %fusion.1 = (bf16[64,2048]{1,0:T(8,128)(2,1)}, bf16[64,2048]{1,0:T(8,128)(2,1)}) fusion(bf16[64,4096]{1,0:T(8,128)(2,1)S(1)} %bitcast.36), kind=kLoop, calls=%fused_computation.22 | loop fusion | bytes 1048576 | tf_op jit(solution)/shard_map/slice | solution.py:151
  7.7 4.1 %collective-permute-start.2 = (bf16[64,2048]{1,0:T(8,128)(2,1)}, bf16[64,2048]{1,0:T(8,128)(2,1)}, u32[]{:S(2)}, u32[]{:S(2)}) collective-permute-start(bf16[64,2048]{1,0:T(8,128)(2,1)} %get-tuple-element.36), channel_id=1, source_target_pairs={{0,4},{4,8},{8,12},{12,16},{16,20},{20,24},{24,28},{28,32},{32,36}... | collective-permute-start | bytes 786440 | tf_op jit(solution)/shard_map/ppermute | solution.py:150
  11.8 1.3 %collective-permute-start.3 = (bf16[64,2048]{1,0:T(8,128)(2,1)}, bf16[64,2048]{1,0:T(8,128)(2,1)}, u32[]{:S(2)}, u32[]{:S(2)}) collective-permute-start(bf16[64,2048]{1,0:T(8,128)(2,1)} %get-tuple-element.35), channel_id=1, source_target_pairs={{4,0},{8,4},{12,8},{16,12},{20,16},{24,20},{28,24},{32,28},{36,32}... | collective-permute-start | bytes 786440 | tf_op jit(solution)/shard_map/ppermute | solution.py:151
  13.1 0.2 stack_reshape.3
  13.3 11.1 %collective-permute-done.refs_1_ = bf16[64,4096]{1,0:T(8,128)(2,1)S(1)} collective-permute-done((bf16[64,4096]{1,0:T(8,128)(2,1)S(1)}, bf16[64,4096]{1,0:T(8,128)(2,1)S(1)}, u32[]{:S(2)}, u32[]{:S(2)}) %collective-permute-start) | collective-permute-done | bytes 524320 | tf_op jit(solution)/shard_map/ppermute | solution.py:149
  24.5 1.3 %collective-permute-start.4 = (bf16[64,2048]{1,0:T(8,128)(2,1)S(1)}, bf16[64,2048]{1,0:T(8,128)(2,1)S(1)}, u32[]{:S(2)}, u32[]{:S(2)}) collective-permute-start(bf16[64,2048]{1,0:T(8,128)(2,1)S(1)} %get-tuple-element.34), channel_id=1, source_target_pairs={{0,4},{4,8},{8,12},{12,16},{16,20},{20,24},{24,28},{28,32},{32,36}... | collective-permute-start | bytes 786440 | tf_op jit(solution)/shard_map/ppermute | solution.py:152
  25.8 1.3 %collective-permute-start.5 = (bf16[64,2048]{1,0:T(8,128)(2,1)S(1)}, bf16[64,2048]{1,0:T(8,128)(2,1)S(1)}, u32[]{:S(2)}, u32[]{:S(2)}) collective-permute-start(bf16[64,2048]{1,0:T(8,128)(2,1)S(1)} %get-tuple-element.33), channel_id=1, source_target_pairs={{4,0},{8,4},{12,8},{16,12},{20,16},{24,20},{28,24},{32,28},{36,32}... | collective-permute-start | bytes 786440 | tf_op jit(solution)/shard_map/ppermute | solution.py:153
  27.1 0.0 copy-start.4
  27.1 1.1 %pad_maximum_fusion = bf16[2,64,4096]{2,1,0:T(8,128)(2,1)} fusion(bf16[1,64,4096]{2,1,0:T(8,128)(2,1)S(1)} %bitcast.39, bf16[1,64,4096]{2,1,0:T(8,128)(2,1)S(1)} %stack_reshape.3), kind=kLoop, calls=%fused_computation.1 | loop fusion | flops 524288 | bytes 2097152 | tf_op jit(solution)/shard_map/stack | solution.py:154
  28.2 0.0 collective-permute-start.1
  28.2 0.0 collective-permute-done.2.refs_3_
  28.2 0.0 collective-permute-done.3.refs_4_
  28.2 2.8 %collective-permute-done.4.refs_5_ = bf16[64,2048]{1,0:T(8,128)(2,1)S(1)} collective-permute-done((bf16[64,2048]{1,0:T(8,128)(2,1)S(1)}, bf16[64,2048]{1,0:T(8,128)(2,1)S(1)}, u32[]{:S(2)}, u32[]{:S(2)}) %collective-permute-start.4) | collective-permute-done | bytes 262176 | tf_op jit(solution)/shard_map/ppermute | solution.py:152
  31.0 4.1 %collective-permute-done.5.refs_6_ = bf16[64,2048]{1,0:T(8,128)(2,1)S(1)} collective-permute-done((bf16[64,2048]{1,0:T(8,128)(2,1)S(1)}, bf16[64,2048]{1,0:T(8,128)(2,1)S(1)}, u32[]{:S(2)}, u32[]{:S(2)}) %collective-permute-start.5) | collective-permute-done | bytes 262176 | tf_op jit(solution)/shard_map/ppermute | solution.py:153
  35.2 0.7 copy-done.6
  35.9 2.1 %pad_maximum_fusion.1 = bf16[4,64,2048]{2,1,0:T(8,128)(2,1)} fusion(bf16[1,64,2048]{2,1,0:T(8,128)(2,1)S(1)} %bitcast.43, bf16[1,64,2048]{2,1,0:T(8,128)(2,1)S(1)} %bitcast.42, bf16[1,64,2048]{2,1,0:T(8,128)(2,1)} %bitcast.2, bf16[1,64,2048]{2,1,0:T(8,128)(2,1)} %bitcast.1), kind=kLoop, calls=%fused_computation.2 | loop fusion | flops 1572864 | bytes 2097152 | tf_op jit(solution)/shard_map/stack | solution.py:155
  38.0 0.0 collective-permute-start.6
  38.0 2.1 %constant_dynamic-slice_fusion.2 = (bf16[27,32,32]{2,1,0:T(8,128)(2,1)}, bf16[27,32,32]{2,1,0:T(8,128)(2,1)}, bf16[27,32,32]{2,1,0:T(8,128)(2,1)S(1)}, bf16[27,3...) fusion(bf16[27,128,128]{2,1,0:T(8,128)(2,1)S(1)} %copy-done.4, ...), kind=kLoop, calls=%fused_computation.16 | loop fusion | bytes 774160 | tf_op jit(solution)/shard_map/dynamic_slice | solution.py:133
  40.1 1.1 %copy.63 = bf16[27,32,32]{1,2,0:T(8,128)(2,1)S(1)} copy(bf16[27,32,32]{2,1,0:T(8,128)(2,1)} %get-tuple-element.30) | data formatting | bytes 110592
  41.2 1.1 %copy.62 = bf16[27,32,32]{1,2,0:T(8,128)(2,1)S(1)} copy(bf16[27,32,32]{2,1,0:T(8,128)(2,1)} %get-tuple-element.27) | data formatting | bytes 110592
  42.3 0.2 copy.61
  42.5 0.2 copy.60
  42.6 1.5 %pad_maximum_fusion.4 = bf16[27,32,128]{2,1,0:T(8,128)(2,1)S(1)} fusion(bf16[27,32,32]{2,1,0:T(8,128)(2,1)} %get-tuple-element.31, bf16[27,32,32]{2,1,0:T(8,128)(2,1)} %get-tuple-element.32, bf16[27,32,32]{2,1,0:T(8,128)(2,1)} %get-tuple-element.26, bf16[27,32,32]{2,1,0:T(8,128)(2,1)S(1)} %get-tuple-element.29), kind=kLoop, calls=%fused_computation.10 | loop fusion | flops 884736 | bytes 442368 | tf_op jit(solution)/shard_map/concatenate | solution.py:132
  44.1 0.7 rev.3
  44.8 1.0 %pad_maximum_fusion.3 = bf16[27,128,32]{1,2,0:T(8,128)(2,1)} fusion(bf16[27,32,32]{1,2,0:T(8,128)(2,1)S(1)} %copy.63, bf16[27,32,32]{1,2,0:T(8,128)(2,1)S(1)} %copy.62, bf16[27,32,32]{1,2,0:T(8,128)(2,1)S(1)} %copy.61, bf16[27,32,32]{1,2,0:T(8,128)(2,1)S(1)} %copy.60), kind=kLoop, calls=%fused_computation.9 | loop fusion | flops 884736 | bytes 442368 | tf_op jit(solution)/shard_map/concatenate | solution.py:132
  45.8 0.0 collective-permute-done.1.refs_2_
  45.8 0.0 collective-permute-done.6.refs_7_
  45.9 1.0 %copy-done.2 = bf16[2,64,4096]{2,1,0:T(8,128)(2,1)} copy-done((bf16[2,64,4096]{2,1,0:T(8,128)(2,1)}, bf16[2,64,4096]{2,1,0:T(8,128)(2,1)S(1)}, u32[]{:S(2)}) %copy-start.2) | copy-done | bytes 1048600
  46.8 0.3 copy-done.3
  47.1 6.5 %shard_map.59 = f32[27,128,32]{2,1,0:T(8,128)} custom-call(bf16[64,4096]{1,0:T(8,128)(2,1)} %bitcast.37, bf16[64,4096]{1,0:T(8,128)(2,1)} %copy-done.1, bf16[2,64,4096]{2,1,0:T(8,128)(2,1)} %copy-done.2, bf16[64,2048]{1,0:T(8,128)(2,1)} %collective-permute-done.2.refs_3_, bf16[64,2048]{1,0:T(8,128)(2,1)} %collective-permute-done.3.refs_4_, ...), custom_call_target="tpu_custom_call" | custom-call | tf_op jit(solution)/shard_map/pallas_call | solution.py:121
  53.6 1.6 %dynamic-slice_convert_fusion.3 = (bf16[27,32,32]{2,1,0:T(8,128)(2,1)S(1)}, bf16[27,32,32]{2,1,0:T(8,128)(2,1)S(1)}, bf16[27,32,32]{2,1,0:T(8,128)(2,1)S(1)}, bf16[27,32,32]{2,1,0:T(8,128)(2,1)S(1)}) fusion(f32[27,128,32]{2,1,0:T(8,128)} %shard_map.59, s32[]{:T(128)S(6)} %select_n.30, s32[]{:T(128)S(6)} %select_n.36, s32[]{:T(128)S(6)} %select_n.34, ...), kind=kLoop, calls=%fused_computation.8 | loop fusion | bytes 442384 | tf_op jit(solution)/shard_map/convert
  55.2 0.2 pad_maximum_fusion.2
  55.5 0.3 copy.57
  55.8 1.4 %reshape.33 = bf16[32,2,1728]{2,1,0:T(2,128)(2,1)} reshape(bf16[32,27,4,32]{3,2,1,0:T(4,128)(2,1)S(1)} %copy.57) | data formatting | bytes 442368
  57.2 8.7 %all-to-all-start = ((bf16[32,2,1728]{2,1,0:T(2,128)(2,1)}), bf16[32,2,1728]{2,1,0:T(2,128)(2,1)S(1)}, u32[]{:S(2)}, u32[]{:S(2)}) async-start(bf16[32,2,1728]{2,1,0:T(2,128)(2,1)} %reshape.33), calls=%async_computation | async-start | bytes 458752 | tf_op jit(solution)/shard_map/all_to_all | solution.py:19
  66.0 9.4 %shard_map.58 = (bf16[2,32,2048]{2,1,0:T(8,128)(2,1)}, bf16[2,32,2048]{2,1,0:T(8,128)(2,1)}) custom-call(bf16[64,4096]{1,0:T(8,128)(2,1)} %bitcast.38, bf16[64,4096]{1,0:T(8,128)(2,1)} %copy-done.1, bf16[2,64,4096]{2,1,0:T(8,128)(2,1)} %copy-done.2, bf16[64,2048]{1,0:T(8,128)(2,1)} %collective-permute-done.2.refs_3_, ...), custom_call_target="tpu_custom_call" | custom-call | tf_op jit(solution)/shard_map/pallas_call | solution.py:121
  75.3 1.0 %copy.65 = bf16[8,8,16,128]{3,2,1,0:T(8,128)(2,1)S(1)} copy(bf16[8,8,16,128]{3,1,2,0:T(8,128)(2,1)} %bitcast.51) | data formatting | bytes 524288
  76.3 0.7 copy.58
  77.0 1.0 %copy.66 = bf16[8,8,16,128]{3,2,1,0:T(8,128)(2,1)S(1)} copy(bf16[8,8,16,128]{3,1,2,0:T(8,128)(2,1)} %bitcast.50) | data formatting | bytes 524288
  78.0 0.7 copy.59
  78.8 0.0 all-to-all-done
  78.8 0.8 reshape.34
  79.5 0.5 convert_reduce_fusion
  80.0 0.6 broadcast_multiply_fusion
  (11 shorter events, 0.1 us)
Async XLA Ops:
  2.8 25.4 %copy-start = (bf16[8,8,32,128]{3,1,2,0:T(8,128)(2,1)}, bf16[8,8,32,128]{3,1,2,0:T(8,128)(2,1)S(1)}, u32[]{:S(2)}) copy-start(bf16[8,8,32,128]{3,1,2,0:T(8,128)(2,1)S(1)} %copy.68) | copy-start | bytes 1572868
  2.8 21.6 %collective-permute-start = (bf16[64,4096]{1,0:T(8,128)(2,1)S(1)}, bf16[64,4096]{1,0:T(8,128)(2,1)S(1)}, u32[]{:S(2)}, u32[]{:S(2)}) collective-permute-start(bf16[64,4096]{1,0:T(8,128)(2,1)S(1)} %bitcast.35), channel_id=1, source_target_pairs={{0,2},{2,0},{1,3},{3,1},{4,6},{6,4},{5,7},{7,5},{8,10},{10,8},{9,1... | collective-permute-start | bytes 1572872 | tf_op jit(solution)/shard_map/ppermute | solution.py:149
  7.7 20.5 %collective-permute-start.2 = (bf16[64,2048]{1,0:T(8,128)(2,1)}, bf16[64,2048]{1,0:T(8,128)(2,1)}, u32[]{:S(2)}, u32[]{:S(2)}) collective-permute-start(bf16[64,2048]{1,0:T(8,128)(2,1)} %get-tuple-element.36), channel_id=1, source_target_pairs={{0,4},{4,8},{8,12},{12,16},{16,20},{20,24},{24,28},{28,32},{32,36}... | collective-permute-start | bytes 786440 | tf_op jit(solution)/shard_map/ppermute | solution.py:150
  11.8 16.4 %collective-permute-start.3 = (bf16[64,2048]{1,0:T(8,128)(2,1)}, bf16[64,2048]{1,0:T(8,128)(2,1)}, u32[]{:S(2)}, u32[]{:S(2)}) collective-permute-start(bf16[64,2048]{1,0:T(8,128)(2,1)} %get-tuple-element.35), channel_id=1, source_target_pairs={{4,0},{8,4},{12,8},{16,12},{20,16},{24,20},{28,24},{32,28},{36,32}... | collective-permute-start | bytes 786440 | tf_op jit(solution)/shard_map/ppermute | solution.py:151
  24.4 13.6 %copy-start.1 = (bf16[64,4096]{1,0:T(8,128)(2,1)}, bf16[64,4096]{1,0:T(8,128)(2,1)S(1)}, u32[]{:S(2)}) copy-start(bf16[64,4096]{1,0:T(8,128)(2,1)S(1)} %collective-permute-done.refs_1_) | copy-start | bytes 1572868
  24.5 6.5 %collective-permute-start.4 = (bf16[64,2048]{1,0:T(8,128)(2,1)S(1)}, bf16[64,2048]{1,0:T(8,128)(2,1)S(1)}, u32[]{:S(2)}, u32[]{:S(2)}) collective-permute-start(bf16[64,2048]{1,0:T(8,128)(2,1)S(1)} %get-tuple-element.34), channel_id=1, source_target_pairs={{0,4},{4,8},{8,12},{12,16},{16,20},{20,24},{24,28},{28,32},{32,36}... | collective-permute-start | bytes 786440 | tf_op jit(solution)/shard_map/ppermute | solution.py:152
  25.8 9.4 %collective-permute-start.5 = (bf16[64,2048]{1,0:T(8,128)(2,1)S(1)}, bf16[64,2048]{1,0:T(8,128)(2,1)S(1)}, u32[]{:S(2)}, u32[]{:S(2)}) collective-permute-start(bf16[64,2048]{1,0:T(8,128)(2,1)S(1)} %get-tuple-element.33), channel_id=1, source_target_pairs={{4,0},{8,4},{12,8},{16,12},{20,16},{24,20},{28,24},{32,28},{36,32}... | collective-permute-start | bytes 786440 | tf_op jit(solution)/shard_map/ppermute | solution.py:153
  27.1 10.9 %copy-start.4 = (bf16[27,128,128]{2,1,0:T(8,128)(2,1)S(1)}, bf16[27,128,128]{2,1,0:T(8,128)(2,1)}, u32[]{:S(2)}) copy-start(bf16[27,128,128]{2,1,0:T(8,128)(2,1)} %param.4) | copy-start | bytes 2654212
  28.2 17.6 %collective-permute-start.1 = (bf16[2,64,4096]{2,1,0:T(8,128)(2,1)}, bf16[2,64,4096]{2,1,0:T(8,128)(2,1)S(1)}, u32[]{:S(2)}, u32[]{:S(2)}) collective-permute-start(bf16[2,64,4096]{2,1,0:T(8,128)(2,1)} %pad_maximum_fusion), channel_id=1, source_target_pairs={{0,1},{1,0},{2,3},{3,2},{4,5},{5,4},{6,7},{7,6},{8,9},{9,8},{10,11... | collective-permute-start | bytes 3145736 | tf_op jit(solution)/shard_map/ppermute | solution.py:154
  31.0 4.1 %copy-start.5 = (bf16[64,2048]{1,0:T(8,128)(2,1)}, bf16[64,2048]{1,0:T(8,128)(2,1)S(1)}, u32[]{:S(2)}) copy-start(bf16[64,2048]{1,0:T(8,128)(2,1)S(1)} %collective-permute-done.4.refs_5_) | copy-start | bytes 786436
  35.2 0.7 copy-start.6
  38.0 7.8 %collective-permute-start.6 = (bf16[4,64,2048]{2,1,0:T(8,128)(2,1)}, bf16[4,64,2048]{2,1,0:T(8,128)(2,1)S(1)}, u32[]{:S(2)}, u32[]{:S(2)}) collective-permute-start(bf16[4,64,2048]{2,1,0:T(8,128)(2,1)} %pad_maximum_fusion.1), channel_id=1, source_target_pairs={{0,1},{1,0},{2,3},{3,2},{4,5},{5,4},{6,7},{7,6},{8,9},{9,8},{10,11... | collective-permute-start | bytes 3145736 | tf_op jit(solution)/shard_map/ppermute | solution.py:155
  45.8 1.0 %copy-start.2 = (bf16[2,64,4096]{2,1,0:T(8,128)(2,1)}, bf16[2,64,4096]{2,1,0:T(8,128)(2,1)S(1)}, u32[]{:S(2)}) copy-start(bf16[2,64,4096]{2,1,0:T(8,128)(2,1)S(1)} %collective-permute-done.1.refs_2_) | copy-start | bytes 3145732
  45.8 1.3 %copy-start.3 = (bf16[4,64,2048]{2,1,0:T(8,128)(2,1)}, bf16[4,64,2048]{2,1,0:T(8,128)(2,1)S(1)}, u32[]{:S(2)}) copy-start(bf16[4,64,2048]{2,1,0:T(8,128)(2,1)S(1)} %collective-permute-done.6.refs_7_) | copy-start | bytes 3145732
  57.2 21.6 %all-to-all-start = ((bf16[32,2,1728]{2,1,0:T(2,128)(2,1)}), bf16[32,2,1728]{2,1,0:T(2,128)(2,1)S(1)}, u32[]{:S(2)}, u32[]{:S(2)}) async-start(bf16[32,2,1728]{2,1,0:T(2,128)(2,1)} %reshape.33), calls=%async_computation | async-start | bytes 458752 | tf_op jit(solution)/shard_map/all_to_all | solution.py:19

commit v8 on v7

--- a/solution.py
+++ b/solution.py
@@ -149,10 +149,6 @@
     got_far = lax.ppermute(both, far, swap)
     low = lax.ppermute(both[:, -width:], "gz", up)
     high = lax.ppermute(both[:, :width], "gz", down)
-    far_low = lax.ppermute(got_far[:, -width:], "gz", up)
-    far_high = lax.ppermute(got_far[:, :width], "gz", down)
-    got_near = lax.ppermute(jnp.stack([both, got_far]), near, swap)
-    halos = lax.ppermute(jnp.stack([low, high, far_low, far_high]), near, swap)
     groups = 4
     order = [jnp.bitwise_xor(my_group, j) for j in range(groups)]
     cin = groups * in_local
@@ -164,6 +160,11 @@
     weight_rows = lax.dynamic_slice_in_dim(weight, my_group * in_local, in_local, 1)
     weight_rows = by_group(weight_rows, order, out_local, 2)
     wb = weight_rows[::-1].reshape(9, 3 * in_local, cout)
+    got_far, wf, wb = lax.optimization_barrier((got_far, wf, wb))
+    far_low = lax.ppermute(got_far[:, -width:], "gz", up)
+    far_high = lax.ppermute(got_far[:, :width], "gz", down)
+    got_near = lax.ppermute(jnp.stack([both, got_far]), near, swap)
+    halos = lax.ppermute(jnp.stack([low, high, far_low, far_high]), near, swap)
     pieces = (both, got_far, got_near, low, high, far_low, far_high, halos)
     (wg,) = fused(pieces, wf, wb, planes_local, width, True)
     wg = by_group(wg, order, in_local, 1)

time: 82.3 us -> 79.6 us (0.967)
  starting transfers between devices: 20.8 us -> 25.3 us
  waiting for transfers between devices: 18 us -> 13.9 us
  other arithmetic: 7.04 us -> 4.78 us
    ppermute x1, waiting for transfers between devices: 11.1 us -> 3.48 us  [body(): got_far = lax.ppermute(both, far, swap)]
    all_to_all x1, starting transfers between devices: 8.74 us -> 13.8 us  [summed_on_arrival(): lax.all_to_all(blocks, axis, split_axis=0, concat_axis=0, tiled=True)]
    ppermute x1, waiting for transfers between devices: 0.01 us -> 2.63 us  [body(): halos = lax.ppermute(jnp.stack([low, high, far_low, far_high]), near, swap)]
    unnamed x26 -> x32, local copies, waits for them, and re-layouts: 11.3 us -> 9.15 us
    another operation x1, other arithmetic: 2.14 us -> 0.13 us  [body(): halos = lax.ppermute(jnp.stack([low, high, far_low, far_high]), near, swap)]
    another operation x1, other arithmetic: 1.09 us -> 0.1 us  [body(): got_near = lax.ppermute(jnp.stack([both, got_far]), near, swap)]
    rev x1, local copies, waits for them, and re-layouts: 0.72 us -> 1.65 us  [body(): wb = weight_rows[::-1].reshape(9, 3 * in_local, cout)]
    ppermute x1, waiting for transfers between devices: 2.81 us -> 3.68 us  [body(): far_low = lax.ppermute(got_far[:, -width:], 'gz', up)]
  transfers between devices with their start and end apart: 8 -> 8, of which waited for: 3 -> 4; matrix products, arithmetic and copies ran while one was open for 19% -> 17% of each run, Pallas kernels for 12% -> 12%
where the time goes in v8:
time: 79.6 us; the launch traced here: 78.4 us
  starting transfers between devices  25.3 us (32%)
  local copies, waits for them, and re-layouts  17.6 us (22%)
  Pallas kernels  15.8 us (20%)
  waiting for transfers between devices  13.9 us (17%)
  other arithmetic  4.78 us (6%)
  between operations  0.91 us (1%)
    pallas_call x2, Pallas kernels, fused(): pl.pallas_call(kernel, out_shape=shapes, scratch_shapes=[pltpu.VMEM((cin,...  15.8 us
    all_to_all x1, starting transfers between devices, summed_on_arrival(): lax.all_to_all(blocks, axis, split_axis=0, concat_axis=0, tiled=True)  13.8 us
    unnamed x32, local copies, waits for them, and re-layouts  9.15 us
    ppermute x1, waiting for transfers between devices, body(): far_high = lax.ppermute(got_far[:, :width], 'gz', down)  4.13 us
    ppermute x1, starting transfers between devices, body(): got_far = lax.ppermute(both, far, swap)  4.07 us
    ppermute x1, waiting for transfers between devices, body(): far_low = lax.ppermute(got_far[:, -width:], 'gz', up)  3.68 us
    ppermute x1, waiting for transfers between devices, body(): got_far = lax.ppermute(both, far, swap)  3.48 us
    concatenate x3, other arithmetic, by_group(): jnp.concatenate([lax.dynamic_slice_in_dim(array, group * size, size, dim)...  3.43 us
  transfers between devices with their start and end apart: 8, of which 4 were waited for; matrix products, arithmetic and copies ran while one was open for 17% of the time, Pallas kernels for 12%

profile of v8, /device:TPU:0, one launch (start us, length us, event | category | flops | bytes accessed | tf_op | source)
XLA Modules:
  0.0 78.4 jit_solution(9016237836406180083)
XLA Ops:
  0.6 1.0 %constant_dynamic-update-slice_fusion.1 = bf16[64,2,16,128]{3,2,1,0:T(8,128)(2,1)S(1)} fusion(bf16[32,2,16,128]{3,2,1,0:T(8,128)(2,1)} %param.3), kind=kLoop, calls=%fused_computation.13 | loop fusion | bytes 524288
  1.6 0.0 copy-start.4
  1.6 1.1 %constant_dynamic-update-slice_fusion = bf16[64,2,16,128]{3,2,1,0:T(8,128)(2,1)S(1)} fusion(bf16[64,2,16,128]{3,2,1,0:T(8,128)(2,1)S(1)} %constant_dynamic-update-slice_fusion.1, bf16[32,2,16,128]{3,2,1,0:T(8,128)(2,1)} %param.5), kind=kLoop, calls=%fused_computation.12 | loop fusion | bytes 524288 | tf_op jit(solution)/shard_map/concatenate | solution.py:144
  2.7 0.2 copy.68
  2.9 4.1 %collective-permute-start = (bf16[64,4096]{1,0:T(8,128)(2,1)S(1)}, bf16[64,4096]{1,0:T(8,128)(2,1)S(1)}, u32[]{:S(2)}, u32[]{:S(2)}) collective-permute-start(bf16[64,4096]{1,0:T(8,128)(2,1)S(1)} %bitcast.35), channel_id=1, source_target_pairs={{0,2},{2,0},{1,3},{3,1},{4,6},{6,4},{5,7},{7,5},{8,10},{10,8},{9,1... | collective-permute-start | bytes 1572872 | tf_op jit(solution)/shard_map/ppermute | solution.py:149
  7.0 0.8 %fusion.1 = (bf16[64,2048]{1,0:T(8,128)(2,1)}, bf16[64,2048]{1,0:T(8,128)(2,1)}) fusion(bf16[64,4096]{1,0:T(8,128)(2,1)S(1)} %bitcast.36), kind=kLoop, calls=%fused_computation.22 | loop fusion | bytes 1048576 | tf_op jit(solution)/shard_map/slice | solution.py:151
  7.8 3.4 %collective-permute-start.2 = (bf16[64,2048]{1,0:T(8,128)(2,1)}, bf16[64,2048]{1,0:T(8,128)(2,1)S(1)}, u32[]{:S(2)}, u32[]{:S(2)}) collective-permute-start(bf16[64,2048]{1,0:T(8,128)(2,1)} %get-tuple-element.42), channel_id=1, source_target_pairs={{0,4},{4,8},{8,12},{12,16},{16,20},{20,24},{24,28},{28,32},{32,36}... | collective-permute-start | bytes 786440 | tf_op jit(solution)/shard_map/ppermute | solution.py:150
  11.2 1.3 %collective-permute-start.3 = (bf16[64,2048]{1,0:T(8,128)(2,1)}, bf16[64,2048]{1,0:T(8,128)(2,1)S(1)}, u32[]{:S(2)}, u32[]{:S(2)}) collective-permute-start(bf16[64,2048]{1,0:T(8,128)(2,1)} %get-tuple-element.41), channel_id=1, source_target_pairs={{4,0},{8,4},{12,8},{16,12},{20,16},{24,20},{28,24},{32,28},{36,32}... | collective-permute-start | bytes 786440 | tf_op jit(solution)/shard_map/ppermute | solution.py:151
  12.5 1.0 %stack_reshape.3 = bf16[1,64,4096]{2,1,0:T(8,128)(2,1)} reshape(bf16[64,2,16,128]{3,2,1,0:T(8,128)(2,1)S(1)} %constant_dynamic-update-slice_fusion) | data formatting | bytes 1048576 | tf_op jit(solution)/shard_map/stack;reshape | solution.py:166
  13.6 2.0 %constant_dynamic-slice_fusion.2 = (bf16[27,32,32]{2,1,0:T(8,128)(2,1)}, bf16[27,32,32]{2,1,0:T(8,128)(2,1)S(1)}, bf16[27,32,32]{2,1,0:T(8,128)(2,1)S(1)}, bf16[...) fusion(bf16[27,128,128]{2,1,0:T(8,128)(2,1)S(1)} %copy-done.4, ...), kind=kLoop, calls=%fused_computation.16 | loop fusion | bytes 774160 | tf_op jit(solution)/shard_map/dynamic_slice | solution.py:133
  15.5 0.2 copy.63
  15.7 0.2 copy.62
  15.8 0.2 copy.61
  16.0 0.2 copy.60
  16.2 2.2 %pad_maximum_fusion.4 = bf16[27,32,128]{2,1,0:T(8,128)(2,1)} fusion(bf16[27,32,32]{2,1,0:T(8,128)(2,1)} %get-tuple-element.37, bf16[27,32,32]{2,1,0:T(8,128)(2,1)} %get-tuple-element.38, bf16[27,32,32]{2,1,0:T(8,128)(2,1)} %get-tuple-element.32, bf16[27,32,32]{2,1,0:T(8,128)(2,1)S(1)} %get-tuple-element.35), kind=kLoop, calls=%fused_computation.10 | loop fusion | flops 884736 | bytes 442368 | tf_op jit(solution)/shard_map/concatenate | solution.py:132
  18.4 1.6 %rev.3 = bf16[27,32,128]{2,1,0:T(8,128)(2,1)} reverse(bf16[27,32,128]{2,1,0:T(8,128)(2,1)} %pad_maximum_fusion.4), dimensions={0} | reverse | bytes 442368 | tf_op jit(solution)/shard_map/rev | solution.py:162
  20.0 1.0 %pad_maximum_fusion.3 = bf16[27,128,32]{1,2,0:T(8,128)(2,1)} fusion(bf16[27,32,32]{1,2,0:T(8,128)(2,1)S(1)} %copy.63, bf16[27,32,32]{1,2,0:T(8,128)(2,1)S(1)} %copy.62, bf16[27,32,32]{1,2,0:T(8,128)(2,1)S(1)} %copy.61, bf16[27,32,32]{1,2,0:T(8,128)(2,1)S(1)} %copy.60), kind=kLoop, calls=%fused_computation.9 | loop fusion | flops 884736 | bytes 442368 | tf_op jit(solution)/shard_map/concatenate | solution.py:132
  21.0 3.5 %collective-permute-done.refs_1_ = bf16[64,4096]{1,0:T(8,128)(2,1)S(1)} collective-permute-done((bf16[64,4096]{1,0:T(8,128)(2,1)S(1)}, bf16[64,4096]{1,0:T(8,128)(2,1)S(1)}, u32[]{:S(2)}, u32[]{:S(2)}) %collective-permute-start) | collective-permute-done | bytes 524320 | tf_op jit(solution)/shard_map/ppermute | solution.py:149
  24.6 1.3 %collective-permute-start.4 = (bf16[64,2048]{1,0:T(8,128)(2,1)S(1)}, bf16[64,2048]{1,0:T(8,128)(2,1)S(1)}, u32[]{:S(2)}, u32[]{:S(2)}) collective-permute-start(bf16[64,2048]{1,0:T(8,128)(2,1)S(1)} %get-tuple-element.40), channel_id=1, source_target_pairs={{0,4},{4,8},{8,12},{12,16},{16,20},{20,24},{24,28},{28,32},{32,36}... | collective-permute-start | bytes 786440 | tf_op jit(solution)/shard_map/ppermute | solution.py:164
  25.9 1.3 %collective-permute-start.5 = (bf16[64,2048]{1,0:T(8,128)(2,1)S(1)}, bf16[64,2048]{1,0:T(8,128)(2,1)S(1)}, u32[]{:S(2)}, u32[]{:S(2)}) collective-permute-start(bf16[64,2048]{1,0:T(8,128)(2,1)S(1)} %get-tuple-element.39), channel_id=1, source_target_pairs={{4,0},{8,4},{12,8},{16,12},{20,16},{24,20},{28,24},{32,28},{36,32}... | collective-permute-start | bytes 786440 | tf_op jit(solution)/shard_map/ppermute | solution.py:165
  27.2 0.1 pad_maximum_fusion
  27.3 0.1 collective-permute-start.1
  27.4 0.0 collective-permute-done.2.refs_3_
  27.4 0.0 copy-start.5
  27.4 0.0 copy-start.6
  27.4 3.7 %collective-permute-done.4.refs_5_ = bf16[64,2048]{1,0:T(8,128)(2,1)S(1)} collective-permute-done((bf16[64,2048]{1,0:T(8,128)(2,1)S(1)}, bf16[64,2048]{1,0:T(8,128)(2,1)S(1)}, u32[]{:S(2)}, u32[]{:S(2)}) %collective-permute-start.4) | collective-permute-done | bytes 262176 | tf_op jit(solution)/shard_map/ppermute | solution.py:164
  31.1 4.1 %collective-permute-done.5.refs_6_ = bf16[64,2048]{1,0:T(8,128)(2,1)S(1)} collective-permute-done((bf16[64,2048]{1,0:T(8,128)(2,1)S(1)}, bf16[64,2048]{1,0:T(8,128)(2,1)S(1)}, u32[]{:S(2)}, u32[]{:S(2)}) %collective-permute-start.5) | collective-permute-done | bytes 262176 | tf_op jit(solution)/shard_map/ppermute | solution.py:165
  35.2 0.7 copy-done.8
  36.0 0.1 pad_maximum_fusion.1
  36.1 0.1 collective-permute-start.6
  36.2 0.0 collective-permute-done.1.refs_2_
  36.2 2.6 %collective-permute-done.6.refs_7_ = bf16[4,64,2048]{2,1,0:T(8,128)(2,1)S(1)} collective-permute-done((bf16[4,64,2048]{2,1,0:T(8,128)(2,1)S(1)}, bf16[4,64,2048]{2,1,0:T(8,128)(2,1)S(1)}, u32[]{:S(2)}, u32[]{:S(2)}) %collective-permute-start.6) | collective-permute-done | bytes 1048608 | tf_op jit(solution)/shard_map/ppermute | solution.py:167
  38.9 1.0 %copy-done.3 = bf16[4,64,2048]{2,1,0:T(8,128)(2,1)} copy-done((bf16[4,64,2048]{2,1,0:T(8,128)(2,1)}, bf16[4,64,2048]{2,1,0:T(8,128)(2,1)S(1)}, u32[]{:S(2)}) %copy-start.3) | copy-done | bytes 1048600
  39.8 6.5 %shard_map.59 = f32[27,128,32]{2,1,0:T(8,128)} custom-call(bf16[64,4096]{1,0:T(8,128)(2,1)} %bitcast.37, bf16[64,4096]{1,0:T(8,128)(2,1)} %copy-done.1, bf16[2,64,4096]{2,1,0:T(8,128)(2,1)} %copy-done.2, bf16[64,2048]{1,0:T(8,128)(2,1)} %copy-done.5, bf16[64,2048]{1,0:T(8,128)(2,1)} %copy-done.6, bf16[64,2048]{1,0:T(8,128)(2,1)} %copy-done.7, ...), custom_call_target="tpu_custom_call" | custom-call | tf_op jit(solution)/shard_map/pallas_call | solution.py:121
  46.3 1.6 %dynamic-slice_convert_fusion.3 = (bf16[27,32,32]{2,1,0:T(8,128)(2,1)S(1)}, bf16[27,32,32]{2,1,0:T(8,128)(2,1)S(1)}, bf16[27,32,32]{2,1,0:T(8,128)(2,1)S(1)}, bf16[27,32,32]{2,1,0:T(8,128)(2,1)S(1)}) fusion(f32[27,128,32]{2,1,0:T(8,128)} %shard_map.59, s32[]{:T(128)S(6)} %select_n.30, s32[]{:T(128)S(6)} %select_n.36, s32[]{:T(128)S(6)} %select_n.34, ...), kind=kLoop, calls=%fused_computation.8 | loop fusion | bytes 442384 | tf_op jit(solution)/shard_map/convert
  47.9 0.2 pad_maximum_fusion.2
  48.2 0.3 copy.57
  48.5 1.4 %reshape.33 = bf16[32,2,1728]{2,1,0:T(2,128)(2,1)} reshape(bf16[32,27,4,32]{3,2,1,0:T(4,128)(2,1)S(1)} %copy.57) | data formatting | bytes 442368
  49.9 13.8 %all-to-all-start = ((bf16[32,2,1728]{2,1,0:T(2,128)(2,1)}), bf16[32,2,1728]{2,1,0:T(2,128)(2,1)S(1)}, u32[]{:S(2)}, u32[]{:S(2)}) async-start(bf16[32,2,1728]{2,1,0:T(2,128)(2,1)} %reshape.33), calls=%async_computation | async-start | bytes 458752 | tf_op jit(solution)/shard_map/all_to_all | solution.py:19
  63.7 9.4 %shard_map.58 = (bf16[2,32,2048]{2,1,0:T(8,128)(2,1)}, bf16[2,32,2048]{2,1,0:T(8,128)(2,1)}) custom-call(bf16[64,4096]{1,0:T(8,128)(2,1)} %bitcast.38, bf16[64,4096]{1,0:T(8,128)(2,1)} %copy-done.1, bf16[2,64,4096]{2,1,0:T(8,128)(2,1)} %copy-done.2, bf16[64,2048]{1,0:T(8,128)(2,1)} %copy-done.5, bf16[64,2048]{1,0:T(8,128)(2,1)} %copy-done.6, ...), custom_call_target="tpu_custom_call" | custom-call | tf_op jit(solution)/shard_map/pallas_call | solution.py:121
  73.1 1.0 %copy.65 = bf16[8,8,16,128]{3,2,1,0:T(8,128)(2,1)S(1)} copy(bf16[8,8,16,128]{3,1,2,0:T(8,128)(2,1)} %bitcast.53) | data formatting | bytes 524288
  74.1 0.7 copy.58
  74.8 1.0 %copy.66 = bf16[8,8,16,128]{3,2,1,0:T(8,128)(2,1)S(1)} copy(bf16[8,8,16,128]{3,1,2,0:T(8,128)(2,1)} %bitcast.52) | data formatting | bytes 524288
  75.8 0.7 copy.59
  76.5 0.0 all-to-all-done
  76.5 0.8 reshape.34
  77.3 0.5 convert_reduce_fusion
  77.8 0.6 broadcast_multiply_fusion
  (17 shorter events, 0.1 us)
Async XLA Ops:
  1.6 12.0 %copy-start.4 = (bf16[27,128,128]{2,1,0:T(8,128)(2,1)S(1)}, bf16[27,128,128]{2,1,0:T(8,128)(2,1)}, u32[]{:S(2)}) copy-start(bf16[27,128,128]{2,1,0:T(8,128)(2,1)} %param.4) | copy-start | bytes 2654212
  2.9 12.6 %copy-start = (bf16[8,8,32,128]{3,1,2,0:T(8,128)(2,1)}, bf16[8,8,32,128]{3,1,2,0:T(8,128)(2,1)S(1)}, u32[]{:S(2)}) copy-start(bf16[8,8,32,128]{3,1,2,0:T(8,128)(2,1)S(1)} %copy.68) | copy-start | bytes 1572868
  2.9 21.6 %collective-permute-start = (bf16[64,4096]{1,0:T(8,128)(2,1)S(1)}, bf16[64,4096]{1,0:T(8,128)(2,1)S(1)}, u32[]{:S(2)}, u32[]{:S(2)}) collective-permute-start(bf16[64,4096]{1,0:T(8,128)(2,1)S(1)} %bitcast.35), channel_id=1, source_target_pairs={{0,2},{2,0},{1,3},{3,1},{4,6},{6,4},{5,7},{7,5},{8,10},{10,8},{9,1... | collective-permute-start | bytes 1572872 | tf_op jit(solution)/shard_map/ppermute | solution.py:149
  7.8 19.6 %collective-permute-start.2 = (bf16[64,2048]{1,0:T(8,128)(2,1)}, bf16[64,2048]{1,0:T(8,128)(2,1)S(1)}, u32[]{:S(2)}, u32[]{:S(2)}) collective-permute-start(bf16[64,2048]{1,0:T(8,128)(2,1)} %get-tuple-element.42), channel_id=1, source_target_pairs={{0,4},{4,8},{8,12},{12,16},{16,20},{20,24},{24,28},{28,32},{32,36}... | collective-permute-start | bytes 786440 | tf_op jit(solution)/shard_map/ppermute | solution.py:150
  11.2 16.2 %collective-permute-start.3 = (bf16[64,2048]{1,0:T(8,128)(2,1)}, bf16[64,2048]{1,0:T(8,128)(2,1)S(1)}, u32[]{:S(2)}, u32[]{:S(2)}) collective-permute-start(bf16[64,2048]{1,0:T(8,128)(2,1)} %get-tuple-element.41), channel_id=1, source_target_pairs={{4,0},{8,4},{12,8},{16,12},{20,16},{24,20},{28,24},{32,28},{36,32}... | collective-permute-start | bytes 786440 | tf_op jit(solution)/shard_map/ppermute | solution.py:151
  16.2 11.0 %copy-start.9 = (bf16[1,64,4096]{2,1,0:T(8,128)(2,1)S(1)}, bf16[1,64,4096]{2,1,0:T(8,128)(2,1)}, u32[]{:S(2)}) copy-start(bf16[1,64,4096]{2,1,0:T(8,128)(2,1)} %stack_reshape.3) | copy-start | bytes 1572868
  24.5 11.6 %copy-start.1 = (bf16[64,4096]{1,0:T(8,128)(2,1)}, bf16[64,4096]{1,0:T(8,128)(2,1)S(1)}, u32[]{:S(2)}) copy-start(bf16[64,4096]{1,0:T(8,128)(2,1)S(1)} %collective-permute-done.refs_1_) | copy-start | bytes 1572868
  24.6 6.5 %collective-permute-start.4 = (bf16[64,2048]{1,0:T(8,128)(2,1)S(1)}, bf16[64,2048]{1,0:T(8,128)(2,1)S(1)}, u32[]{:S(2)}, u32[]{:S(2)}) collective-permute-start(bf16[64,2048]{1,0:T(8,128)(2,1)S(1)} %get-tuple-element.40), channel_id=1, source_target_pairs={{0,4},{4,8},{8,12},{12,16},{16,20},{20,24},{24,28},{28,32},{32,36}... | collective-permute-start | bytes 786440 | tf_op jit(solution)/shard_map/ppermute | solution.py:164
  25.9 9.4 %collective-permute-start.5 = (bf16[64,2048]{1,0:T(8,128)(2,1)S(1)}, bf16[64,2048]{1,0:T(8,128)(2,1)S(1)}, u32[]{:S(2)}, u32[]{:S(2)}) collective-permute-start(bf16[64,2048]{1,0:T(8,128)(2,1)S(1)} %get-tuple-element.39), channel_id=1, source_target_pairs={{4,0},{8,4},{12,8},{16,12},{20,16},{24,20},{28,24},{32,28},{36,32}... | collective-permute-start | bytes 786440 | tf_op jit(solution)/shard_map/ppermute | solution.py:165
  27.3 8.9 %collective-permute-start.1 = (bf16[2,64,4096]{2,1,0:T(8,128)(2,1)S(1)}, bf16[2,64,4096]{2,1,0:T(8,128)(2,1)S(1)}, u32[]{:S(2)}, u32[]{:S(2)}) collective-permute-start(bf16[2,64,4096]{2,1,0:T(8,128)(2,1)S(1)} %pad_maximum_fusion), channel_id=1, source_target_pairs={{0,1},{1,0},{2,3},{3,2},{4,5},{5,4},{6,7},{7,6},{8,9},{9,8},{10,11... | collective-permute-start | bytes 3145736 | tf_op jit(solution)/shard_map/ppermute | solution.py:166
  27.4 11.5 %copy-start.5 = (bf16[64,2048]{1,0:T(8,128)(2,1)}, bf16[64,2048]{1,0:T(8,128)(2,1)S(1)}, u32[]{:S(2)}) copy-start(bf16[64,2048]{1,0:T(8,128)(2,1)S(1)} %collective-permute-done.2.refs_3_) | copy-start | bytes 786436
  27.4 11.4 %copy-start.6 = (bf16[64,2048]{1,0:T(8,128)(2,1)}, bf16[64,2048]{1,0:T(8,128)(2,1)S(1)}, u32[]{:S(2)}) copy-start(bf16[64,2048]{1,0:T(8,128)(2,1)S(1)} %collective-permute-done.3.refs_4_) | copy-start | bytes 786436
  31.1 7.7 %copy-start.7 = (bf16[64,2048]{1,0:T(8,128)(2,1)}, bf16[64,2048]{1,0:T(8,128)(2,1)S(1)}, u32[]{:S(2)}) copy-start(bf16[64,2048]{1,0:T(8,128)(2,1)S(1)} %collective-permute-done.4.refs_5_) | copy-start | bytes 786436
  35.2 0.7 copy-start.8
  36.1 2.7 %collective-permute-start.6 = (bf16[4,64,2048]{2,1,0:T(8,128)(2,1)S(1)}, bf16[4,64,2048]{2,1,0:T(8,128)(2,1)S(1)}, u32[]{:S(2)}, u32[]{:S(2)}) collective-permute-start(bf16[4,64,2048]{2,1,0:T(8,128)(2,1)S(1)} %pad_maximum_fusion.1), channel_id=1, source_target_pairs={{0,1},{1,0},{2,3},{3,2},{4,5},{5,4},{6,7},{7,6},{8,9},{9,8},{10,11... | collective-permute-start | bytes 3145736 | tf_op jit(solution)/shard_map/ppermute | solution.py:167
  36.2 2.6 %copy-start.2 = (bf16[2,64,4096]{2,1,0:T(8,128)(2,1)}, bf16[2,64,4096]{2,1,0:T(8,128)(2,1)S(1)}, u32[]{:S(2)}) copy-start(bf16[2,64,4096]{2,1,0:T(8,128)(2,1)S(1)} %collective-permute-done.1.refs_2_) | copy-start | bytes 3145732
  38.9 1.0 %copy-start.3 = (bf16[4,64,2048]{2,1,0:T(8,128)(2,1)}, bf16[4,64,2048]{2,1,0:T(8,128)(2,1)S(1)}, u32[]{:S(2)}) copy-start(bf16[4,64,2048]{2,1,0:T(8,128)(2,1)S(1)} %collective-permute-done.6.refs_7_) | copy-start | bytes 3145732
  49.9 26.6 %all-to-all-start = ((bf16[32,2,1728]{2,1,0:T(2,128)(2,1)}), bf16[32,2,1728]{2,1,0:T(2,128)(2,1)S(1)}, u32[]{:S(2)}, u32[]{:S(2)}) async-start(bf16[32,2,1728]{2,1,0:T(2,128)(2,1)} %reshape.33), calls=%async_computation | async-start | bytes 458752 | tf_op jit(solution)/shard_map/all_to_all | solution.py:19

commit v9 on v4

--- a/solution.py
+++ b/solution.py
@@ -25,7 +25,8 @@
 ):
     both = own_ref.shape[0]
     loc = both // 2
-    planes, _, width = out_ref.shape
+    planes = out_ref.shape[1]
+    width = out_ref.shape[2] * out_ref.shape[3]
     plane = width + 2 * ROW
     span = (planes - 1) * plane + width
     blank = jnp.zeros((loc, ROW), jnp.bfloat16)
@@ -82,10 +83,11 @@
             )
             for tap_x in range(3):
                 wg_ref[3 * pair + tap_x] = w[:, tap_x * loc : (tap_x + 1) * loc]
-    width = out_ref.shape[2]
+    rows, cols = out_ref.shape[2], out_ref.shape[3]
     for z in range(planes):
-        out_ref[z] = acc_o[:, z * plane : z * plane + width].astype(out_ref.dtype)
-        ing_ref[z] = acc_i[:, z * plane : z * plane + width].astype(ing_ref.dtype)
+        for acc, ref in ((acc_o, out_ref), (acc_i, ing_ref)):
+            part = acc[:, z * plane : z * plane + width].reshape(loc, rows, cols)
+            ref[:, z] = part.astype(ref.dtype)
 
 
 def fused(own, far, near, low, high, far_low, far_high, halos, wf, wb, planes, width):
@@ -96,8 +98,8 @@
     return pl.pallas_call(
         fused_kernel,
         out_shape=(
-            jax.ShapeDtypeStruct((planes, loc, width), jnp.bfloat16),
-            jax.ShapeDtypeStruct((planes, loc, width), jnp.bfloat16),
+            jax.ShapeDtypeStruct((loc, planes, width // ROW, ROW), jnp.bfloat16),
+            jax.ShapeDtypeStruct((loc, planes, width // ROW, ROW), jnp.bfloat16),
             jax.ShapeDtypeStruct((27, cin, loc), jnp.float32),
         ),
         scratch_shapes=[
@@ -148,8 +150,8 @@
     )
     wg = by_group(wg, order, in_local, 1)
     shape = (out_local, planes_local, grid_rows, grid_cols)
-    out = jnp.transpose(out, (1, 0, 2)).reshape(shape)
-    ing = jnp.transpose(ing, (1, 0, 2)).reshape(shape)
+    out = out.reshape(shape)
+    ing = ing.reshape(shape)
     weight_grad = summed_on_arrival(wg.astype(jnp.bfloat16), "gz", 1) * jnp.float32(
         1.0 / math.sqrt(voxels)
     )

time: 76.5 us -> 75.4 us (0.986)
  blocking collectives: 0 us -> 22.2 us
  starting transfers between devices: 29.7 us -> 16.6 us
  waiting for transfers between devices: 16.5 us -> 8.76 us
  local copies, waits for them, and re-layouts: 11.6 us -> 9.34 us
    all_to_all x0 -> x1, blocking collectives: none -> 22.2 us  [summed_on_arrival(): lax.all_to_all(blocks, axis, split_axis=0, concat_axis=0, tiled=True)]
    all_to_all x1 -> x0, starting transfers between devices: 13.1 us -> none  [summed_on_arrival(): lax.all_to_all(blocks, axis, split_axis=0, concat_axis=0, tiled=True)]
    all_to_all x1 -> x0, waiting for transfers between devices: 7.73 us -> none  [summed_on_arrival(): lax.all_to_all(blocks, axis, split_axis=0, concat_axis=0, tiled=True)]
    unnamed x26 -> x18, local copies, waits for them, and re-layouts: 5.72 us -> 3.32 us
  transfers between devices with their start and end apart: 8 -> 7, of which waited for: 4 -> 3; matrix products, arithmetic and copies ran while one was open for 11% -> 10% of each run, Pallas kernels for 0% -> 0%
where the time goes in v9:
time: 75.4 us; the launch traced here: 75.1 us
  blocking collectives  22.2 us (29%)
  starting transfers between devices  16.6 us (22%)
  Pallas kernels  12.4 us (16%)
  local copies, waits for them, and re-layouts  9.34 us (12%)
  waiting for transfers between devices  8.76 us (12%)
  other arithmetic  4.96 us (7%)
  between operations  0.85 us (1%)
    all_to_all x1, blocking collectives, summed_on_arrival(): lax.all_to_all(blocks, axis, split_axis=0, concat_axis=0, tiled=True)  22.2 us
    pallas_call x1, Pallas kernels, fused(): pl.pallas_call(fused_kernel, out_shape=(jax.ShapeDtypeStruct((loc, planes...  12.4 us
    ppermute x1, starting transfers between devices, body(): low = lax.ppermute(both[:, -width:], 'gz', up)  5.26 us
    ppermute x1, starting transfers between devices, body(): far_low = lax.ppermute(got_far[:, -width:], 'gz', up)  4.56 us
    ppermute x1, waiting for transfers between devices, body(): got_far = lax.ppermute(both, far, swap)  4.32 us
    ppermute x1, starting transfers between devices, body(): got_far = lax.ppermute(both, far, swap)  4.07 us
    unnamed x18, local copies, waits for them, and re-layouts  3.32 us
    ppermute x1, waiting for transfers between devices, body(): far_high = lax.ppermute(got_far[:, :width], 'gz', down)  3.25 us
  transfers between devices with their start and end apart: 7, of which 3 were waited for; matrix products, arithmetic and copies ran while one was open for 10% of the time, Pallas kernels for 0%

profile of v9, /device:TPU:0, one launch (start us, length us, event | category | flops | bytes accessed | tf_op | source)
XLA Modules:
  0.0 75.1 jit_solution(3554440945960187336)
XLA Ops:
  0.6 1.0 %constant_dynamic-update-slice_fusion.1 = bf16[64,2,16,128]{3,2,1,0:T(8,128)(2,1)S(1)} fusion(bf16[32,2,16,128]{3,2,1,0:T(8,128)(2,1)} %param.3), kind=kLoop, calls=%fused_computation.13 | loop fusion | bytes 524288
  1.6 1.0 %constant_dynamic-update-slice_fusion = bf16[64,2,16,128]{3,2,1,0:T(8,128)(2,1)S(1)} fusion(bf16[64,2,16,128]{3,2,1,0:T(8,128)(2,1)S(1)} %constant_dynamic-update-slice_fusion.1, bf16[32,2,16,128]{3,2,1,0:T(8,128)(2,1)} %param.5), kind=kLoop, calls=%fused_computation.12 | loop fusion | bytes 524288 | tf_op jit(solution)/shard_map/concatenate | solution.py:125
  2.6 0.2 copy.56
  2.8 0.0 copy-start
  2.8 4.1 %collective-permute-start = (bf16[64,4096]{1,0:T(8,128)(2,1)S(1)}, bf16[64,4096]{1,0:T(8,128)(2,1)S(1)}, u32[]{:S(2)}, u32[]{:S(2)}) collective-permute-start(bf16[64,4096]{1,0:T(8,128)(2,1)S(1)} %bitcast.21), channel_id=1, source_target_pairs={{0,2},{2,0},{1,3},{3,1},{4,6},{6,4},{5,7},{7,5},{8,10},{10,8},{9,1... | collective-permute-start | bytes 1572872 | tf_op jit(solution)/shard_map/ppermute | solution.py:130
  6.9 0.8 %fusion.1 = (bf16[64,2048]{1,0:T(8,128)(2,1)}, bf16[64,2048]{1,0:T(8,128)(2,1)}) fusion(bf16[64,4096]{1,0:T(8,128)(2,1)S(1)} %bitcast.22), kind=kLoop, calls=%fused_computation.22 | loop fusion | bytes 1048576 | tf_op jit(solution)/shard_map/slice | solution.py:132
  7.7 1.3 %collective-permute-start.3 = (bf16[64,2048]{1,0:T(8,128)(2,1)}, bf16[64,2048]{1,0:T(8,128)(2,1)}, u32[]{:S(2)}, u32[]{:S(2)}) collective-permute-start(bf16[64,2048]{1,0:T(8,128)(2,1)} %get-tuple-element.22), channel_id=1, source_target_pairs={{4,0},{8,4},{12,8},{16,12},{20,16},{24,20},{28,24},{32,28},{36,32}... | collective-permute-start | bytes 786440 | tf_op jit(solution)/shard_map/ppermute | solution.py:132
  9.0 5.3 %collective-permute-start.2 = (bf16[64,2048]{1,0:T(8,128)(2,1)}, bf16[64,2048]{1,0:T(8,128)(2,1)}, u32[]{:S(2)}, u32[]{:S(2)}) collective-permute-start(bf16[64,2048]{1,0:T(8,128)(2,1)} %get-tuple-element.23), channel_id=1, source_target_pairs={{0,4},{4,8},{8,12},{12,16},{16,20},{20,24},{24,28},{28,32},{32,36}... | collective-permute-start | bytes 786440 | tf_op jit(solution)/shard_map/ppermute | solution.py:131
  14.3 0.2 stack_reshape.3
  14.5 4.3 %collective-permute-done.far_ref = bf16[64,4096]{1,0:T(8,128)(2,1)S(1)} collective-permute-done((bf16[64,4096]{1,0:T(8,128)(2,1)S(1)}, bf16[64,4096]{1,0:T(8,128)(2,1)S(1)}, u32[]{:S(2)}, u32[]{:S(2)}) %collective-permute-start) | collective-permute-done | bytes 524320 | tf_op jit(solution)/shard_map/ppermute | solution.py:130
  18.8 0.0 copy-start.1
  18.9 1.3 %collective-permute-start.5 = (bf16[64,2048]{1,0:T(8,128)(2,1)S(1)}, bf16[64,2048]{1,0:T(8,128)(2,1)S(1)}, u32[]{:S(2)}, u32[]{:S(2)}) collective-permute-start(bf16[64,2048]{1,0:T(8,128)(2,1)S(1)} %get-tuple-element.20), channel_id=1, source_target_pairs={{4,0},{8,4},{12,8},{16,12},{20,16},{24,20},{28,24},{32,28},{36,32}... | collective-permute-start | bytes 786440 | tf_op jit(solution)/shard_map/ppermute | solution.py:134
  20.2 4.6 %collective-permute-start.4 = (bf16[64,2048]{1,0:T(8,128)(2,1)S(1)}, bf16[64,2048]{1,0:T(8,128)(2,1)S(1)}, u32[]{:S(2)}, u32[]{:S(2)}) collective-permute-start(bf16[64,2048]{1,0:T(8,128)(2,1)S(1)} %get-tuple-element.21), channel_id=1, source_target_pairs={{0,4},{4,8},{8,12},{12,16},{16,20},{20,24},{24,28},{28,32},{32,36}... | collective-permute-start | bytes 786440 | tf_op jit(solution)/shard_map/ppermute | solution.py:133
  24.7 0.0 copy-start.2
  24.7 0.1 pad_maximum_fusion
  24.8 0.0 copy-done
  24.9 0.1 collective-permute-start.1
  25.0 0.0 collective-permute-done.3.hi_ref
  25.0 0.0 collective-permute-done.2.lo_ref
  25.0 3.2 %collective-permute-done.5.fhi_ref = bf16[64,2048]{1,0:T(8,128)(2,1)S(1)} collective-permute-done((bf16[64,2048]{1,0:T(8,128)(2,1)S(1)}, bf16[64,2048]{1,0:T(8,128)(2,1)S(1)}, u32[]{:S(2)}, u32[]{:S(2)}) %collective-permute-start.5) | collective-permute-done | bytes 262176 | tf_op jit(solution)/shard_map/ppermute | solution.py:134
  28.2 0.0 copy-start.3
  28.2 1.2 %collective-permute-done.4.flo_ref = bf16[64,2048]{1,0:T(8,128)(2,1)S(1)} collective-permute-done((bf16[64,2048]{1,0:T(8,128)(2,1)S(1)}, bf16[64,2048]{1,0:T(8,128)(2,1)S(1)}, u32[]{:S(2)}, u32[]{:S(2)}) %collective-permute-start.4) | collective-permute-done | bytes 262176 | tf_op jit(solution)/shard_map/ppermute | solution.py:133
  29.4 0.0 copy-start.4
  29.4 2.2 %pad_maximum_fusion.1 = bf16[4,64,2048]{2,1,0:T(8,128)(2,1)} fusion(bf16[1,64,2048]{2,1,0:T(8,128)(2,1)S(1)} %bitcast.27, bf16[1,64,2048]{2,1,0:T(8,128)(2,1)S(1)} %bitcast.28, bf16[1,64,2048]{2,1,0:T(8,128)(2,1)} %bitcast.2, bf16[1,64,2048]{2,1,0:T(8,128)(2,1)} %bitcast.1), kind=kLoop, calls=%fused_computation.2 | loop fusion | flops 1572864 | bytes 2097152 | tf_op jit(solution)/shard_map/stack | solution.py:136
  31.6 0.0 copy-done.1
  31.6 0.0 collective-permute-start.6
  31.6 0.0 copy-done.3
  31.7 0.0 copy-done.4
  31.7 0.0 copy-done.2
  31.7 1.2 %constant_dynamic-slice_fusion.2 = (bf16[27,32,32]{2,1,0:T(8,128)(2,1)S(1)}, bf16[27,32,32]{2,1,0:T(8,128)(2,1)S(1)}, bf16[27,32,32]{2,1,0:T(8,128)(2,1)S(1)}, b...) fusion(bf16[27,128,128]{2,1,0:T(8,128)(2,1)S(1)} %copy-done.2, ...), kind=kLoop, calls=%fused_computation.16 | loop fusion | bytes 774160 | tf_op jit(solution)/shard_map/dynamic_slice | solution.py:114
  32.9 0.2 copy.50
  33.0 0.3 pad_maximum_fusion.4
  33.3 0.7 rev.3
  34.0 0.2 copy.52
  34.2 0.2 copy.51
  34.4 0.2 copy.53
  34.5 1.0 %pad_maximum_fusion.3 = bf16[27,128,32]{1,2,0:T(8,128)(2,1)} fusion(bf16[27,32,32]{1,2,0:T(8,128)(2,1)S(1)} %copy.53, bf16[27,32,32]{1,2,0:T(8,128)(2,1)S(1)} %copy.52, bf16[27,32,32]{1,2,0:T(8,128)(2,1)S(1)} %copy.51, bf16[27,32,32]{1,2,0:T(8,128)(2,1)S(1)} %copy.50), kind=kLoop, calls=%fused_computation.9 | loop fusion | flops 884736 | bytes 442368 | tf_op jit(solution)/shard_map/concatenate | solution.py:113
  35.5 0.0 collective-permute-done.1.near_ref
  35.5 0.0 collective-permute-done.6.hal_ref
  35.5 12.4 %shard_map.58 = (bf16[32,2,16,128]{3,2,1,0:T(8,128)(2,1)}, bf16[32,2,16,128]{3,2,1,0:T(8,128)(2,1)}, f32[27,128,32]{2,1,0:T(8,128)}) custom-call(bf16[64,4096]{1,0:T(8,128)(2,1)} %bitcast.23, bf16[64,4096]{1,0:T(8,128)(2,1)} %copy-done.1, bf16[2,64,4096]{2,1,0:T(8,128)(2,1)} %collective-permute-done.1.near_ref, ...), custom_call_target="tpu_custom_call" | custom-call | tf_op jit(solution)/shard_map/pallas_call | solution.py:98
  47.9 1.6 %dynamic-slice_convert_fusion.3 = (bf16[27,32,32]{2,1,0:T(8,128)(2,1)S(1)}, bf16[27,32,32]{2,1,0:T(8,128)(2,1)S(1)}, bf16[27,32,32]{2,1,0:T(8,128)(2,1)S(1)}, bf16[27,32,32]{2,1,0:T(8,128)(2,1)S(1)}) fusion(f32[27,128,32]{2,1,0:T(8,128)} %get-tuple-element.8, s32[]{:T(128)S(6)} %select_n.30, s32[]{:T(128)S(6)} %select_n.36, s32[]{:T(128)S(6)} %select_n.34, ...), kind=kLoop, calls=%fused_computation.8 | loop fusion | bytes 442384 | tf_op jit(solution)/shard_map/convert
  49.5 0.2 pad_maximum_fusion.2
  49.8 0.5 copy.49
  50.3 0.7 reshape.25
  51.0 22.2 %all_to_all.5 = bf16[32,2,1728]{2,1,0:T(2,128)(2,1)S(1)} all-to-all(bf16[32,2,1728]{2,1,0:T(2,128)(2,1)S(1)} %reshape.25), channel_id=1, replica_groups=mesh['gz'=32,'ch_0'=2,'ch_1'=2] {'gz'}, dimensions={0} | all-to-all | bytes 442368 | tf_op jit(solution)/shard_map/all_to_all | solution.py:19
  73.2 0.8 %reshape.26 = bf16[32,27,4,32]{3,2,1,0:T(4,128)(2,1)S(1)} reshape(bf16[32,2,1728]{2,1,0:T(2,128)(2,1)S(1)} %all_to_all.5) | data formatting | bytes 442368
  74.0 0.5 convert_reduce_fusion
  74.4 0.6 broadcast_multiply_fusion
  (1 shorter events, 0.0 us)
Async XLA Ops:
  2.8 22.0 %copy-start = (bf16[8,8,32,128]{3,1,2,0:T(8,128)(2,1)}, bf16[8,8,32,128]{3,1,2,0:T(8,128)(2,1)S(1)}, u32[]{:S(2)}) copy-start(bf16[8,8,32,128]{3,1,2,0:T(8,128)(2,1)S(1)} %copy.56) | copy-start | bytes 1572868
  2.8 16.0 %collective-permute-start = (bf16[64,4096]{1,0:T(8,128)(2,1)S(1)}, bf16[64,4096]{1,0:T(8,128)(2,1)S(1)}, u32[]{:S(2)}, u32[]{:S(2)}) collective-permute-start(bf16[64,4096]{1,0:T(8,128)(2,1)S(1)} %bitcast.21), channel_id=1, source_target_pairs={{0,2},{2,0},{1,3},{3,1},{4,6},{6,4},{5,7},{7,5},{8,10},{10,8},{9,1... | collective-permute-start | bytes 1572872 | tf_op jit(solution)/shard_map/ppermute | solution.py:130
  7.7 17.2 %collective-permute-start.3 = (bf16[64,2048]{1,0:T(8,128)(2,1)}, bf16[64,2048]{1,0:T(8,128)(2,1)}, u32[]{:S(2)}, u32[]{:S(2)}) collective-permute-start(bf16[64,2048]{1,0:T(8,128)(2,1)} %get-tuple-element.22), channel_id=1, source_target_pairs={{4,0},{8,4},{12,8},{16,12},{20,16},{24,20},{28,24},{32,28},{36,32}... | collective-permute-start | bytes 786440 | tf_op jit(solution)/shard_map/ppermute | solution.py:132
  9.0 16.0 %collective-permute-start.2 = (bf16[64,2048]{1,0:T(8,128)(2,1)}, bf16[64,2048]{1,0:T(8,128)(2,1)}, u32[]{:S(2)}, u32[]{:S(2)}) collective-permute-start(bf16[64,2048]{1,0:T(8,128)(2,1)} %get-tuple-element.23), channel_id=1, source_target_pairs={{0,4},{4,8},{8,12},{12,16},{16,20},{20,24},{24,28},{28,32},{32,36}... | collective-permute-start | bytes 786440 | tf_op jit(solution)/shard_map/ppermute | solution.py:131
  18.8 12.8 %copy-start.1 = (bf16[64,4096]{1,0:T(8,128)(2,1)}, bf16[64,4096]{1,0:T(8,128)(2,1)S(1)}, u32[]{:S(2)}) copy-start(bf16[64,4096]{1,0:T(8,128)(2,1)S(1)} %collective-permute-done.far_ref) | copy-start | bytes 1572868
  18.9 9.4 %collective-permute-start.5 = (bf16[64,2048]{1,0:T(8,128)(2,1)S(1)}, bf16[64,2048]{1,0:T(8,128)(2,1)S(1)}, u32[]{:S(2)}, u32[]{:S(2)}) collective-permute-start(bf16[64,2048]{1,0:T(8,128)(2,1)S(1)} %get-tuple-element.20), channel_id=1, source_target_pairs={{4,0},{8,4},{12,8},{16,12},{20,16},{24,20},{28,24},{32,28},{36,32}... | collective-permute-start | bytes 786440 | tf_op jit(solution)/shard_map/ppermute | solution.py:134
  20.2 9.2 %collective-permute-start.4 = (bf16[64,2048]{1,0:T(8,128)(2,1)S(1)}, bf16[64,2048]{1,0:T(8,128)(2,1)S(1)}, u32[]{:S(2)}, u32[]{:S(2)}) collective-permute-start(bf16[64,2048]{1,0:T(8,128)(2,1)S(1)} %get-tuple-element.21), channel_id=1, source_target_pairs={{0,4},{4,8},{8,12},{12,16},{16,20},{20,24},{24,28},{28,32},{32,36}... | collective-permute-start | bytes 786440 | tf_op jit(solution)/shard_map/ppermute | solution.py:133
  24.7 7.0 %copy-start.2 = (bf16[27,128,128]{2,1,0:T(8,128)(2,1)S(1)}, bf16[27,128,128]{2,1,0:T(8,128)(2,1)}, u32[]{:S(2)}) copy-start(bf16[27,128,128]{2,1,0:T(8,128)(2,1)} %param.4) | copy-start | bytes 2654212
  24.9 10.7 %collective-permute-start.1 = (bf16[2,64,4096]{2,1,0:T(8,128)(2,1)S(1)}, bf16[2,64,4096]{2,1,0:T(8,128)(2,1)}, u32[]{:S(2)}, u32[]{:S(2)}) collective-permute-start(bf16[2,64,4096]{2,1,0:T(8,128)(2,1)S(1)} %pad_maximum_fusion), channel_id=1, source_target_pairs={{0,1},{1,0},{2,3},{3,2},{4,5},{5,4},{6,7},{7,6},{8,9},{9,8},{10,11... | collective-permute-start | bytes 3145736 | tf_op jit(solution)/shard_map/ppermute | solution.py:135
  28.2 3.4 %copy-start.3 = (bf16[64,2048]{1,0:T(8,128)(2,1)}, bf16[64,2048]{1,0:T(8,128)(2,1)S(1)}, u32[]{:S(2)}) copy-start(bf16[64,2048]{1,0:T(8,128)(2,1)S(1)} %collective-permute-done.5.fhi_ref) | copy-start | bytes 786436
  29.4 2.3 %copy-start.4 = (bf16[64,2048]{1,0:T(8,128)(2,1)}, bf16[64,2048]{1,0:T(8,128)(2,1)S(1)}, u32[]{:S(2)}) copy-start(bf16[64,2048]{1,0:T(8,128)(2,1)S(1)} %collective-permute-done.4.flo_ref) | copy-start | bytes 786436
  31.6 3.9 %collective-permute-start.6 = (bf16[4,64,2048]{2,1,0:T(8,128)(2,1)}, bf16[4,64,2048]{2,1,0:T(8,128)(2,1)}, u32[]{:S(2)}, u32[]{:S(2)}) collective-permute-start(bf16[4,64,2048]{2,1,0:T(8,128)(2,1)} %pad_maximum_fusion.1), channel_id=1, source_target_pairs={{0,1},{1,0},{2,3},{3,2},{4,5},{5,4},{6,7},{7,6},{8,9},{9,8},{10,11... | collective-permute-start | bytes 3145736 | tf_op jit(solution)/shard_map/ppermute | solution.py:136

commit v10 on v9

--- a/solution.py
+++ b/solution.py
@@ -64,25 +64,25 @@
         right = jnp.where(last, zero, pltpu.roll(r[2 * loc : 3 * loc], span - 1, 1))
         return left + r[loc : 2 * loc] + right
 
-    acc_o = zero
-    acc_i = zero
+    acc_o = None
+    acc_i = None
     for tap_z in range(3):
         for tap_y in range(3):
             base = tap_z * plane + tap_y * ROW
             pair = 3 * tap_z + tap_y
             sv = vs_ref[:, base : base + span]
             sc = cs_ref[:, base : base + span]
-            acc_o = acc_o + shifted_sum(
-                jnp.dot(wf_ref[pair], sv, preferred_element_type=jnp.float32)
-            )
-            acc_i = acc_i + shifted_sum(
-                jnp.dot(wb_ref[pair], sc, preferred_element_type=jnp.float32)
-            )
+            r = jnp.dot(wf_ref[pair], sv, preferred_element_type=jnp.float32)
+            acc_o = r if acc_o is None else acc_o + r
+            r = jnp.dot(wb_ref[pair], sc, preferred_element_type=jnp.float32)
+            acc_i = r if acc_i is None else acc_i + r
             w = lax.dot_general(
                 sv, cstack, (((1,), (1,)), ((), ())), preferred_element_type=jnp.float32
             )
             for tap_x in range(3):
                 wg_ref[3 * pair + tap_x] = w[:, tap_x * loc : (tap_x + 1) * loc]
+    acc_o = shifted_sum(acc_o)
+    acc_i = shifted_sum(acc_i)
     rows, cols = out_ref.shape[2], out_ref.shape[3]
     for z in range(planes):
         for acc, ref in ((acc_o, out_ref), (acc_i, ing_ref)):

time: 75.4 us -> 73.5 us (0.975)
  Pallas kernels: 12.4 us -> 10.7 us
    pallas_call x1, Pallas kernels: 12.4 us -> 10.7 us  [fused(): pl.pallas_call(fused_kernel, out_shape=(jax.ShapeDtypeStruct((loc, planes...]
where the time goes in v10:
time: 73.5 us; the launch traced here: 73.1 us
  blocking collectives  22.2 us (30%)
  starting transfers between devices  16.6 us (23%)
  Pallas kernels  10.7 us (15%)
  local copies, waits for them, and re-layouts  9.16 us (12%)
  waiting for transfers between devices  8.76 us (12%)
  other arithmetic  4.96 us (7%)
  between operations  0.85 us (1%)
    all_to_all x1, blocking collectives, summed_on_arrival(): lax.all_to_all(blocks, axis, split_axis=0, concat_axis=0, tiled=True)  22.2 us
    pallas_call x1, Pallas kernels, fused(): pl.pallas_call(fused_kernel, out_shape=(jax.ShapeDtypeStruct((loc, planes...  10.7 us
    ppermute x1, starting transfers between devices, body(): low = lax.ppermute(both[:, -width:], 'gz', up)  5.26 us
    ppermute x1, starting transfers between devices, body(): far_low = lax.ppermute(got_far[:, -width:], 'gz', up)  4.56 us
    ppermute x1, waiting for transfers between devices, body(): got_far = lax.ppermute(both, far, swap)  4.32 us
    ppermute x1, starting transfers between devices, body(): got_far = lax.ppermute(both, far, swap)  4.07 us
    unnamed x18, local copies, waits for them, and re-layouts  3.32 us
    ppermute x1, waiting for transfers between devices, body(): far_high = lax.ppermute(got_far[:, :width], 'gz', down)  3.25 us
  transfers between devices with their start and end apart: 7, of which 3 were waited for; matrix products, arithmetic and copies ran while one was open for 10% of the time, Pallas kernels for 0%

profile of v10, /device:TPU:0, one launch (start us, length us, event | category | flops | bytes accessed | tf_op | source)
XLA Modules:
  0.0 73.1 jit_solution(2000630268511489800)
XLA Ops:
  0.6 1.0 %constant_dynamic-update-slice_fusion.1 = bf16[64,2,16,128]{3,2,1,0:T(8,128)(2,1)S(1)} fusion(bf16[32,2,16,128]{3,2,1,0:T(8,128)(2,1)} %param.3), kind=kLoop, calls=%fused_computation.13 | loop fusion | bytes 524288
  1.6 1.0 %constant_dynamic-update-slice_fusion = bf16[64,2,16,128]{3,2,1,0:T(8,128)(2,1)S(1)} fusion(bf16[64,2,16,128]{3,2,1,0:T(8,128)(2,1)S(1)} %constant_dynamic-update-slice_fusion.1, bf16[32,2,16,128]{3,2,1,0:T(8,128)(2,1)} %param.5), kind=kLoop, calls=%fused_computation.12 | loop fusion | bytes 524288 | tf_op jit(solution)/shard_map/concatenate | solution.py:125
  2.6 0.2 copy.56
  2.8 0.0 copy-start
  2.8 4.1 %collective-permute-start = (bf16[64,4096]{1,0:T(8,128)(2,1)S(1)}, bf16[64,4096]{1,0:T(8,128)(2,1)S(1)}, u32[]{:S(2)}, u32[]{:S(2)}) collective-permute-start(bf16[64,4096]{1,0:T(8,128)(2,1)S(1)} %bitcast.21), channel_id=1, source_target_pairs={{0,2},{2,0},{1,3},{3,1},{4,6},{6,4},{5,7},{7,5},{8,10},{10,8},{9,1... | collective-permute-start | bytes 1572872 | tf_op jit(solution)/shard_map/ppermute | solution.py:130
  6.9 0.8 %fusion.1 = (bf16[64,2048]{1,0:T(8,128)(2,1)}, bf16[64,2048]{1,0:T(8,128)(2,1)}) fusion(bf16[64,4096]{1,0:T(8,128)(2,1)S(1)} %bitcast.22), kind=kLoop, calls=%fused_computation.22 | loop fusion | bytes 1048576 | tf_op jit(solution)/shard_map/slice | solution.py:132
  7.7 1.3 %collective-permute-start.3 = (bf16[64,2048]{1,0:T(8,128)(2,1)}, bf16[64,2048]{1,0:T(8,128)(2,1)}, u32[]{:S(2)}, u32[]{:S(2)}) collective-permute-start(bf16[64,2048]{1,0:T(8,128)(2,1)} %get-tuple-element.22), channel_id=1, source_target_pairs={{4,0},{8,4},{12,8},{16,12},{20,16},{24,20},{28,24},{32,28},{36,32}... | collective-permute-start | bytes 786440 | tf_op jit(solution)/shard_map/ppermute | solution.py:132
  9.0 5.3 %collective-permute-start.2 = (bf16[64,2048]{1,0:T(8,128)(2,1)}, bf16[64,2048]{1,0:T(8,128)(2,1)}, u32[]{:S(2)}, u32[]{:S(2)}) collective-permute-start(bf16[64,2048]{1,0:T(8,128)(2,1)} %get-tuple-element.23), channel_id=1, source_target_pairs={{0,4},{4,8},{8,12},{12,16},{16,20},{20,24},{24,28},{28,32},{32,36}... | collective-permute-start | bytes 786440 | tf_op jit(solution)/shard_map/ppermute | solution.py:131
  14.3 0.2 stack_reshape.3
  14.5 4.3 %collective-permute-done.far_ref = bf16[64,4096]{1,0:T(8,128)(2,1)S(1)} collective-permute-done((bf16[64,4096]{1,0:T(8,128)(2,1)S(1)}, bf16[64,4096]{1,0:T(8,128)(2,1)S(1)}, u32[]{:S(2)}, u32[]{:S(2)}) %collective-permute-start) | collective-permute-done | bytes 524320 | tf_op jit(solution)/shard_map/ppermute | solution.py:130
  18.8 0.0 copy-start.1
  18.9 1.3 %collective-permute-start.5 = (bf16[64,2048]{1,0:T(8,128)(2,1)S(1)}, bf16[64,2048]{1,0:T(8,128)(2,1)S(1)}, u32[]{:S(2)}, u32[]{:S(2)}) collective-permute-start(bf16[64,2048]{1,0:T(8,128)(2,1)S(1)} %get-tuple-element.20), channel_id=1, source_target_pairs={{4,0},{8,4},{12,8},{16,12},{20,16},{24,20},{28,24},{32,28},{36,32}... | collective-permute-start | bytes 786440 | tf_op jit(solution)/shard_map/ppermute | solution.py:134
  20.2 4.6 %collective-permute-start.4 = (bf16[64,2048]{1,0:T(8,128)(2,1)S(1)}, bf16[64,2048]{1,0:T(8,128)(2,1)S(1)}, u32[]{:S(2)}, u32[]{:S(2)}) collective-permute-start(bf16[64,2048]{1,0:T(8,128)(2,1)S(1)} %get-tuple-element.21), channel_id=1, source_target_pairs={{0,4},{4,8},{8,12},{12,16},{16,20},{20,24},{24,28},{28,32},{32,36}... | collective-permute-start | bytes 786440 | tf_op jit(solution)/shard_map/ppermute | solution.py:133
  24.7 0.0 copy-start.2
  24.7 0.1 pad_maximum_fusion
  24.8 0.0 copy-done
  24.9 0.1 collective-permute-start.1
  25.0 0.0 collective-permute-done.3.hi_ref
  25.0 0.0 collective-permute-done.2.lo_ref
  25.0 3.2 %collective-permute-done.5.fhi_ref = bf16[64,2048]{1,0:T(8,128)(2,1)S(1)} collective-permute-done((bf16[64,2048]{1,0:T(8,128)(2,1)S(1)}, bf16[64,2048]{1,0:T(8,128)(2,1)S(1)}, u32[]{:S(2)}, u32[]{:S(2)}) %collective-permute-start.5) | collective-permute-done | bytes 262176 | tf_op jit(solution)/shard_map/ppermute | solution.py:134
  28.2 0.0 copy-start.3
  28.2 1.2 %collective-permute-done.4.flo_ref = bf16[64,2048]{1,0:T(8,128)(2,1)S(1)} collective-permute-done((bf16[64,2048]{1,0:T(8,128)(2,1)S(1)}, bf16[64,2048]{1,0:T(8,128)(2,1)S(1)}, u32[]{:S(2)}, u32[]{:S(2)}) %collective-permute-start.4) | collective-permute-done | bytes 262176 | tf_op jit(solution)/shard_map/ppermute | solution.py:133
  29.4 0.0 copy-start.4
  29.4 2.2 %pad_maximum_fusion.1 = bf16[4,64,2048]{2,1,0:T(8,128)(2,1)} fusion(bf16[1,64,2048]{2,1,0:T(8,128)(2,1)S(1)} %bitcast.27, bf16[1,64,2048]{2,1,0:T(8,128)(2,1)S(1)} %bitcast.28, bf16[1,64,2048]{2,1,0:T(8,128)(2,1)} %bitcast.2, bf16[1,64,2048]{2,1,0:T(8,128)(2,1)} %bitcast.1), kind=kLoop, calls=%fused_computation.2 | loop fusion | flops 1572864 | bytes 2097152 | tf_op jit(solution)/shard_map/stack | solution.py:136
  31.6 0.0 copy-done.1
  31.6 0.0 collective-permute-start.6
  31.6 0.0 copy-done.3
  31.7 0.0 copy-done.4
  31.7 0.0 copy-done.2
  31.7 1.2 %constant_dynamic-slice_fusion.2 = (bf16[27,32,32]{2,1,0:T(8,128)(2,1)S(1)}, bf16[27,32,32]{2,1,0:T(8,128)(2,1)S(1)}, bf16[27,32,32]{2,1,0:T(8,128)(2,1)S(1)}, b...) fusion(bf16[27,128,128]{2,1,0:T(8,128)(2,1)S(1)} %copy-done.2, ...), kind=kLoop, calls=%fused_computation.16 | loop fusion | bytes 774160 | tf_op jit(solution)/shard_map/dynamic_slice | solution.py:114
  32.9 0.2 copy.50
  33.0 0.3 pad_maximum_fusion.4
  33.3 0.7 rev.3
  34.0 0.2 copy.52
  34.2 0.2 copy.51
  34.4 0.2 copy.53
  34.5 1.0 %pad_maximum_fusion.3 = bf16[27,128,32]{1,2,0:T(8,128)(2,1)} fusion(bf16[27,32,32]{1,2,0:T(8,128)(2,1)S(1)} %copy.53, bf16[27,32,32]{1,2,0:T(8,128)(2,1)S(1)} %copy.52, bf16[27,32,32]{1,2,0:T(8,128)(2,1)S(1)} %copy.51, bf16[27,32,32]{1,2,0:T(8,128)(2,1)S(1)} %copy.50), kind=kLoop, calls=%fused_computation.9 | loop fusion | flops 884736 | bytes 442368 | tf_op jit(solution)/shard_map/concatenate | solution.py:113
  35.5 0.0 collective-permute-done.1.near_ref
  35.5 0.0 collective-permute-done.6.hal_ref
  35.5 10.7 %shard_map.58 = (bf16[32,2,16,128]{3,2,1,0:T(8,128)(2,1)}, bf16[32,2,16,128]{3,2,1,0:T(8,128)(2,1)}, f32[27,128,32]{2,1,0:T(8,128)}) custom-call(bf16[64,4096]{1,0:T(8,128)(2,1)} %bitcast.23, bf16[64,4096]{1,0:T(8,128)(2,1)} %copy-done.1, bf16[2,64,4096]{2,1,0:T(8,128)(2,1)} %collective-permute-done.1.near_ref, ...), custom_call_target="tpu_custom_call" | custom-call | tf_op jit(solution)/shard_map/pallas_call | solution.py:98
  46.2 1.6 %dynamic-slice_convert_fusion.3 = (bf16[27,32,32]{2,1,0:T(8,128)(2,1)S(1)}, bf16[27,32,32]{2,1,0:T(8,128)(2,1)S(1)}, bf16[27,32,32]{2,1,0:T(8,128)(2,1)S(1)}, bf16[27,32,32]{2,1,0:T(8,128)(2,1)S(1)}) fusion(f32[27,128,32]{2,1,0:T(8,128)} %get-tuple-element.8, s32[]{:T(128)S(6)} %select_n.30, s32[]{:T(128)S(6)} %select_n.36, s32[]{:T(128)S(6)} %select_n.34, ...), kind=kLoop, calls=%fused_computation.8 | loop fusion | bytes 442384 | tf_op jit(solution)/shard_map/convert
  47.8 0.2 pad_maximum_fusion.2
  48.0 0.3 copy.49
  48.3 0.7 reshape.25
  49.1 22.2 %all_to_all.5 = bf16[32,2,1728]{2,1,0:T(2,128)(2,1)S(1)} all-to-all(bf16[32,2,1728]{2,1,0:T(2,128)(2,1)S(1)} %reshape.25), channel_id=1, replica_groups=mesh['gz'=32,'ch_0'=2,'ch_1'=2] {'gz'}, dimensions={0} | all-to-all | bytes 442368 | tf_op jit(solution)/shard_map/all_to_all | solution.py:19
  71.3 0.8 %reshape.26 = bf16[32,27,4,32]{3,2,1,0:T(4,128)(2,1)S(1)} reshape(bf16[32,2,1728]{2,1,0:T(2,128)(2,1)S(1)} %all_to_all.5) | data formatting | bytes 442368
  72.0 0.5 convert_reduce_fusion
  72.5 0.6 broadcast_multiply_fusion
  (1 shorter events, 0.0 us)
Async XLA Ops:
  2.8 22.0 %copy-start = (bf16[8,8,32,128]{3,1,2,0:T(8,128)(2,1)}, bf16[8,8,32,128]{3,1,2,0:T(8,128)(2,1)S(1)}, u32[]{:S(2)}) copy-start(bf16[8,8,32,128]{3,1,2,0:T(8,128)(2,1)S(1)} %copy.56) | copy-start | bytes 1572868
  2.8 16.0 %collective-permute-start = (bf16[64,4096]{1,0:T(8,128)(2,1)S(1)}, bf16[64,4096]{1,0:T(8,128)(2,1)S(1)}, u32[]{:S(2)}, u32[]{:S(2)}) collective-permute-start(bf16[64,4096]{1,0:T(8,128)(2,1)S(1)} %bitcast.21), channel_id=1, source_target_pairs={{0,2},{2,0},{1,3},{3,1},{4,6},{6,4},{5,7},{7,5},{8,10},{10,8},{9,1... | collective-permute-start | bytes 1572872 | tf_op jit(solution)/shard_map/ppermute | solution.py:130
  7.7 17.2 %collective-permute-start.3 = (bf16[64,2048]{1,0:T(8,128)(2,1)}, bf16[64,2048]{1,0:T(8,128)(2,1)}, u32[]{:S(2)}, u32[]{:S(2)}) collective-permute-start(bf16[64,2048]{1,0:T(8,128)(2,1)} %get-tuple-element.22), channel_id=1, source_target_pairs={{4,0},{8,4},{12,8},{16,12},{20,16},{24,20},{28,24},{32,28},{36,32}... | collective-permute-start | bytes 786440 | tf_op jit(solution)/shard_map/ppermute | solution.py:132
  9.0 16.0 %collective-permute-start.2 = (bf16[64,2048]{1,0:T(8,128)(2,1)}, bf16[64,2048]{1,0:T(8,128)(2,1)}, u32[]{:S(2)}, u32[]{:S(2)}) collective-permute-start(bf16[64,2048]{1,0:T(8,128)(2,1)} %get-tuple-element.23), channel_id=1, source_target_pairs={{0,4},{4,8},{8,12},{12,16},{16,20},{20,24},{24,28},{28,32},{32,36}... | collective-permute-start | bytes 786440 | tf_op jit(solution)/shard_map/ppermute | solution.py:131
  18.8 12.8 %copy-start.1 = (bf16[64,4096]{1,0:T(8,128)(2,1)}, bf16[64,4096]{1,0:T(8,128)(2,1)S(1)}, u32[]{:S(2)}) copy-start(bf16[64,4096]{1,0:T(8,128)(2,1)S(1)} %collective-permute-done.far_ref) | copy-start | bytes 1572868
  18.9 9.4 %collective-permute-start.5 = (bf16[64,2048]{1,0:T(8,128)(2,1)S(1)}, bf16[64,2048]{1,0:T(8,128)(2,1)S(1)}, u32[]{:S(2)}, u32[]{:S(2)}) collective-permute-start(bf16[64,2048]{1,0:T(8,128)(2,1)S(1)} %get-tuple-element.20), channel_id=1, source_target_pairs={{4,0},{8,4},{12,8},{16,12},{20,16},{24,20},{28,24},{32,28},{36,32}... | collective-permute-start | bytes 786440 | tf_op jit(solution)/shard_map/ppermute | solution.py:134
  20.2 9.2 %collective-permute-start.4 = (bf16[64,2048]{1,0:T(8,128)(2,1)S(1)}, bf16[64,2048]{1,0:T(8,128)(2,1)S(1)}, u32[]{:S(2)}, u32[]{:S(2)}) collective-permute-start(bf16[64,2048]{1,0:T(8,128)(2,1)S(1)} %get-tuple-element.21), channel_id=1, source_target_pairs={{0,4},{4,8},{8,12},{12,16},{16,20},{20,24},{24,28},{28,32},{32,36}... | collective-permute-start | bytes 786440 | tf_op jit(solution)/shard_map/ppermute | solution.py:133
  24.7 7.0 %copy-start.2 = (bf16[27,128,128]{2,1,0:T(8,128)(2,1)S(1)}, bf16[27,128,128]{2,1,0:T(8,128)(2,1)}, u32[]{:S(2)}) copy-start(bf16[27,128,128]{2,1,0:T(8,128)(2,1)} %param.4) | copy-start | bytes 2654212
  24.9 10.7 %collective-permute-start.1 = (bf16[2,64,4096]{2,1,0:T(8,128)(2,1)S(1)}, bf16[2,64,4096]{2,1,0:T(8,128)(2,1)}, u32[]{:S(2)}, u32[]{:S(2)}) collective-permute-start(bf16[2,64,4096]{2,1,0:T(8,128)(2,1)S(1)} %pad_maximum_fusion), channel_id=1, source_target_pairs={{0,1},{1,0},{2,3},{3,2},{4,5},{5,4},{6,7},{7,6},{8,9},{9,8},{10,11... | collective-permute-start | bytes 3145736 | tf_op jit(solution)/shard_map/ppermute | solution.py:135
  28.2 3.4 %copy-start.3 = (bf16[64,2048]{1,0:T(8,128)(2,1)}, bf16[64,2048]{1,0:T(8,128)(2,1)S(1)}, u32[]{:S(2)}) copy-start(bf16[64,2048]{1,0:T(8,128)(2,1)S(1)} %collective-permute-done.5.fhi_ref) | copy-start | bytes 786436
  29.4 2.3 %copy-start.4 = (bf16[64,2048]{1,0:T(8,128)(2,1)}, bf16[64,2048]{1,0:T(8,128)(2,1)S(1)}, u32[]{:S(2)}) copy-start(bf16[64,2048]{1,0:T(8,128)(2,1)S(1)} %collective-permute-done.4.flo_ref) | copy-start | bytes 786436
  31.6 3.9 %collective-permute-start.6 = (bf16[4,64,2048]{2,1,0:T(8,128)(2,1)}, bf16[4,64,2048]{2,1,0:T(8,128)(2,1)}, u32[]{:S(2)}, u32[]{:S(2)}) collective-permute-start(bf16[4,64,2048]{2,1,0:T(8,128)(2,1)} %pad_maximum_fusion.1), channel_id=1, source_target_pairs={{0,1},{1,0},{2,3},{3,2},{4,5},{5,4},{6,7},{7,6},{8,9},{9,8},{10,11... | collective-permute-start | bytes 3145736 | tf_op jit(solution)/shard_map/ppermute | solution.py:136

commit v11 on v7

--- a/solution.py
+++ b/solution.py
@@ -66,8 +66,8 @@
         right = jnp.where(last, zero, pltpu.roll(r[2 * loc : 3 * loc], span - 1, 1))
         return left + r[loc : 2 * loc] + right
 
-    acc_o = zero
-    acc_i = zero
+    acc_o = None
+    acc_i = None
     for tap_z in range(3):
         for tap_y in range(3):
             base = tap_z * plane + tap_y * ROW
@@ -81,18 +81,19 @@
                     wg_ref[3 * pair + tap_x] = w[:, tap_x * loc : (tap_x + 1) * loc]
                 continue
             sc = cs_ref[:, base : base + span]
-            acc_o = acc_o + shifted_sum(
-                jnp.dot(wf_ref[pair], sv, preferred_element_type=jnp.float32)
-            )
-            acc_i = acc_i + shifted_sum(
-                jnp.dot(wb_ref[pair], sc, preferred_element_type=jnp.float32)
-            )
+            r = jnp.dot(wf_ref[pair], sv, preferred_element_type=jnp.float32)
+            acc_o = r if acc_o is None else acc_o + r
+            r = jnp.dot(wb_ref[pair], sc, preferred_element_type=jnp.float32)
+            acc_i = r if acc_i is None else acc_i + r
     if grads:
         return
-    width = out_ref.shape[2]
+    acc_o = shifted_sum(acc_o)
+    acc_i = shifted_sum(acc_i)
+    rows, cols = out_ref.shape[2], out_ref.shape[3]
     for z in range(planes):
-        out_ref[z] = acc_o[:, z * plane : z * plane + width].astype(out_ref.dtype)
-        ing_ref[z] = acc_i[:, z * plane : z * plane + width].astype(ing_ref.dtype)
+        for acc, ref in ((acc_o, out_ref), (acc_i, ing_ref)):
+            part = acc[:, z * plane : z * plane + width].reshape(loc, rows, cols)
+            ref[:, z] = part.astype(ref.dtype)
 
 
 def fused(pieces, wf, wb, planes, width, grads):
@@ -104,19 +105,18 @@
         shapes = (jax.ShapeDtypeStruct((27, cin, loc), jnp.float32),)
     else:
         shapes = (
-            jax.ShapeDtypeStruct((planes, loc, width), jnp.bfloat16),
-            jax.ShapeDtypeStruct((planes, loc, width), jnp.bfloat16),
+            jax.ShapeDtypeStruct((loc, planes, width // ROW, ROW), jnp.bfloat16),
+            jax.ShapeDtypeStruct((loc, planes, width // ROW, ROW), jnp.bfloat16),
         )
 
     def kernel(*refs):
         ins = refs[:10]
         outs = refs[10:-2]
-        scratch = refs[-2:]
         if grads:
             outs = (None, None) + tuple(outs)
         else:
             outs = tuple(outs) + (None,)
-        fused_kernel(*ins, *outs, *scratch, grads=grads)
+        fused_kernel(*ins, *outs, *refs[-2:], grads=grads)
 
     return pl.pallas_call(
         kernel,
@@ -169,8 +169,8 @@
     wg = by_group(wg, order, in_local, 1)
     out, ing = fused(pieces, wf, wb, planes_local, width, False)
     shape = (out_local, planes_local, grid_rows, grid_cols)
-    out = jnp.transpose(out, (1, 0, 2)).reshape(shape)
-    ing = jnp.transpose(ing, (1, 0, 2)).reshape(shape)
+    out = out.reshape(shape)
+    ing = ing.reshape(shape)
     weight_grad = summed_on_arrival(wg.astype(jnp.bfloat16), "gz", 1) * jnp.float32(
         1.0 / math.sqrt(voxels)
     )

time: 82.3 us -> 77.4 us (0.940); the launches traced: 80.6 us -> 76.9 us
  local copies, waits for them, and re-layouts: 18.1 us -> 14.7 us
  Pallas kernels: 15.8 us -> 14 us
  waiting for transfers between devices: 18 us -> 19.6 us
    unnamed x26 -> x22, local copies, waits for them, and re-layouts: 11.3 us -> 7.87 us
    pallas_call x2, Pallas kernels: 15.8 us -> 14 us  [fused(): pl.pallas_call(kernel, out_shape=shapes, scratch_shapes=[pltpu.VMEM((cin,...]
    all_to_all x1, waiting for transfers between devices: 0.01 us -> 1.58 us  [summed_on_arrival(): lax.all_to_all(blocks, axis, split_axis=0, concat_axis=0, tiled=True)]
  transfers between devices with their start and end apart: 8 -> 8, of which waited for: 3 -> 4; matrix products, arithmetic and copies ran while one was open for 19% -> 16% of each run, Pallas kernels for 12% -> 10%
where the time goes in v11:
time: 77.4 us; the launch traced here: 76.9 us
  starting transfers between devices  20.8 us (27%)
  waiting for transfers between devices  19.6 us (25%)
  local copies, waits for them, and re-layouts  14.7 us (19%)
  Pallas kernels  14 us (18%)
  other arithmetic  6.99 us (9%)
  between operations  0.79 us (1%)
    pallas_call x2, Pallas kernels, fused(): pl.pallas_call(kernel, out_shape=shapes, scratch_shapes=[pltpu.VMEM((cin,...  14 us
    ppermute x1, waiting for transfers between devices, body(): got_far = lax.ppermute(both, far, swap)  11.1 us
    all_to_all x1, starting transfers between devices, summed_on_arrival(): lax.all_to_all(blocks, axis, split_axis=0, concat_axis=0, tiled=True)  8.74 us
    unnamed x22, local copies, waits for them, and re-layouts  7.87 us
    ppermute x1, waiting for transfers between devices, body(): far_high = lax.ppermute(got_far[:, :width], 'gz', down)  4.13 us
    ppermute x1, starting transfers between devices, body(): low = lax.ppermute(both[:, -width:], 'gz', up)  4.1 us
    ppermute x1, starting transfers between devices, body(): got_far = lax.ppermute(both, far, swap)  4.07 us
    ppermute x1, waiting for transfers between devices, body(): far_low = lax.ppermute(got_far[:, -width:], 'gz', up)  2.83 us
  transfers between devices with their start and end apart: 8, of which 4 were waited for; matrix products, arithmetic and copies ran while one was open for 16% of the time, Pallas kernels for 10%

profile of v11, /device:TPU:0, one launch (start us, length us, event | category | flops | bytes accessed | tf_op | source)
XLA Modules:
  0.0 76.9 jit_solution(1486615948531009438)
XLA Ops:
  0.6 1.0 %constant_dynamic-update-slice_fusion.1 = bf16[64,2,16,128]{3,2,1,0:T(8,128)(2,1)S(1)} fusion(bf16[32,2,16,128]{3,2,1,0:T(8,128)(2,1)} %param.3), kind=kLoop, calls=%fused_computation.13 | loop fusion | bytes 524288
  1.6 1.0 %constant_dynamic-update-slice_fusion = bf16[64,2,16,128]{3,2,1,0:T(8,128)(2,1)S(1)} fusion(bf16[64,2,16,128]{3,2,1,0:T(8,128)(2,1)S(1)} %constant_dynamic-update-slice_fusion.1, bf16[32,2,16,128]{3,2,1,0:T(8,128)(2,1)} %param.5), kind=kLoop, calls=%fused_computation.12 | loop fusion | bytes 524288 | tf_op jit(solution)/shard_map/concatenate | solution.py:144
  2.6 0.2 copy.56
  2.8 0.0 copy-start
  2.8 4.1 %collective-permute-start = (bf16[64,4096]{1,0:T(8,128)(2,1)S(1)}, bf16[64,4096]{1,0:T(8,128)(2,1)S(1)}, u32[]{:S(2)}, u32[]{:S(2)}) collective-permute-start(bf16[64,4096]{1,0:T(8,128)(2,1)S(1)} %bitcast.21), channel_id=1, source_target_pairs={{0,2},{2,0},{1,3},{3,1},{4,6},{6,4},{5,7},{7,5},{8,10},{10,8},{9,1... | collective-permute-start | bytes 1572872 | tf_op jit(solution)/shard_map/ppermute | solution.py:149
  6.9 0.8 %fusion.1 = (bf16[64,2048]{1,0:T(8,128)(2,1)}, bf16[64,2048]{1,0:T(8,128)(2,1)}) fusion(bf16[64,4096]{1,0:T(8,128)(2,1)S(1)} %bitcast.22), kind=kLoop, calls=%fused_computation.22 | loop fusion | bytes 1048576 | tf_op jit(solution)/shard_map/slice | solution.py:151
  7.7 4.1 %collective-permute-start.2 = (bf16[64,2048]{1,0:T(8,128)(2,1)}, bf16[64,2048]{1,0:T(8,128)(2,1)}, u32[]{:S(2)}, u32[]{:S(2)}) collective-permute-start(bf16[64,2048]{1,0:T(8,128)(2,1)} %get-tuple-element.21), channel_id=1, source_target_pairs={{0,4},{4,8},{8,12},{12,16},{16,20},{20,24},{24,28},{28,32},{32,36}... | collective-permute-start | bytes 786440 | tf_op jit(solution)/shard_map/ppermute | solution.py:150
  11.8 1.3 %collective-permute-start.3 = (bf16[64,2048]{1,0:T(8,128)(2,1)}, bf16[64,2048]{1,0:T(8,128)(2,1)}, u32[]{:S(2)}, u32[]{:S(2)}) collective-permute-start(bf16[64,2048]{1,0:T(8,128)(2,1)} %get-tuple-element.20), channel_id=1, source_target_pairs={{4,0},{8,4},{12,8},{16,12},{20,16},{24,20},{28,24},{32,28},{36,32}... | collective-permute-start | bytes 786440 | tf_op jit(solution)/shard_map/ppermute | solution.py:151
  13.1 0.2 stack_reshape.3
  13.3 11.1 %collective-permute-done.refs_1_ = bf16[64,4096]{1,0:T(8,128)(2,1)S(1)} collective-permute-done((bf16[64,4096]{1,0:T(8,128)(2,1)S(1)}, bf16[64,4096]{1,0:T(8,128)(2,1)S(1)}, u32[]{:S(2)}, u32[]{:S(2)}) %collective-permute-start) | collective-permute-done | bytes 524320 | tf_op jit(solution)/shard_map/ppermute | solution.py:149
  24.5 1.3 %collective-permute-start.4 = (bf16[64,2048]{1,0:T(8,128)(2,1)S(1)}, bf16[64,2048]{1,0:T(8,128)(2,1)S(1)}, u32[]{:S(2)}, u32[]{:S(2)}) collective-permute-start(bf16[64,2048]{1,0:T(8,128)(2,1)S(1)} %get-tuple-element.19), channel_id=1, source_target_pairs={{0,4},{4,8},{8,12},{12,16},{16,20},{20,24},{24,28},{28,32},{32,36}... | collective-permute-start | bytes 786440 | tf_op jit(solution)/shard_map/ppermute | solution.py:152
  25.8 1.3 %collective-permute-start.5 = (bf16[64,2048]{1,0:T(8,128)(2,1)S(1)}, bf16[64,2048]{1,0:T(8,128)(2,1)S(1)}, u32[]{:S(2)}, u32[]{:S(2)}) collective-permute-start(bf16[64,2048]{1,0:T(8,128)(2,1)S(1)} %get-tuple-element.18), channel_id=1, source_target_pairs={{4,0},{8,4},{12,8},{16,12},{20,16},{24,20},{28,24},{32,28},{36,32}... | collective-permute-start | bytes 786440 | tf_op jit(solution)/shard_map/ppermute | solution.py:153
  27.1 0.0 copy-start.4
  27.1 1.1 %pad_maximum_fusion = bf16[2,64,4096]{2,1,0:T(8,128)(2,1)} fusion(bf16[1,64,4096]{2,1,0:T(8,128)(2,1)S(1)} %bitcast.25, bf16[1,64,4096]{2,1,0:T(8,128)(2,1)S(1)} %stack_reshape.3), kind=kLoop, calls=%fused_computation.1 | loop fusion | flops 524288 | bytes 2097152 | tf_op jit(solution)/shard_map/stack | solution.py:154
  28.2 0.0 copy-done
  28.2 0.0 collective-permute-start.1
  28.2 0.0 collective-permute-done.2.refs_3_
  28.2 0.0 collective-permute-done.3.refs_4_
  28.2 2.8 %collective-permute-done.4.refs_5_ = bf16[64,2048]{1,0:T(8,128)(2,1)S(1)} collective-permute-done((bf16[64,2048]{1,0:T(8,128)(2,1)S(1)}, bf16[64,2048]{1,0:T(8,128)(2,1)S(1)}, u32[]{:S(2)}, u32[]{:S(2)}) %collective-permute-start.4) | collective-permute-done | bytes 262176 | tf_op jit(solution)/shard_map/ppermute | solution.py:152
  31.0 4.1 %collective-permute-done.5.refs_6_ = bf16[64,2048]{1,0:T(8,128)(2,1)S(1)} collective-permute-done((bf16[64,2048]{1,0:T(8,128)(2,1)S(1)}, bf16[64,2048]{1,0:T(8,128)(2,1)S(1)}, u32[]{:S(2)}, u32[]{:S(2)}) %collective-permute-start.5) | collective-permute-done | bytes 262176 | tf_op jit(solution)/shard_map/ppermute | solution.py:153
  35.2 0.0 copy-done.5
  35.2 0.7 copy-done.6
  35.9 2.1 %pad_maximum_fusion.1 = bf16[4,64,2048]{2,1,0:T(8,128)(2,1)} fusion(bf16[1,64,2048]{2,1,0:T(8,128)(2,1)S(1)} %bitcast.29, bf16[1,64,2048]{2,1,0:T(8,128)(2,1)S(1)} %bitcast.28, bf16[1,64,2048]{2,1,0:T(8,128)(2,1)} %bitcast.2, bf16[1,64,2048]{2,1,0:T(8,128)(2,1)} %bitcast.1), kind=kLoop, calls=%fused_computation.2 | loop fusion | flops 1572864 | bytes 2097152 | tf_op jit(solution)/shard_map/stack | solution.py:155
  38.0 0.0 copy-done.1
  38.0 0.0 collective-permute-start.6
  38.0 2.1 %constant_dynamic-slice_fusion.2 = (bf16[27,32,32]{2,1,0:T(8,128)(2,1)}, bf16[27,32,32]{2,1,0:T(8,128)(2,1)}, bf16[27,32,32]{2,1,0:T(8,128)(2,1)S(1)}, bf16[27,3...) fusion(bf16[27,128,128]{2,1,0:T(8,128)(2,1)S(1)} %copy-done.4, ...), kind=kLoop, calls=%fused_computation.16 | loop fusion | bytes 774160 | tf_op jit(solution)/shard_map/dynamic_slice | solution.py:133
  40.1 1.1 %copy.53 = bf16[27,32,32]{1,2,0:T(8,128)(2,1)S(1)} copy(bf16[27,32,32]{2,1,0:T(8,128)(2,1)} %get-tuple-element.15) | data formatting | bytes 110592
  41.2 1.1 %copy.52 = bf16[27,32,32]{1,2,0:T(8,128)(2,1)S(1)} copy(bf16[27,32,32]{2,1,0:T(8,128)(2,1)} %get-tuple-element.12) | data formatting | bytes 110592
  42.3 0.2 copy.51
  42.5 0.2 copy.50
  42.6 1.5 %pad_maximum_fusion.4 = bf16[27,32,128]{2,1,0:T(8,128)(2,1)S(1)} fusion(bf16[27,32,32]{2,1,0:T(8,128)(2,1)} %get-tuple-element.16, bf16[27,32,32]{2,1,0:T(8,128)(2,1)} %get-tuple-element.17, bf16[27,32,32]{2,1,0:T(8,128)(2,1)} %get-tuple-element.11, bf16[27,32,32]{2,1,0:T(8,128)(2,1)S(1)} %get-tuple-element.14), kind=kLoop, calls=%fused_computation.10 | loop fusion | flops 884736 | bytes 442368 | tf_op jit(solution)/shard_map/concatenate | solution.py:132
  44.1 0.7 rev.3
  44.8 1.0 %pad_maximum_fusion.3 = bf16[27,128,32]{1,2,0:T(8,128)(2,1)} fusion(bf16[27,32,32]{1,2,0:T(8,128)(2,1)S(1)} %copy.53, bf16[27,32,32]{1,2,0:T(8,128)(2,1)S(1)} %copy.52, bf16[27,32,32]{1,2,0:T(8,128)(2,1)S(1)} %copy.51, bf16[27,32,32]{1,2,0:T(8,128)(2,1)S(1)} %copy.50), kind=kLoop, calls=%fused_computation.9 | loop fusion | flops 884736 | bytes 442368 | tf_op jit(solution)/shard_map/concatenate | solution.py:132
  45.8 0.0 collective-permute-done.1.refs_2_
  45.8 0.0 collective-permute-done.6.refs_7_
  45.8 1.0 %copy-done.2 = bf16[2,64,4096]{2,1,0:T(8,128)(2,1)} copy-done((bf16[2,64,4096]{2,1,0:T(8,128)(2,1)}, bf16[2,64,4096]{2,1,0:T(8,128)(2,1)S(1)}, u32[]{:S(2)}) %copy-start.2) | copy-done | bytes 1048600
  46.8 0.3 copy-done.3
  47.1 6.5 %shard_map.59 = f32[27,128,32]{2,1,0:T(8,128)} custom-call(bf16[64,4096]{1,0:T(8,128)(2,1)} %bitcast.23, bf16[64,4096]{1,0:T(8,128)(2,1)} %copy-done.1, bf16[2,64,4096]{2,1,0:T(8,128)(2,1)} %copy-done.2, bf16[64,2048]{1,0:T(8,128)(2,1)} %collective-permute-done.2.refs_3_, bf16[64,2048]{1,0:T(8,128)(2,1)} %collective-permute-done.3.refs_4_, ...), custom_call_target="tpu_custom_call" | custom-call | tf_op jit(solution)/shard_map/pallas_call | solution.py:121
  53.6 1.6 %dynamic-slice_convert_fusion.3 = (bf16[27,32,32]{2,1,0:T(8,128)(2,1)S(1)}, bf16[27,32,32]{2,1,0:T(8,128)(2,1)S(1)}, bf16[27,32,32]{2,1,0:T(8,128)(2,1)S(1)}, bf16[27,32,32]{2,1,0:T(8,128)(2,1)S(1)}) fusion(f32[27,128,32]{2,1,0:T(8,128)} %shard_map.59, s32[]{:T(128)S(6)} %select_n.30, s32[]{:T(128)S(6)} %select_n.36, s32[]{:T(128)S(6)} %select_n.34, ...), kind=kLoop, calls=%fused_computation.8 | loop fusion | bytes 442384 | tf_op jit(solution)/shard_map/convert
  55.2 0.2 pad_maximum_fusion.2
  55.4 0.3 copy.49
  55.7 1.4 %reshape.25 = bf16[32,2,1728]{2,1,0:T(2,128)(2,1)} reshape(bf16[32,27,4,32]{3,2,1,0:T(4,128)(2,1)S(1)} %copy.49) | data formatting | bytes 442368
  57.2 8.7 %all-to-all-start = ((bf16[32,2,1728]{2,1,0:T(2,128)(2,1)}), bf16[32,2,1728]{2,1,0:T(2,128)(2,1)S(1)}, u32[]{:S(2)}, u32[]{:S(2)}) async-start(bf16[32,2,1728]{2,1,0:T(2,128)(2,1)} %reshape.25), calls=%async_computation | async-start | bytes 458752 | tf_op jit(solution)/shard_map/all_to_all | solution.py:19
  65.9 7.5 %shard_map.58 = (bf16[32,2,16,128]{3,2,1,0:T(8,128)(2,1)}, bf16[32,2,16,128]{3,2,1,0:T(8,128)(2,1)}) custom-call(bf16[64,4096]{1,0:T(8,128)(2,1)} %bitcast.24, bf16[64,4096]{1,0:T(8,128)(2,1)} %copy-done.1, bf16[2,64,4096]{2,1,0:T(8,128)(2,1)} %copy-done.2, bf16[64,2048]{1,0:T(8,128)(2,1)} %collective-permute-done.2.refs_3_, ...), custom_call_target="tpu_custom_call" | custom-call | tf_op jit(solution)/shard_map/pallas_call | solution.py:121
  73.4 1.6 %all-to-all-done = bf16[32,2,1728]{2,1,0:T(2,128)(2,1)S(1)} async-done(((bf16[32,2,1728]{2,1,0:T(2,128)(2,1)}), bf16[32,2,1728]{2,1,0:T(2,128)(2,1)S(1)}, u32[]{:S(2)}, u32[]{:S(2)}) %all-to-all-start) | async-done | bytes 221216 | tf_op jit(solution)/shard_map/all_to_all | solution.py:19
  75.0 0.8 reshape.26
  75.8 0.5 convert_reduce_fusion
  76.3 0.6 broadcast_multiply_fusion
  (7 shorter events, 0.1 us)
Async XLA Ops:
  2.8 25.4 %copy-start = (bf16[8,8,32,128]{3,1,2,0:T(8,128)(2,1)}, bf16[8,8,32,128]{3,1,2,0:T(8,128)(2,1)S(1)}, u32[]{:S(2)}) copy-start(bf16[8,8,32,128]{3,1,2,0:T(8,128)(2,1)S(1)} %copy.56) | copy-start | bytes 1572868
  2.8 21.6 %collective-permute-start = (bf16[64,4096]{1,0:T(8,128)(2,1)S(1)}, bf16[64,4096]{1,0:T(8,128)(2,1)S(1)}, u32[]{:S(2)}, u32[]{:S(2)}) collective-permute-start(bf16[64,4096]{1,0:T(8,128)(2,1)S(1)} %bitcast.21), channel_id=1, source_target_pairs={{0,2},{2,0},{1,3},{3,1},{4,6},{6,4},{5,7},{7,5},{8,10},{10,8},{9,1... | collective-permute-start | bytes 1572872 | tf_op jit(solution)/shard_map/ppermute | solution.py:149
  7.7 20.5 %collective-permute-start.2 = (bf16[64,2048]{1,0:T(8,128)(2,1)}, bf16[64,2048]{1,0:T(8,128)(2,1)}, u32[]{:S(2)}, u32[]{:S(2)}) collective-permute-start(bf16[64,2048]{1,0:T(8,128)(2,1)} %get-tuple-element.21), channel_id=1, source_target_pairs={{0,4},{4,8},{8,12},{12,16},{16,20},{20,24},{24,28},{28,32},{32,36}... | collective-permute-start | bytes 786440 | tf_op jit(solution)/shard_map/ppermute | solution.py:150
  11.8 16.4 %collective-permute-start.3 = (bf16[64,2048]{1,0:T(8,128)(2,1)}, bf16[64,2048]{1,0:T(8,128)(2,1)}, u32[]{:S(2)}, u32[]{:S(2)}) collective-permute-start(bf16[64,2048]{1,0:T(8,128)(2,1)} %get-tuple-element.20), channel_id=1, source_target_pairs={{4,0},{8,4},{12,8},{16,12},{20,16},{24,20},{28,24},{32,28},{36,32}... | collective-permute-start | bytes 786440 | tf_op jit(solution)/shard_map/ppermute | solution.py:151
  24.4 13.6 %copy-start.1 = (bf16[64,4096]{1,0:T(8,128)(2,1)}, bf16[64,4096]{1,0:T(8,128)(2,1)S(1)}, u32[]{:S(2)}) copy-start(bf16[64,4096]{1,0:T(8,128)(2,1)S(1)} %collective-permute-done.refs_1_) | copy-start | bytes 1572868
  24.5 6.5 %collective-permute-start.4 = (bf16[64,2048]{1,0:T(8,128)(2,1)S(1)}, bf16[64,2048]{1,0:T(8,128)(2,1)S(1)}, u32[]{:S(2)}, u32[]{:S(2)}) collective-permute-start(bf16[64,2048]{1,0:T(8,128)(2,1)S(1)} %get-tuple-element.19), channel_id=1, source_target_pairs={{0,4},{4,8},{8,12},{12,16},{16,20},{20,24},{24,28},{28,32},{32,36}... | collective-permute-start | bytes 786440 | tf_op jit(solution)/shard_map/ppermute | solution.py:152
  25.8 9.4 %collective-permute-start.5 = (bf16[64,2048]{1,0:T(8,128)(2,1)S(1)}, bf16[64,2048]{1,0:T(8,128)(2,1)S(1)}, u32[]{:S(2)}, u32[]{:S(2)}) collective-permute-start(bf16[64,2048]{1,0:T(8,128)(2,1)S(1)} %get-tuple-element.18), channel_id=1, source_target_pairs={{4,0},{8,4},{12,8},{16,12},{20,16},{24,20},{28,24},{32,28},{36,32}... | collective-permute-start | bytes 786440 | tf_op jit(solution)/shard_map/ppermute | solution.py:153
  27.1 10.9 %copy-start.4 = (bf16[27,128,128]{2,1,0:T(8,128)(2,1)S(1)}, bf16[27,128,128]{2,1,0:T(8,128)(2,1)}, u32[]{:S(2)}) copy-start(bf16[27,128,128]{2,1,0:T(8,128)(2,1)} %param.4) | copy-start | bytes 2654212
  28.2 17.6 %collective-permute-start.1 = (bf16[2,64,4096]{2,1,0:T(8,128)(2,1)}, bf16[2,64,4096]{2,1,0:T(8,128)(2,1)S(1)}, u32[]{:S(2)}, u32[]{:S(2)}) collective-permute-start(bf16[2,64,4096]{2,1,0:T(8,128)(2,1)} %pad_maximum_fusion), channel_id=1, source_target_pairs={{0,1},{1,0},{2,3},{3,2},{4,5},{5,4},{6,7},{7,6},{8,9},{9,8},{10,11... | collective-permute-start | bytes 3145736 | tf_op jit(solution)/shard_map/ppermute | solution.py:154
  31.0 4.1 %copy-start.5 = (bf16[64,2048]{1,0:T(8,128)(2,1)}, bf16[64,2048]{1,0:T(8,128)(2,1)S(1)}, u32[]{:S(2)}) copy-start(bf16[64,2048]{1,0:T(8,128)(2,1)S(1)} %collective-permute-done.4.refs_5_) | copy-start | bytes 786436
  35.2 0.7 copy-start.6
  38.0 7.8 %collective-permute-start.6 = (bf16[4,64,2048]{2,1,0:T(8,128)(2,1)}, bf16[4,64,2048]{2,1,0:T(8,128)(2,1)S(1)}, u32[]{:S(2)}, u32[]{:S(2)}) collective-permute-start(bf16[4,64,2048]{2,1,0:T(8,128)(2,1)} %pad_maximum_fusion.1), channel_id=1, source_target_pairs={{0,1},{1,0},{2,3},{3,2},{4,5},{5,4},{6,7},{7,6},{8,9},{9,8},{10,11... | collective-permute-start | bytes 3145736 | tf_op jit(solution)/shard_map/ppermute | solution.py:155
  45.8 1.0 %copy-start.2 = (bf16[2,64,4096]{2,1,0:T(8,128)(2,1)}, bf16[2,64,4096]{2,1,0:T(8,128)(2,1)S(1)}, u32[]{:S(2)}) copy-start(bf16[2,64,4096]{2,1,0:T(8,128)(2,1)S(1)} %collective-permute-done.1.refs_2_) | copy-start | bytes 3145732
  45.8 1.3 %copy-start.3 = (bf16[4,64,2048]{2,1,0:T(8,128)(2,1)}, bf16[4,64,2048]{2,1,0:T(8,128)(2,1)S(1)}, u32[]{:S(2)}) copy-start(bf16[4,64,2048]{2,1,0:T(8,128)(2,1)S(1)} %collective-permute-done.6.refs_7_) | copy-start | bytes 3145732
  57.2 17.9 %all-to-all-start = ((bf16[32,2,1728]{2,1,0:T(2,128)(2,1)}), bf16[32,2,1728]{2,1,0:T(2,128)(2,1)S(1)}, u32[]{:S(2)}, u32[]{:S(2)}) async-start(bf16[32,2,1728]{2,1,0:T(2,128)(2,1)} %reshape.25), calls=%async_computation | async-start | bytes 458752 | tf_op jit(solution)/shard_map/all_to_all | solution.py:19

commit v12 on v11

--- a/solution.py
+++ b/solution.py
@@ -109,10 +109,13 @@
             jax.ShapeDtypeStruct((loc, planes, width // ROW, ROW), jnp.bfloat16),
         )
 
+    count = len(pieces) if grads else len(pieces) + 2
+
     def kernel(*refs):
-        ins = refs[:10]
-        outs = refs[10:-2]
+        ins = refs[:count]
+        outs = refs[count:-2]
         if grads:
+            ins = tuple(ins) + (None, None)
             outs = (None, None) + tuple(outs)
         else:
             outs = tuple(outs) + (None,)
@@ -125,7 +128,7 @@
             pltpu.VMEM((cin, flat), jnp.bfloat16),
             pltpu.VMEM((cin, flat), jnp.bfloat16),
         ],
-    )(*pieces, wf, wb)
+    )(*(pieces if grads else pieces + (wf, wb)))
 
 
 def by_group(array, order, size, dim):

time: 77.4 us -> 76.3 us (0.986)
  the two profiles are of different devices: /device:TPU:0 before, /device:TPU:1 now
where the time goes in v12:
time: 76.3 us; the launch traced here: 75.9 us
  starting transfers between devices  24 us (31%)
  waiting for transfers between devices  15.9 us (21%)
  local copies, waits for them, and re-layouts  15.3 us (20%)
  Pallas kernels  13.9 us (18%)
  other arithmetic  5.84 us (8%)
  between operations  0.84 us (1%)
    pallas_call x2, Pallas kernels, fused(): pl.pallas_call(kernel, out_shape=shapes, scratch_shapes=[pltpu.VMEM((cin,...  13.9 us
    ppermute x1, waiting for transfers between devices, body(): got_far = lax.ppermute(both, far, swap)  11.1 us
    unnamed x28, local copies, waits for them, and re-layouts  8.54 us
    all_to_all x1, starting transfers between devices, summed_on_arrival(): lax.all_to_all(blocks, axis, split_axis=0, concat_axis=0, tiled=True)  8.46 us
    ppermute x1, starting transfers between devices, body(): got_far = lax.ppermute(both, far, swap)  4.49 us
    ppermute x1, waiting for transfers between devices, body(): far_high = lax.ppermute(got_far[:, :width], 'gz', down)  3.85 us
    ppermute x1, starting transfers between devices, body(): low = lax.ppermute(both[:, -width:], 'gz', up)  3.82 us
    another operation x1, other arithmetic, body(): halos = lax.ppermute(jnp.stack([low, high, far_low, far_high]), near, swap)  2.14 us
  transfers between devices with their start and end apart: 8, of which 3 were waited for; matrix products, arithmetic and copies ran while one was open for 14% of the time, Pallas kernels for 10%

profile of v12, /device:TPU:1, one launch (start us, length us, event | category | flops | bytes accessed | tf_op | source)
XLA Modules:
  0.0 75.9 jit_solution(8435814328912852457)
XLA Ops:
  0.6 1.0 %constant_dynamic-update-slice_fusion.1 = bf16[64,2,16,128]{3,2,1,0:T(8,128)(2,1)S(1)} fusion(bf16[32,2,16,128]{3,2,1,0:T(8,128)(2,1)} %param.3), kind=kLoop, calls=%fused_computation.13 | loop fusion | bytes 524288
  1.6 1.0 %constant_dynamic-update-slice_fusion = bf16[64,2,16,128]{3,2,1,0:T(8,128)(2,1)S(1)} fusion(bf16[64,2,16,128]{3,2,1,0:T(8,128)(2,1)S(1)} %constant_dynamic-update-slice_fusion.1, bf16[32,2,16,128]{3,2,1,0:T(8,128)(2,1)} %param.5), kind=kLoop, calls=%fused_computation.12 | loop fusion | bytes 524288 | tf_op jit(solution)/shard_map/concatenate | solution.py:147
  2.6 0.2 copy.56
  2.8 0.0 copy-start
  2.8 4.5 %collective-permute-start = (bf16[64,4096]{1,0:T(8,128)(2,1)S(1)}, bf16[64,4096]{1,0:T(8,128)(2,1)S(1)}, u32[]{:S(2)}, u32[]{:S(2)}) collective-permute-start(bf16[64,4096]{1,0:T(8,128)(2,1)S(1)} %bitcast.21), channel_id=1, source_target_pairs={{0,2},{2,0},{1,3},{3,1},{4,6},{6,4},{5,7},{7,5},{8,10},{10,8},{9,1... | collective-permute-start | bytes 1572872 | tf_op jit(solution)/shard_map/ppermute | solution.py:152
  7.3 0.8 %fusion.1 = (bf16[64,2048]{1,0:T(8,128)(2,1)}, bf16[64,2048]{1,0:T(8,128)(2,1)}) fusion(bf16[64,4096]{1,0:T(8,128)(2,1)S(1)} %bitcast.22), kind=kLoop, calls=%fused_computation.22 | loop fusion | bytes 1048576 | tf_op jit(solution)/shard_map/slice | solution.py:154
  8.1 3.8 %collective-permute-start.2 = (bf16[64,2048]{1,0:T(8,128)(2,1)}, bf16[64,2048]{1,0:T(8,128)(2,1)}, u32[]{:S(2)}, u32[]{:S(2)}) collective-permute-start(bf16[64,2048]{1,0:T(8,128)(2,1)} %get-tuple-element.21), channel_id=1, source_target_pairs={{0,4},{4,8},{8,12},{12,16},{16,20},{20,24},{24,28},{28,32},{32,36}... | collective-permute-start | bytes 786440 | tf_op jit(solution)/shard_map/ppermute | solution.py:153
  12.0 1.3 %collective-permute-start.3 = (bf16[64,2048]{1,0:T(8,128)(2,1)}, bf16[64,2048]{1,0:T(8,128)(2,1)}, u32[]{:S(2)}, u32[]{:S(2)}) collective-permute-start(bf16[64,2048]{1,0:T(8,128)(2,1)} %get-tuple-element.20), channel_id=1, source_target_pairs={{4,0},{8,4},{12,8},{16,12},{20,16},{24,20},{28,24},{32,28},{36,32}... | collective-permute-start | bytes 786440 | tf_op jit(solution)/shard_map/ppermute | solution.py:154
  13.2 0.2 stack_reshape.3
  13.5 11.1 %collective-permute-done.refs_1_ = bf16[64,4096]{1,0:T(8,128)(2,1)S(1)} collective-permute-done((bf16[64,4096]{1,0:T(8,128)(2,1)S(1)}, bf16[64,4096]{1,0:T(8,128)(2,1)S(1)}, u32[]{:S(2)}, u32[]{:S(2)}) %collective-permute-start) | collective-permute-done | bytes 524320 | tf_op jit(solution)/shard_map/ppermute | solution.py:152
  24.6 1.3 %collective-permute-start.4 = (bf16[64,2048]{1,0:T(8,128)(2,1)S(1)}, bf16[64,2048]{1,0:T(8,128)(2,1)S(1)}, u32[]{:S(2)}, u32[]{:S(2)}) collective-permute-start(bf16[64,2048]{1,0:T(8,128)(2,1)S(1)} %get-tuple-element.19), channel_id=1, source_target_pairs={{0,4},{4,8},{8,12},{12,16},{16,20},{20,24},{24,28},{28,32},{32,36}... | collective-permute-start | bytes 786440 | tf_op jit(solution)/shard_map/ppermute | solution.py:155
  25.9 1.3 %collective-permute-start.5 = (bf16[64,2048]{1,0:T(8,128)(2,1)S(1)}, bf16[64,2048]{1,0:T(8,128)(2,1)S(1)}, u32[]{:S(2)}, u32[]{:S(2)}) collective-permute-start(bf16[64,2048]{1,0:T(8,128)(2,1)S(1)} %get-tuple-element.18), channel_id=1, source_target_pairs={{4,0},{8,4},{12,8},{16,12},{20,16},{24,20},{28,24},{32,28},{36,32}... | collective-permute-start | bytes 786440 | tf_op jit(solution)/shard_map/ppermute | solution.py:156
  27.2 0.0 copy-start.4
  27.2 1.1 %pad_maximum_fusion = bf16[2,64,4096]{2,1,0:T(8,128)(2,1)} fusion(bf16[1,64,4096]{2,1,0:T(8,128)(2,1)S(1)} %bitcast.25, bf16[1,64,4096]{2,1,0:T(8,128)(2,1)S(1)} %stack_reshape.3), kind=kLoop, calls=%fused_computation.1 | loop fusion | flops 524288 | bytes 2097152 | tf_op jit(solution)/shard_map/stack | solution.py:157
  28.3 0.0 copy-done
  28.3 1.3 %collective-permute-start.1 = (bf16[2,64,4096]{2,1,0:T(8,128)(2,1)}, bf16[2,64,4096]{2,1,0:T(8,128)(2,1)S(1)}, u32[]{:S(2)}, u32[]{:S(2)}) collective-permute-start(bf16[2,64,4096]{2,1,0:T(8,128)(2,1)} %pad_maximum_fusion), channel_id=1, source_target_pairs={{0,1},{1,0},{2,3},{3,2},{4,5},{5,4},{6,7},{7,6},{8,9},{9,8},{10,11... | collective-permute-start | bytes 3145736 | tf_op jit(solution)/shard_map/ppermute | solution.py:157
  29.6 0.0 collective-permute-done.2.refs_3_
  29.6 0.0 collective-permute-done.3.refs_4_
  29.6 1.0 %collective-permute-done.4.refs_5_ = bf16[64,2048]{1,0:T(8,128)(2,1)S(1)} collective-permute-done((bf16[64,2048]{1,0:T(8,128)(2,1)S(1)}, bf16[64,2048]{1,0:T(8,128)(2,1)S(1)}, u32[]{:S(2)}, u32[]{:S(2)}) %collective-permute-start.4) | collective-permute-done | bytes 262176 | tf_op jit(solution)/shard_map/ppermute | solution.py:155
  30.6 3.8 %collective-permute-done.5.refs_6_ = bf16[64,2048]{1,0:T(8,128)(2,1)S(1)} collective-permute-done((bf16[64,2048]{1,0:T(8,128)(2,1)S(1)}, bf16[64,2048]{1,0:T(8,128)(2,1)S(1)}, u32[]{:S(2)}, u32[]{:S(2)}) %collective-permute-start.5) | collective-permute-done | bytes 262176 | tf_op jit(solution)/shard_map/ppermute | solution.py:156
  34.4 0.7 copy-done.6
  35.1 2.1 %pad_maximum_fusion.1 = bf16[4,64,2048]{2,1,0:T(8,128)(2,1)} fusion(bf16[1,64,2048]{2,1,0:T(8,128)(2,1)S(1)} %bitcast.29, bf16[1,64,2048]{2,1,0:T(8,128)(2,1)S(1)} %bitcast.28, bf16[1,64,2048]{2,1,0:T(8,128)(2,1)} %bitcast.2, bf16[1,64,2048]{2,1,0:T(8,128)(2,1)} %bitcast.1), kind=kLoop, calls=%fused_computation.2 | loop fusion | flops 1572864 | bytes 2097152 | tf_op jit(solution)/shard_map/stack | solution.py:158
  37.3 2.1 %collective-permute-start.6 = (bf16[4,64,2048]{2,1,0:T(8,128)(2,1)}, bf16[4,64,2048]{2,1,0:T(8,128)(2,1)S(1)}, u32[]{:S(2)}, u32[]{:S(2)}) collective-permute-start(bf16[4,64,2048]{2,1,0:T(8,128)(2,1)} %pad_maximum_fusion.1), channel_id=1, source_target_pairs={{0,1},{1,0},{2,3},{3,2},{4,5},{5,4},{6,7},{7,6},{8,9},{9,8},{10,11... | collective-permute-start | bytes 3145736 | tf_op jit(solution)/shard_map/ppermute | solution.py:158
  39.4 2.1 %constant_dynamic-slice_fusion.2 = (bf16[27,32,32]{2,1,0:T(8,128)(2,1)}, bf16[27,32,32]{2,1,0:T(8,128)(2,1)}, bf16[27,32,32]{2,1,0:T(8,128)(2,1)S(1)}, bf16[27,3...) fusion(bf16[27,128,128]{2,1,0:T(8,128)(2,1)S(1)} %copy-done.4, ...), kind=kLoop, calls=%fused_computation.16 | loop fusion | bytes 774160 | tf_op jit(solution)/shard_map/dynamic_slice | solution.py:136
  41.5 1.1 %copy.53 = bf16[27,32,32]{1,2,0:T(8,128)(2,1)S(1)} copy(bf16[27,32,32]{2,1,0:T(8,128)(2,1)} %get-tuple-element.15) | data formatting | bytes 110592
  42.6 1.1 %copy.52 = bf16[27,32,32]{1,2,0:T(8,128)(2,1)S(1)} copy(bf16[27,32,32]{2,1,0:T(8,128)(2,1)} %get-tuple-element.12) | data formatting | bytes 110592
  43.7 0.2 copy.51
  43.8 0.2 copy.50
  44.0 0.0 collective-permute-done.1.refs_2_
  44.0 0.0 copy-start.2
  44.0 0.0 collective-permute-done.6.refs_7_
  44.0 1.0 %copy-done.2 = bf16[2,64,4096]{2,1,0:T(8,128)(2,1)} copy-done((bf16[2,64,4096]{2,1,0:T(8,128)(2,1)}, bf16[2,64,4096]{2,1,0:T(8,128)(2,1)S(1)}, u32[]{:S(2)}) %copy-start.2) | copy-done | bytes 1048600
  45.0 1.0 %copy-done.3 = bf16[4,64,2048]{2,1,0:T(8,128)(2,1)} copy-done((bf16[4,64,2048]{2,1,0:T(8,128)(2,1)}, bf16[4,64,2048]{2,1,0:T(8,128)(2,1)S(1)}, u32[]{:S(2)}) %copy-start.3) | copy-done | bytes 1048600
  46.0 6.4 %shard_map.59 = f32[27,128,32]{2,1,0:T(8,128)} custom-call(bf16[64,4096]{1,0:T(8,128)(2,1)} %bitcast.23, bf16[64,4096]{1,0:T(8,128)(2,1)} %copy-done.1, bf16[2,64,4096]{2,1,0:T(8,128)(2,1)} %copy-done.2, bf16[64,2048]{1,0:T(8,128)(2,1)} %collective-permute-done.2.refs_3_, bf16[64,2048]{1,0:T(8,128)(2,1)} %collective-permute-done.3.refs_4_, ...), custom_call_target="tpu_custom_call" | custom-call | tf_op jit(solution)/shard_map/pallas_call | solution.py:124
  52.4 1.6 %dynamic-slice_convert_fusion.3 = (bf16[27,32,32]{2,1,0:T(8,128)(2,1)S(1)}, bf16[27,32,32]{2,1,0:T(8,128)(2,1)S(1)}, bf16[27,32,32]{2,1,0:T(8,128)(2,1)S(1)}, bf16[27,32,32]{2,1,0:T(8,128)(2,1)S(1)}) fusion(f32[27,128,32]{2,1,0:T(8,128)} %shard_map.59, s32[]{:T(128)S(6)} %select_n.30, s32[]{:T(128)S(6)} %select_n.36, s32[]{:T(128)S(6)} %select_n.34, ...), kind=kLoop, calls=%fused_computation.8 | loop fusion | bytes 442384 | tf_op jit(solution)/shard_map/convert
  54.0 0.2 pad_maximum_fusion.2
  54.2 0.0 copy-start.7
  54.2 0.3 copy.49
  54.6 1.4 %reshape.25 = bf16[32,2,1728]{2,1,0:T(2,128)(2,1)} reshape(bf16[32,27,4,32]{3,2,1,0:T(4,128)(2,1)S(1)} %copy.49) | data formatting | bytes 442368
  56.0 8.5 %all-to-all-start = ((bf16[32,2,1728]{2,1,0:T(2,128)(2,1)}), bf16[32,2,1728]{2,1,0:T(2,128)(2,1)S(1)}, u32[]{:S(2)}, u32[]{:S(2)}) async-start(bf16[32,2,1728]{2,1,0:T(2,128)(2,1)} %reshape.25), calls=%async_computation | async-start | bytes 458752 | tf_op jit(solution)/shard_map/all_to_all | solution.py:19
  64.5 0.3 pad_maximum_fusion.4
  64.8 0.7 rev.3
  65.5 1.0 %pad_maximum_fusion.3 = bf16[27,128,32]{1,2,0:T(8,128)(2,1)} fusion(bf16[27,32,32]{1,2,0:T(8,128)(2,1)S(1)} %copy.53, bf16[27,32,32]{1,2,0:T(8,128)(2,1)S(1)} %copy.52, bf16[27,32,32]{1,2,0:T(8,128)(2,1)S(1)} %copy.51, bf16[27,32,32]{1,2,0:T(8,128)(2,1)S(1)} %copy.50), kind=kLoop, calls=%fused_computation.9 | loop fusion | flops 884736 | bytes 442368 | tf_op jit(solution)/shard_map/concatenate | solution.py:135
  66.5 7.5 %shard_map.58 = (bf16[32,2,16,128]{3,2,1,0:T(8,128)(2,1)}, bf16[32,2,16,128]{3,2,1,0:T(8,128)(2,1)}) custom-call(bf16[64,4096]{1,0:T(8,128)(2,1)} %bitcast.24, bf16[64,4096]{1,0:T(8,128)(2,1)} %copy-done.1, bf16[2,64,4096]{2,1,0:T(8,128)(2,1)} %copy-done.2, bf16[64,2048]{1,0:T(8,128)(2,1)} %collective-permute-done.2.refs_3_, ...), custom_call_target="tpu_custom_call" | custom-call | tf_op jit(solution)/shard_map/pallas_call | solution.py:124
  74.0 0.0 all-to-all-done
  74.0 0.8 reshape.26
  74.8 0.5 convert_reduce_fusion
  75.2 0.6 broadcast_multiply_fusion
  (13 shorter events, 0.1 us)
Async XLA Ops:
  2.8 25.5 %copy-start = (bf16[8,8,32,128]{3,1,2,0:T(8,128)(2,1)}, bf16[8,8,32,128]{3,1,2,0:T(8,128)(2,1)S(1)}, u32[]{:S(2)}) copy-start(bf16[8,8,32,128]{3,1,2,0:T(8,128)(2,1)S(1)} %copy.56) | copy-start | bytes 1572868
  2.8 21.7 %collective-permute-start = (bf16[64,4096]{1,0:T(8,128)(2,1)S(1)}, bf16[64,4096]{1,0:T(8,128)(2,1)S(1)}, u32[]{:S(2)}, u32[]{:S(2)}) collective-permute-start(bf16[64,4096]{1,0:T(8,128)(2,1)S(1)} %bitcast.21), channel_id=1, source_target_pairs={{0,2},{2,0},{1,3},{3,1},{4,6},{6,4},{5,7},{7,5},{8,10},{10,8},{9,1... | collective-permute-start | bytes 1572872 | tf_op jit(solution)/shard_map/ppermute | solution.py:152
  8.1 21.4 %collective-permute-start.2 = (bf16[64,2048]{1,0:T(8,128)(2,1)}, bf16[64,2048]{1,0:T(8,128)(2,1)}, u32[]{:S(2)}, u32[]{:S(2)}) collective-permute-start(bf16[64,2048]{1,0:T(8,128)(2,1)} %get-tuple-element.21), channel_id=1, source_target_pairs={{0,4},{4,8},{8,12},{12,16},{16,20},{20,24},{24,28},{28,32},{32,36}... | collective-permute-start | bytes 786440 | tf_op jit(solution)/shard_map/ppermute | solution.py:153
  12.0 17.6 %collective-permute-start.3 = (bf16[64,2048]{1,0:T(8,128)(2,1)}, bf16[64,2048]{1,0:T(8,128)(2,1)}, u32[]{:S(2)}, u32[]{:S(2)}) collective-permute-start(bf16[64,2048]{1,0:T(8,128)(2,1)} %get-tuple-element.20), channel_id=1, source_target_pairs={{4,0},{8,4},{12,8},{16,12},{20,16},{24,20},{28,24},{32,28},{36,32}... | collective-permute-start | bytes 786440 | tf_op jit(solution)/shard_map/ppermute | solution.py:154
  24.6 12.7 %copy-start.1 = (bf16[64,4096]{1,0:T(8,128)(2,1)}, bf16[64,4096]{1,0:T(8,128)(2,1)S(1)}, u32[]{:S(2)}) copy-start(bf16[64,4096]{1,0:T(8,128)(2,1)S(1)} %collective-permute-done.refs_1_) | copy-start | bytes 1572868
  24.6 6.0 %collective-permute-start.4 = (bf16[64,2048]{1,0:T(8,128)(2,1)S(1)}, bf16[64,2048]{1,0:T(8,128)(2,1)S(1)}, u32[]{:S(2)}, u32[]{:S(2)}) collective-permute-start(bf16[64,2048]{1,0:T(8,128)(2,1)S(1)} %get-tuple-element.19), channel_id=1, source_target_pairs={{0,4},{4,8},{8,12},{12,16},{16,20},{20,24},{24,28},{28,32},{32,36}... | collective-permute-start | bytes 786440 | tf_op jit(solution)/shard_map/ppermute | solution.py:155
  25.9 8.5 %collective-permute-start.5 = (bf16[64,2048]{1,0:T(8,128)(2,1)S(1)}, bf16[64,2048]{1,0:T(8,128)(2,1)S(1)}, u32[]{:S(2)}, u32[]{:S(2)}) collective-permute-start(bf16[64,2048]{1,0:T(8,128)(2,1)S(1)} %get-tuple-element.18), channel_id=1, source_target_pairs={{4,0},{8,4},{12,8},{16,12},{20,16},{24,20},{28,24},{32,28},{36,32}... | collective-permute-start | bytes 786440 | tf_op jit(solution)/shard_map/ppermute | solution.py:156
  27.2 12.2 %copy-start.4 = (bf16[27,128,128]{2,1,0:T(8,128)(2,1)S(1)}, bf16[27,128,128]{2,1,0:T(8,128)(2,1)}, u32[]{:S(2)}) copy-start(bf16[27,128,128]{2,1,0:T(8,128)(2,1)} %param.4) | copy-start | bytes 2654212
  28.3 15.7 %collective-permute-start.1 = (bf16[2,64,4096]{2,1,0:T(8,128)(2,1)}, bf16[2,64,4096]{2,1,0:T(8,128)(2,1)S(1)}, u32[]{:S(2)}, u32[]{:S(2)}) collective-permute-start(bf16[2,64,4096]{2,1,0:T(8,128)(2,1)} %pad_maximum_fusion), channel_id=1, source_target_pairs={{0,1},{1,0},{2,3},{3,2},{4,5},{5,4},{6,7},{7,6},{8,9},{9,8},{10,11... | collective-permute-start | bytes 3145736 | tf_op jit(solution)/shard_map/ppermute | solution.py:157
  30.6 3.9 %copy-start.5 = (bf16[64,2048]{1,0:T(8,128)(2,1)}, bf16[64,2048]{1,0:T(8,128)(2,1)S(1)}, u32[]{:S(2)}) copy-start(bf16[64,2048]{1,0:T(8,128)(2,1)S(1)} %collective-permute-done.4.refs_5_) | copy-start | bytes 786436
  34.4 0.7 copy-start.6
  37.3 6.7 %collective-permute-start.6 = (bf16[4,64,2048]{2,1,0:T(8,128)(2,1)}, bf16[4,64,2048]{2,1,0:T(8,128)(2,1)S(1)}, u32[]{:S(2)}, u32[]{:S(2)}) collective-permute-start(bf16[4,64,2048]{2,1,0:T(8,128)(2,1)} %pad_maximum_fusion.1), channel_id=1, source_target_pairs={{0,1},{1,0},{2,3},{3,2},{4,5},{5,4},{6,7},{7,6},{8,9},{9,8},{10,11... | collective-permute-start | bytes 3145736 | tf_op jit(solution)/shard_map/ppermute | solution.py:158
  44.0 1.0 %copy-start.2 = (bf16[2,64,4096]{2,1,0:T(8,128)(2,1)}, bf16[2,64,4096]{2,1,0:T(8,128)(2,1)S(1)}, u32[]{:S(2)}) copy-start(bf16[2,64,4096]{2,1,0:T(8,128)(2,1)S(1)} %collective-permute-done.1.refs_2_) | copy-start | bytes 3145732
  45.0 1.0 %copy-start.3 = (bf16[4,64,2048]{2,1,0:T(8,128)(2,1)}, bf16[4,64,2048]{2,1,0:T(8,128)(2,1)S(1)}, u32[]{:S(2)}) copy-start(bf16[4,64,2048]{2,1,0:T(8,128)(2,1)S(1)} %collective-permute-done.6.refs_7_) | copy-start | bytes 3145732
  54.2 10.2 %copy-start.7 = (bf16[27,32,32]{2,1,0:T(8,128)(2,1)S(1)}, bf16[27,32,32]{2,1,0:T(8,128)(2,1)}, u32[]{:S(2)}) copy-start(bf16[27,32,32]{2,1,0:T(8,128)(2,1)} %get-tuple-element.11) | copy-start | bytes 165892
  54.2 10.2 %copy-start.8 = (bf16[27,32,32]{2,1,0:T(8,128)(2,1)S(1)}, bf16[27,32,32]{2,1,0:T(8,128)(2,1)}, u32[]{:S(2)}) copy-start(bf16[27,32,32]{2,1,0:T(8,128)(2,1)} %get-tuple-element.16) | copy-start | bytes 165892
  54.2 10.2 %copy-start.9 = (bf16[27,32,32]{2,1,0:T(8,128)(2,1)S(1)}, bf16[27,32,32]{2,1,0:T(8,128)(2,1)}, u32[]{:S(2)}) copy-start(bf16[27,32,32]{2,1,0:T(8,128)(2,1)} %get-tuple-element.17) | copy-start | bytes 165892
  56.0 18.0 %all-to-all-start = ((bf16[32,2,1728]{2,1,0:T(2,128)(2,1)}), bf16[32,2,1728]{2,1,0:T(2,128)(2,1)S(1)}, u32[]{:S(2)}, u32[]{:S(2)}) async-start(bf16[32,2,1728]{2,1,0:T(2,128)(2,1)} %reshape.25), calls=%async_computation | async-start | bytes 458752 | tf_op jit(solution)/shard_map/all_to_all | solution.py:19

commit v13 on v12

--- a/solution.py
+++ b/solution.py
@@ -152,10 +152,6 @@
     got_far = lax.ppermute(both, far, swap)
     low = lax.ppermute(both[:, -width:], "gz", up)
     high = lax.ppermute(both[:, :width], "gz", down)
-    far_low = lax.ppermute(got_far[:, -width:], "gz", up)
-    far_high = lax.ppermute(got_far[:, :width], "gz", down)
-    got_near = lax.ppermute(jnp.stack([both, got_far]), near, swap)
-    halos = lax.ppermute(jnp.stack([low, high, far_low, far_high]), near, swap)
     groups = 4
     order = [jnp.bitwise_xor(my_group, j) for j in range(groups)]
     cin = groups * in_local
@@ -167,6 +163,11 @@
     weight_rows = lax.dynamic_slice_in_dim(weight, my_group * in_local, in_local, 1)
     weight_rows = by_group(weight_rows, order, out_local, 2)
     wb = weight_rows[::-1].reshape(9, 3 * in_local, cout)
+    got_far, wf, wb = lax.optimization_barrier((got_far, wf, wb))
+    far_low = lax.ppermute(got_far[:, -width:], "gz", up)
+    far_high = lax.ppermute(got_far[:, :width], "gz", down)
+    got_near = lax.ppermute(jnp.stack([both, got_far]), near, swap)
+    halos = lax.ppermute(jnp.stack([low, high, far_low, far_high]), near, swap)
     pieces = (both, got_far, got_near, low, high, far_low, far_high, halos)
     (wg,) = fused(pieces, wf, wb, planes_local, width, True)
     wg = by_group(wg, order, in_local, 1)

time: 76.3 us -> 75 us (0.983)
  the two profiles are of different devices: /device:TPU:1 before, /device:TPU:0 now
where the time goes in v13:
time: 75 us; the launch traced here: 74.5 us
  starting transfers between devices  26.9 us (36%)
  local copies, waits for them, and re-layouts  14.5 us (19%)
  Pallas kernels  13.9 us (19%)
  waiting for transfers between devices  13.6 us (18%)
  other arithmetic  4.75 us (6%)
  between operations  0.89 us (1%)
    all_to_all x1, starting transfers between devices, summed_on_arrival(): lax.all_to_all(blocks, axis, split_axis=0, concat_axis=0, tiled=True)  14.6 us
    pallas_call x2, Pallas kernels, fused(): pl.pallas_call(kernel, out_shape=shapes, scratch_shapes=[pltpu.VMEM((cin,...  13.9 us
    unnamed x28, local copies, waits for them, and re-layouts  5.93 us
    ppermute x1, waiting for transfers between devices, body(): far_high = lax.ppermute(got_far[:, :width], 'gz', down)  4.13 us
    ppermute x1, starting transfers between devices, body(): got_far = lax.ppermute(both, far, swap)  4.07 us
    concatenate x3, other arithmetic, by_group(): jnp.concatenate([lax.dynamic_slice_in_dim(array, group * size, size, dim)...  3.41 us
    ppermute x1, starting transfers between devices, body(): low = lax.ppermute(both[:, -width:], 'gz', up)  3.4 us
    ppermute x1, waiting for transfers between devices, body(): far_low = lax.ppermute(got_far[:, -width:], 'gz', up)  3.15 us
  transfers between devices with their start and end apart: 8, of which 5 were waited for; matrix products, arithmetic and copies ran while one was open for 14% of the time, Pallas kernels for 10%

profile of v13, /device:TPU:0, one launch (start us, length us, event | category | flops | bytes accessed | tf_op | source)
XLA Modules:
  0.0 74.5 jit_solution(15626535160816819804)
XLA Ops:
  0.6 1.0 %constant_dynamic-update-slice_fusion.1 = bf16[64,2,16,128]{3,2,1,0:T(8,128)(2,1)S(1)} fusion(bf16[32,2,16,128]{3,2,1,0:T(8,128)(2,1)} %param.3), kind=kLoop, calls=%fused_computation.13 | loop fusion | bytes 524288
  1.6 0.0 copy-start.4
  1.6 1.1 %constant_dynamic-update-slice_fusion = bf16[64,2,16,128]{3,2,1,0:T(8,128)(2,1)S(1)} fusion(bf16[64,2,16,128]{3,2,1,0:T(8,128)(2,1)S(1)} %constant_dynamic-update-slice_fusion.1, bf16[32,2,16,128]{3,2,1,0:T(8,128)(2,1)} %param.5), kind=kLoop, calls=%fused_computation.12 | loop fusion | bytes 524288 | tf_op jit(solution)/shard_map/concatenate | solution.py:147
  2.7 0.2 copy.56
  2.9 4.1 %collective-permute-start = (bf16[64,4096]{1,0:T(8,128)(2,1)S(1)}, bf16[64,4096]{1,0:T(8,128)(2,1)S(1)}, u32[]{:S(2)}, u32[]{:S(2)}) collective-permute-start(bf16[64,4096]{1,0:T(8,128)(2,1)S(1)} %bitcast.21), channel_id=1, source_target_pairs={{0,2},{2,0},{1,3},{3,1},{4,6},{6,4},{5,7},{7,5},{8,10},{10,8},{9,1... | collective-permute-start | bytes 1572872 | tf_op jit(solution)/shard_map/ppermute | solution.py:152
  7.0 0.8 %fusion.1 = (bf16[64,2048]{1,0:T(8,128)(2,1)}, bf16[64,2048]{1,0:T(8,128)(2,1)}) fusion(bf16[64,4096]{1,0:T(8,128)(2,1)S(1)} %bitcast.22), kind=kLoop, calls=%fused_computation.22 | loop fusion | bytes 1048576 | tf_op jit(solution)/shard_map/slice | solution.py:154
  7.8 3.4 %collective-permute-start.2 = (bf16[64,2048]{1,0:T(8,128)(2,1)}, bf16[64,2048]{1,0:T(8,128)(2,1)S(1)}, u32[]{:S(2)}, u32[]{:S(2)}) collective-permute-start(bf16[64,2048]{1,0:T(8,128)(2,1)} %get-tuple-element.27), channel_id=1, source_target_pairs={{0,4},{4,8},{8,12},{12,16},{16,20},{20,24},{24,28},{28,32},{32,36}... | collective-permute-start | bytes 786440 | tf_op jit(solution)/shard_map/ppermute | solution.py:153
  11.2 1.3 %collective-permute-start.3 = (bf16[64,2048]{1,0:T(8,128)(2,1)}, bf16[64,2048]{1,0:T(8,128)(2,1)S(1)}, u32[]{:S(2)}, u32[]{:S(2)}) collective-permute-start(bf16[64,2048]{1,0:T(8,128)(2,1)} %get-tuple-element.26), channel_id=1, source_target_pairs={{4,0},{8,4},{12,8},{16,12},{20,16},{24,20},{28,24},{32,28},{36,32}... | collective-permute-start | bytes 786440 | tf_op jit(solution)/shard_map/ppermute | solution.py:154
  12.5 1.0 %stack_reshape.3 = bf16[1,64,4096]{2,1,0:T(8,128)(2,1)} reshape(bf16[64,2,16,128]{3,2,1,0:T(8,128)(2,1)S(1)} %constant_dynamic-update-slice_fusion) | data formatting | bytes 1048576 | tf_op jit(solution)/shard_map/stack;reshape | solution.py:169
  13.6 2.0 %constant_dynamic-slice_fusion.2 = (bf16[27,32,32]{2,1,0:T(8,128)(2,1)}, bf16[27,32,32]{2,1,0:T(8,128)(2,1)S(1)}, bf16[27,32,32]{2,1,0:T(8,128)(2,1)S(1)}, bf16[...) fusion(bf16[27,128,128]{2,1,0:T(8,128)(2,1)S(1)} %copy-done.4, ...), kind=kLoop, calls=%fused_computation.16 | loop fusion | bytes 774160 | tf_op jit(solution)/shard_map/dynamic_slice | solution.py:136
  15.6 0.0 copy-done
  15.6 1.1 %copy.53 = bf16[27,32,32]{1,2,0:T(8,128)(2,1)S(1)} copy(bf16[27,32,32]{2,1,0:T(8,128)(2,1)} %get-tuple-element.21) | data formatting | bytes 110592
  16.7 0.2 copy.52
  16.9 0.2 copy.51
  17.0 0.2 copy.50
  17.2 2.2 %pad_maximum_fusion.4 = bf16[27,32,128]{2,1,0:T(8,128)(2,1)} fusion(bf16[27,32,32]{2,1,0:T(8,128)(2,1)} %get-tuple-element.22, bf16[27,32,32]{2,1,0:T(8,128)(2,1)} %get-tuple-element.23, bf16[27,32,32]{2,1,0:T(8,128)(2,1)} %get-tuple-element.17, bf16[27,32,32]{2,1,0:T(8,128)(2,1)S(1)} %get-tuple-element.20), kind=kLoop, calls=%fused_computation.10 | loop fusion | flops 884736 | bytes 442368 | tf_op jit(solution)/shard_map/concatenate | solution.py:135
  19.4 1.6 %rev.3 = bf16[27,32,128]{2,1,0:T(8,128)(2,1)} reverse(bf16[27,32,128]{2,1,0:T(8,128)(2,1)} %pad_maximum_fusion.4), dimensions={0} | reverse | bytes 442368 | tf_op jit(solution)/shard_map/rev | solution.py:165
  21.1 1.0 %pad_maximum_fusion.3 = bf16[27,128,32]{1,2,0:T(8,128)(2,1)} fusion(bf16[27,32,32]{1,2,0:T(8,128)(2,1)S(1)} %copy.53, bf16[27,32,32]{1,2,0:T(8,128)(2,1)S(1)} %copy.52, bf16[27,32,32]{1,2,0:T(8,128)(2,1)S(1)} %copy.51, bf16[27,32,32]{1,2,0:T(8,128)(2,1)S(1)} %copy.50), kind=kLoop, calls=%fused_computation.9 | loop fusion | flops 884736 | bytes 442368 | tf_op jit(solution)/shard_map/concatenate | solution.py:135
  22.0 2.5 %collective-permute-done.refs_1_ = bf16[64,4096]{1,0:T(8,128)(2,1)S(1)} collective-permute-done((bf16[64,4096]{1,0:T(8,128)(2,1)S(1)}, bf16[64,4096]{1,0:T(8,128)(2,1)S(1)}, u32[]{:S(2)}, u32[]{:S(2)}) %collective-permute-start) | collective-permute-done | bytes 524320 | tf_op jit(solution)/shard_map/ppermute | solution.py:152
  24.6 2.1 %collective-permute-start.4 = (bf16[64,2048]{1,0:T(8,128)(2,1)S(1)}, bf16[64,2048]{1,0:T(8,128)(2,1)S(1)}, u32[]{:S(2)}, u32[]{:S(2)}) collective-permute-start(bf16[64,2048]{1,0:T(8,128)(2,1)S(1)} %get-tuple-element.25), channel_id=1, source_target_pairs={{0,4},{4,8},{8,12},{12,16},{16,20},{20,24},{24,28},{28,32},{32,36}... | collective-permute-start | bytes 786440 | tf_op jit(solution)/shard_map/ppermute | solution.py:167
  26.7 1.3 %collective-permute-start.5 = (bf16[64,2048]{1,0:T(8,128)(2,1)S(1)}, bf16[64,2048]{1,0:T(8,128)(2,1)S(1)}, u32[]{:S(2)}, u32[]{:S(2)}) collective-permute-start(bf16[64,2048]{1,0:T(8,128)(2,1)S(1)} %get-tuple-element.24), channel_id=1, source_target_pairs={{4,0},{8,4},{12,8},{16,12},{20,16},{24,20},{28,24},{32,28},{36,32}... | collective-permute-start | bytes 786440 | tf_op jit(solution)/shard_map/ppermute | solution.py:168
  28.0 0.1 pad_maximum_fusion
  28.1 0.1 collective-permute-start.1
  28.2 0.0 collective-permute-done.2.refs_3_
  28.2 0.0 copy-start.5
  28.2 0.0 collective-permute-done.3.refs_4_
  28.2 3.1 %collective-permute-done.4.refs_5_ = bf16[64,2048]{1,0:T(8,128)(2,1)S(1)} collective-permute-done((bf16[64,2048]{1,0:T(8,128)(2,1)S(1)}, bf16[64,2048]{1,0:T(8,128)(2,1)S(1)}, u32[]{:S(2)}, u32[]{:S(2)}) %collective-permute-start.4) | collective-permute-done | bytes 262176 | tf_op jit(solution)/shard_map/ppermute | solution.py:167
  31.4 4.1 %collective-permute-done.5.refs_6_ = bf16[64,2048]{1,0:T(8,128)(2,1)S(1)} collective-permute-done((bf16[64,2048]{1,0:T(8,128)(2,1)S(1)}, bf16[64,2048]{1,0:T(8,128)(2,1)S(1)}, u32[]{:S(2)}, u32[]{:S(2)}) %collective-permute-start.5) | collective-permute-done | bytes 262176 | tf_op jit(solution)/shard_map/ppermute | solution.py:168
  35.5 0.0 copy-done.6
  35.5 0.1 pad_maximum_fusion.1
  35.6 0.1 collective-permute-start.6
  35.7 0.0 collective-permute-done.1.refs_2_
  35.7 2.6 %collective-permute-done.6.refs_7_ = bf16[4,64,2048]{2,1,0:T(8,128)(2,1)S(1)} collective-permute-done((bf16[4,64,2048]{2,1,0:T(8,128)(2,1)S(1)}, bf16[4,64,2048]{2,1,0:T(8,128)(2,1)S(1)}, u32[]{:S(2)}, u32[]{:S(2)}) %collective-permute-start.6) | collective-permute-done | bytes 1048608 | tf_op jit(solution)/shard_map/ppermute | solution.py:170
  38.4 0.0 copy-done.8
  38.4 0.0 copy-done.2
  38.4 0.0 copy-start.3
  38.4 1.0 %copy-done.3 = bf16[4,64,2048]{2,1,0:T(8,128)(2,1)} copy-done((bf16[4,64,2048]{2,1,0:T(8,128)(2,1)}, bf16[4,64,2048]{2,1,0:T(8,128)(2,1)S(1)}, u32[]{:S(2)}) %copy-start.3) | copy-done | bytes 1048600
  39.4 6.4 %shard_map.59 = f32[27,128,32]{2,1,0:T(8,128)} custom-call(bf16[64,4096]{1,0:T(8,128)(2,1)} %bitcast.23, bf16[64,4096]{1,0:T(8,128)(2,1)} %copy-done.1, bf16[2,64,4096]{2,1,0:T(8,128)(2,1)} %copy-done.2, bf16[64,2048]{1,0:T(8,128)(2,1)} %copy-done.5, bf16[64,2048]{1,0:T(8,128)(2,1)} %copy-done.6, bf16[64,2048]{1,0:T(8,128)(2,1)} %copy-done.7, ...), custom_call_target="tpu_custom_call" | custom-call | tf_op jit(solution)/shard_map/pallas_call | solution.py:124
  45.7 1.6 %dynamic-slice_convert_fusion.3 = (bf16[27,32,32]{2,1,0:T(8,128)(2,1)S(1)}, bf16[27,32,32]{2,1,0:T(8,128)(2,1)S(1)}, bf16[27,32,32]{2,1,0:T(8,128)(2,1)S(1)}, bf16[27,32,32]{2,1,0:T(8,128)(2,1)S(1)}) fusion(f32[27,128,32]{2,1,0:T(8,128)} %shard_map.59, s32[]{:T(128)S(6)} %select_n.30, s32[]{:T(128)S(6)} %select_n.36, s32[]{:T(128)S(6)} %select_n.34, ...), kind=kLoop, calls=%fused_computation.8 | loop fusion | bytes 442384 | tf_op jit(solution)/shard_map/convert
  47.4 0.2 pad_maximum_fusion.2
  47.6 0.3 copy.49
  47.9 1.4 %reshape.25 = bf16[32,2,1728]{2,1,0:T(2,128)(2,1)} reshape(bf16[32,27,4,32]{3,2,1,0:T(4,128)(2,1)S(1)} %copy.49) | data formatting | bytes 442368
  49.3 14.6 %all-to-all-start = ((bf16[32,2,1728]{2,1,0:T(2,128)(2,1)}), bf16[32,2,1728]{2,1,0:T(2,128)(2,1)S(1)}, u32[]{:S(2)}, u32[]{:S(2)}) async-start(bf16[32,2,1728]{2,1,0:T(2,128)(2,1)} %reshape.25), calls=%async_computation | async-start | bytes 458752 | tf_op jit(solution)/shard_map/all_to_all | solution.py:19
  63.9 7.5 %shard_map.58 = (bf16[32,2,16,128]{3,2,1,0:T(8,128)(2,1)}, bf16[32,2,16,128]{3,2,1,0:T(8,128)(2,1)}) custom-call(bf16[64,4096]{1,0:T(8,128)(2,1)} %bitcast.24, bf16[64,4096]{1,0:T(8,128)(2,1)} %copy-done.1, bf16[2,64,4096]{2,1,0:T(8,128)(2,1)} %copy-done.2, bf16[64,2048]{1,0:T(8,128)(2,1)} %copy-done.5, bf16[64,2048]{1,0:T(8,128)(2,1)} %copy-done.6, ...), custom_call_target="tpu_custom_call" | custom-call | tf_op jit(solution)/shard_map/pallas_call | solution.py:124
  71.4 1.2 %all-to-all-done = bf16[32,2,1728]{2,1,0:T(2,128)(2,1)S(1)} async-done(((bf16[32,2,1728]{2,1,0:T(2,128)(2,1)}), bf16[32,2,1728]{2,1,0:T(2,128)(2,1)S(1)}, u32[]{:S(2)}, u32[]{:S(2)}) %all-to-all-start) | async-done | bytes 221216 | tf_op jit(solution)/shard_map/all_to_all | solution.py:19
  72.7 0.8 %reshape.26 = bf16[32,27,4,32]{3,2,1,0:T(4,128)(2,1)S(1)} reshape(bf16[32,2,1728]{2,1,0:T(2,128)(2,1)S(1)} %all-to-all-done) | data formatting | bytes 442368
  73.4 0.5 convert_reduce_fusion
  73.9 0.6 broadcast_multiply_fusion
  (13 shorter events, 0.1 us)
Async XLA Ops:
  1.6 12.0 %copy-start.4 = (bf16[27,128,128]{2,1,0:T(8,128)(2,1)S(1)}, bf16[27,128,128]{2,1,0:T(8,128)(2,1)}, u32[]{:S(2)}) copy-start(bf16[27,128,128]{2,1,0:T(8,128)(2,1)} %param.4) | copy-start | bytes 2654212
  2.9 12.7 %copy-start = (bf16[8,8,32,128]{3,1,2,0:T(8,128)(2,1)}, bf16[8,8,32,128]{3,1,2,0:T(8,128)(2,1)S(1)}, u32[]{:S(2)}) copy-start(bf16[8,8,32,128]{3,1,2,0:T(8,128)(2,1)S(1)} %copy.56) | copy-start | bytes 1572868
  2.9 21.6 %collective-permute-start = (bf16[64,4096]{1,0:T(8,128)(2,1)S(1)}, bf16[64,4096]{1,0:T(8,128)(2,1)S(1)}, u32[]{:S(2)}, u32[]{:S(2)}) collective-permute-start(bf16[64,4096]{1,0:T(8,128)(2,1)S(1)} %bitcast.21), channel_id=1, source_target_pairs={{0,2},{2,0},{1,3},{3,1},{4,6},{6,4},{5,7},{7,5},{8,10},{10,8},{9,1... | collective-permute-start | bytes 1572872 | tf_op jit(solution)/shard_map/ppermute | solution.py:152
  7.8 20.4 %collective-permute-start.2 = (bf16[64,2048]{1,0:T(8,128)(2,1)}, bf16[64,2048]{1,0:T(8,128)(2,1)S(1)}, u32[]{:S(2)}, u32[]{:S(2)}) collective-permute-start(bf16[64,2048]{1,0:T(8,128)(2,1)} %get-tuple-element.27), channel_id=1, source_target_pairs={{0,4},{4,8},{8,12},{12,16},{16,20},{20,24},{24,28},{28,32},{32,36}... | collective-permute-start | bytes 786440 | tf_op jit(solution)/shard_map/ppermute | solution.py:153
  11.2 17.0 %collective-permute-start.3 = (bf16[64,2048]{1,0:T(8,128)(2,1)}, bf16[64,2048]{1,0:T(8,128)(2,1)S(1)}, u32[]{:S(2)}, u32[]{:S(2)}) collective-permute-start(bf16[64,2048]{1,0:T(8,128)(2,1)} %get-tuple-element.26), channel_id=1, source_target_pairs={{4,0},{8,4},{12,8},{16,12},{20,16},{24,20},{28,24},{32,28},{36,32}... | collective-permute-start | bytes 786440 | tf_op jit(solution)/shard_map/ppermute | solution.py:154
  17.2 10.8 %copy-start.9 = (bf16[1,64,4096]{2,1,0:T(8,128)(2,1)S(1)}, bf16[1,64,4096]{2,1,0:T(8,128)(2,1)}, u32[]{:S(2)}) copy-start(bf16[1,64,4096]{2,1,0:T(8,128)(2,1)} %stack_reshape.3) | copy-start | bytes 1572868
  24.5 11.1 %copy-start.1 = (bf16[64,4096]{1,0:T(8,128)(2,1)}, bf16[64,4096]{1,0:T(8,128)(2,1)S(1)}, u32[]{:S(2)}) copy-start(bf16[64,4096]{1,0:T(8,128)(2,1)S(1)} %collective-permute-done.refs_1_) | copy-start | bytes 1572868
  24.6 6.8 %collective-permute-start.4 = (bf16[64,2048]{1,0:T(8,128)(2,1)S(1)}, bf16[64,2048]{1,0:T(8,128)(2,1)S(1)}, u32[]{:S(2)}, u32[]{:S(2)}) collective-permute-start(bf16[64,2048]{1,0:T(8,128)(2,1)S(1)} %get-tuple-element.25), channel_id=1, source_target_pairs={{0,4},{4,8},{8,12},{12,16},{16,20},{20,24},{24,28},{28,32},{32,36}... | collective-permute-start | bytes 786440 | tf_op jit(solution)/shard_map/ppermute | solution.py:167
  26.7 8.8 %collective-permute-start.5 = (bf16[64,2048]{1,0:T(8,128)(2,1)S(1)}, bf16[64,2048]{1,0:T(8,128)(2,1)S(1)}, u32[]{:S(2)}, u32[]{:S(2)}) collective-permute-start(bf16[64,2048]{1,0:T(8,128)(2,1)S(1)} %get-tuple-element.24), channel_id=1, source_target_pairs={{4,0},{8,4},{12,8},{16,12},{20,16},{24,20},{28,24},{32,28},{36,32}... | collective-permute-start | bytes 786440 | tf_op jit(solution)/shard_map/ppermute | solution.py:168
  28.1 7.7 %collective-permute-start.1 = (bf16[2,64,4096]{2,1,0:T(8,128)(2,1)S(1)}, bf16[2,64,4096]{2,1,0:T(8,128)(2,1)S(1)}, u32[]{:S(2)}, u32[]{:S(2)}) collective-permute-start(bf16[2,64,4096]{2,1,0:T(8,128)(2,1)S(1)} %pad_maximum_fusion), channel_id=1, source_target_pairs={{0,1},{1,0},{2,3},{3,2},{4,5},{5,4},{6,7},{7,6},{8,9},{9,8},{10,11... | collective-permute-start | bytes 3145736 | tf_op jit(solution)/shard_map/ppermute | solution.py:169
  28.2 10.2 %copy-start.5 = (bf16[64,2048]{1,0:T(8,128)(2,1)}, bf16[64,2048]{1,0:T(8,128)(2,1)S(1)}, u32[]{:S(2)}) copy-start(bf16[64,2048]{1,0:T(8,128)(2,1)S(1)} %collective-permute-done.2.refs_3_) | copy-start | bytes 786436
  28.2 7.3 %copy-start.6 = (bf16[64,2048]{1,0:T(8,128)(2,1)}, bf16[64,2048]{1,0:T(8,128)(2,1)S(1)}, u32[]{:S(2)}) copy-start(bf16[64,2048]{1,0:T(8,128)(2,1)S(1)} %collective-permute-done.3.refs_4_) | copy-start | bytes 786436
  31.3 7.0 %copy-start.7 = (bf16[64,2048]{1,0:T(8,128)(2,1)}, bf16[64,2048]{1,0:T(8,128)(2,1)S(1)}, u32[]{:S(2)}) copy-start(bf16[64,2048]{1,0:T(8,128)(2,1)S(1)} %collective-permute-done.4.refs_5_) | copy-start | bytes 786436
  35.5 2.9 %copy-start.8 = (bf16[64,2048]{1,0:T(8,128)(2,1)}, bf16[64,2048]{1,0:T(8,128)(2,1)S(1)}, u32[]{:S(2)}) copy-start(bf16[64,2048]{1,0:T(8,128)(2,1)S(1)} %collective-permute-done.5.refs_6_) | copy-start | bytes 786436
  35.6 2.7 %collective-permute-start.6 = (bf16[4,64,2048]{2,1,0:T(8,128)(2,1)S(1)}, bf16[4,64,2048]{2,1,0:T(8,128)(2,1)S(1)}, u32[]{:S(2)}, u32[]{:S(2)}) collective-permute-start(bf16[4,64,2048]{2,1,0:T(8,128)(2,1)S(1)} %pad_maximum_fusion.1), channel_id=1, source_target_pairs={{0,1},{1,0},{2,3},{3,2},{4,5},{5,4},{6,7},{7,6},{8,9},{9,8},{10,11... | collective-permute-start | bytes 3145736 | tf_op jit(solution)/shard_map/ppermute | solution.py:170
  35.7 2.6 %copy-start.2 = (bf16[2,64,4096]{2,1,0:T(8,128)(2,1)}, bf16[2,64,4096]{2,1,0:T(8,128)(2,1)S(1)}, u32[]{:S(2)}) copy-start(bf16[2,64,4096]{2,1,0:T(8,128)(2,1)S(1)} %collective-permute-done.1.refs_2_) | copy-start | bytes 3145732
  38.4 1.0 %copy-start.3 = (bf16[4,64,2048]{2,1,0:T(8,128)(2,1)}, bf16[4,64,2048]{2,1,0:T(8,128)(2,1)S(1)}, u32[]{:S(2)}) copy-start(bf16[4,64,2048]{2,1,0:T(8,128)(2,1)S(1)} %collective-permute-done.6.refs_7_) | copy-start | bytes 3145732
  49.3 23.3 %all-to-all-start = ((bf16[32,2,1728]{2,1,0:T(2,128)(2,1)}), bf16[32,2,1728]{2,1,0:T(2,128)(2,1)S(1)}, u32[]{:S(2)}, u32[]{:S(2)}) async-start(bf16[32,2,1728]{2,1,0:T(2,128)(2,1)} %reshape.25), calls=%async_computation | async-start | bytes 458752 | tf_op jit(solution)/shard_map/all_to_all | solution.py:19

commit v14 on v10

--- a/solution.py
+++ b/solution.py
@@ -20,7 +20,7 @@
     return arrived.astype(jnp.float32).sum(axis=0)
 
 def fused_kernel(
-    own_ref, far_ref, near_ref, lo_ref, hi_ref, flo_ref, fhi_ref, hal_ref, wf_ref, wb_ref,
+    own_ref, far_ref, near_ref, lo_ref, hi_ref, flo_ref, fhi_ref, ohal_ref, fhal_ref, wf_ref, wb_ref,
     out_ref, ing_ref, wg_ref, vs_ref, cs_ref,
 ):
     both = own_ref.shape[0]
@@ -32,9 +32,9 @@
     blank = jnp.zeros((loc, ROW), jnp.bfloat16)
     pieces = (
         (lambda c: own_ref[c, :], lambda c: lo_ref[c, :], lambda c: hi_ref[c, :]),
-        (lambda c: near_ref[0, c, :], lambda c: hal_ref[0, c, :], lambda c: hal_ref[1, c, :]),
+        (lambda c: near_ref[0, c, :], lambda c: ohal_ref[0, c, :], lambda c: ohal_ref[1, c, :]),
         (lambda c: far_ref[c, :], lambda c: flo_ref[c, :], lambda c: fhi_ref[c, :]),
-        (lambda c: near_ref[1, c, :], lambda c: hal_ref[2, c, :], lambda c: hal_ref[3, c, :]),
+        (lambda c: near_ref[1, c, :], lambda c: fhal_ref[0, c, :], lambda c: fhal_ref[1, c, :]),
     )
     for k, (body_of, low_of, high_of) in enumerate(pieces):
         rows = slice(k * loc, (k + 1) * loc)
@@ -90,7 +90,7 @@
             ref[:, z] = part.astype(ref.dtype)
 
 
-def fused(own, far, near, low, high, far_low, far_high, halos, wf, wb, planes, width):
+def fused(own, far, near, low, high, far_low, far_high, own_halos, far_halos, wf, wb, planes, width):
     both = own.shape[0]
     loc = both // 2
     cin = 4 * loc
@@ -106,7 +106,7 @@
             pltpu.VMEM((cin, flat), jnp.bfloat16),
             pltpu.VMEM((cin, flat), jnp.bfloat16),
         ],
-    )(own, far, near, low, high, far_low, far_high, halos, wf, wb)
+    )(own, far, near, low, high, far_low, far_high, own_halos, far_halos, wf, wb)
 
 
 def by_group(array, order, size, dim):
@@ -133,7 +133,8 @@
     far_low = lax.ppermute(got_far[:, -width:], "gz", up)
     far_high = lax.ppermute(got_far[:, :width], "gz", down)
     got_near = lax.ppermute(jnp.stack([both, got_far]), near, swap)
-    halos = lax.ppermute(jnp.stack([low, high, far_low, far_high]), near, swap)
+    own_halos = lax.ppermute(jnp.stack([low, high]), near, swap)
+    far_halos = lax.ppermute(jnp.stack([far_low, far_high]), near, swap)
     groups = 4
     order = [jnp.bitwise_xor(my_group, j) for j in range(groups)]
     cin = groups * in_local
@@ -146,7 +147,8 @@
     weight_rows = by_group(weight_rows, order, out_local, 2)
     wb = weight_rows[::-1].reshape(9, 3 * in_local, cout)
     out, ing, wg = fused(
-        both, got_far, got_near, low, high, far_low, far_high, halos, wf, wb, planes_local, width
+        both, got_far, got_near, low, high, far_low, far_high, own_halos, far_halos, wf, wb,
+        planes_local, width,
     )
     wg = by_group(wg, order, in_local, 1)
     shape = (out_local, planes_local, grid_rows, grid_cols)

time: 73.5 us -> 76.4 us (1.039)
  other arithmetic: 4.96 us -> 6.51 us
  local copies, waits for them, and re-layouts: 9.16 us -> 10.7 us
    concatenate x3, other arithmetic: 1.52 us -> 2.56 us  [by_group(): jnp.concatenate([lax.dynamic_slice_in_dim(array, group * size, size, dim)...]
    dynamic_slice x1, local copies, waits for them, and re-layouts: 1.15 us -> 1.94 us  [by_group(): lax.dynamic_slice_in_dim(array, group * size, size, dim)]
    unnamed x18 -> x22, local copies, waits for them, and re-layouts: 3.32 us -> 4.04 us
    another operation x1 -> x2, other arithmetic: 2.24 us -> 2.74 us  [the longest x1 1.88 us: body(): own_halos = lax.ppermute(jnp.stack([low, high]), near, swap)]
  transfers between devices with their start and end apart: 7 -> 8, of which waited for: 3 -> 3; matrix products, arithmetic and copies ran while one was open for 10% -> 13% of each run, Pallas kernels for 0% -> 0%
where the time goes in v14:
time: 76.4 us; the launch traced here: 76 us
  blocking collectives  22.4 us (29%)
  starting transfers between devices  16.7 us (22%)
  local copies, waits for them, and re-layouts  10.7 us (14%)
  Pallas kernels  10.7 us (14%)
  waiting for transfers between devices  8.19 us (11%)
  other arithmetic  6.51 us (9%)
  between operations  0.81 us (1%)
    all_to_all x1, blocking collectives, summed_on_arrival(): lax.all_to_all(blocks, axis, split_axis=0, concat_axis=0, tiled=True)  22.4 us
    pallas_call x1, Pallas kernels, fused(): pl.pallas_call(fused_kernel, out_shape=(jax.ShapeDtypeStruct((loc, planes...  10.7 us
    ppermute x1, starting transfers between devices, body(): low = lax.ppermute(both[:, -width:], 'gz', up)  5.26 us
    ppermute x1, starting transfers between devices, body(): far_low = lax.ppermute(got_far[:, -width:], 'gz', up)  4.56 us
    ppermute x1, waiting for transfers between devices, body(): got_far = lax.ppermute(both, far, swap)  4.33 us
    ppermute x1, starting transfers between devices, body(): got_far = lax.ppermute(both, far, swap)  4.07 us
    unnamed x22, local copies, waits for them, and re-layouts  4.04 us
    ppermute x1, waiting for transfers between devices, body(): far_high = lax.ppermute(got_far[:, :width], 'gz', down)  2.68 us
  transfers between devices with their start and end apart: 8, of which 3 were waited for; matrix products, arithmetic and copies ran while one was open for 13% of the time, Pallas kernels for 0%

profile of v14, /device:TPU:0, one launch (start us, length us, event | category | flops | bytes accessed | tf_op | source)
XLA Modules:
  0.0 76.0 jit_solution(915803722399413325)
XLA Ops:
  0.6 1.0 %constant_dynamic-update-slice_fusion.1 = bf16[64,2,16,128]{3,2,1,0:T(8,128)(2,1)S(1)} fusion(bf16[32,2,16,128]{3,2,1,0:T(8,128)(2,1)} %param.3), kind=kLoop, calls=%fused_computation.14 | loop fusion | bytes 524288
  1.6 1.0 %constant_dynamic-update-slice_fusion = bf16[64,2,16,128]{3,2,1,0:T(8,128)(2,1)S(1)} fusion(bf16[64,2,16,128]{3,2,1,0:T(8,128)(2,1)S(1)} %constant_dynamic-update-slice_fusion.1, bf16[32,2,16,128]{3,2,1,0:T(8,128)(2,1)} %param.5), kind=kLoop, calls=%fused_computation.13 | loop fusion | bytes 524288 | tf_op jit(solution)/shard_map/concatenate | solution.py:125
  2.6 0.2 copy.56
  2.8 0.0 copy-start
  2.8 4.1 %collective-permute-start = (bf16[64,4096]{1,0:T(8,128)(2,1)S(1)}, bf16[64,4096]{1,0:T(8,128)(2,1)S(1)}, u32[]{:S(2)}, u32[]{:S(2)}) collective-permute-start(bf16[64,4096]{1,0:T(8,128)(2,1)S(1)} %bitcast.21), channel_id=1, source_target_pairs={{0,2},{2,0},{1,3},{3,1},{4,6},{6,4},{5,7},{7,5},{8,10},{10,8},{9,1... | collective-permute-start | bytes 1572872 | tf_op jit(solution)/shard_map/ppermute | solution.py:130
  6.9 0.8 %fusion.1 = (bf16[64,2048]{1,0:T(8,128)(2,1)}, bf16[64,2048]{1,0:T(8,128)(2,1)}) fusion(bf16[64,4096]{1,0:T(8,128)(2,1)S(1)} %bitcast.22), kind=kLoop, calls=%fused_computation.23 | loop fusion | bytes 1048576 | tf_op jit(solution)/shard_map/slice | solution.py:132
  7.7 1.3 %collective-permute-start.3 = (bf16[64,2048]{1,0:T(8,128)(2,1)}, bf16[64,2048]{1,0:T(8,128)(2,1)S(1)}, u32[]{:S(2)}, u32[]{:S(2)}) collective-permute-start(bf16[64,2048]{1,0:T(8,128)(2,1)} %get-tuple-element.22), channel_id=1, source_target_pairs={{4,0},{8,4},{12,8},{16,12},{20,16},{24,20},{28,24},{32,28},{36,32}... | collective-permute-start | bytes 786440 | tf_op jit(solution)/shard_map/ppermute | solution.py:132
  9.0 5.3 %collective-permute-start.2 = (bf16[64,2048]{1,0:T(8,128)(2,1)}, bf16[64,2048]{1,0:T(8,128)(2,1)}, u32[]{:S(2)}, u32[]{:S(2)}) collective-permute-start(bf16[64,2048]{1,0:T(8,128)(2,1)} %get-tuple-element.23), channel_id=1, source_target_pairs={{0,4},{4,8},{8,12},{12,16},{16,20},{20,24},{24,28},{28,32},{32,36}... | collective-permute-start | bytes 786440 | tf_op jit(solution)/shard_map/ppermute | solution.py:131
  14.3 0.2 stack_reshape.3
  14.5 4.3 %collective-permute-done.far_ref = bf16[64,4096]{1,0:T(8,128)(2,1)S(1)} collective-permute-done((bf16[64,4096]{1,0:T(8,128)(2,1)S(1)}, bf16[64,4096]{1,0:T(8,128)(2,1)S(1)}, u32[]{:S(2)}, u32[]{:S(2)}) %collective-permute-start) | collective-permute-done | bytes 524320 | tf_op jit(solution)/shard_map/ppermute | solution.py:130
  18.8 0.1 pad_maximum_fusion
  18.9 0.0 copy-done
  18.9 0.0 copy-start.2
  18.9 0.1 collective-permute-start.1
  19.1 1.4 %collective-permute-start.5 = (bf16[64,2048]{1,0:T(8,128)(2,1)S(1)}, bf16[64,2048]{1,0:T(8,128)(2,1)S(1)}, u32[]{:S(2)}, u32[]{:S(2)}) collective-permute-start(bf16[64,2048]{1,0:T(8,128)(2,1)S(1)} %get-tuple-element.20), channel_id=1, source_target_pairs={{4,0},{8,4},{12,8},{16,12},{20,16},{24,20},{28,24},{32,28},{36,32}... | collective-permute-start | bytes 786440 | tf_op jit(solution)/shard_map/ppermute | solution.py:134
  20.5 4.6 %collective-permute-start.4 = (bf16[64,2048]{1,0:T(8,128)(2,1)S(1)}, bf16[64,2048]{1,0:T(8,128)(2,1)S(1)}, u32[]{:S(2)}, u32[]{:S(2)}) collective-permute-start(bf16[64,2048]{1,0:T(8,128)(2,1)S(1)} %get-tuple-element.21), channel_id=1, source_target_pairs={{0,4},{4,8},{8,12},{12,16},{16,20},{20,24},{24,28},{28,32},{32,36}... | collective-permute-start | bytes 786440 | tf_op jit(solution)/shard_map/ppermute | solution.py:133
  25.1 0.0 collective-permute-done.3.hi_ref
  25.1 0.0 copy-start.3
  25.1 0.0 collective-permute-done.2.lo_ref
  25.1 1.9 %pad_maximum_fusion.2 = bf16[2,64,2048]{2,1,0:T(8,128)(2,1)} fusion(bf16[1,64,2048]{2,1,0:T(8,128)(2,1)S(1)} %bitcast.27, bf16[1,64,2048]{2,1,0:T(8,128)(2,1)} %bitcast.1), kind=kLoop, calls=%fused_computation.4 | loop fusion | flops 262144 | bytes 1048576 | tf_op jit(solution)/shard_map/stack | solution.py:136
  27.0 0.0 copy-done.1
  27.0 0.0 collective-permute-start.6
  27.0 2.7 %collective-permute-done.5.fhi_ref = bf16[64,2048]{1,0:T(8,128)(2,1)S(1)} collective-permute-done((bf16[64,2048]{1,0:T(8,128)(2,1)S(1)}, bf16[64,2048]{1,0:T(8,128)(2,1)S(1)}, u32[]{:S(2)}, u32[]{:S(2)}) %collective-permute-start.5) | collective-permute-done | bytes 262176 | tf_op jit(solution)/shard_map/ppermute | solution.py:134
  29.7 1.2 %collective-permute-done.4.flo_ref = bf16[64,2048]{1,0:T(8,128)(2,1)S(1)} collective-permute-done((bf16[64,2048]{1,0:T(8,128)(2,1)S(1)}, bf16[64,2048]{1,0:T(8,128)(2,1)S(1)}, u32[]{:S(2)}, u32[]{:S(2)}) %collective-permute-start.4) | collective-permute-done | bytes 262176 | tf_op jit(solution)/shard_map/ppermute | solution.py:133
  30.9 0.7 copy-done.5
  31.6 0.9 %pad_maximum_fusion.3 = bf16[2,64,2048]{2,1,0:T(8,128)(2,1)} fusion(bf16[1,64,2048]{2,1,0:T(8,128)(2,1)S(1)} %bitcast.28, bf16[1,64,2048]{2,1,0:T(8,128)(2,1)S(1)} %bitcast.29), kind=kLoop, calls=%fused_computation.5 | loop fusion | flops 262144 | bytes 1048576 | tf_op jit(solution)/shard_map/stack | solution.py:137
  32.4 0.0 collective-permute-start.7
  32.4 0.0 copy-done.2
  32.4 1.9 %constant_dynamic-slice_fusion.2 = (bf16[27,32,32]{2,1,0:T(8,128)(2,1)S(1)}, bf16[27,32,32]{2,1,0:T(8,128)(2,1)}, bf16[27,32,32]{2,1,0:T(8,128)(2,1)S(1)}, bf16[...) fusion(bf16[27,128,128]{2,1,0:T(8,128)(2,1)S(1)} %copy-done.2, ...), kind=kLoop, calls=%fused_computation.17 | loop fusion | bytes 774160 | tf_op jit(solution)/shard_map/dynamic_slice | solution.py:114
  34.4 0.2 copy.50
  34.5 1.3 %pad_maximum_fusion.5 = bf16[27,32,128]{2,1,0:T(8,128)(2,1)S(1)} fusion(bf16[27,32,32]{2,1,0:T(8,128)(2,1)} %get-tuple-element.18, bf16[27,32,32]{2,1,0:T(8,128)(2,1)} %get-tuple-element.19, bf16[27,32,32]{2,1,0:T(8,128)(2,1)S(1)} %get-tuple-element.13, bf16[27,32,32]{2,1,0:T(8,128)(2,1)S(1)} %get-tuple-element.16), kind=kLoop, calls=%fused_computation.11 | loop fusion | flops 884736 | bytes 442368 | tf_op jit(solution)/shard_map/concatenate | solution.py:113
  35.9 0.7 rev.3
  36.6 0.2 copy.52
  36.8 0.2 copy.51
  36.9 0.2 copy.53
  37.1 1.0 %pad_maximum_fusion.4 = bf16[27,128,32]{1,2,0:T(8,128)(2,1)} fusion(bf16[27,32,32]{1,2,0:T(8,128)(2,1)S(1)} %copy.53, bf16[27,32,32]{1,2,0:T(8,128)(2,1)S(1)} %copy.52, bf16[27,32,32]{1,2,0:T(8,128)(2,1)S(1)} %copy.51, bf16[27,32,32]{1,2,0:T(8,128)(2,1)S(1)} %copy.50), kind=kLoop, calls=%fused_computation.10 | loop fusion | flops 884736 | bytes 442368 | tf_op jit(solution)/shard_map/concatenate | solution.py:113
  38.1 0.0 collective-permute-done.6.ohal_ref
  38.1 0.0 collective-permute-done.7.fhal_ref
  38.1 0.0 collective-permute-done.1.near_ref
  38.1 10.7 %shard_map.58 = (bf16[32,2,16,128]{3,2,1,0:T(8,128)(2,1)}, bf16[32,2,16,128]{3,2,1,0:T(8,128)(2,1)}, f32[27,128,32]{2,1,0:T(8,128)}) custom-call(bf16[64,4096]{1,0:T(8,128)(2,1)} %bitcast.23, bf16[64,4096]{1,0:T(8,128)(2,1)} %copy-done.1, bf16[2,64,4096]{2,1,0:T(8,128)(2,1)} %collective-permute-done.1.near_ref, ...), custom_call_target="tpu_custom_call" | custom-call | tf_op jit(solution)/shard_map/pallas_call | solution.py:98
  48.7 1.6 %dynamic-slice_convert_fusion.3 = (bf16[27,32,32]{2,1,0:T(8,128)(2,1)S(1)}, bf16[27,32,32]{2,1,0:T(8,128)(2,1)S(1)}, bf16[27,32,32]{2,1,0:T(8,128)(2,1)S(1)}, bf16[27,32,32]{2,1,0:T(8,128)(2,1)S(1)}) fusion(f32[27,128,32]{2,1,0:T(8,128)} %get-tuple-element.8, s32[]{:T(128)S(6)} %select_n.30, s32[]{:T(128)S(6)} %select_n.36, s32[]{:T(128)S(6)} %select_n.34, ...), kind=kLoop, calls=%fused_computation.9 | loop fusion | bytes 442384 | tf_op jit(solution)/shard_map/convert
  50.4 0.2 pad_maximum_fusion.1
  50.6 0.3 copy.49
  50.9 0.7 reshape.25
  51.6 22.4 %all_to_all.5 = bf16[32,2,1728]{2,1,0:T(2,128)(2,1)S(1)} all-to-all(bf16[32,2,1728]{2,1,0:T(2,128)(2,1)S(1)} %reshape.25), channel_id=1, replica_groups=mesh['gz'=32,'ch_0'=2,'ch_1'=2] {'gz'}, dimensions={0} | all-to-all | bytes 442368 | tf_op jit(solution)/shard_map/all_to_all | solution.py:19
  74.1 0.8 reshape.26
  74.9 0.5 convert_reduce_fusion
  75.3 0.6 broadcast_multiply_fusion
  (8 shorter events, 0.1 us)
Async XLA Ops:
  2.8 16.1 %copy-start = (bf16[8,8,32,128]{3,1,2,0:T(8,128)(2,1)}, bf16[8,8,32,128]{3,1,2,0:T(8,128)(2,1)S(1)}, u32[]{:S(2)}) copy-start(bf16[8,8,32,128]{3,1,2,0:T(8,128)(2,1)S(1)} %copy.56) | copy-start | bytes 1572868
  2.8 16.0 %collective-permute-start = (bf16[64,4096]{1,0:T(8,128)(2,1)S(1)}, bf16[64,4096]{1,0:T(8,128)(2,1)S(1)}, u32[]{:S(2)}, u32[]{:S(2)}) collective-permute-start(bf16[64,4096]{1,0:T(8,128)(2,1)S(1)} %bitcast.21), channel_id=1, source_target_pairs={{0,2},{2,0},{1,3},{3,1},{4,6},{6,4},{5,7},{7,5},{8,10},{10,8},{9,1... | collective-permute-start | bytes 1572872 | tf_op jit(solution)/shard_map/ppermute | solution.py:130
  7.7 17.4 %collective-permute-start.3 = (bf16[64,2048]{1,0:T(8,128)(2,1)}, bf16[64,2048]{1,0:T(8,128)(2,1)S(1)}, u32[]{:S(2)}, u32[]{:S(2)}) collective-permute-start(bf16[64,2048]{1,0:T(8,128)(2,1)} %get-tuple-element.22), channel_id=1, source_target_pairs={{4,0},{8,4},{12,8},{16,12},{20,16},{24,20},{28,24},{32,28},{36,32}... | collective-permute-start | bytes 786440 | tf_op jit(solution)/shard_map/ppermute | solution.py:132
  9.0 16.1 %collective-permute-start.2 = (bf16[64,2048]{1,0:T(8,128)(2,1)}, bf16[64,2048]{1,0:T(8,128)(2,1)}, u32[]{:S(2)}, u32[]{:S(2)}) collective-permute-start(bf16[64,2048]{1,0:T(8,128)(2,1)} %get-tuple-element.23), channel_id=1, source_target_pairs={{0,4},{4,8},{8,12},{12,16},{16,20},{20,24},{24,28},{28,32},{32,36}... | collective-permute-start | bytes 786440 | tf_op jit(solution)/shard_map/ppermute | solution.py:131
  18.8 8.2 %copy-start.1 = (bf16[64,4096]{1,0:T(8,128)(2,1)}, bf16[64,4096]{1,0:T(8,128)(2,1)S(1)}, u32[]{:S(2)}) copy-start(bf16[64,4096]{1,0:T(8,128)(2,1)S(1)} %collective-permute-done.far_ref) | copy-start | bytes 1572868
  18.9 13.5 %copy-start.2 = (bf16[27,128,128]{2,1,0:T(8,128)(2,1)S(1)}, bf16[27,128,128]{2,1,0:T(8,128)(2,1)}, u32[]{:S(2)}) copy-start(bf16[27,128,128]{2,1,0:T(8,128)(2,1)} %param.4) | copy-start | bytes 2654212
  18.9 19.1 %collective-permute-start.1 = (bf16[2,64,4096]{2,1,0:T(8,128)(2,1)S(1)}, bf16[2,64,4096]{2,1,0:T(8,128)(2,1)}, u32[]{:S(2)}, u32[]{:S(2)}) collective-permute-start(bf16[2,64,4096]{2,1,0:T(8,128)(2,1)S(1)} %pad_maximum_fusion), channel_id=1, source_target_pairs={{0,1},{1,0},{2,3},{3,2},{4,5},{5,4},{6,7},{7,6},{8,9},{9,8},{10,11... | collective-permute-start | bytes 3145736 | tf_op jit(solution)/shard_map/ppermute | solution.py:135
  19.1 10.6 %collective-permute-start.5 = (bf16[64,2048]{1,0:T(8,128)(2,1)S(1)}, bf16[64,2048]{1,0:T(8,128)(2,1)S(1)}, u32[]{:S(2)}, u32[]{:S(2)}) collective-permute-start(bf16[64,2048]{1,0:T(8,128)(2,1)S(1)} %get-tuple-element.20), channel_id=1, source_target_pairs={{4,0},{8,4},{12,8},{16,12},{20,16},{24,20},{28,24},{32,28},{36,32}... | collective-permute-start | bytes 786440 | tf_op jit(solution)/shard_map/ppermute | solution.py:134
  20.5 10.3 %collective-permute-start.4 = (bf16[64,2048]{1,0:T(8,128)(2,1)S(1)}, bf16[64,2048]{1,0:T(8,128)(2,1)S(1)}, u32[]{:S(2)}, u32[]{:S(2)}) collective-permute-start(bf16[64,2048]{1,0:T(8,128)(2,1)S(1)} %get-tuple-element.21), channel_id=1, source_target_pairs={{0,4},{4,8},{8,12},{12,16},{16,20},{20,24},{24,28},{28,32},{32,36}... | collective-permute-start | bytes 786440 | tf_op jit(solution)/shard_map/ppermute | solution.py:133
  25.1 9.3 %copy-start.3 = (bf16[64,2048]{1,0:T(8,128)(2,1)}, bf16[64,2048]{1,0:T(8,128)(2,1)S(1)}, u32[]{:S(2)}) copy-start(bf16[64,2048]{1,0:T(8,128)(2,1)S(1)} %collective-permute-done.3.hi_ref) | copy-start | bytes 786436
  27.0 11.1 %collective-permute-start.6 = (bf16[2,64,2048]{2,1,0:T(8,128)(2,1)}, bf16[2,64,2048]{2,1,0:T(8,128)(2,1)}, u32[]{:S(2)}, u32[]{:S(2)}) collective-permute-start(bf16[2,64,2048]{2,1,0:T(8,128)(2,1)} %pad_maximum_fusion.2), channel_id=1, source_target_pairs={{0,1},{1,0},{2,3},{3,2},{4,5},{5,4},{6,7},{7,6},{8,9},{9,8},{10,11... | collective-permute-start | bytes 1572872 | tf_op jit(solution)/shard_map/ppermute | solution.py:136
  29.7 4.7 %copy-start.4 = (bf16[64,2048]{1,0:T(8,128)(2,1)}, bf16[64,2048]{1,0:T(8,128)(2,1)S(1)}, u32[]{:S(2)}) copy-start(bf16[64,2048]{1,0:T(8,128)(2,1)S(1)} %collective-permute-done.5.fhi_ref) | copy-start | bytes 786436
  30.9 0.7 copy-start.5
  32.4 5.7 %collective-permute-start.7 = (bf16[2,64,2048]{2,1,0:T(8,128)(2,1)}, bf16[2,64,2048]{2,1,0:T(8,128)(2,1)}, u32[]{:S(2)}, u32[]{:S(2)}) collective-permute-start(bf16[2,64,2048]{2,1,0:T(8,128)(2,1)} %pad_maximum_fusion.3), channel_id=1, source_target_pairs={{0,1},{1,0},{2,3},{3,2},{4,5},{5,4},{6,7},{7,6},{8,9},{9,8},{10,11... | collective-permute-start | bytes 1572872 | tf_op jit(solution)/shard_map/ppermute | solution.py:137
  34.4 2.2 %copy-start.6 = (bf16[27,32,32]{2,1,0:T(8,128)(2,1)S(1)}, bf16[27,32,32]{2,1,0:T(8,128)(2,1)}, u32[]{:S(2)}) copy-start(bf16[27,32,32]{2,1,0:T(8,128)(2,1)} %get-tuple-element.14) | copy-start | bytes 165892

commit v15 on v10

--- a/solution.py
+++ b/solution.py
@@ -127,7 +127,8 @@
     swap = [(0, 1), (1, 0)]
     up = [(i, i + 1) for i in range(slabs - 1)]
     down = [(j, i) for i, j in up]
-    got_far = lax.ppermute(both, far, swap)
+    far_vol, far_cot = lax.ppermute((volume, cotangent), far, swap)
+    got_far = jnp.concatenate([far_vol, far_cot], axis=0).reshape(both.shape)
     low = lax.ppermute(both[:, -width:], "gz", up)
     high = lax.ppermute(both[:, :width], "gz", down)
     far_low = lax.ppermute(got_far[:, -width:], "gz", up)

time: 73.5 us -> 73.8 us (level)
  waiting for transfers between devices: 8.76 us -> 7.45 us
    ppermute x1 -> x2, waiting for transfers between devices: 4.32 us -> 2.99 us  [body(): far_vol, far_cot = lax.ppermute((volume, cotangent), far, swap)]
    concatenate x3, other arithmetic: 1.52 us -> 2.71 us  [by_group(): jnp.concatenate([lax.dynamic_slice_in_dim(array, group * size, size, dim)...]
    another operation x1, other arithmetic: 2.24 us -> 1.25 us  [body(): halos = lax.ppermute(jnp.stack([low, high, far_low, far_high]), near, swap)]
    dynamic_slice x1, local copies, waits for them, and re-layouts: 1.15 us -> 2.1 us  [by_group(): lax.dynamic_slice_in_dim(array, group * size, size, dim)]
    slice x1, local copies, waits for them, and re-layouts: 0.82 us -> 0.04 us  [body(): high = lax.ppermute(both[:, :width], 'gz', down)]
    unnamed x18 -> x24, local copies, waits for them, and re-layouts: 3.32 us -> 3.56 us
    ppermute x1 -> x2, starting transfers between devices: 4.07 us -> 4.16 us  [body(): far_vol, far_cot = lax.ppermute((volume, cotangent), far, swap)]
  transfers between devices with their start and end apart: 7 -> 8, of which waited for: 3 -> 3; matrix products, arithmetic and copies ran while one was open for 10% -> 14% of each run, Pallas kernels for 0% -> 0%
where the time goes in v15:
time: 73.8 us; the launch traced here: 73.4 us
  blocking collectives  22.4 us (30%)
  starting transfers between devices  17.1 us (23%)
  Pallas kernels  10.7 us (14%)
  local copies, waits for them, and re-layouts  9.81 us (13%)
  waiting for transfers between devices  7.45 us (10%)
  other arithmetic  5.17 us (7%)
  between operations  0.93 us (1%)
    all_to_all x1, blocking collectives, summed_on_arrival(): lax.all_to_all(blocks, axis, split_axis=0, concat_axis=0, tiled=True)  22.4 us
    pallas_call x1, Pallas kernels, fused(): pl.pallas_call(fused_kernel, out_shape=(jax.ShapeDtypeStruct((loc, planes...  10.7 us
    ppermute x1, starting transfers between devices, body(): low = lax.ppermute(both[:, -width:], 'gz', up)  5.26 us
    ppermute x1, starting transfers between devices, body(): far_low = lax.ppermute(got_far[:, -width:], 'gz', up)  4.69 us
    ppermute x2, starting transfers between devices, body(): far_vol, far_cot = lax.ppermute((volume, cotangent), far, swap)  4.16 us
    unnamed x24, local copies, waits for them, and re-layouts  3.56 us
    ppermute x1, waiting for transfers between devices, body(): far_high = lax.ppermute(got_far[:, :width], 'gz', down)  3.13 us
    ppermute x2, waiting for transfers between devices, body(): far_vol, far_cot = lax.ppermute((volume, cotangent), far, swap)  2.99 us
  transfers between devices with their start and end apart: 8, of which 3 were waited for; matrix products, arithmetic and copies ran while one was open for 14% of the time, Pallas kernels for 0%

profile of v15, /device:TPU:0, one launch (start us, length us, event | category | flops | bytes accessed | tf_op | source)
XLA Modules:
  0.0 73.4 jit_solution(15808415942016842956)
XLA Ops:
  0.6 4.1 %collective-permute-start = (bf16[32,2,16,128]{3,2,1,0:T(8,128)(2,1)}, bf16[32,2,16,128]{3,2,1,0:T(8,128)(2,1)S(1)}, u32[]{:S(2)}, u32[]{:S(2)}) collective-permute-start(bf16[32,2,16,128]{3,2,1,0:T(8,128)(2,1)} %param.3), channel_id=1, source_target_pairs={{0,2},{2,0},{1,3},{3,1},{4,6},{6,4},{5,7},{7,5},{8,10},{10,8},{9,1... | collective-permute-start | bytes 786440 | tf_op jit(solution)/shard_map/ppermute | solution.py:130
  4.7 0.1 collective-permute-start.1
  4.8 1.0 %constant_dynamic-update-slice_fusion.1 = bf16[64,2,16,128]{3,2,1,0:T(8,128)(2,1)S(1)} fusion(bf16[32,2,16,128]{3,2,1,0:T(8,128)(2,1)} %param.3), kind=kLoop, calls=%fused_computation.14 | loop fusion | bytes 524288
  5.8 1.0 %constant_dynamic-update-slice_fusion = bf16[64,2,16,128]{3,2,1,0:T(8,128)(2,1)S(1)} fusion(bf16[64,2,16,128]{3,2,1,0:T(8,128)(2,1)S(1)} %constant_dynamic-update-slice_fusion.1, bf16[32,2,16,128]{3,2,1,0:T(8,128)(2,1)} %param.5), kind=kLoop, calls=%fused_computation.13 | loop fusion | bytes 524288 | tf_op jit(solution)/shard_map/concatenate | solution.py:125
  6.7 0.2 copy.59
  7.0 0.0 copy-start
  7.0 1.3 %collective-permute-start.4 = (bf16[64,2048]{1,0:T(8,128)(2,1)S(1)}, bf16[64,2048]{1,0:T(8,128)(2,1)}, u32[]{:S(2)}, u32[]{:S(2)}) collective-permute-start(bf16[64,2048]{1,0:T(8,128)(2,1)S(1)} %get-tuple-element.22), channel_id=1, source_target_pairs={{4,0},{8,4},{12,8},{16,12},{20,16},{24,20},{28,24},{32,28},{36,32}... | collective-permute-start | bytes 786440 | tf_op jit(solution)/shard_map/ppermute | solution.py:133
  8.3 5.3 %collective-permute-start.3 = (bf16[64,2048]{1,0:T(8,128)(2,1)S(1)}, bf16[64,2048]{1,0:T(8,128)(2,1)}, u32[]{:S(2)}, u32[]{:S(2)}) collective-permute-start(bf16[64,2048]{1,0:T(8,128)(2,1)S(1)} %get-tuple-element.23), channel_id=1, source_target_pairs={{0,4},{4,8},{8,12},{12,16},{16,20},{20,24},{24,28},{28,32},{32,36}... | collective-permute-start | bytes 786440 | tf_op jit(solution)/shard_map/ppermute | solution.py:132
  13.6 0.2 stack_reshape.6
  13.8 0.0 collective-permute-done
  13.8 3.0 %collective-permute-done.1 = bf16[32,2,16,128]{3,2,1,0:T(8,128)(2,1)S(1)} collective-permute-done((bf16[32,2,16,128]{3,2,1,0:T(8,128)(2,1)}, bf16[32,2,16,128]{3,2,1,0:T(8,128)(2,1)S(1)}, u32[]{:S(2)}, u32[]{:S(2)}) %collective-permute-start.1) | collective-permute-done | bytes 262176 | tf_op jit(solution)/shard_map/ppermute | solution.py:130
  16.9 0.2 stack_reshape.7
  17.1 0.0 copy-done
  17.1 0.2 copy.58
  17.3 0.0 copy-start.1
  17.4 1.3 %collective-permute-start.6 = (bf16[64,2048]{1,0:T(8,128)(2,1)S(1)}, bf16[64,2048]{1,0:T(8,128)(2,1)S(1)}, u32[]{:S(2)}, u32[]{:S(2)}) collective-permute-start(bf16[64,2048]{1,0:T(8,128)(2,1)S(1)} %get-tuple-element.20), channel_id=1, source_target_pairs={{4,0},{8,4},{12,8},{16,12},{20,16},{24,20},{28,24},{32,28},{36,32}... | collective-permute-start | bytes 786440 | tf_op jit(solution)/shard_map/ppermute | solution.py:135
  18.7 0.0 copy-start.2
  18.7 4.7 %collective-permute-start.5 = (bf16[64,2048]{1,0:T(8,128)(2,1)S(1)}, bf16[64,2048]{1,0:T(8,128)(2,1)S(1)}, u32[]{:S(2)}, u32[]{:S(2)}) collective-permute-start(bf16[64,2048]{1,0:T(8,128)(2,1)S(1)} %get-tuple-element.21), channel_id=1, source_target_pairs={{0,4},{4,8},{8,12},{12,16},{16,20},{20,24},{24,28},{28,32},{32,36}... | collective-permute-start | bytes 786440 | tf_op jit(solution)/shard_map/ppermute | solution.py:134
  23.4 0.1 pad_maximum_fusion
  23.5 0.1 collective-permute-start.2
  23.6 0.0 collective-permute-done.4.hi_ref
  23.6 0.0 collective-permute-done.3.lo_ref
  23.6 3.1 %collective-permute-done.6.fhi_ref = bf16[64,2048]{1,0:T(8,128)(2,1)S(1)} collective-permute-done((bf16[64,2048]{1,0:T(8,128)(2,1)S(1)}, bf16[64,2048]{1,0:T(8,128)(2,1)S(1)}, u32[]{:S(2)}, u32[]{:S(2)}) %collective-permute-start.6) | collective-permute-done | bytes 262176 | tf_op jit(solution)/shard_map/ppermute | solution.py:135
  26.8 1.3 %collective-permute-done.5.flo_ref = bf16[64,2048]{1,0:T(8,128)(2,1)S(1)} collective-permute-done((bf16[64,2048]{1,0:T(8,128)(2,1)S(1)}, bf16[64,2048]{1,0:T(8,128)(2,1)S(1)}, u32[]{:S(2)}, u32[]{:S(2)}) %collective-permute-start.5) | collective-permute-done | bytes 262176 | tf_op jit(solution)/shard_map/ppermute | solution.py:134
  28.1 1.3 %pad_maximum_fusion.1 = bf16[4,64,2048]{2,1,0:T(8,128)(2,1)S(1)} fusion(bf16[1,64,2048]{2,1,0:T(8,128)(2,1)S(1)} %bitcast.34, bf16[1,64,2048]{2,1,0:T(8,128)(2,1)S(1)} %bitcast.35, bf16[1,64,2048]{2,1,0:T(8,128)(2,1)} %bitcast.1, bf16[1,64,2048]{2,1,0:T(8,128)(2,1)} %bitcast), kind=kLoop, calls=%fused_computation.2 | loop fusion | flops 1572864 | bytes 2097152 | tf_op jit(solution)/shard_map/stack | solution.py:137
  29.3 0.0 copy-done.1
  29.3 0.3 collective-permute-start.7
  29.6 0.0 copy-done.3
  29.6 0.0 copy-done.4
  29.7 2.1 %constant_dynamic-slice_fusion.2 = (bf16[27,32,32]{2,1,0:T(8,128)(2,1)}, bf16[27,32,32]{2,1,0:T(8,128)(2,1)}, bf16[27,32,32]{2,1,0:T(8,128)(2,1)}, bf16[27,32,32...) fusion(bf16[27,128,128]{2,1,0:T(8,128)(2,1)S(1)} %copy-done.2, ...), kind=kLoop, calls=%fused_computation.19 | loop fusion | bytes 774160 | tf_op jit(solution)/shard_map/dynamic_slice | solution.py:114
  31.8 0.2 copy.50
  32.0 1.5 %pad_maximum_fusion.4 = bf16[27,32,128]{2,1,0:T(8,128)(2,1)S(1)} fusion(bf16[27,32,32]{2,1,0:T(8,128)(2,1)} %get-tuple-element.18, bf16[27,32,32]{2,1,0:T(8,128)(2,1)} %get-tuple-element.19, bf16[27,32,32]{2,1,0:T(8,128)(2,1)} %get-tuple-element.13, bf16[27,32,32]{2,1,0:T(8,128)(2,1)S(1)} %get-tuple-element.16), kind=kLoop, calls=%fused_computation.11 | loop fusion | flops 884736 | bytes 442368 | tf_op jit(solution)/shard_map/concatenate | solution.py:113
  33.5 0.7 rev.3
  34.2 0.2 copy.52
  34.3 0.2 copy.51
  34.5 0.2 copy.53
  34.7 1.0 %pad_maximum_fusion.3 = bf16[27,128,32]{1,2,0:T(8,128)(2,1)} fusion(bf16[27,32,32]{1,2,0:T(8,128)(2,1)S(1)} %copy.53, bf16[27,32,32]{1,2,0:T(8,128)(2,1)S(1)} %copy.52, bf16[27,32,32]{1,2,0:T(8,128)(2,1)S(1)} %copy.51, bf16[27,32,32]{1,2,0:T(8,128)(2,1)S(1)} %copy.50), kind=kLoop, calls=%fused_computation.10 | loop fusion | flops 884736 | bytes 442368 | tf_op jit(solution)/shard_map/concatenate | solution.py:113
  35.6 0.0 collective-permute-done.2.near_ref
  35.6 0.0 collective-permute-done.7.hal_ref
  35.6 10.7 %shard_map.58 = (bf16[32,2,16,128]{3,2,1,0:T(8,128)(2,1)}, bf16[32,2,16,128]{3,2,1,0:T(8,128)(2,1)}, f32[27,128,32]{2,1,0:T(8,128)}) custom-call(bf16[64,4096]{1,0:T(8,128)(2,1)} %bitcast.28, bf16[64,4096]{1,0:T(8,128)(2,1)} %bitcast.30, bf16[2,64,4096]{2,1,0:T(8,128)(2,1)} %collective-permute-done.2.near_ref, ...), custom_call_target="tpu_custom_call" | custom-call | tf_op jit(solution)/shard_map/pallas_call | solution.py:98
  46.3 1.6 %dynamic-slice_convert_fusion.3 = (bf16[27,32,32]{2,1,0:T(8,128)(2,1)S(1)}, bf16[27,32,32]{2,1,0:T(8,128)(2,1)S(1)}, bf16[27,32,32]{2,1,0:T(8,128)(2,1)S(1)}, bf16[27,32,32]{2,1,0:T(8,128)(2,1)S(1)}) fusion(f32[27,128,32]{2,1,0:T(8,128)} %get-tuple-element.8, s32[]{:T(128)S(6)} %select_n.30, s32[]{:T(128)S(6)} %select_n.36, s32[]{:T(128)S(6)} %select_n.34, ...), kind=kLoop, calls=%fused_computation.9 | loop fusion | bytes 442384 | tf_op jit(solution)/shard_map/convert
  47.9 0.2 pad_maximum_fusion.2
  48.2 0.3 copy.49
  48.5 0.7 reshape.29
  49.2 22.4 %all_to_all.5 = bf16[32,2,1728]{2,1,0:T(2,128)(2,1)S(1)} all-to-all(bf16[32,2,1728]{2,1,0:T(2,128)(2,1)S(1)} %reshape.29), channel_id=1, replica_groups=mesh['gz'=32,'ch_0'=2,'ch_1'=2] {'gz'}, dimensions={0} | all-to-all | bytes 442368 | tf_op jit(solution)/shard_map/all_to_all | solution.py:19
  71.6 0.8 %reshape.30 = bf16[32,27,4,32]{3,2,1,0:T(4,128)(2,1)S(1)} reshape(bf16[32,2,1728]{2,1,0:T(2,128)(2,1)S(1)} %all_to_all.5) | data formatting | bytes 442368
  72.3 0.5 convert_reduce_fusion
  72.8 0.6 broadcast_multiply_fusion
  (11 shorter events, 0.1 us)
Async XLA Ops:
  0.6 13.2 %collective-permute-start = (bf16[32,2,16,128]{3,2,1,0:T(8,128)(2,1)}, bf16[32,2,16,128]{3,2,1,0:T(8,128)(2,1)S(1)}, u32[]{:S(2)}, u32[]{:S(2)}) collective-permute-start(bf16[32,2,16,128]{3,2,1,0:T(8,128)(2,1)} %param.3), channel_id=1, source_target_pairs={{0,2},{2,0},{1,3},{3,1},{4,6},{6,4},{5,7},{7,5},{8,10},{10,8},{9,1... | collective-permute-start | bytes 786440 | tf_op jit(solution)/shard_map/ppermute | solution.py:130
  4.7 12.1 %collective-permute-start.1 = (bf16[32,2,16,128]{3,2,1,0:T(8,128)(2,1)}, bf16[32,2,16,128]{3,2,1,0:T(8,128)(2,1)S(1)}, u32[]{:S(2)}, u32[]{:S(2)}) collective-permute-start(bf16[32,2,16,128]{3,2,1,0:T(8,128)(2,1)} %param.5), channel_id=1, source_target_pairs={{0,2},{2,0},{1,3},{3,1},{4,6},{6,4},{5,7},{7,5},{8,10},{10,8},{9,1... | collective-permute-start | bytes 786440 | tf_op jit(solution)/shard_map/ppermute | solution.py:130
  7.0 10.1 %copy-start = (bf16[8,8,32,128]{3,1,2,0:T(8,128)(2,1)}, bf16[8,8,32,128]{3,1,2,0:T(8,128)(2,1)S(1)}, u32[]{:S(2)}) copy-start(bf16[8,8,32,128]{3,1,2,0:T(8,128)(2,1)S(1)} %copy.59) | copy-start | bytes 1572868
  7.0 16.6 %collective-permute-start.4 = (bf16[64,2048]{1,0:T(8,128)(2,1)S(1)}, bf16[64,2048]{1,0:T(8,128)(2,1)}, u32[]{:S(2)}, u32[]{:S(2)}) collective-permute-start(bf16[64,2048]{1,0:T(8,128)(2,1)S(1)} %get-tuple-element.22), channel_id=1, source_target_pairs={{4,0},{8,4},{12,8},{16,12},{20,16},{24,20},{28,24},{32,28},{36,32}... | collective-permute-start | bytes 786440 | tf_op jit(solution)/shard_map/ppermute | solution.py:133
  8.3 15.3 %collective-permute-start.3 = (bf16[64,2048]{1,0:T(8,128)(2,1)S(1)}, bf16[64,2048]{1,0:T(8,128)(2,1)}, u32[]{:S(2)}, u32[]{:S(2)}) collective-permute-start(bf16[64,2048]{1,0:T(8,128)(2,1)S(1)} %get-tuple-element.23), channel_id=1, source_target_pairs={{0,4},{4,8},{8,12},{12,16},{16,20},{20,24},{24,28},{28,32},{32,36}... | collective-permute-start | bytes 786440 | tf_op jit(solution)/shard_map/ppermute | solution.py:132
  17.3 12.0 %copy-start.1 = (bf16[8,8,32,128]{3,1,2,0:T(8,128)(2,1)}, bf16[8,8,32,128]{3,1,2,0:T(8,128)(2,1)S(1)}, u32[]{:S(2)}) copy-start(bf16[8,8,32,128]{3,1,2,0:T(8,128)(2,1)S(1)} %copy.58) | copy-start | bytes 1572868
  17.4 9.4 %collective-permute-start.6 = (bf16[64,2048]{1,0:T(8,128)(2,1)S(1)}, bf16[64,2048]{1,0:T(8,128)(2,1)S(1)}, u32[]{:S(2)}, u32[]{:S(2)}) collective-permute-start(bf16[64,2048]{1,0:T(8,128)(2,1)S(1)} %get-tuple-element.20), channel_id=1, source_target_pairs={{4,0},{8,4},{12,8},{16,12},{20,16},{24,20},{28,24},{32,28},{36,32}... | collective-permute-start | bytes 786440 | tf_op jit(solution)/shard_map/ppermute | solution.py:135
  18.7 11.0 %copy-start.2 = (bf16[27,128,128]{2,1,0:T(8,128)(2,1)S(1)}, bf16[27,128,128]{2,1,0:T(8,128)(2,1)}, u32[]{:S(2)}) copy-start(bf16[27,128,128]{2,1,0:T(8,128)(2,1)} %param.4) | copy-start | bytes 2654212
  18.7 9.4 %collective-permute-start.5 = (bf16[64,2048]{1,0:T(8,128)(2,1)S(1)}, bf16[64,2048]{1,0:T(8,128)(2,1)S(1)}, u32[]{:S(2)}, u32[]{:S(2)}) collective-permute-start(bf16[64,2048]{1,0:T(8,128)(2,1)S(1)} %get-tuple-element.21), channel_id=1, source_target_pairs={{0,4},{4,8},{8,12},{12,16},{16,20},{20,24},{24,28},{28,32},{32,36}... | collective-permute-start | bytes 786440 | tf_op jit(solution)/shard_map/ppermute | solution.py:134
  23.5 12.1 %collective-permute-start.2 = (bf16[2,64,4096]{2,1,0:T(8,128)(2,1)S(1)}, bf16[2,64,4096]{2,1,0:T(8,128)(2,1)}, u32[]{:S(2)}, u32[]{:S(2)}) collective-permute-start(bf16[2,64,4096]{2,1,0:T(8,128)(2,1)S(1)} %pad_maximum_fusion), channel_id=1, source_target_pairs={{0,1},{1,0},{2,3},{3,2},{4,5},{5,4},{6,7},{7,6},{8,9},{9,8},{10,11... | collective-permute-start | bytes 3145736 | tf_op jit(solution)/shard_map/ppermute | solution.py:136
  26.8 2.9 %copy-start.3 = (bf16[64,2048]{1,0:T(8,128)(2,1)}, bf16[64,2048]{1,0:T(8,128)(2,1)S(1)}, u32[]{:S(2)}) copy-start(bf16[64,2048]{1,0:T(8,128)(2,1)S(1)} %collective-permute-done.6.fhi_ref) | copy-start | bytes 786436
  28.1 1.6 %copy-start.4 = (bf16[64,2048]{1,0:T(8,128)(2,1)}, bf16[64,2048]{1,0:T(8,128)(2,1)S(1)}, u32[]{:S(2)}) copy-start(bf16[64,2048]{1,0:T(8,128)(2,1)S(1)} %collective-permute-done.5.flo_ref) | copy-start | bytes 786436
  29.3 6.3 %collective-permute-start.7 = (bf16[4,64,2048]{2,1,0:T(8,128)(2,1)S(1)}, bf16[4,64,2048]{2,1,0:T(8,128)(2,1)}, u32[]{:S(2)}, u32[]{:S(2)}) collective-permute-start(bf16[4,64,2048]{2,1,0:T(8,128)(2,1)S(1)} %pad_maximum_fusion.1), channel_id=1, source_target_pairs={{0,1},{1,0},{2,3},{3,2},{4,5},{5,4},{6,7},{7,6},{8,9},{9,8},{10,11... | collective-permute-start | bytes 3145736 | tf_op jit(solution)/shard_map/ppermute | solution.py:137
  31.8 2.4 %copy-start.6 = (bf16[27,32,32]{2,1,0:T(8,128)(2,1)S(1)}, bf16[27,32,32]{2,1,0:T(8,128)(2,1)}, u32[]{:S(2)}) copy-start(bf16[27,32,32]{2,1,0:T(8,128)(2,1)} %get-tuple-element.14) | copy-start | bytes 165892
  31.8 2.5 %copy-start.5 = (bf16[27,32,32]{2,1,0:T(8,128)(2,1)S(1)}, bf16[27,32,32]{2,1,0:T(8,128)(2,1)}, u32[]{:S(2)}) copy-start(bf16[27,32,32]{2,1,0:T(8,128)(2,1)} %get-tuple-element.15) | copy-start | bytes 165892

commit v16 on v10

--- a/solution.py
+++ b/solution.py
@@ -80,7 +80,7 @@
                 sv, cstack, (((1,), (1,)), ((), ())), preferred_element_type=jnp.float32
             )
             for tap_x in range(3):
-                wg_ref[3 * pair + tap_x] = w[:, tap_x * loc : (tap_x + 1) * loc]
+                wg_ref[3 * pair + tap_x] = w[:, tap_x * loc : (tap_x + 1) * loc].astype(wg_ref.dtype)
     acc_o = shifted_sum(acc_o)
     acc_i = shifted_sum(acc_i)
     rows, cols = out_ref.shape[2], out_ref.shape[3]
@@ -100,7 +100,7 @@
         out_shape=(
             jax.ShapeDtypeStruct((loc, planes, width // ROW, ROW), jnp.bfloat16),
             jax.ShapeDtypeStruct((loc, planes, width // ROW, ROW), jnp.bfloat16),
-            jax.ShapeDtypeStruct((27, cin, loc), jnp.float32),
+            jax.ShapeDtypeStruct((27, cin, loc), jnp.bfloat16),
         ),
         scratch_shapes=[
             pltpu.VMEM((cin, flat), jnp.bfloat16),

time: 73.5 us -> 72.9 us (level)
  local copies, waits for them, and re-layouts: 9.16 us -> 8.11 us
  waiting for transfers between devices: 8.76 us -> 9.53 us
    another operation x1 -> x0, local copies, waits for them, and re-layouts: 1.6 us -> none
    dynamic_slice x1 -> x2, local copies, waits for them, and re-layouts: 1.15 us -> 2.48 us  [by_group(): lax.dynamic_slice_in_dim(array, group * size, size, dim)]
    slice x1, local copies, waits for them, and re-layouts: 0.82 us -> 0.03 us  [body(): high = lax.ppermute(both[:, :width], 'gz', down)]
    ppermute x1, waiting for transfers between devices: 4.32 us -> 5.09 us  [body(): got_far = lax.ppermute(both, far, swap)]
    unnamed x18 -> x20, local copies, waits for them, and re-layouts: 3.32 us -> 3.33 us
  transfers between devices with their start and end apart: 7 -> 7, of which waited for: 3 -> 3; matrix products, arithmetic and copies ran while one was open for 10% -> 9% of each run, Pallas kernels for 0% -> 0%
where the time goes in v16:
time: 72.9 us; the launch traced here: 72.6 us
  blocking collectives  22.1 us (30%)
  starting transfers between devices  16.6 us (23%)
  Pallas kernels  10.3 us (14%)
  waiting for transfers between devices  9.53 us (13%)
  local copies, waits for them, and re-layouts  8.11 us (11%)
  other arithmetic  4.92 us (7%)
  between operations  0.86 us (1%)
    all_to_all x1, blocking collectives, summed_on_arrival(): lax.all_to_all(blocks, axis, split_axis=0, concat_axis=0, tiled=True)  22.1 us
    pallas_call x1, Pallas kernels, fused(): pl.pallas_call(fused_kernel, out_shape=(jax.ShapeDtypeStruct((loc, planes...  10.3 us
    ppermute x1, starting transfers between devices, body(): low = lax.ppermute(both[:, -width:], 'gz', up)  5.25 us
    ppermute x1, waiting for transfers between devices, body(): got_far = lax.ppermute(both, far, swap)  5.09 us
    ppermute x1, starting transfers between devices, body(): far_low = lax.ppermute(got_far[:, -width:], 'gz', up)  4.56 us
    ppermute x1, starting transfers between devices, body(): got_far = lax.ppermute(both, far, swap)  4.07 us
    unnamed x20, local copies, waits for them, and re-layouts  3.33 us
    ppermute x1, waiting for transfers between devices, body(): far_high = lax.ppermute(got_far[:, :width], 'gz', down)  3.25 us
  transfers between devices with their start and end apart: 7, of which 3 were waited for; matrix products, arithmetic and copies ran while one was open for 9% of the time, Pallas kernels for 0%

profile of v16, /device:TPU:0, one launch (start us, length us, event | category | flops | bytes accessed | tf_op | source)
XLA Modules:
  0.0 72.6 jit_solution(10203941941605181807)
XLA Ops:
  0.6 1.0 %constant_dynamic-update-slice_fusion.1 = bf16[64,2,16,128]{3,2,1,0:T(8,128)(2,1)S(1)} fusion(bf16[32,2,16,128]{3,2,1,0:T(8,128)(2,1)} %param.3), kind=kLoop, calls=%fused_computation.9 | loop fusion | bytes 524288
  1.6 1.0 %constant_dynamic-update-slice_fusion = bf16[64,2,16,128]{3,2,1,0:T(8,128)(2,1)S(1)} fusion(bf16[64,2,16,128]{3,2,1,0:T(8,128)(2,1)S(1)} %constant_dynamic-update-slice_fusion.1, bf16[32,2,16,128]{3,2,1,0:T(8,128)(2,1)} %param.5), kind=kLoop, calls=%fused_computation.8 | loop fusion | bytes 524288 | tf_op jit(solution)/shard_map/concatenate | solution.py:125
  2.6 0.2 copy.56
  2.8 0.0 copy-start
  2.8 4.1 %collective-permute-start = (bf16[64,4096]{1,0:T(8,128)(2,1)S(1)}, bf16[64,4096]{1,0:T(8,128)(2,1)S(1)}, u32[]{:S(2)}, u32[]{:S(2)}) collective-permute-start(bf16[64,4096]{1,0:T(8,128)(2,1)S(1)} %bitcast.21), channel_id=1, source_target_pairs={{0,2},{2,0},{1,3},{3,1},{4,6},{6,4},{5,7},{7,5},{8,10},{10,8},{9,1... | collective-permute-start | bytes 1572872 | tf_op jit(solution)/shard_map/ppermute | solution.py:130
  6.9 1.3 %collective-permute-start.3 = (bf16[64,2048]{1,0:T(8,128)(2,1)S(1)}, bf16[64,2048]{1,0:T(8,128)(2,1)S(1)}, u32[]{:S(2)}, u32[]{:S(2)}) collective-permute-start(bf16[64,2048]{1,0:T(8,128)(2,1)S(1)} %get-tuple-element.22), channel_id=1, source_target_pairs={{4,0},{8,4},{12,8},{16,12},{20,16},{24,20},{28,24},{32,28},{36,32}... | collective-permute-start | bytes 786440 | tf_op jit(solution)/shard_map/ppermute | solution.py:132
  8.2 5.3 %collective-permute-start.2 = (bf16[64,2048]{1,0:T(8,128)(2,1)S(1)}, bf16[64,2048]{1,0:T(8,128)(2,1)}, u32[]{:S(2)}, u32[]{:S(2)}) collective-permute-start(bf16[64,2048]{1,0:T(8,128)(2,1)S(1)} %get-tuple-element.23), channel_id=1, source_target_pairs={{0,4},{4,8},{8,12},{12,16},{16,20},{20,24},{24,28},{28,32},{32,36}... | collective-permute-start | bytes 786440 | tf_op jit(solution)/shard_map/ppermute | solution.py:131
  13.5 0.2 stack_reshape.3
  13.7 0.0 copy-done
  13.7 5.1 %collective-permute-done.far_ref = bf16[64,4096]{1,0:T(8,128)(2,1)S(1)} collective-permute-done((bf16[64,4096]{1,0:T(8,128)(2,1)S(1)}, bf16[64,4096]{1,0:T(8,128)(2,1)S(1)}, u32[]{:S(2)}, u32[]{:S(2)}) %collective-permute-start) | collective-permute-done | bytes 524320 | tf_op jit(solution)/shard_map/ppermute | solution.py:130
  18.8 0.0 copy-start.1
  18.9 1.3 %collective-permute-start.5 = (bf16[64,2048]{1,0:T(8,128)(2,1)S(1)}, bf16[64,2048]{1,0:T(8,128)(2,1)S(1)}, u32[]{:S(2)}, u32[]{:S(2)}) collective-permute-start(bf16[64,2048]{1,0:T(8,128)(2,1)S(1)} %get-tuple-element.20), channel_id=1, source_target_pairs={{4,0},{8,4},{12,8},{16,12},{20,16},{24,20},{28,24},{32,28},{36,32}... | collective-permute-start | bytes 786440 | tf_op jit(solution)/shard_map/ppermute | solution.py:134
  20.2 4.6 %collective-permute-start.4 = (bf16[64,2048]{1,0:T(8,128)(2,1)S(1)}, bf16[64,2048]{1,0:T(8,128)(2,1)S(1)}, u32[]{:S(2)}, u32[]{:S(2)}) collective-permute-start(bf16[64,2048]{1,0:T(8,128)(2,1)S(1)} %get-tuple-element.21), channel_id=1, source_target_pairs={{0,4},{4,8},{8,12},{12,16},{16,20},{20,24},{24,28},{28,32},{32,36}... | collective-permute-start | bytes 786440 | tf_op jit(solution)/shard_map/ppermute | solution.py:133
  24.7 0.1 pad_maximum_fusion
  24.8 0.0 copy-done.1
  24.8 0.1 collective-permute-start.1
  24.9 0.0 collective-permute-done.3.hi_ref
  25.0 0.0 copy-start.3
  25.0 0.0 collective-permute-done.2.lo_ref
  25.0 3.3 %collective-permute-done.5.fhi_ref = bf16[64,2048]{1,0:T(8,128)(2,1)S(1)} collective-permute-done((bf16[64,2048]{1,0:T(8,128)(2,1)S(1)}, bf16[64,2048]{1,0:T(8,128)(2,1)S(1)}, u32[]{:S(2)}, u32[]{:S(2)}) %collective-permute-start.5) | collective-permute-done | bytes 262176 | tf_op jit(solution)/shard_map/ppermute | solution.py:134
  28.2 0.0 copy-start.4
  28.2 1.2 %collective-permute-done.4.flo_ref = bf16[64,2048]{1,0:T(8,128)(2,1)S(1)} collective-permute-done((bf16[64,2048]{1,0:T(8,128)(2,1)S(1)}, bf16[64,2048]{1,0:T(8,128)(2,1)S(1)}, u32[]{:S(2)}, u32[]{:S(2)}) %collective-permute-start.4) | collective-permute-done | bytes 262176 | tf_op jit(solution)/shard_map/ppermute | solution.py:133
  29.4 0.0 copy-start.5
  29.4 2.2 %pad_maximum_fusion.1 = bf16[4,64,2048]{2,1,0:T(8,128)(2,1)} fusion(bf16[1,64,2048]{2,1,0:T(8,128)(2,1)S(1)} %bitcast.28, bf16[1,64,2048]{2,1,0:T(8,128)(2,1)S(1)} %bitcast.29, bf16[1,64,2048]{2,1,0:T(8,128)(2,1)S(1)} %bitcast.27, bf16[1,64,2048]{2,1,0:T(8,128)(2,1)} %bitcast.1), kind=kLoop, calls=%fused_computation.2 | loop fusion | flops 1572864 | bytes 2097152 | tf_op jit(solution)/shard_map/stack | solution.py:136
  31.6 0.0 copy-done.3
  31.6 0.0 copy-done.4
  31.6 0.0 copy-done.5
  31.6 0.1 collective-permute-start.6
  31.7 0.0 copy-done.2
  31.7 1.2 %constant_dynamic-slice_fusion.6 = (bf16[27,32,32]{2,1,0:T(8,128)(2,1)S(1)}, bf16[27,32,32]{2,1,0:T(8,128)(2,1)S(1)}, bf16[27,32,32]{2,1,0:T(8,128)(2,1)S(1)}, b...) fusion(bf16[27,128,128]{2,1,0:T(8,128)(2,1)S(1)} %copy-done.2, ...), kind=kLoop, calls=%fused_computation.16 | loop fusion | bytes 774160 | tf_op jit(solution)/shard_map/dynamic_slice | solution.py:114
  32.9 0.2 copy.50
  33.1 0.3 pad_maximum_fusion.4
  33.4 0.7 rev.3
  34.1 0.2 copy.52
  34.2 0.2 copy.51
  34.4 0.2 copy.53
  34.6 1.0 %pad_maximum_fusion.3 = bf16[27,128,32]{1,2,0:T(8,128)(2,1)} fusion(bf16[27,32,32]{1,2,0:T(8,128)(2,1)S(1)} %copy.53, bf16[27,32,32]{1,2,0:T(8,128)(2,1)S(1)} %copy.52, bf16[27,32,32]{1,2,0:T(8,128)(2,1)S(1)} %copy.51, bf16[27,32,32]{1,2,0:T(8,128)(2,1)S(1)} %copy.50), kind=kLoop, calls=%fused_computation.5 | loop fusion | flops 884736 | bytes 442368 | tf_op jit(solution)/shard_map/concatenate | solution.py:113
  35.6 0.0 collective-permute-done.1.near_ref
  35.6 0.0 collective-permute-done.6.hal_ref
  35.6 10.3 %shard_map.58 = (bf16[32,2,16,128]{3,2,1,0:T(8,128)(2,1)}, bf16[32,2,16,128]{3,2,1,0:T(8,128)(2,1)}, bf16[27,128,32]{2,1,0:T(8,128)(2,1)}) custom-call(bf16[64,4096]{1,0:T(8,128)(2,1)} %bitcast.23, bf16[64,4096]{1,0:T(8,128)(2,1)} %copy-done.1, bf16[2,64,4096]{2,1,0:T(8,128)(2,1)} %collective-permute-done.1.near_ref, ...), custom_call_target="tpu_custom_call" | custom-call | tf_op jit(solution)/shard_map/pallas_call | solution.py:98
  45.9 1.3 %constant_dynamic-slice_fusion.3 = (bf16[27,32,32]{2,1,0:T(8,128)(2,1)S(1)}, bf16[27,32,32]{2,1,0:T(8,128)(2,1)S(1)}, bf16[27,32,32]{2,1,0:T(8,128)(2,1)S(1)}, bf16[27,32,32]{2,1,0:T(8,128)(2,1)S(1)}) fusion(bf16[27,128,32]{2,1,0:T(8,128)(2,1)} %get-tuple-element.8, s32[]{:T(128)S(6)} %select_n.30, s32[]{:T(128)S(6)} %select_n.36, s32[]{:T(128)S(6)} %select_n.34, ...), kind=kLoop, calls=%fused_computation.13 | loop fusion | bytes 442384 | tf_op jit(solution)/shard_map/dynamic_slice | solution.py:114
  47.3 0.2 pad_maximum_fusion.2
  47.5 0.3 copy.49
  47.8 0.7 %reshape.26 = bf16[32,2,1728]{2,1,0:T(2,128)(2,1)S(1)} reshape(bf16[32,27,4,32]{3,2,1,0:T(4,128)(2,1)S(1)} %copy.49) | data formatting | bytes 442368
  48.5 22.1 %all_to_all.5 = bf16[32,2,1728]{2,1,0:T(2,128)(2,1)S(1)} all-to-all(bf16[32,2,1728]{2,1,0:T(2,128)(2,1)S(1)} %reshape.26), channel_id=1, replica_groups=mesh['gz'=32,'ch_0'=2,'ch_1'=2] {'gz'}, dimensions={0} | all-to-all | bytes 442368 | tf_op jit(solution)/shard_map/all_to_all | solution.py:19
  70.7 0.8 %reshape.27 = bf16[32,27,4,32]{3,2,1,0:T(4,128)(2,1)S(1)} reshape(bf16[32,2,1728]{2,1,0:T(2,128)(2,1)S(1)} %all_to_all.5) | data formatting | bytes 442368
  71.4 0.5 convert_reduce_fusion
  71.9 0.6 broadcast_multiply_fusion
  (3 shorter events, 0.1 us)
Async XLA Ops:
  2.8 10.9 %copy-start = (bf16[8,8,32,128]{3,1,2,0:T(8,128)(2,1)}, bf16[8,8,32,128]{3,1,2,0:T(8,128)(2,1)S(1)}, u32[]{:S(2)}) copy-start(bf16[8,8,32,128]{3,1,2,0:T(8,128)(2,1)S(1)} %copy.56) | copy-start | bytes 1572868
  2.8 16.0 %collective-permute-start = (bf16[64,4096]{1,0:T(8,128)(2,1)S(1)}, bf16[64,4096]{1,0:T(8,128)(2,1)S(1)}, u32[]{:S(2)}, u32[]{:S(2)}) collective-permute-start(bf16[64,4096]{1,0:T(8,128)(2,1)S(1)} %bitcast.21), channel_id=1, source_target_pairs={{0,2},{2,0},{1,3},{3,1},{4,6},{6,4},{5,7},{7,5},{8,10},{10,8},{9,1... | collective-permute-start | bytes 1572872 | tf_op jit(solution)/shard_map/ppermute | solution.py:130
  6.9 18.0 %collective-permute-start.3 = (bf16[64,2048]{1,0:T(8,128)(2,1)S(1)}, bf16[64,2048]{1,0:T(8,128)(2,1)S(1)}, u32[]{:S(2)}, u32[]{:S(2)}) collective-permute-start(bf16[64,2048]{1,0:T(8,128)(2,1)S(1)} %get-tuple-element.22), channel_id=1, source_target_pairs={{4,0},{8,4},{12,8},{16,12},{20,16},{24,20},{28,24},{32,28},{36,32}... | collective-permute-start | bytes 786440 | tf_op jit(solution)/shard_map/ppermute | solution.py:132
  8.2 16.7 %collective-permute-start.2 = (bf16[64,2048]{1,0:T(8,128)(2,1)S(1)}, bf16[64,2048]{1,0:T(8,128)(2,1)}, u32[]{:S(2)}, u32[]{:S(2)}) collective-permute-start(bf16[64,2048]{1,0:T(8,128)(2,1)S(1)} %get-tuple-element.23), channel_id=1, source_target_pairs={{0,4},{4,8},{8,12},{12,16},{16,20},{20,24},{24,28},{28,32},{32,36}... | collective-permute-start | bytes 786440 | tf_op jit(solution)/shard_map/ppermute | solution.py:131
  18.8 6.0 %copy-start.1 = (bf16[64,4096]{1,0:T(8,128)(2,1)}, bf16[64,4096]{1,0:T(8,128)(2,1)S(1)}, u32[]{:S(2)}) copy-start(bf16[64,4096]{1,0:T(8,128)(2,1)S(1)} %collective-permute-done.far_ref) | copy-start | bytes 1572868
  18.9 9.4 %collective-permute-start.5 = (bf16[64,2048]{1,0:T(8,128)(2,1)S(1)}, bf16[64,2048]{1,0:T(8,128)(2,1)S(1)}, u32[]{:S(2)}, u32[]{:S(2)}) collective-permute-start(bf16[64,2048]{1,0:T(8,128)(2,1)S(1)} %get-tuple-element.20), channel_id=1, source_target_pairs={{4,0},{8,4},{12,8},{16,12},{20,16},{24,20},{28,24},{32,28},{36,32}... | collective-permute-start | bytes 786440 | tf_op jit(solution)/shard_map/ppermute | solution.py:134
  20.2 9.2 %collective-permute-start.4 = (bf16[64,2048]{1,0:T(8,128)(2,1)S(1)}, bf16[64,2048]{1,0:T(8,128)(2,1)S(1)}, u32[]{:S(2)}, u32[]{:S(2)}) collective-permute-start(bf16[64,2048]{1,0:T(8,128)(2,1)S(1)} %get-tuple-element.21), channel_id=1, source_target_pairs={{0,4},{4,8},{8,12},{12,16},{16,20},{20,24},{24,28},{28,32},{32,36}... | collective-permute-start | bytes 786440 | tf_op jit(solution)/shard_map/ppermute | solution.py:133
  24.8 10.7 %collective-permute-start.1 = (bf16[2,64,4096]{2,1,0:T(8,128)(2,1)S(1)}, bf16[2,64,4096]{2,1,0:T(8,128)(2,1)}, u32[]{:S(2)}, u32[]{:S(2)}) collective-permute-start(bf16[2,64,4096]{2,1,0:T(8,128)(2,1)S(1)} %pad_maximum_fusion), channel_id=1, source_target_pairs={{0,1},{1,0},{2,3},{3,2},{4,5},{5,4},{6,7},{7,6},{8,9},{9,8},{10,11... | collective-permute-start | bytes 3145736 | tf_op jit(solution)/shard_map/ppermute | solution.py:135
  25.0 6.6 %copy-start.3 = (bf16[64,2048]{1,0:T(8,128)(2,1)}, bf16[64,2048]{1,0:T(8,128)(2,1)S(1)}, u32[]{:S(2)}) copy-start(bf16[64,2048]{1,0:T(8,128)(2,1)S(1)} %collective-permute-done.3.hi_ref) | copy-start | bytes 786436
  28.2 3.4 %copy-start.4 = (bf16[64,2048]{1,0:T(8,128)(2,1)}, bf16[64,2048]{1,0:T(8,128)(2,1)S(1)}, u32[]{:S(2)}) copy-start(bf16[64,2048]{1,0:T(8,128)(2,1)S(1)} %collective-permute-done.5.fhi_ref) | copy-start | bytes 786436
  29.4 2.2 %copy-start.5 = (bf16[64,2048]{1,0:T(8,128)(2,1)}, bf16[64,2048]{1,0:T(8,128)(2,1)S(1)}, u32[]{:S(2)}) copy-start(bf16[64,2048]{1,0:T(8,128)(2,1)S(1)} %collective-permute-done.4.flo_ref) | copy-start | bytes 786436
  29.4 2.3 %copy-start.2 = (bf16[27,128,128]{2,1,0:T(8,128)(2,1)S(1)}, bf16[27,128,128]{2,1,0:T(8,128)(2,1)}, u32[]{:S(2)}) copy-start(bf16[27,128,128]{2,1,0:T(8,128)(2,1)} %param.4) | copy-start | bytes 2654212
  31.6 4.0 %collective-permute-start.6 = (bf16[4,64,2048]{2,1,0:T(8,128)(2,1)}, bf16[4,64,2048]{2,1,0:T(8,128)(2,1)}, u32[]{:S(2)}, u32[]{:S(2)}) collective-permute-start(bf16[4,64,2048]{2,1,0:T(8,128)(2,1)} %pad_maximum_fusion.1), channel_id=1, source_target_pairs={{0,1},{1,0},{2,3},{3,2},{4,5},{5,4},{6,7},{7,6},{8,9},{9,8},{10,11... | collective-permute-start | bytes 3145736 | tf_op jit(solution)/shard_map/ppermute | solution.py:136

commit v17 on v16

--- a/solution.py
+++ b/solution.py
@@ -1,3 +1,4 @@
+import functools
 import math
 
 import jax
@@ -21,7 +22,7 @@
 
 def fused_kernel(
     own_ref, far_ref, near_ref, lo_ref, hi_ref, flo_ref, fhi_ref, hal_ref, wf_ref, wb_ref,
-    out_ref, ing_ref, wg_ref, vs_ref, cs_ref,
+    out_ref, ing_ref, wg_ref, vs_ref, cs_ref, *, scale,
 ):
     both = own_ref.shape[0]
     loc = both // 2
@@ -80,7 +81,7 @@
                 sv, cstack, (((1,), (1,)), ((), ())), preferred_element_type=jnp.float32
             )
             for tap_x in range(3):
-                wg_ref[3 * pair + tap_x] = w[:, tap_x * loc : (tap_x + 1) * loc].astype(wg_ref.dtype)
+                wg_ref[3 * pair + tap_x] = (w[:, tap_x * loc : (tap_x + 1) * loc] * scale).astype(wg_ref.dtype)
     acc_o = shifted_sum(acc_o)
     acc_i = shifted_sum(acc_i)
     rows, cols = out_ref.shape[2], out_ref.shape[3]
@@ -90,13 +91,13 @@
             ref[:, z] = part.astype(ref.dtype)
 
 
-def fused(own, far, near, low, high, far_low, far_high, halos, wf, wb, planes, width):
+def fused(own, far, near, low, high, far_low, far_high, halos, wf, wb, planes, width, scale):
     both = own.shape[0]
     loc = both // 2
     cin = 4 * loc
     flat = (planes + 2) * (width + 2 * ROW)
     return pl.pallas_call(
-        fused_kernel,
+        functools.partial(fused_kernel, scale=scale),
         out_shape=(
             jax.ShapeDtypeStruct((loc, planes, width // ROW, ROW), jnp.bfloat16),
             jax.ShapeDtypeStruct((loc, planes, width // ROW, ROW), jnp.bfloat16),
@@ -146,15 +147,14 @@
     weight_rows = by_group(weight_rows, order, out_local, 2)
     wb = weight_rows[::-1].reshape(9, 3 * in_local, cout)
     out, ing, wg = fused(
-        both, got_far, got_near, low, high, far_low, far_high, halos, wf, wb, planes_local, width
+        both, got_far, got_near, low, high, far_low, far_high, halos, wf, wb, planes_local, width,
+        1.0 / math.sqrt(voxels),
     )
     wg = by_group(wg, order, in_local, 1)
     shape = (out_local, planes_local, grid_rows, grid_cols)
     out = out.reshape(shape)
     ing = ing.reshape(shape)
-    weight_grad = summed_on_arrival(wg.astype(jnp.bfloat16), "gz", 1) * jnp.float32(
-        1.0 / math.sqrt(voxels)
-    )
+    weight_grad = summed_on_arrival(wg.astype(jnp.bfloat16), "gz", 1)
     return out, ing, weight_grad
 
 

time: 72.9 us -> 72.9 us (level)
  no operation moved by 1% of the time
where the time goes in v17:
time: 72.9 us; the launch traced here: 72.5 us
  blocking collectives  22.1 us (30%)
  starting transfers between devices  16.6 us (23%)
  Pallas kernels  10.4 us (14%)
  waiting for transfers between devices  9.53 us (13%)
  local copies, waits for them, and re-layouts  8.11 us (11%)
  other arithmetic  4.91 us (7%)
  between operations  0.86 us (1%)
    all_to_all x1, blocking collectives, summed_on_arrival(): lax.all_to_all(blocks, axis, split_axis=0, concat_axis=0, tiled=True)  22.1 us
    pallas_call x1, Pallas kernels, fused(): pl.pallas_call(functools.partial(fused_kernel, scale=scale), out_shape=(j...  10.4 us
    ppermute x1, starting transfers between devices, body(): low = lax.ppermute(both[:, -width:], 'gz', up)  5.25 us
    ppermute x1, waiting for transfers between devices, body(): got_far = lax.ppermute(both, far, swap)  5.09 us
    ppermute x1, starting transfers between devices, body(): far_low = lax.ppermute(got_far[:, -width:], 'gz', up)  4.56 us
    ppermute x1, starting transfers between devices, body(): got_far = lax.ppermute(both, far, swap)  4.07 us
    unnamed x20, local copies, waits for them, and re-layouts  3.33 us
    ppermute x1, waiting for transfers between devices, body(): far_high = lax.ppermute(got_far[:, :width], 'gz', down)  3.25 us
  transfers between devices with their start and end apart: 7, of which 3 were waited for; matrix products, arithmetic and copies ran while one was open for 9% of the time, Pallas kernels for 0%

profile of v17, /device:TPU:0, one launch (start us, length us, event | category | flops | bytes accessed | tf_op | source)
XLA Modules:
  0.0 72.5 jit_solution(18234391552548110007)
XLA Ops:
  0.6 1.0 %constant_dynamic-update-slice_fusion.1 = bf16[64,2,16,128]{3,2,1,0:T(8,128)(2,1)S(1)} fusion(bf16[32,2,16,128]{3,2,1,0:T(8,128)(2,1)} %param.3), kind=kLoop, calls=%fused_computation.8 | loop fusion | bytes 524288
  1.6 1.0 %constant_dynamic-update-slice_fusion = bf16[64,2,16,128]{3,2,1,0:T(8,128)(2,1)S(1)} fusion(bf16[64,2,16,128]{3,2,1,0:T(8,128)(2,1)S(1)} %constant_dynamic-update-slice_fusion.1, bf16[32,2,16,128]{3,2,1,0:T(8,128)(2,1)} %param.5), kind=kLoop, calls=%fused_computation.7 | loop fusion | bytes 524288 | tf_op jit(solution)/shard_map/concatenate | solution.py:126
  2.6 0.2 copy.56
  2.8 0.0 copy-start
  2.8 4.1 %collective-permute-start = (bf16[64,4096]{1,0:T(8,128)(2,1)S(1)}, bf16[64,4096]{1,0:T(8,128)(2,1)S(1)}, u32[]{:S(2)}, u32[]{:S(2)}) collective-permute-start(bf16[64,4096]{1,0:T(8,128)(2,1)S(1)} %bitcast.21), channel_id=1, source_target_pairs={{0,2},{2,0},{1,3},{3,1},{4,6},{6,4},{5,7},{7,5},{8,10},{10,8},{9,1... | collective-permute-start | bytes 1572872 | tf_op jit(solution)/shard_map/ppermute | solution.py:131
  6.9 1.3 %collective-permute-start.3 = (bf16[64,2048]{1,0:T(8,128)(2,1)S(1)}, bf16[64,2048]{1,0:T(8,128)(2,1)S(1)}, u32[]{:S(2)}, u32[]{:S(2)}) collective-permute-start(bf16[64,2048]{1,0:T(8,128)(2,1)S(1)} %get-tuple-element.22), channel_id=1, source_target_pairs={{4,0},{8,4},{12,8},{16,12},{20,16},{24,20},{28,24},{32,28},{36,32}... | collective-permute-start | bytes 786440 | tf_op jit(solution)/shard_map/ppermute | solution.py:133
  8.2 5.3 %collective-permute-start.2 = (bf16[64,2048]{1,0:T(8,128)(2,1)S(1)}, bf16[64,2048]{1,0:T(8,128)(2,1)}, u32[]{:S(2)}, u32[]{:S(2)}) collective-permute-start(bf16[64,2048]{1,0:T(8,128)(2,1)S(1)} %get-tuple-element.23), channel_id=1, source_target_pairs={{0,4},{4,8},{8,12},{12,16},{16,20},{20,24},{24,28},{28,32},{32,36}... | collective-permute-start | bytes 786440 | tf_op jit(solution)/shard_map/ppermute | solution.py:132
  13.5 0.2 stack_reshape.3
  13.7 0.0 copy-done
  13.7 5.1 %collective-permute-done.far_ref = bf16[64,4096]{1,0:T(8,128)(2,1)S(1)} collective-permute-done((bf16[64,4096]{1,0:T(8,128)(2,1)S(1)}, bf16[64,4096]{1,0:T(8,128)(2,1)S(1)}, u32[]{:S(2)}, u32[]{:S(2)}) %collective-permute-start) | collective-permute-done | bytes 524320 | tf_op jit(solution)/shard_map/ppermute | solution.py:131
  18.8 0.0 copy-start.1
  18.9 1.3 %collective-permute-start.5 = (bf16[64,2048]{1,0:T(8,128)(2,1)S(1)}, bf16[64,2048]{1,0:T(8,128)(2,1)S(1)}, u32[]{:S(2)}, u32[]{:S(2)}) collective-permute-start(bf16[64,2048]{1,0:T(8,128)(2,1)S(1)} %get-tuple-element.20), channel_id=1, source_target_pairs={{4,0},{8,4},{12,8},{16,12},{20,16},{24,20},{28,24},{32,28},{36,32}... | collective-permute-start | bytes 786440 | tf_op jit(solution)/shard_map/ppermute | solution.py:135
  20.2 4.6 %collective-permute-start.4 = (bf16[64,2048]{1,0:T(8,128)(2,1)S(1)}, bf16[64,2048]{1,0:T(8,128)(2,1)S(1)}, u32[]{:S(2)}, u32[]{:S(2)}) collective-permute-start(bf16[64,2048]{1,0:T(8,128)(2,1)S(1)} %get-tuple-element.21), channel_id=1, source_target_pairs={{0,4},{4,8},{8,12},{12,16},{16,20},{20,24},{24,28},{28,32},{32,36}... | collective-permute-start | bytes 786440 | tf_op jit(solution)/shard_map/ppermute | solution.py:134
  24.7 0.1 pad_maximum_fusion
  24.8 0.0 copy-done.1
  24.8 0.1 collective-permute-start.1
  24.9 0.0 collective-permute-done.3.hi_ref
  25.0 0.0 copy-start.3
  25.0 0.0 collective-permute-done.2.lo_ref
  25.0 3.3 %collective-permute-done.5.fhi_ref = bf16[64,2048]{1,0:T(8,128)(2,1)S(1)} collective-permute-done((bf16[64,2048]{1,0:T(8,128)(2,1)S(1)}, bf16[64,2048]{1,0:T(8,128)(2,1)S(1)}, u32[]{:S(2)}, u32[]{:S(2)}) %collective-permute-start.5) | collective-permute-done | bytes 262176 | tf_op jit(solution)/shard_map/ppermute | solution.py:135
  28.2 0.0 copy-start.4
  28.2 1.2 %collective-permute-done.4.flo_ref = bf16[64,2048]{1,0:T(8,128)(2,1)S(1)} collective-permute-done((bf16[64,2048]{1,0:T(8,128)(2,1)S(1)}, bf16[64,2048]{1,0:T(8,128)(2,1)S(1)}, u32[]{:S(2)}, u32[]{:S(2)}) %collective-permute-start.4) | collective-permute-done | bytes 262176 | tf_op jit(solution)/shard_map/ppermute | solution.py:134
  29.4 0.0 copy-start.5
  29.4 0.0 copy-start.2
  29.4 2.2 %pad_maximum_fusion.1 = bf16[4,64,2048]{2,1,0:T(8,128)(2,1)} fusion(bf16[1,64,2048]{2,1,0:T(8,128)(2,1)S(1)} %bitcast.28, bf16[1,64,2048]{2,1,0:T(8,128)(2,1)S(1)} %bitcast.29, bf16[1,64,2048]{2,1,0:T(8,128)(2,1)S(1)} %bitcast.27, bf16[1,64,2048]{2,1,0:T(8,128)(2,1)} %bitcast.1), kind=kLoop, calls=%fused_computation.2 | loop fusion | flops 1572864 | bytes 2097152 | tf_op jit(solution)/shard_map/stack | solution.py:137
  31.6 0.0 copy-done.3
  31.6 0.0 copy-done.4
  31.6 0.0 copy-done.5
  31.6 0.1 collective-permute-start.6
  31.7 0.0 copy-done.2
  31.7 1.2 %constant_dynamic-slice_fusion.6 = (bf16[27,32,32]{2,1,0:T(8,128)(2,1)S(1)}, bf16[27,32,32]{2,1,0:T(8,128)(2,1)S(1)}, bf16[27,32,32]{2,1,0:T(8,128)(2,1)S(1)}, b...) fusion(bf16[27,128,128]{2,1,0:T(8,128)(2,1)S(1)} %copy-done.2, ...), kind=kLoop, calls=%fused_computation.15 | loop fusion | bytes 774160 | tf_op jit(solution)/shard_map/dynamic_slice | solution.py:115
  32.9 0.2 copy.50
  33.1 0.3 pad_maximum_fusion.4
  33.4 0.7 rev.3
  34.1 0.2 copy.52
  34.2 0.2 copy.51
  34.4 0.2 copy.53
  34.6 1.0 %pad_maximum_fusion.3 = bf16[27,128,32]{1,2,0:T(8,128)(2,1)} fusion(bf16[27,32,32]{1,2,0:T(8,128)(2,1)S(1)} %copy.53, bf16[27,32,32]{1,2,0:T(8,128)(2,1)S(1)} %copy.52, bf16[27,32,32]{1,2,0:T(8,128)(2,1)S(1)} %copy.51, bf16[27,32,32]{1,2,0:T(8,128)(2,1)S(1)} %copy.50), kind=kLoop, calls=%fused_computation.5 | loop fusion | flops 884736 | bytes 442368 | tf_op jit(solution)/shard_map/concatenate | solution.py:114
  35.6 0.0 collective-permute-done.1.near_ref
  35.6 0.0 collective-permute-done.6.hal_ref
  35.6 10.4 %shard_map.58 = (bf16[32,2,16,128]{3,2,1,0:T(8,128)(2,1)}, bf16[32,2,16,128]{3,2,1,0:T(8,128)(2,1)}, bf16[27,128,32]{2,1,0:T(8,128)(2,1)}) custom-call(bf16[64,4096]{1,0:T(8,128)(2,1)} %bitcast.23, bf16[64,4096]{1,0:T(8,128)(2,1)} %copy-done.1, bf16[2,64,4096]{2,1,0:T(8,128)(2,1)} %collective-permute-done.1.near_ref, ...), custom_call_target="tpu_custom_call" | custom-call | tf_op jit(solution)/shard_map/pallas_call | solution.py:99
  45.9 1.3 %constant_dynamic-slice_fusion.3 = (bf16[27,32,32]{2,1,0:T(8,128)(2,1)S(1)}, bf16[27,32,32]{2,1,0:T(8,128)(2,1)S(1)}, bf16[27,32,32]{2,1,0:T(8,128)(2,1)S(1)}, bf16[27,32,32]{2,1,0:T(8,128)(2,1)S(1)}) fusion(bf16[27,128,32]{2,1,0:T(8,128)(2,1)} %get-tuple-element.8, s32[]{:T(128)S(6)} %select_n.30, s32[]{:T(128)S(6)} %select_n.36, s32[]{:T(128)S(6)} %select_n.34, ...), kind=kLoop, calls=%fused_computation.12 | loop fusion | bytes 442384 | tf_op jit(solution)/shard_map/dynamic_slice | solution.py:115
  47.3 0.2 pad_maximum_fusion.2
  47.5 0.3 copy.49
  47.8 0.7 %reshape.26 = bf16[32,2,1728]{2,1,0:T(2,128)(2,1)S(1)} reshape(bf16[32,27,4,32]{3,2,1,0:T(4,128)(2,1)S(1)} %copy.49) | data formatting | bytes 442368
  48.6 22.1 %all_to_all.5 = bf16[32,2,1728]{2,1,0:T(2,128)(2,1)S(1)} all-to-all(bf16[32,2,1728]{2,1,0:T(2,128)(2,1)S(1)} %reshape.26), channel_id=1, replica_groups=mesh['gz'=32,'ch_0'=2,'ch_1'=2] {'gz'}, dimensions={0} | all-to-all | bytes 442368 | tf_op jit(solution)/shard_map/all_to_all | solution.py:20
  70.7 0.8 %reshape.27 = bf16[32,27,4,32]{3,2,1,0:T(4,128)(2,1)S(1)} reshape(bf16[32,2,1728]{2,1,0:T(2,128)(2,1)S(1)} %all_to_all.5) | data formatting | bytes 442368
  71.5 1.1 %convert_reduce_fusion = f32[27,4,32]{2,1,0:T(4,128)} fusion(bf16[32,27,4,32]{3,2,1,0:T(4,128)(2,1)S(1)} %reshape.27), kind=kLoop, calls=%fused_computation | loop fusion | flops 217728 | bytes 235008 | tf_op jit(solution)/shard_map/reduce_sum | solution.py:21
  (2 shorter events, 0.1 us)
Async XLA Ops:
  2.8 10.9 %copy-start = (bf16[8,8,32,128]{3,1,2,0:T(8,128)(2,1)}, bf16[8,8,32,128]{3,1,2,0:T(8,128)(2,1)S(1)}, u32[]{:S(2)}) copy-start(bf16[8,8,32,128]{3,1,2,0:T(8,128)(2,1)S(1)} %copy.56) | copy-start | bytes 1572868
  2.8 16.0 %collective-permute-start = (bf16[64,4096]{1,0:T(8,128)(2,1)S(1)}, bf16[64,4096]{1,0:T(8,128)(2,1)S(1)}, u32[]{:S(2)}, u32[]{:S(2)}) collective-permute-start(bf16[64,4096]{1,0:T(8,128)(2,1)S(1)} %bitcast.21), channel_id=1, source_target_pairs={{0,2},{2,0},{1,3},{3,1},{4,6},{6,4},{5,7},{7,5},{8,10},{10,8},{9,1... | collective-permute-start | bytes 1572872 | tf_op jit(solution)/shard_map/ppermute | solution.py:131
  6.9 18.0 %collective-permute-start.3 = (bf16[64,2048]{1,0:T(8,128)(2,1)S(1)}, bf16[64,2048]{1,0:T(8,128)(2,1)S(1)}, u32[]{:S(2)}, u32[]{:S(2)}) collective-permute-start(bf16[64,2048]{1,0:T(8,128)(2,1)S(1)} %get-tuple-element.22), channel_id=1, source_target_pairs={{4,0},{8,4},{12,8},{16,12},{20,16},{24,20},{28,24},{32,28},{36,32}... | collective-permute-start | bytes 786440 | tf_op jit(solution)/shard_map/ppermute | solution.py:133
  8.2 16.7 %collective-permute-start.2 = (bf16[64,2048]{1,0:T(8,128)(2,1)S(1)}, bf16[64,2048]{1,0:T(8,128)(2,1)}, u32[]{:S(2)}, u32[]{:S(2)}) collective-permute-start(bf16[64,2048]{1,0:T(8,128)(2,1)S(1)} %get-tuple-element.23), channel_id=1, source_target_pairs={{0,4},{4,8},{8,12},{12,16},{16,20},{20,24},{24,28},{28,32},{32,36}... | collective-permute-start | bytes 786440 | tf_op jit(solution)/shard_map/ppermute | solution.py:132
  18.8 6.0 %copy-start.1 = (bf16[64,4096]{1,0:T(8,128)(2,1)}, bf16[64,4096]{1,0:T(8,128)(2,1)S(1)}, u32[]{:S(2)}) copy-start(bf16[64,4096]{1,0:T(8,128)(2,1)S(1)} %collective-permute-done.far_ref) | copy-start | bytes 1572868
  18.9 9.4 %collective-permute-start.5 = (bf16[64,2048]{1,0:T(8,128)(2,1)S(1)}, bf16[64,2048]{1,0:T(8,128)(2,1)S(1)}, u32[]{:S(2)}, u32[]{:S(2)}) collective-permute-start(bf16[64,2048]{1,0:T(8,128)(2,1)S(1)} %get-tuple-element.20), channel_id=1, source_target_pairs={{4,0},{8,4},{12,8},{16,12},{20,16},{24,20},{28,24},{32,28},{36,32}... | collective-permute-start | bytes 786440 | tf_op jit(solution)/shard_map/ppermute | solution.py:135
  20.2 9.2 %collective-permute-start.4 = (bf16[64,2048]{1,0:T(8,128)(2,1)S(1)}, bf16[64,2048]{1,0:T(8,128)(2,1)S(1)}, u32[]{:S(2)}, u32[]{:S(2)}) collective-permute-start(bf16[64,2048]{1,0:T(8,128)(2,1)S(1)} %get-tuple-element.21), channel_id=1, source_target_pairs={{0,4},{4,8},{8,12},{12,16},{16,20},{20,24},{24,28},{28,32},{32,36}... | collective-permute-start | bytes 786440 | tf_op jit(solution)/shard_map/ppermute | solution.py:134
  24.8 10.7 %collective-permute-start.1 = (bf16[2,64,4096]{2,1,0:T(8,128)(2,1)S(1)}, bf16[2,64,4096]{2,1,0:T(8,128)(2,1)}, u32[]{:S(2)}, u32[]{:S(2)}) collective-permute-start(bf16[2,64,4096]{2,1,0:T(8,128)(2,1)S(1)} %pad_maximum_fusion), channel_id=1, source_target_pairs={{0,1},{1,0},{2,3},{3,2},{4,5},{5,4},{6,7},{7,6},{8,9},{9,8},{10,11... | collective-permute-start | bytes 3145736 | tf_op jit(solution)/shard_map/ppermute | solution.py:136
  25.0 6.6 %copy-start.3 = (bf16[64,2048]{1,0:T(8,128)(2,1)}, bf16[64,2048]{1,0:T(8,128)(2,1)S(1)}, u32[]{:S(2)}) copy-start(bf16[64,2048]{1,0:T(8,128)(2,1)S(1)} %collective-permute-done.3.hi_ref) | copy-start | bytes 786436
  28.2 3.4 %copy-start.4 = (bf16[64,2048]{1,0:T(8,128)(2,1)}, bf16[64,2048]{1,0:T(8,128)(2,1)S(1)}, u32[]{:S(2)}) copy-start(bf16[64,2048]{1,0:T(8,128)(2,1)S(1)} %collective-permute-done.5.fhi_ref) | copy-start | bytes 786436
  29.4 2.2 %copy-start.5 = (bf16[64,2048]{1,0:T(8,128)(2,1)}, bf16[64,2048]{1,0:T(8,128)(2,1)S(1)}, u32[]{:S(2)}) copy-start(bf16[64,2048]{1,0:T(8,128)(2,1)S(1)} %collective-permute-done.4.flo_ref) | copy-start | bytes 786436
  29.4 2.3 %copy-start.2 = (bf16[27,128,128]{2,1,0:T(8,128)(2,1)S(1)}, bf16[27,128,128]{2,1,0:T(8,128)(2,1)}, u32[]{:S(2)}) copy-start(bf16[27,128,128]{2,1,0:T(8,128)(2,1)} %param.4) | copy-start | bytes 2654212
  31.6 4.0 %collective-permute-start.6 = (bf16[4,64,2048]{2,1,0:T(8,128)(2,1)}, bf16[4,64,2048]{2,1,0:T(8,128)(2,1)}, u32[]{:S(2)}, u32[]{:S(2)}) collective-permute-start(bf16[4,64,2048]{2,1,0:T(8,128)(2,1)} %pad_maximum_fusion.1), channel_id=1, source_target_pairs={{0,1},{1,0},{2,3},{3,2},{4,5},{5,4},{6,7},{7,6},{8,9},{9,8},{10,11... | collective-permute-start | bytes 3145736 | tf_op jit(solution)/shard_map/ppermute | solution.py:137

commit v18 on v16

--- a/solution.py
+++ b/solution.py
@@ -130,10 +130,6 @@
     got_far = lax.ppermute(both, far, swap)
     low = lax.ppermute(both[:, -width:], "gz", up)
     high = lax.ppermute(both[:, :width], "gz", down)
-    far_low = lax.ppermute(got_far[:, -width:], "gz", up)
-    far_high = lax.ppermute(got_far[:, :width], "gz", down)
-    got_near = lax.ppermute(jnp.stack([both, got_far]), near, swap)
-    halos = lax.ppermute(jnp.stack([low, high, far_low, far_high]), near, swap)
     groups = 4
     order = [jnp.bitwise_xor(my_group, j) for j in range(groups)]
     cin = groups * in_local
@@ -145,6 +141,11 @@
     weight_rows = lax.dynamic_slice_in_dim(weight, my_group * in_local, in_local, 1)
     weight_rows = by_group(weight_rows, order, out_local, 2)
     wb = weight_rows[::-1].reshape(9, 3 * in_local, cout)
+    got_far, wf, wb = lax.optimization_barrier((got_far, wf, wb))
+    far_low = lax.ppermute(got_far[:, -width:], "gz", up)
+    far_high = lax.ppermute(got_far[:, :width], "gz", down)
+    got_near = lax.ppermute(jnp.stack([both, got_far]), near, swap)
+    halos = lax.ppermute(jnp.stack([low, high, far_low, far_high]), near, swap)
     out, ing, wg = fused(
         both, got_far, got_near, low, high, far_low, far_high, halos, wf, wb, planes_local, width
     )

time: 72.9 us -> 76.5 us (1.049)
  blocking collectives: 22.1 us -> 25.3 us
  waiting for transfers between devices: 9.53 us -> 6.81 us
  local copies, waits for them, and re-layouts: 8.11 us -> 10.8 us
    ppermute x1, waiting for transfers between devices: 5.09 us -> 0.01 us  [body(): got_far = lax.ppermute(both, far, swap)]
    all_to_all x1, blocking collectives: 22.1 us -> 25.3 us  [summed_on_arrival(): lax.all_to_all(blocks, axis, split_axis=0, concat_axis=0, tiled=True)]
    ppermute x1, waiting for transfers between devices: 0.01 us -> 2.63 us  [body(): halos = lax.ppermute(jnp.stack([low, high, far_low, far_high]), near, swap)]
    concatenate x3, other arithmetic: 1.54 us -> 2.72 us  [by_group(): jnp.concatenate([lax.dynamic_slice_in_dim(array, group * size, size, dim)...]
    another operation x1, other arithmetic: 2.18 us -> 1.18 us  [body(): halos = lax.ppermute(jnp.stack([low, high, far_low, far_high]), near, swap)]
    unnamed x20 -> x28, local copies, waits for them, and re-layouts: 3.33 us -> 4.32 us
    dynamic_slice x2, local copies, waits for them, and re-layouts: 2.48 us -> 3.44 us  [by_group(): lax.dynamic_slice_in_dim(array, group * size, size, dim)]
    slice x1, local copies, waits for them, and re-layouts: 0.03 us -> 0.82 us  [body(): high = lax.ppermute(both[:, :width], 'gz', down)]
  transfers between devices with their start and end apart: 7 -> 7, of which waited for: 3 -> 3; matrix products, arithmetic and copies ran while one was open for 9% -> 11% of each run, Pallas kernels for 0% -> 0%
where the time goes in v18:
time: 76.5 us; the launch traced here: 76.1 us
  blocking collectives  25.3 us (33%)
  starting transfers between devices  16.8 us (22%)
  local copies, waits for them, and re-layouts  10.8 us (14%)
  Pallas kernels  10.3 us (13%)
  waiting for transfers between devices  6.81 us (9%)
  other arithmetic  5.1 us (7%)
  between operations  0.91 us (1%)
    all_to_all x1, blocking collectives, summed_on_arrival(): lax.all_to_all(blocks, axis, split_axis=0, concat_axis=0, tiled=True)  25.3 us
    pallas_call x1, Pallas kernels, fused(): pl.pallas_call(fused_kernel, out_shape=(jax.ShapeDtypeStruct((loc, planes...  10.3 us
    ppermute x1, starting transfers between devices, body(): low = lax.ppermute(both[:, -width:], 'gz', up)  5.25 us
    ppermute x1, starting transfers between devices, body(): far_low = lax.ppermute(got_far[:, -width:], 'gz', up)  4.56 us
    unnamed x28, local copies, waits for them, and re-layouts  4.32 us
    ppermute x1, starting transfers between devices, body(): got_far = lax.ppermute(both, far, swap)  4.07 us
    dynamic_slice x2, local copies, waits for them, and re-layouts, by_group(): lax.dynamic_slice_in_dim(array, group * size, size, dim)  3.44 us
    ppermute x1, waiting for transfers between devices, body(): far_high = lax.ppermute(got_far[:, :width], 'gz', down)  2.99 us
  transfers between devices with their start and end apart: 7, of which 3 were waited for; matrix products, arithmetic and copies ran while one was open for 11% of the time, Pallas kernels for 0%

profile of v18, /device:TPU:0, one launch (start us, length us, event | category | flops | bytes accessed | tf_op | source)
XLA Modules:
  0.0 76.1 jit_solution(11442427110072039782)
XLA Ops:
  0.6 1.0 %constant_dynamic-update-slice_fusion.1 = bf16[64,2,16,128]{3,2,1,0:T(8,128)(2,1)S(1)} fusion(bf16[32,2,16,128]{3,2,1,0:T(8,128)(2,1)} %param.3), kind=kLoop, calls=%fused_computation.9 | loop fusion | bytes 524288
  1.6 1.0 %constant_dynamic-update-slice_fusion = bf16[64,2,16,128]{3,2,1,0:T(8,128)(2,1)S(1)} fusion(bf16[64,2,16,128]{3,2,1,0:T(8,128)(2,1)S(1)} %constant_dynamic-update-slice_fusion.1, bf16[32,2,16,128]{3,2,1,0:T(8,128)(2,1)} %param.5), kind=kLoop, calls=%fused_computation.8 | loop fusion | bytes 524288 | tf_op jit(solution)/shard_map/concatenate | solution.py:125
  2.6 0.2 copy.56
  2.8 0.0 copy-start
  2.8 0.0 copy-start.2
  2.8 4.1 %collective-permute-start = (bf16[64,4096]{1,0:T(8,128)(2,1)S(1)}, bf16[64,4096]{1,0:T(8,128)(2,1)S(1)}, u32[]{:S(2)}, u32[]{:S(2)}) collective-permute-start(bf16[64,4096]{1,0:T(8,128)(2,1)S(1)} %bitcast.21), channel_id=1, source_target_pairs={{0,2},{2,0},{1,3},{3,1},{4,6},{6,4},{5,7},{7,5},{8,10},{10,8},{9,1... | collective-permute-start | bytes 1572872 | tf_op jit(solution)/shard_map/ppermute | solution.py:130
  6.9 0.8 %fusion.1 = (bf16[64,2048]{1,0:T(8,128)(2,1)}, bf16[64,2048]{1,0:T(8,128)(2,1)}) fusion(bf16[64,4096]{1,0:T(8,128)(2,1)S(1)} %bitcast.22), kind=kLoop, calls=%fused_computation.22 | loop fusion | bytes 1048576 | tf_op jit(solution)/shard_map/slice | solution.py:132
  7.7 1.3 %collective-permute-start.3 = (bf16[64,2048]{1,0:T(8,128)(2,1)}, bf16[64,2048]{1,0:T(8,128)(2,1)S(1)}, u32[]{:S(2)}, u32[]{:S(2)}) collective-permute-start(bf16[64,2048]{1,0:T(8,128)(2,1)} %get-tuple-element.28), channel_id=1, source_target_pairs={{4,0},{8,4},{12,8},{16,12},{20,16},{24,20},{28,24},{32,28},{36,32}... | collective-permute-start | bytes 786440 | tf_op jit(solution)/shard_map/ppermute | solution.py:132
  9.0 5.3 %collective-permute-start.2 = (bf16[64,2048]{1,0:T(8,128)(2,1)}, bf16[64,2048]{1,0:T(8,128)(2,1)}, u32[]{:S(2)}, u32[]{:S(2)}) collective-permute-start(bf16[64,2048]{1,0:T(8,128)(2,1)} %get-tuple-element.29), channel_id=1, source_target_pairs={{0,4},{4,8},{8,12},{12,16},{16,20},{20,24},{24,28},{28,32},{32,36}... | collective-permute-start | bytes 786440 | tf_op jit(solution)/shard_map/ppermute | solution.py:131
  14.3 0.2 stack_reshape.3
  14.5 0.0 copy-done
  14.5 0.0 copy-done.2
  14.5 2.1 %constant_dynamic-slice_fusion.6 = (bf16[27,32,32]{2,1,0:T(8,128)(2,1)}, bf16[27,32,32]{2,1,0:T(8,128)(2,1)}, bf16[27,32,32]{2,1,0:T(8,128)(2,1)}, bf16[27,32,32...) fusion(bf16[27,128,128]{2,1,0:T(8,128)(2,1)S(1)} %copy-done.2, ...), kind=kLoop, calls=%fused_computation.16 | loop fusion | bytes 774160 | tf_op jit(solution)/shard_map/dynamic_slice | solution.py:114
  16.6 0.2 copy.50
  16.8 0.0 copy-start.8
  16.8 1.5 %pad_maximum_fusion.4 = bf16[27,32,128]{2,1,0:T(8,128)(2,1)S(1)} fusion(bf16[27,32,32]{2,1,0:T(8,128)(2,1)} %get-tuple-element.24, bf16[27,32,32]{2,1,0:T(8,128)(2,1)} %get-tuple-element.25, bf16[27,32,32]{2,1,0:T(8,128)(2,1)} %get-tuple-element.19, bf16[27,32,32]{2,1,0:T(8,128)(2,1)S(1)} %get-tuple-element.22), kind=kLoop, calls=%fused_computation.6 | loop fusion | flops 884736 | bytes 442368 | tf_op jit(solution)/shard_map/concatenate | solution.py:113
  18.3 0.7 rev.3
  19.0 0.0 copy-done.9
  19.0 0.2 copy.52
  19.2 0.0 copy-done.8
  19.2 0.2 copy.51
  19.4 0.2 copy.53
  19.5 1.0 %pad_maximum_fusion.3 = bf16[27,128,32]{1,2,0:T(8,128)(2,1)} fusion(bf16[27,32,32]{1,2,0:T(8,128)(2,1)S(1)} %copy.53, bf16[27,32,32]{1,2,0:T(8,128)(2,1)S(1)} %copy.52, bf16[27,32,32]{1,2,0:T(8,128)(2,1)S(1)} %copy.51, bf16[27,32,32]{1,2,0:T(8,128)(2,1)S(1)} %copy.50), kind=kLoop, calls=%fused_computation.5 | loop fusion | flops 884736 | bytes 442368 | tf_op jit(solution)/shard_map/concatenate | solution.py:113
  20.5 0.0 collective-permute-done.far_ref
  20.6 1.3 %collective-permute-start.5 = (bf16[64,2048]{1,0:T(8,128)(2,1)S(1)}, bf16[64,2048]{1,0:T(8,128)(2,1)S(1)}, u32[]{:S(2)}, u32[]{:S(2)}) collective-permute-start(bf16[64,2048]{1,0:T(8,128)(2,1)S(1)} %get-tuple-element.26), channel_id=1, source_target_pairs={{4,0},{8,4},{12,8},{16,12},{20,16},{24,20},{28,24},{32,28},{36,32}... | collective-permute-start | bytes 786440 | tf_op jit(solution)/shard_map/ppermute | solution.py:146
  21.9 4.6 %collective-permute-start.4 = (bf16[64,2048]{1,0:T(8,128)(2,1)S(1)}, bf16[64,2048]{1,0:T(8,128)(2,1)S(1)}, u32[]{:S(2)}, u32[]{:S(2)}) collective-permute-start(bf16[64,2048]{1,0:T(8,128)(2,1)S(1)} %get-tuple-element.27), channel_id=1, source_target_pairs={{0,4},{4,8},{8,12},{12,16},{16,20},{20,24},{24,28},{28,32},{32,36}... | collective-permute-start | bytes 786440 | tf_op jit(solution)/shard_map/ppermute | solution.py:145
  26.4 0.1 pad_maximum_fusion
  26.5 0.0 copy-done.1
  26.6 0.1 collective-permute-start.1
  26.6 0.0 collective-permute-done.3.hi_ref
  26.7 0.0 collective-permute-done.2.lo_ref
  26.7 3.0 %collective-permute-done.5.fhi_ref = bf16[64,2048]{1,0:T(8,128)(2,1)S(1)} collective-permute-done((bf16[64,2048]{1,0:T(8,128)(2,1)S(1)}, bf16[64,2048]{1,0:T(8,128)(2,1)S(1)}, u32[]{:S(2)}, u32[]{:S(2)}) %collective-permute-start.5) | collective-permute-done | bytes 262176 | tf_op jit(solution)/shard_map/ppermute | solution.py:146
  29.7 1.2 %collective-permute-done.4.flo_ref = bf16[64,2048]{1,0:T(8,128)(2,1)S(1)} collective-permute-done((bf16[64,2048]{1,0:T(8,128)(2,1)S(1)}, bf16[64,2048]{1,0:T(8,128)(2,1)S(1)}, u32[]{:S(2)}, u32[]{:S(2)}) %collective-permute-start.4) | collective-permute-done | bytes 262176 | tf_op jit(solution)/shard_map/ppermute | solution.py:145
  30.9 1.2 %pad_maximum_fusion.1 = bf16[4,64,2048]{2,1,0:T(8,128)(2,1)S(1)} fusion(bf16[1,64,2048]{2,1,0:T(8,128)(2,1)S(1)} %bitcast.28, bf16[1,64,2048]{2,1,0:T(8,128)(2,1)S(1)} %bitcast.29, bf16[1,64,2048]{2,1,0:T(8,128)(2,1)S(1)} %bitcast.27, bf16[1,64,2048]{2,1,0:T(8,128)(2,1)} %bitcast.5), kind=kLoop, calls=%fused_computation.2 | loop fusion | flops 1572864 | bytes 2097152 | tf_op jit(solution)/shard_map/stack | solution.py:148
  32.1 0.3 collective-permute-start.6
  32.3 0.0 collective-permute-done.1.near_ref
  32.4 2.6 %collective-permute-done.6.hal_ref = bf16[4,64,2048]{2,1,0:T(8,128)(2,1)S(1)} collective-permute-done((bf16[4,64,2048]{2,1,0:T(8,128)(2,1)S(1)}, bf16[4,64,2048]{2,1,0:T(8,128)(2,1)S(1)}, u32[]{:S(2)}, u32[]{:S(2)}) %collective-permute-start.6) | collective-permute-done | bytes 1048608 | tf_op jit(solution)/shard_map/ppermute | solution.py:148
  35.0 0.0 copy-done.3
  35.0 1.0 %copy-done.4 = bf16[4,64,2048]{2,1,0:T(8,128)(2,1)} copy-done((bf16[4,64,2048]{2,1,0:T(8,128)(2,1)}, bf16[4,64,2048]{2,1,0:T(8,128)(2,1)S(1)}, u32[]{:S(2)}) %copy-start.4) | copy-done | bytes 1048600
  36.0 10.3 %shard_map.58 = (bf16[32,2,16,128]{3,2,1,0:T(8,128)(2,1)}, bf16[32,2,16,128]{3,2,1,0:T(8,128)(2,1)}, bf16[27,128,32]{2,1,0:T(8,128)(2,1)}) custom-call(bf16[64,4096]{1,0:T(8,128)(2,1)} %bitcast.23, bf16[64,4096]{1,0:T(8,128)(2,1)} %copy-done.1, bf16[2,64,4096]{2,1,0:T(8,128)(2,1)} %copy-done.3, bf16[64,2048]{1,0:T(8,128)(2,1)} %collective-permute-done.2.lo_ref, ...), custom_call_target="tpu_custom_call" | custom-call | tf_op jit(solution)/shard_map/pallas_call | solution.py:98
  46.3 1.3 %constant_dynamic-slice_fusion.3 = (bf16[27,32,32]{2,1,0:T(8,128)(2,1)S(1)}, bf16[27,32,32]{2,1,0:T(8,128)(2,1)S(1)}, bf16[27,32,32]{2,1,0:T(8,128)(2,1)S(1)}, bf16[27,32,32]{2,1,0:T(8,128)(2,1)S(1)}) fusion(bf16[27,128,32]{2,1,0:T(8,128)(2,1)} %get-tuple-element.14, s32[]{:T(128)S(6)} %select_n.30, s32[]{:T(128)S(6)} %select_n.36, s32[]{:T(128)S(6)} %select_n.34, ...), kind=kLoop, calls=%fused_computation.13 | loop fusion | bytes 442384 | tf_op jit(solution)/shard_map/dynamic_slice | solution.py:114
  47.6 0.2 pad_maximum_fusion.2
  47.9 0.3 copy.49
  48.2 0.7 reshape.26
  48.9 25.3 %all_to_all.5 = bf16[32,2,1728]{2,1,0:T(2,128)(2,1)S(1)} all-to-all(bf16[32,2,1728]{2,1,0:T(2,128)(2,1)S(1)} %reshape.26), channel_id=1, replica_groups=mesh['gz'=32,'ch_0'=2,'ch_1'=2] {'gz'}, dimensions={0} | all-to-all | bytes 442368 | tf_op jit(solution)/shard_map/all_to_all | solution.py:19
  74.2 0.8 reshape.27
  75.0 0.5 convert_reduce_fusion
  75.5 0.6 broadcast_multiply_fusion
  (11 shorter events, 0.1 us)
Async XLA Ops:
  2.8 11.7 %copy-start = (bf16[8,8,32,128]{3,1,2,0:T(8,128)(2,1)}, bf16[8,8,32,128]{3,1,2,0:T(8,128)(2,1)S(1)}, u32[]{:S(2)}) copy-start(bf16[8,8,32,128]{3,1,2,0:T(8,128)(2,1)S(1)} %copy.56) | copy-start | bytes 1572868
  2.8 11.7 %copy-start.2 = (bf16[27,128,128]{2,1,0:T(8,128)(2,1)S(1)}, bf16[27,128,128]{2,1,0:T(8,128)(2,1)}, u32[]{:S(2)}) copy-start(bf16[27,128,128]{2,1,0:T(8,128)(2,1)} %param.4) | copy-start | bytes 2654212
  2.8 17.7 %collective-permute-start = (bf16[64,4096]{1,0:T(8,128)(2,1)S(1)}, bf16[64,4096]{1,0:T(8,128)(2,1)S(1)}, u32[]{:S(2)}, u32[]{:S(2)}) collective-permute-start(bf16[64,4096]{1,0:T(8,128)(2,1)S(1)} %bitcast.21), channel_id=1, source_target_pairs={{0,2},{2,0},{1,3},{3,1},{4,6},{6,4},{5,7},{7,5},{8,10},{10,8},{9,1... | collective-permute-start | bytes 1572872 | tf_op jit(solution)/shard_map/ppermute | solution.py:130
  7.7 18.9 %collective-permute-start.3 = (bf16[64,2048]{1,0:T(8,128)(2,1)}, bf16[64,2048]{1,0:T(8,128)(2,1)S(1)}, u32[]{:S(2)}, u32[]{:S(2)}) collective-permute-start(bf16[64,2048]{1,0:T(8,128)(2,1)} %get-tuple-element.28), channel_id=1, source_target_pairs={{4,0},{8,4},{12,8},{16,12},{20,16},{24,20},{28,24},{32,28},{36,32}... | collective-permute-start | bytes 786440 | tf_op jit(solution)/shard_map/ppermute | solution.py:132
  9.0 17.7 %collective-permute-start.2 = (bf16[64,2048]{1,0:T(8,128)(2,1)}, bf16[64,2048]{1,0:T(8,128)(2,1)}, u32[]{:S(2)}, u32[]{:S(2)}) collective-permute-start(bf16[64,2048]{1,0:T(8,128)(2,1)} %get-tuple-element.29), channel_id=1, source_target_pairs={{0,4},{4,8},{8,12},{12,16},{16,20},{20,24},{24,28},{28,32},{32,36}... | collective-permute-start | bytes 786440 | tf_op jit(solution)/shard_map/ppermute | solution.py:131
  16.6 2.4 %copy-start.9 = (bf16[27,32,32]{2,1,0:T(8,128)(2,1)S(1)}, bf16[27,32,32]{2,1,0:T(8,128)(2,1)}, u32[]{:S(2)}) copy-start(bf16[27,32,32]{2,1,0:T(8,128)(2,1)} %get-tuple-element.20) | copy-start | bytes 165892
  16.8 2.4 %copy-start.8 = (bf16[27,32,32]{2,1,0:T(8,128)(2,1)S(1)}, bf16[27,32,32]{2,1,0:T(8,128)(2,1)}, u32[]{:S(2)}) copy-start(bf16[27,32,32]{2,1,0:T(8,128)(2,1)} %get-tuple-element.21) | copy-start | bytes 165892
  20.5 6.0 %copy-start.1 = (bf16[64,4096]{1,0:T(8,128)(2,1)}, bf16[64,4096]{1,0:T(8,128)(2,1)S(1)}, u32[]{:S(2)}) copy-start(bf16[64,4096]{1,0:T(8,128)(2,1)S(1)} %collective-permute-done.far_ref) | copy-start | bytes 1572868
  20.6 9.1 %collective-permute-start.5 = (bf16[64,2048]{1,0:T(8,128)(2,1)S(1)}, bf16[64,2048]{1,0:T(8,128)(2,1)S(1)}, u32[]{:S(2)}, u32[]{:S(2)}) collective-permute-start(bf16[64,2048]{1,0:T(8,128)(2,1)S(1)} %get-tuple-element.26), channel_id=1, source_target_pairs={{4,0},{8,4},{12,8},{16,12},{20,16},{24,20},{28,24},{32,28},{36,32}... | collective-permute-start | bytes 786440 | tf_op jit(solution)/shard_map/ppermute | solution.py:146
  21.9 9.0 %collective-permute-start.4 = (bf16[64,2048]{1,0:T(8,128)(2,1)S(1)}, bf16[64,2048]{1,0:T(8,128)(2,1)S(1)}, u32[]{:S(2)}, u32[]{:S(2)}) collective-permute-start(bf16[64,2048]{1,0:T(8,128)(2,1)S(1)} %get-tuple-element.27), channel_id=1, source_target_pairs={{0,4},{4,8},{8,12},{12,16},{16,20},{20,24},{24,28},{28,32},{32,36}... | collective-permute-start | bytes 786440 | tf_op jit(solution)/shard_map/ppermute | solution.py:145
  26.6 5.8 %collective-permute-start.1 = (bf16[2,64,4096]{2,1,0:T(8,128)(2,1)S(1)}, bf16[2,64,4096]{2,1,0:T(8,128)(2,1)S(1)}, u32[]{:S(2)}, u32[]{:S(2)}) collective-permute-start(bf16[2,64,4096]{2,1,0:T(8,128)(2,1)S(1)} %pad_maximum_fusion), channel_id=1, source_target_pairs={{0,1},{1,0},{2,3},{3,2},{4,5},{5,4},{6,7},{7,6},{8,9},{9,8},{10,11... | collective-permute-start | bytes 3145736 | tf_op jit(solution)/shard_map/ppermute | solution.py:147
  26.7 5.4 %copy-start.5 = (bf16[64,2048]{1,0:T(8,128)(2,1)}, bf16[64,2048]{1,0:T(8,128)(2,1)S(1)}, u32[]{:S(2)}) copy-start(bf16[64,2048]{1,0:T(8,128)(2,1)S(1)} %collective-permute-done.3.hi_ref) | copy-start | bytes 786436
  29.7 2.4 %copy-start.6 = (bf16[64,2048]{1,0:T(8,128)(2,1)}, bf16[64,2048]{1,0:T(8,128)(2,1)S(1)}, u32[]{:S(2)}) copy-start(bf16[64,2048]{1,0:T(8,128)(2,1)S(1)} %collective-permute-done.5.fhi_ref) | copy-start | bytes 786436
  30.9 1.2 %copy-start.7 = (bf16[64,2048]{1,0:T(8,128)(2,1)}, bf16[64,2048]{1,0:T(8,128)(2,1)S(1)}, u32[]{:S(2)}) copy-start(bf16[64,2048]{1,0:T(8,128)(2,1)S(1)} %collective-permute-done.4.flo_ref) | copy-start | bytes 786436
  32.1 2.9 %collective-permute-start.6 = (bf16[4,64,2048]{2,1,0:T(8,128)(2,1)S(1)}, bf16[4,64,2048]{2,1,0:T(8,128)(2,1)S(1)}, u32[]{:S(2)}, u32[]{:S(2)}) collective-permute-start(bf16[4,64,2048]{2,1,0:T(8,128)(2,1)S(1)} %pad_maximum_fusion.1), channel_id=1, source_target_pairs={{0,1},{1,0},{2,3},{3,2},{4,5},{5,4},{6,7},{7,6},{8,9},{9,8},{10,11... | collective-permute-start | bytes 3145736 | tf_op jit(solution)/shard_map/ppermute | solution.py:148
  32.3 2.6 %copy-start.3 = (bf16[2,64,4096]{2,1,0:T(8,128)(2,1)}, bf16[2,64,4096]{2,1,0:T(8,128)(2,1)S(1)}, u32[]{:S(2)}) copy-start(bf16[2,64,4096]{2,1,0:T(8,128)(2,1)S(1)} %collective-permute-done.1.near_ref) | copy-start | bytes 3145732
  35.0 1.0 %copy-start.4 = (bf16[4,64,2048]{2,1,0:T(8,128)(2,1)}, bf16[4,64,2048]{2,1,0:T(8,128)(2,1)S(1)}, u32[]{:S(2)}) copy-start(bf16[4,64,2048]{2,1,0:T(8,128)(2,1)S(1)} %collective-permute-done.6.hal_ref) | copy-start | bytes 3145732
